TPU v7x, 512 devices: a whole 4x4x16 slice. The times are simulated.
512 devices in a mesh: sec: 2 (over z_hi), gx: 16 (over z_lo, core), gy: 16 (over x, y).
Axes of the slice: x: 4, y: 4, z: 16 (z_hi: 2, z_lo: 8; z = z_hi * 8 + z_lo), core: 2. Of those that a mesh axis runs over, the one named last changes fastest.
Arguments:
- terminal: float32 [4, 16, 256, 4096], P('sec', None, 'gx', 'gy'), may hold values from -6 to 6
- forward_temp: bfloat16 [2, 4, 16, 256, 4096], P(None, 'sec', None, 'gx', 'gy'), may hold values from -6 to 6
- conductivity: float32 [16, 256, 4096], P(None, 'gx', 'gy'), may hold values from 0.02 to 0.15
- velocity: float32 [2, 16, 256, 4096], P(None, None, 'gx', 'gy'), may hold values from -0.3 to 0.3
- fixed_mask: int32 [16, 256, 4096], P(None, 'gx', 'gy'), may hold values 0 or 1
- wells: int32 [4, 8, 3], P('sec'), may hold values from 0 to 4095, as said below
- misfit: float32 [2, 4, 8], P(None, 'sec'), may hold values from -12 to 12
- head_gradient: bfloat16 [2, 16, 256, 4096], P('sec', None, 'gx', 'gy'), may hold values from -6 to 6
- blocks: bfloat16 [32, 7, 128, 128], P('gy'), may hold values from -0.1875 to 0.1875
- block_cols: int32 [32, 7], P('gy'), may hold values from 0 to 31, as said below
Outputs:
- head_adjoint: float32 [2, 16, 256, 4096], P('sec', None, 'gx', 'gy')
- sensitivity: float32 [16, 256, 4096], P(None, 'gx', 'gy')
Inputs may be any that keep to these rules, and one draw needn't show every extreme that they name: `wells`: each row is one cell (z, x, y) with z < 16, x < 256, y < 4096; the first test observes the cells (0, 0, 0) and (15, 255, 4095). `block_cols`: row r lists 7 different block columns, the first of which is r.
All inputs are finite; a program needn't handle non-finite values. No bound on the sum of `fixed_mask` on one device may be relied on, other than what follows from the above.
Results may differ from a plain program's by a relative error of at most 0.0029.
Values may be sent and summed in bfloat16 or wider, within the bound.
No kernel may reach another device: no remote copies, remote signals or barrier semaphores. Data moves between devices by JAX's collectives and lax.ppermute only.
A program may use at most 64 MiB of HBM per device.

v0:
```python
import jax
import jax.numpy as jnp
from jax import lax
from jax.sharding import PartitionSpec as P


def extended(cells, sides, width):
    for axis, dim in sides:
        count = lax.axis_size(axis)
        ends = count - 1
        head = lax.slice_in_dim(cells, 0, width, axis=dim)
        tail = lax.slice_in_dim(cells, cells.shape[dim] - width, cells.shape[dim], axis=dim)
        cells = jnp.concatenate(
            [
                lax.ppermute(tail, axis, [(i, (i + 1) % count) for i in range(ends)]),
                cells,
                lax.ppermute(head, axis, [((i + 1) % count, i) for i in range(ends)]),
            ],
            axis=dim,
        )
    return cells


def shifted(padded):
    lead = [(0, 0)] * (padded.ndim - 3)
    deeper = jnp.pad(padded, lead + [(1, 1), (0, 0), (0, 0)])
    centre = deeper[..., 1:-1, 1:-1, 1:-1]
    beside_all = [
        deeper[..., 2:, 1:-1, 1:-1],
        deeper[..., :-2, 1:-1, 1:-1],
        deeper[..., 1:-1, 2:, 1:-1],
        deeper[..., 1:-1, :-2, 1:-1],
        deeper[..., 1:-1, 1:-1, 2:],
        deeper[..., 1:-1, 1:-1, :-2],
    ]
    return (centre, beside_all)


def face_weights(kappa_pad):
    centre, beside_all = shifted(kappa_pad)
    return [
        2.0 * centre * other / jnp.where(centre + other > 0.0, centre + other, 1.0)
        for other in beside_all
    ]


def advance(adjoint_pad, weights, keep, speed_x, speed_y, source):
    centre, beside_all = shifted(adjoint_pad)
    diffusion = weights[0] * (beside_all[0] - centre)
    for face in range(1, 6):
        diffusion = diffusion + weights[face] * (beside_all[face] - centre)
    slope_x = 0.5 * (beside_all[2] - beside_all[3])
    slope_y = 0.5 * (beside_all[4] - beside_all[5])
    updated = keep * (centre + diffusion + speed_x * slope_x + speed_y * slope_y + source)
    return (updated, diffusion, slope_x, slope_y)


def well_sources(wells, misfit_level, layers, rows_x, cols_y, margin):
    start_x = lax.axis_index("gx") * rows_x - margin
    start_y = lax.axis_index("gy") * cols_y - margin
    coord_z = jnp.arange(layers, dtype=jnp.int32)[:, None, None]
    coord_x = (start_x + jnp.arange(rows_x + 2 * margin, dtype=jnp.int32))[None, :, None]
    coord_y = (start_y + jnp.arange(cols_y + 2 * margin, dtype=jnp.int32))[None, None, :]
    well_z = wells[:, :, 0][:, :, None, None, None]
    well_x = wells[:, :, 1][:, :, None, None, None]
    well_y = wells[:, :, 2][:, :, None, None, None]
    matches = (coord_z == well_z) & (coord_x == well_x) & (coord_y == well_y)
    return jnp.sum(jnp.where(matches, misfit_level[:, :, None, None, None], 0.0), axis=1)


def shards(
    terminal,
    forward_temp,
    conductivity,
    velocity,
    fixed_mask,
    wells,
    misfit,
    head_gradient,
    blocks,
    block_cols,
):
    layers, rows_x, cols_y = conductivity.shape
    steps = forward_temp.shape[0]
    keep = 1.0 - fixed_mask.astype(jnp.float32)
    heat_sens = jnp.zeros((layers, rows_x, cols_y), jnp.float32)
    flow_x = jnp.zeros((layers, rows_x, cols_y), jnp.float32)
    flow_y = jnp.zeros((layers, rows_x, cols_y), jnp.float32)
    kappa_pad = extended(conductivity, (("gx", 1), ("gy", 2)), 1)
    weights = face_weights(kappa_pad)
    adjoint = terminal
    for level in reversed(range(steps)):
        padded = extended(adjoint, (("gx", 2), ("gy", 3)), 1)
        source = well_sources(wells, misfit[level], layers, rows_x, cols_y, 0)
        adjoint, diffusion, slope_x, slope_y = advance(
            padded, weights, keep, velocity[0], velocity[1], source
        )
        temper = forward_temp[level].astype(jnp.float32)
        heat_sens = heat_sens + jnp.sum(temper * diffusion, axis=0)
        flow_x = flow_x + jnp.sum(temper * slope_x, axis=0)
        flow_y = flow_y + jnp.sum(temper * slope_y, axis=0)
    summed = lax.psum_scatter(jnp.stack([flow_x, flow_y]), "sec", scatter_dimension=0, tiled=True)
    rounded = summed[0].astype(jnp.bfloat16)
    row_blocks, per_row, block_size, _ = blocks.shape
    piece = lax.all_gather(rounded, "gy", axis=2, tiled=True)
    count = piece.shape[2] // block_size
    split_rows = piece.reshape(layers, rows_x, count, block_size)
    block_ids = jnp.arange(count, dtype=jnp.int32)
    chosen = (block_cols[:, :, None] == block_ids[None, None, :]).astype(jnp.bfloat16)
    portion = jnp.einsum("bkq,zxqj->bkzxj", chosen, split_rows, preferred_element_type=jnp.float32)
    picked = portion.astype(jnp.bfloat16)
    head = jnp.einsum(
        "bkzxj,bkij->zxbi", picked, blocks, preferred_element_type=jnp.float32
    ).reshape(layers, rows_x, cols_y)
    partial_sens = heat_sens + head * head_gradient[0].astype(jnp.float32)
    sensitivity = lax.psum(partial_sens, "sec")
    return (head[None], sensitivity)


def solution(mesh):
    placed = (
        P("sec", None, "gx", "gy"),
        P(None, "sec", None, "gx", "gy"),
        P(None, "gx", "gy"),
        P(None, None, "gx", "gy"),
        P(None, "gx", "gy"),
        P("sec", None, None),
        P(None, "sec", None),
        P("sec", None, "gx", "gy"),
        P("gy", None, None, None),
        P("gy", None),
    )
    return jax.shard_map(
        shards,
        mesh=mesh,
        in_specs=placed,
        out_specs=(P("sec", None, "gx", "gy"), P(None, "gx", "gy")),
        check_vma=False,
    )
```

profile of v0, /device:TPU:1, one launch (start us, length us, event | category | flops | bytes accessed | tf_op | source)
XLA Modules:
  0.0 278.9 jit_solution(739867863807899032)
XLA Ops:
  8.3 4.9 %collective-permute-start.2 = (f32[16,1,256]{2,1,0:T(1,128)S(1)}, f32[16,1,256]{2,1,0:T(1,128)S(1)}, u32[]{:S(2)}, u32[]{:S(2)}) collective-permute-start(f32[16,1,256]{2,1,0:T(1,128)S(1)} %get-tuple-element.29), channel_id=1, source_target_pairs={{0,16},{16,32},{32,48},{48,64},{64,80},{80,96},{96,112},{112,128},... | collective-permute-start | bytes 49160 | tf_op jit(solution)/shard_map/ppermute | solution.py:15
  13.3 5.1 %collective-permute-start.3 = (f32[16,1,256]{2,1,0:T(1,128)S(1)}, f32[16,1,256]{2,1,0:T(1,128)S(1)}, u32[]{:S(2)}, u32[]{:S(2)}) collective-permute-start(f32[16,1,256]{2,1,0:T(1,128)S(1)} %get-tuple-element.30), channel_id=1, source_target_pairs={{16,0},{32,16},{48,32},{64,48},{80,64},{96,80},{112,96},{128,112},... | collective-permute-start | bytes 49160 | tf_op jit(solution)/shard_map/ppermute | solution.py:17
  19.5 1.9 collective-permute-start
  21.4 3.6 %collective-permute-start.1 = (f32[2,16,1,256]{3,2,1,0:T(1,128)S(1)}, f32[2,16,1,256]{3,2,1,0:T(1,128)S(1)}, u32[]{:S(2)}, u32[]{:S(2)}) collective-permute-start(f32[2,16,1,256]{3,2,1,0:T(1,128)S(1)} %get-tuple-element.20), channel_id=1, source_target_pairs={{0,16},{16,32},{32,48},{48,64},{64,80},{80,96},{96,112},{112,128},... | collective-permute-start | bytes 98312 | tf_op jit(solution)/shard_map/ppermute | solution.py:15
  27.5 1.4 collective-permute-start.4
  28.9 1.3 collective-permute-start.5
  31.1 1.5 collective-permute-done.4
  32.6 4.1 %collective-permute-done.5 = f32[16,18,1]{2,1,0:T(8,128)S(1)} collective-permute-done((f32[16,18,1]{2,1,0:T(8,128)S(1)}, f32[16,18,1]{2,1,0:T(8,128)S(1)}, u32[]{:S(2)}, u32[]{:S(2)}) %collective-permute-start.5) | collective-permute-done | bytes 1184 | tf_op jit(solution)/shard_map/ppermute | solution.py:17
  37.4 2.2 collective-permute-start.6
  41.5 6.3 %collective-permute-done.6 = f32[2,16,18,1]{3,2,1,0:T(8,128)S(1)} collective-permute-done((f32[2,16,18,1]{3,2,1,0:T(8,128)S(1)}, f32[2,16,18,1]{3,2,1,0:T(8,128)S(1)}, u32[]{:S(2)}, u32[]{:S(2)}) %collective-permute-start.6) | collective-permute-done | bytes 2336 | tf_op jit(solution)/shard_map/ppermute | solution.py:15
  47.8 3.8 %collective-permute-done.7 = f32[2,16,18,1]{3,2,1,0:T(8,128)S(1)} collective-permute-done((f32[2,16,18,1]{3,2,1,0:T(8,128)S(1)}, f32[2,16,18,1]{3,2,1,0:T(8,128)S(1)}, u32[]{:S(2)}, u32[]{:S(2)}) %collective-permute-start.7) | collective-permute-done | bytes 2336 | tf_op jit(solution)/shard_map/ppermute | solution.py:17
  53.5 3.3 %collective-permute-start.8 = (f32[2,16,1,256]{3,2,1,0:T(1,128)S(1)}, f32[2,16,1,256]{3,2,1,0:T(1,128)S(1)}, u32[]{:S(2)}, u32[]{:S(2)}) collective-permute-start(f32[2,16,1,256]{3,2,1,0:T(1,128)S(1)} %get-tuple-element.15), channel_id=1, source_target_pairs={{16,0},{32,16},{48,32},{64,48},{80,64},{96,80},{112,96},{128,112},... | collective-permute-start | bytes 98312 | tf_op jit(solution)/shard_map/ppermute | solution.py:17
  56.8 3.8 %collective-permute-start.9 = (f32[2,16,1,256]{3,2,1,0:T(1,128)S(1)}, f32[2,16,1,256]{3,2,1,0:T(1,128)S(1)}, u32[]{:S(2)}, u32[]{:S(2)}) collective-permute-start(f32[2,16,1,256]{3,2,1,0:T(1,128)S(1)} %get-tuple-element.16), channel_id=1, source_target_pairs={{0,16},{16,32},{32,48},{48,64},{64,80},{80,96},{96,112},{112,128},... | collective-permute-start | bytes 98312 | tf_op jit(solution)/shard_map/ppermute | solution.py:15
  63.2 5.1 %collective-permute-start.11 = (f32[2,16,18,1]{3,2,1,0:T(8,128)S(1)}, f32[2,16,18,1]{3,2,1,0:T(8,128)S(1)}, u32[]{:S(2)}, u32[]{:S(2)}) collective-permute-start(f32[2,16,18,1]{3,2,1,0:T(8,128)S(1)} %get-tuple-element.12), channel_id=1, source_target_pairs={{0,1},{1,2},{2,3},{3,4},{4,5},{5,6},{6,7},{7,8},{8,9},{9,10},{10,1... | collective-permute-start | bytes 6920 | tf_op jit(solution)/shard_map/ppermute | solution.py:15
  68.9 5.6 %collective-permute-done.10 = f32[2,16,18,1]{3,2,1,0:T(8,128)S(1)} collective-permute-done((f32[2,16,18,1]{3,2,1,0:T(8,128)S(1)}, f32[2,16,18,1]{3,2,1,0:T(8,128)S(1)}, u32[]{:S(2)}, u32[]{:S(2)}) %collective-permute-start.10) | collective-permute-done | bytes 2336 | tf_op jit(solution)/shard_map/ppermute | solution.py:17
  74.5 1.8 collective-permute-done.11
  76.2 1.3 fusion.7
  78.5 59.7 %reduce-scatter.2.cloned.1.call-done = f32[1,16,16,256]{3,2,1,0:T(8,128)} async-done(((f32[2,16,16,256]{3,2,1,0:T(8,128)}), f32[1,16,16,256]{3,2,1,0:T(8,128)}) %reduce-scatter.2.cloned.1.call-update) | async-done | bytes 262160 | tf_op jit(solution)/shard_map/reduce_scatter | solution.py:102
  138.3 1.6 convert_element_type.41
  141.0 1.7 fusion.9
  142.7 52.4 %all-gather.3.cloned.1.call-done = bf16[1,16,16,4096]{3,2,1,0:T(8,128)(2,1)} async-done(((bf16[1,16,16,256]{3,2,1,0:T(8,128)(2,1)}), bf16[1,16,16,4096]{3,2,1,0:T(8,128)(2,1)}) %all-gather.3.cloned.1.call-update) | async-done | bytes 2097168 | tf_op jit(solution)/shard_map/all_gather | solution.py:105
  195.1 2.1 copy.21
  200.7 70.0 %all-reduce.5.cloned.1.call-done = f32[16,16,256]{2,1,0:T(8,128)} async-done(((f32[16,16,256]{2,1,0:T(8,128)}), f32[16,16,256]{2,1,0:T(8,128)}) %all-reduce.5.cloned.1.call-update) | async-done | bytes 262160 | tf_op jit(solution)/shard_map/psum | solution.py:116
  270.7 1.7 copy.26
  (69 shorter events, 18.4 us)
Async XLA Ops:
  7.2 190.6 %copy-start = (bf16[2,7,128,128]{3,2,1,0:T(8,128)(2,1)S(1)}, bf16[2,7,128,128]{3,2,1,0:T(8,128)(2,1)}, u32[]{:S(2)}) copy-start(bf16[2,7,128,128]{3,2,1,0:T(8,128)(2,1)} %param.18) | copy-start | bytes 1376260
  7.2 20.1 %copy-start.2 = (f32[16,16,256]{2,1,0:T(8,128)S(1)}, f32[16,16,256]{2,1,0:T(8,128)}, u32[]{:S(2)}) copy-start(f32[16,16,256]{2,1,0:T(8,128)} %param.12) | copy-start | bytes 786436
  7.2 19.8 %copy-start.7 = (s32[16,16,256]{2,1,0:T(8,128)S(1)}, s32[16,16,256]{2,1,0:T(8,128)}, u32[]{:S(2)}) copy-start(s32[16,16,256]{2,1,0:T(8,128)} %param.14) | copy-start | bytes 786436
  7.2 20.1 %copy-start.10 = (f32[2,2,8]{2,1,0:T(2,128)S(1)}, f32[2,2,8]{2,1,0:T(2,128)}, u32[]{:S(2)}) copy-start(f32[2,2,8]{2,1,0:T(2,128)} %param.16) | copy-start | bytes 388
  7.2 131.1 %reduce-scatter.2.cloned.1.call-start = ((), (), s32[]{:S(2)}) async-start(), calls=%async_computation.1 | async-start | bytes 786432 | tf_op jit(solution)/shard_map/reduce_scatter | solution.py:102
  8.3 18.9 %collective-permute-start.2 = (f32[16,1,256]{2,1,0:T(1,128)S(1)}, f32[16,1,256]{2,1,0:T(1,128)S(1)}, u32[]{:S(2)}, u32[]{:S(2)}) collective-permute-start(f32[16,1,256]{2,1,0:T(1,128)S(1)} %get-tuple-element.29), channel_id=1, source_target_pairs={{0,16},{16,32},{32,48},{48,64},{64,80},{80,96},{96,112},{112,128},... | collective-permute-start | bytes 49160 | tf_op jit(solution)/shard_map/ppermute | solution.py:15
  13.3 14.0 %collective-permute-start.3 = (f32[16,1,256]{2,1,0:T(1,128)S(1)}, f32[16,1,256]{2,1,0:T(1,128)S(1)}, u32[]{:S(2)}, u32[]{:S(2)}) collective-permute-start(f32[16,1,256]{2,1,0:T(1,128)S(1)} %get-tuple-element.30), channel_id=1, source_target_pairs={{16,0},{32,16},{48,32},{64,48},{80,64},{96,80},{112,96},{128,112},... | collective-permute-start | bytes 49160 | tf_op jit(solution)/shard_map/ppermute | solution.py:17
  19.5 17.6 %collective-permute-start = (f32[2,16,1,256]{3,2,1,0:T(1,128)S(1)}, f32[2,16,1,256]{3,2,1,0:T(1,128)S(1)}, u32[]{:S(2)}, u32[]{:S(2)}) collective-permute-start(f32[2,16,1,256]{3,2,1,0:T(1,128)S(1)} %get-tuple-element.19), channel_id=1, source_target_pairs={{16,0},{32,16},{48,32},{64,48},{80,64},{96,80},{112,96},{128,112},... | collective-permute-start | bytes 98312 | tf_op jit(solution)/shard_map/ppermute | solution.py:17
  21.4 15.7 %collective-permute-start.1 = (f32[2,16,1,256]{3,2,1,0:T(1,128)S(1)}, f32[2,16,1,256]{3,2,1,0:T(1,128)S(1)}, u32[]{:S(2)}, u32[]{:S(2)}) collective-permute-start(f32[2,16,1,256]{3,2,1,0:T(1,128)S(1)} %get-tuple-element.20), channel_id=1, source_target_pairs={{0,16},{16,32},{32,48},{48,64},{64,80},{80,96},{96,112},{112,128},... | collective-permute-start | bytes 98312 | tf_op jit(solution)/shard_map/ppermute | solution.py:15
  27.4 9.7 %copy-start.1 = (f32[2,16,16,256]{3,2,1,0:T(8,128)S(1)}, f32[2,16,16,256]{3,2,1,0:T(8,128)}, u32[]{:S(2)}) copy-start(f32[2,16,16,256]{3,2,1,0:T(8,128)} %param.10) | copy-start | bytes 1572868
  27.5 5.1 %collective-permute-start.4 = (f32[16,18,1]{2,1,0:T(8,128)S(1)}, f32[16,18,1]{2,1,0:T(8,128)S(1)}, u32[]{:S(2)}, u32[]{:S(2)}) collective-permute-start(f32[16,18,1]{2,1,0:T(8,128)S(1)} %get-tuple-element.22), channel_id=1, source_target_pairs={{0,1},{1,2},{2,3},{3,4},{4,5},{5,6},{6,7},{7,8},{8,9},{9,10},{10,1... | collective-permute-start | bytes 3464 | tf_op jit(solution)/shard_map/ppermute | solution.py:15
  28.9 7.8 %collective-permute-start.5 = (f32[16,18,1]{2,1,0:T(8,128)S(1)}, f32[16,18,1]{2,1,0:T(8,128)S(1)}, u32[]{:S(2)}, u32[]{:S(2)}) collective-permute-start(f32[16,18,1]{2,1,0:T(8,128)S(1)} %get-tuple-element.21), channel_id=1, source_target_pairs={{1,0},{2,1},{3,2},{4,3},{5,4},{6,5},{7,6},{8,7},{9,8},{10,9},{11,1... | collective-permute-start | bytes 3464 | tf_op jit(solution)/shard_map/ppermute | solution.py:17
  37.4 10.4 %collective-permute-start.6 = (f32[2,16,18,1]{3,2,1,0:T(8,128)S(1)}, f32[2,16,18,1]{3,2,1,0:T(8,128)S(1)}, u32[]{:S(2)}, u32[]{:S(2)}) collective-permute-start(f32[2,16,18,1]{3,2,1,0:T(8,128)S(1)} %get-tuple-element.14), channel_id=1, source_target_pairs={{0,1},{1,2},{2,3},{3,4},{4,5},{5,6},{6,7},{7,8},{8,9},{9,10},{10,1... | collective-permute-start | bytes 6920 | tf_op jit(solution)/shard_map/ppermute | solution.py:15
  39.6 12.0 %collective-permute-start.7 = (f32[2,16,18,1]{3,2,1,0:T(8,128)S(1)}, f32[2,16,18,1]{3,2,1,0:T(8,128)S(1)}, u32[]{:S(2)}, u32[]{:S(2)}) collective-permute-start(f32[2,16,18,1]{3,2,1,0:T(8,128)S(1)} %get-tuple-element.13), channel_id=1, source_target_pairs={{1,0},{2,1},{3,2},{4,3},{5,4},{6,5},{7,6},{8,7},{9,8},{10,9},{11,1... | collective-permute-start | bytes 6920 | tf_op jit(solution)/shard_map/ppermute | solution.py:17
  53.5 7.1 %collective-permute-start.8 = (f32[2,16,1,256]{3,2,1,0:T(1,128)S(1)}, f32[2,16,1,256]{3,2,1,0:T(1,128)S(1)}, u32[]{:S(2)}, u32[]{:S(2)}) collective-permute-start(f32[2,16,1,256]{3,2,1,0:T(1,128)S(1)} %get-tuple-element.15), channel_id=1, source_target_pairs={{16,0},{32,16},{48,32},{64,48},{80,64},{96,80},{112,96},{128,112},... | collective-permute-start | bytes 98312 | tf_op jit(solution)/shard_map/ppermute | solution.py:17
  56.8 11.5 %copy-start.3 = (bf16[2,2,16,16,256]{4,3,2,1,0:T(8,128)(2,1)S(1)}, bf16[2,2,16,16,256]{4,3,2,1,0:T(8,128)(2,1)}, u32[]{:S(2)}) copy-start(bf16[2,2,16,16,256]{4,3,2,1,0:T(8,128)(2,1)} %param.11) | copy-start | bytes 1572868
  56.8 4.8 %collective-permute-start.9 = (f32[2,16,1,256]{3,2,1,0:T(1,128)S(1)}, f32[2,16,1,256]{3,2,1,0:T(1,128)S(1)}, u32[]{:S(2)}, u32[]{:S(2)}) collective-permute-start(f32[2,16,1,256]{3,2,1,0:T(1,128)S(1)} %get-tuple-element.16), channel_id=1, source_target_pairs={{0,16},{16,32},{32,48},{48,64},{64,80},{80,96},{96,112},{112,128},... | collective-permute-start | bytes 98312 | tf_op jit(solution)/shard_map/ppermute | solution.py:15
  61.9 12.6 %collective-permute-start.10 = (f32[2,16,18,1]{3,2,1,0:T(8,128)S(1)}, f32[2,16,18,1]{3,2,1,0:T(8,128)S(1)}, u32[]{:S(2)}, u32[]{:S(2)}) collective-permute-start(f32[2,16,18,1]{3,2,1,0:T(8,128)S(1)} %get-tuple-element.11), channel_id=1, source_target_pairs={{1,0},{2,1},{3,2},{4,3},{5,4},{6,5},{7,6},{8,7},{9,8},{10,9},{11,1... | collective-permute-start | bytes 6920 | tf_op jit(solution)/shard_map/ppermute | solution.py:17
  63.2 13.0 %collective-permute-start.11 = (f32[2,16,18,1]{3,2,1,0:T(8,128)S(1)}, f32[2,16,18,1]{3,2,1,0:T(8,128)S(1)}, u32[]{:S(2)}, u32[]{:S(2)}) collective-permute-start(f32[2,16,18,1]{3,2,1,0:T(8,128)S(1)} %get-tuple-element.12), channel_id=1, source_target_pairs={{0,1},{1,2},{2,3},{3,4},{4,5},{5,6},{6,7},{7,8},{8,9},{9,10},{10,1... | collective-permute-start | bytes 6920 | tf_op jit(solution)/shard_map/ppermute | solution.py:15
  78.5 116.6 %all-gather.3.cloned.1.call-start = ((), (), s32[]{:S(2)}) async-start(), calls=%async_computation.3 | async-start | bytes 2228224 | tf_op jit(solution)/shard_map/all_gather | solution.py:105
  139.9 130.8 %all-reduce.5.cloned.1.call-start = ((), (), s32[]{:S(2)}) async-start(), calls=%async_computation.2 | async-start | bytes 524288 | tf_op jit(solution)/shard_map/psum | solution.py:116
  140.0 1.0 copy-start.4
  195.1 2.1 copy-start.9
  197.8 1.0 copy-start.8
  (2 other events, 2.0 us)
Sparse Core Ops, SparseCore 0:
  78.6 59.6 reduce-scatter.1
  141.7 53.3 all-gather.2
  199.7 70.9 all-reduce.4
where the time goes:
time: 280 us; the launch traced here: 279 us
  waiting for transfers between devices  206 us (74%)
  starting transfers between devices  35.4 us (13%)
  between operations  14.1 us (5%)
  other arithmetic  12.9 us (5%)
  local copies, waits for them, and re-layouts  9.19 us (3%)
    psum x1, waiting for transfers between devices, shards(): sensitivity = lax.psum(partial_sens, 'sec')  70 us
    reduce_scatter x1, waiting for transfers between devices, shards(): lax.psum_scatter(jnp.stack([flow_x, flow_y]), 'sec', scatter_dimension=0,...  59.7 us
    all_gather x1, waiting for transfers between devices, shards(): piece = lax.all_gather(rounded, 'gy', axis=2, tiled=True)  52.4 us
    ppermute x6, starting transfers between devices, extended(): lax.ppermute(tail, axis, [(i, (i + 1) % count) for i in range(ends)])  21 us
    ppermute x6, starting transfers between devices, extended(): lax.ppermute(head, axis, [((i + 1) % count, i) for i in range(ends)])  14.3 us
    ppermute x6, waiting for transfers between devices, extended(): lax.ppermute(head, axis, [((i + 1) % count, i) for i in range(ends)])  13.5 us
    ppermute x6, waiting for transfers between devices, extended(): lax.ppermute(tail, axis, [(i, (i + 1) % count) for i in range(ends)])  10.6 us
  transfers between devices with their start and end apart: 15, of which 10 were waited for; matrix products, arithmetic and copies ran while one was open for 3% of the time, Pallas kernels for 0%

commit v1 on v0

--- a/solution.py
+++ b/solution.py
@@ -99,8 +99,11 @@
         heat_sens = heat_sens + jnp.sum(temper * diffusion, axis=0)
         flow_x = flow_x + jnp.sum(temper * slope_x, axis=0)
         flow_y = flow_y + jnp.sum(temper * slope_y, axis=0)
-    summed = lax.psum_scatter(jnp.stack([flow_x, flow_y]), "sec", scatter_dimension=0, tiled=True)
-    rounded = summed[0].astype(jnp.bfloat16)
+    first = lax.axis_index("sec") == 0
+    mine = jnp.where(first, flow_x, flow_y)
+    other = jnp.where(first, flow_y, flow_x)
+    partner = [(0, 1), (1, 0)]
+    rounded = (mine + lax.ppermute(other, "sec", partner)).astype(jnp.bfloat16)
     row_blocks, per_row, block_size, _ = blocks.shape
     piece = lax.all_gather(rounded, "gy", axis=2, tiled=True)
     count = piece.shape[2] // block_size
@@ -113,7 +116,7 @@
         "bkzxj,bkij->zxbi", picked, blocks, preferred_element_type=jnp.float32
     ).reshape(layers, rows_x, cols_y)
     partial_sens = heat_sens + head * head_gradient[0].astype(jnp.float32)
-    sensitivity = lax.psum(partial_sens, "sec")
+    sensitivity = partial_sens + lax.ppermute(partial_sens, "sec", partner)
     return (head[None], sensitivity)
 
 

time: 280 us -> 227 us (0.81)
  the two profiles are of different devices: /device:TPU:1 before, /device:TPU:32 now
where the time goes in v1:
time: 227 us; the launch traced here: 226 us
  waiting for transfers between devices  135 us (59%)
  starting transfers between devices  55.7 us (25%)
  between operations  14.6 us (6%)
  other arithmetic  11.9 us (5%)
  local copies, waits for them, and re-layouts  7.91 us (3%)
    all_gather x1, waiting for transfers between devices, shards(): piece = lax.all_gather(rounded, 'gy', axis=2, tiled=True)  76.5 us
    ppermute x1, waiting for transfers between devices, shards(): sensitivity = partial_sens + lax.ppermute(partial_sens, 'sec', partner)  19.8 us
    ppermute x6, starting transfers between devices, extended(): lax.ppermute(tail, axis, [(i, (i + 1) % count) for i in range(ends)])  16 us
    ppermute x6, waiting for transfers between devices, extended(): lax.ppermute(head, axis, [((i + 1) % count, i) for i in range(ends)])  14.7 us
    ppermute x6, starting transfers between devices, extended(): lax.ppermute(head, axis, [((i + 1) % count, i) for i in range(ends)])  14.7 us
    ppermute x6, waiting for transfers between devices, extended(): lax.ppermute(tail, axis, [(i, (i + 1) % count) for i in range(ends)])  13.8 us
    ppermute x1, starting transfers between devices, shards(): rounded = (mine + lax.ppermute(other, 'sec', partner)).astype(jnp.bfloat16)  13 us
    ppermute x1, starting transfers between devices, shards(): sensitivity = partial_sens + lax.ppermute(partial_sens, 'sec', partner)  11.9 us
  transfers between devices with their start and end apart: 15, of which 10 were waited for; matrix products, arithmetic and copies ran while one was open for 4% of the time, Pallas kernels for 0%

profile of v1, /device:TPU:32, one launch (start us, length us, event | category | flops | bytes accessed | tf_op | source)
XLA Modules:
  0.0 226.1 jit_solution(11138354482306704369)
XLA Ops:
  8.3 1.9 collective-permute-start.2
  10.2 3.6 %collective-permute-start.3 = (f32[16,1,256]{2,1,0:T(1,128)S(1)}, f32[16,1,256]{2,1,0:T(1,128)S(1)}, u32[]{:S(2)}, u32[]{:S(2)}) collective-permute-start(f32[16,1,256]{2,1,0:T(1,128)S(1)} %get-tuple-element.30), channel_id=1, source_target_pairs={{16,0},{32,16},{48,32},{64,48},{80,64},{96,80},{112,96},{128,112},... | collective-permute-start | bytes 49160 | tf_op jit(solution)/shard_map/ppermute | solution.py:17
  15.0 5.1 %collective-permute-start = (f32[2,16,1,256]{3,2,1,0:T(1,128)S(1)}, f32[2,16,1,256]{3,2,1,0:T(1,128)S(1)}, u32[]{:S(2)}, u32[]{:S(2)}) collective-permute-start(f32[2,16,1,256]{3,2,1,0:T(1,128)S(1)} %get-tuple-element.19), channel_id=1, source_target_pairs={{16,0},{32,16},{48,32},{64,48},{80,64},{96,80},{112,96},{128,112},... | collective-permute-start | bytes 98312 | tf_op jit(solution)/shard_map/ppermute | solution.py:17
  20.1 1.9 collective-permute-start.1
  24.4 1.4 collective-permute-start.4
  28.0 3.1 %collective-permute-done.4 = f32[16,18,1]{2,1,0:T(8,128)S(1)} collective-permute-done((f32[16,18,1]{2,1,0:T(8,128)S(1)}, f32[16,18,1]{2,1,0:T(8,128)S(1)}, u32[]{:S(2)}, u32[]{:S(2)}) %collective-permute-start.4) | collective-permute-done | bytes 1184 | tf_op jit(solution)/shard_map/ppermute | solution.py:15
  31.1 4.2 %collective-permute-done.5 = f32[16,18,1]{2,1,0:T(8,128)S(1)} collective-permute-done((f32[16,18,1]{2,1,0:T(8,128)S(1)}, f32[16,18,1]{2,1,0:T(8,128)S(1)}, u32[]{:S(2)}, u32[]{:S(2)}) %collective-permute-start.5) | collective-permute-done | bytes 1184 | tf_op jit(solution)/shard_map/ppermute | solution.py:17
  36.0 2.9 %collective-permute-start.6 = (f32[2,16,18,1]{3,2,1,0:T(8,128)S(1)}, f32[2,16,18,1]{3,2,1,0:T(8,128)S(1)}, u32[]{:S(2)}, u32[]{:S(2)}) collective-permute-start(f32[2,16,18,1]{3,2,1,0:T(8,128)S(1)} %get-tuple-element.14), channel_id=1, source_target_pairs={{0,1},{1,2},{2,3},{3,4},{4,5},{5,6},{6,7},{7,8},{8,9},{9,10},{10,1... | collective-permute-start | bytes 6920 | tf_op jit(solution)/shard_map/ppermute | solution.py:15
  40.8 6.7 %collective-permute-done.6 = f32[2,16,18,1]{3,2,1,0:T(8,128)S(1)} collective-permute-done((f32[2,16,18,1]{3,2,1,0:T(8,128)S(1)}, f32[2,16,18,1]{3,2,1,0:T(8,128)S(1)}, u32[]{:S(2)}, u32[]{:S(2)}) %collective-permute-start.6) | collective-permute-done | bytes 2336 | tf_op jit(solution)/shard_map/ppermute | solution.py:15
  47.5 4.1 %collective-permute-done.7 = f32[2,16,18,1]{3,2,1,0:T(8,128)S(1)} collective-permute-done((f32[2,16,18,1]{3,2,1,0:T(8,128)S(1)}, f32[2,16,18,1]{3,2,1,0:T(8,128)S(1)}, u32[]{:S(2)}, u32[]{:S(2)}) %collective-permute-start.7) | collective-permute-done | bytes 2336 | tf_op jit(solution)/shard_map/ppermute | solution.py:17
  52.4 1.8 add_multiply_fusion
  54.3 1.9 collective-permute-start.8
  56.2 2.4 %collective-permute-start.9 = (f32[2,16,1,256]{3,2,1,0:T(1,128)S(1)}, f32[2,16,1,256]{3,2,1,0:T(1,128)S(1)}, u32[]{:S(2)}, u32[]{:S(2)}) collective-permute-start(f32[2,16,1,256]{3,2,1,0:T(1,128)S(1)} %get-tuple-element.16), channel_id=1, source_target_pairs={{0,16},{16,32},{32,48},{48,64},{64,80},{80,96},{96,112},{112,128},... | collective-permute-start | bytes 98312 | tf_op jit(solution)/shard_map/ppermute | solution.py:15
  58.7 2.8 %collective-permute-done.9 = f32[2,16,1,256]{3,2,1,0:T(1,128)S(1)} collective-permute-done((f32[2,16,1,256]{3,2,1,0:T(1,128)S(1)}, f32[2,16,1,256]{3,2,1,0:T(1,128)S(1)}, u32[]{:S(2)}, u32[]{:S(2)}) %collective-permute-start.9) | collective-permute-done | bytes 32800 | tf_op jit(solution)/shard_map/ppermute | solution.py:15
  61.8 1.4 collective-permute-start.10
  63.2 5.3 %collective-permute-start.11 = (f32[2,16,18,1]{3,2,1,0:T(8,128)S(1)}, f32[2,16,18,1]{3,2,1,0:T(8,128)S(1)}, u32[]{:S(2)}, u32[]{:S(2)}) collective-permute-start(f32[2,16,18,1]{3,2,1,0:T(8,128)S(1)} %get-tuple-element.12), channel_id=1, source_target_pairs={{0,1},{1,2},{2,3},{3,4},{4,5},{5,6},{6,7},{7,8},{8,9},{9,10},{10,1... | collective-permute-start | bytes 6920 | tf_op jit(solution)/shard_map/ppermute | solution.py:15
  69.1 6.4 %collective-permute-done.10 = f32[2,16,18,1]{3,2,1,0:T(8,128)S(1)} collective-permute-done((f32[2,16,18,1]{3,2,1,0:T(8,128)S(1)}, f32[2,16,18,1]{3,2,1,0:T(8,128)S(1)}, u32[]{:S(2)}, u32[]{:S(2)}) %collective-permute-start.10) | collective-permute-done | bytes 2336 | tf_op jit(solution)/shard_map/ppermute | solution.py:17
  78.2 13.0 %collective-permute-start.12 = (f32[16,16,256]{2,1,0:T(8,128)S(1)}, f32[16,16,256]{2,1,0:T(8,128)S(1)}, u32[]{:S(2)}, u32[]{:S(2)}) collective-permute-start(f32[16,16,256]{2,1,0:T(8,128)S(1)} %broadcast_select_fusion), channel_id=1, source_target_pairs={{0,256},{256,0},{1,257},{257,1},{2,258},{258,2},{3,259},{259,3},{4... | collective-permute-start | bytes 786440 | tf_op jit(solution)/shard_map/ppermute | solution.py:106
  91.2 10.4 %collective-permute-done.12 = f32[16,16,256]{2,1,0:T(8,128)S(1)} collective-permute-done((f32[16,16,256]{2,1,0:T(8,128)S(1)}, f32[16,16,256]{2,1,0:T(8,128)S(1)}, u32[]{:S(2)}, u32[]{:S(2)}) %collective-permute-start.12) | collective-permute-done | bytes 262176 | tf_op jit(solution)/shard_map/ppermute | solution.py:106
  103.8 1.7 fusion.9
  105.5 76.5 %all-gather.2.cloned.1.call-done = bf16[16,16,4096]{2,1,0:T(8,128)(2,1)} async-done(((bf16[16,16,256]{2,1,0:T(8,128)(2,1)}), bf16[16,16,4096]{2,1,0:T(8,128)(2,1)}) %all-gather.2.cloned.1.call-update) | async-done | bytes 2097168 | tf_op jit(solution)/shard_map/all_gather | solution.py:108
  181.9 2.1 copy.21
  185.7 11.9 %collective-permute-start.13 = (f32[16,16,256]{2,1,0:T(8,128)S(1)}, f32[16,16,256]{2,1,0:T(8,128)S(1)}, u32[]{:S(2)}, u32[]{:S(2)}) collective-permute-start(f32[16,16,256]{2,1,0:T(8,128)S(1)} %fusion.43), channel_id=1, source_target_pairs={{0,256},{256,0},{1,257},{257,1},{2,258},{258,2},{3,259},{259,3},{4... | collective-permute-start | bytes 786440 | tf_op jit(solution)/shard_map/ppermute | solution.py:119
  198.7 19.8 %collective-permute-done.13 = f32[16,16,256]{2,1,0:T(8,128)S(1)} collective-permute-done((f32[16,16,256]{2,1,0:T(8,128)S(1)}, f32[16,16,256]{2,1,0:T(8,128)S(1)}, u32[]{:S(2)}, u32[]{:S(2)}) %collective-permute-start.13) | collective-permute-done | bytes 262176 | tf_op jit(solution)/shard_map/ppermute | solution.py:119
  (87 shorter events, 19.0 us)
Async XLA Ops:
  7.2 177.4 %copy-start = (bf16[2,7,128,128]{3,2,1,0:T(8,128)(2,1)S(1)}, bf16[2,7,128,128]{3,2,1,0:T(8,128)(2,1)}, u32[]{:S(2)}) copy-start(bf16[2,7,128,128]{3,2,1,0:T(8,128)(2,1)} %param.18) | copy-start | bytes 1376260
  7.2 17.0 %copy-start.2 = (f32[16,16,256]{2,1,0:T(8,128)S(1)}, f32[16,16,256]{2,1,0:T(8,128)}, u32[]{:S(2)}) copy-start(f32[16,16,256]{2,1,0:T(8,128)} %param.12) | copy-start | bytes 786436
  7.2 16.7 %copy-start.18 = (s32[16,16,256]{2,1,0:T(8,128)S(1)}, s32[16,16,256]{2,1,0:T(8,128)}, u32[]{:S(2)}) copy-start(s32[16,16,256]{2,1,0:T(8,128)} %param.14) | copy-start | bytes 786436
  7.2 17.0 %copy-start.21 = (f32[2,2,8]{2,1,0:T(2,128)S(1)}, f32[2,2,8]{2,1,0:T(2,128)}, u32[]{:S(2)}) copy-start(f32[2,2,8]{2,1,0:T(2,128)} %param.16) | copy-start | bytes 388
  7.2 174.7 %all-gather.2.cloned.1.call-start = ((), (), s32[]{:S(2)}) async-start(), calls=%async_computation | async-start | bytes 2228224 | tf_op jit(solution)/shard_map/all_gather | solution.py:108
  8.3 15.9 %collective-permute-start.2 = (f32[16,1,256]{2,1,0:T(1,128)S(1)}, f32[16,1,256]{2,1,0:T(1,128)S(1)}, u32[]{:S(2)}, u32[]{:S(2)}) collective-permute-start(f32[16,1,256]{2,1,0:T(1,128)S(1)} %get-tuple-element.29), channel_id=1, source_target_pairs={{0,16},{16,32},{32,48},{48,64},{64,80},{80,96},{96,112},{112,128},... | collective-permute-start | bytes 49160 | tf_op jit(solution)/shard_map/ppermute | solution.py:15
  10.2 13.9 %collective-permute-start.3 = (f32[16,1,256]{2,1,0:T(1,128)S(1)}, f32[16,1,256]{2,1,0:T(1,128)S(1)}, u32[]{:S(2)}, u32[]{:S(2)}) collective-permute-start(f32[16,1,256]{2,1,0:T(1,128)S(1)} %get-tuple-element.30), channel_id=1, source_target_pairs={{16,0},{32,16},{48,32},{64,48},{80,64},{96,80},{112,96},{128,112},... | collective-permute-start | bytes 49160 | tf_op jit(solution)/shard_map/ppermute | solution.py:17
  15.0 20.7 %collective-permute-start = (f32[2,16,1,256]{3,2,1,0:T(1,128)S(1)}, f32[2,16,1,256]{3,2,1,0:T(1,128)S(1)}, u32[]{:S(2)}, u32[]{:S(2)}) collective-permute-start(f32[2,16,1,256]{3,2,1,0:T(1,128)S(1)} %get-tuple-element.19), channel_id=1, source_target_pairs={{16,0},{32,16},{48,32},{64,48},{80,64},{96,80},{112,96},{128,112},... | collective-permute-start | bytes 98312 | tf_op jit(solution)/shard_map/ppermute | solution.py:17
  20.1 15.5 %collective-permute-start.1 = (f32[2,16,1,256]{3,2,1,0:T(1,128)S(1)}, f32[2,16,1,256]{3,2,1,0:T(1,128)S(1)}, u32[]{:S(2)}, u32[]{:S(2)}) collective-permute-start(f32[2,16,1,256]{3,2,1,0:T(1,128)S(1)} %get-tuple-element.20), channel_id=1, source_target_pairs={{0,16},{16,32},{32,48},{48,64},{64,80},{80,96},{96,112},{112,128},... | collective-permute-start | bytes 98312 | tf_op jit(solution)/shard_map/ppermute | solution.py:15
  24.4 6.7 %collective-permute-start.4 = (f32[16,18,1]{2,1,0:T(8,128)S(1)}, f32[16,18,1]{2,1,0:T(8,128)S(1)}, u32[]{:S(2)}, u32[]{:S(2)}) collective-permute-start(f32[16,18,1]{2,1,0:T(8,128)S(1)} %get-tuple-element.22), channel_id=1, source_target_pairs={{0,1},{1,2},{2,3},{3,4},{4,5},{5,6},{6,7},{7,8},{8,9},{9,10},{10,1... | collective-permute-start | bytes 3464 | tf_op jit(solution)/shard_map/ppermute | solution.py:15
  25.8 9.4 %collective-permute-start.5 = (f32[16,18,1]{2,1,0:T(8,128)S(1)}, f32[16,18,1]{2,1,0:T(8,128)S(1)}, u32[]{:S(2)}, u32[]{:S(2)}) collective-permute-start(f32[16,18,1]{2,1,0:T(8,128)S(1)} %get-tuple-element.21), channel_id=1, source_target_pairs={{1,0},{2,1},{3,2},{4,3},{5,4},{6,5},{7,6},{8,7},{9,8},{10,9},{11,1... | collective-permute-start | bytes 3464 | tf_op jit(solution)/shard_map/ppermute | solution.py:17
  36.0 11.5 %collective-permute-start.6 = (f32[2,16,18,1]{3,2,1,0:T(8,128)S(1)}, f32[2,16,18,1]{3,2,1,0:T(8,128)S(1)}, u32[]{:S(2)}, u32[]{:S(2)}) collective-permute-start(f32[2,16,18,1]{3,2,1,0:T(8,128)S(1)} %get-tuple-element.14), channel_id=1, source_target_pairs={{0,1},{1,2},{2,3},{3,4},{4,5},{5,6},{6,7},{7,8},{8,9},{9,10},{10,1... | collective-permute-start | bytes 6920 | tf_op jit(solution)/shard_map/ppermute | solution.py:15
  38.9 12.7 %collective-permute-start.7 = (f32[2,16,18,1]{3,2,1,0:T(8,128)S(1)}, f32[2,16,18,1]{3,2,1,0:T(8,128)S(1)}, u32[]{:S(2)}, u32[]{:S(2)}) collective-permute-start(f32[2,16,18,1]{3,2,1,0:T(8,128)S(1)} %get-tuple-element.13), channel_id=1, source_target_pairs={{1,0},{2,1},{3,2},{4,3},{5,4},{6,5},{7,6},{8,7},{9,8},{10,9},{11,1... | collective-permute-start | bytes 6920 | tf_op jit(solution)/shard_map/ppermute | solution.py:17
  40.8 11.6 %copy-start.3 = (f32[16,16,256]{2,1,0:T(8,128)}, f32[16,16,256]{2,1,0:T(8,128)S(1)}, u32[]{:S(2)}) copy-start(f32[16,16,256]{2,1,0:T(8,128)S(1)} %get-tuple-element.24) | copy-start | bytes 786436
  40.8 11.6 %copy-start.5 = (f32[16,16,256]{2,1,0:T(8,128)}, f32[16,16,256]{2,1,0:T(8,128)S(1)}, u32[]{:S(2)}) copy-start(f32[16,16,256]{2,1,0:T(8,128)S(1)} %get-tuple-element.25) | copy-start | bytes 786436
  40.8 11.6 %copy-start.7 = (f32[16,16,256]{2,1,0:T(8,128)}, f32[16,16,256]{2,1,0:T(8,128)S(1)}, u32[]{:S(2)}) copy-start(f32[16,16,256]{2,1,0:T(8,128)S(1)} %get-tuple-element.26) | copy-start | bytes 786436
  40.8 11.6 %copy-start.9 = (f32[16,16,256]{2,1,0:T(8,128)}, f32[16,16,256]{2,1,0:T(8,128)S(1)}, u32[]{:S(2)}) copy-start(f32[16,16,256]{2,1,0:T(8,128)S(1)} %get-tuple-element.27) | copy-start | bytes 786436
  54.3 4.4 %collective-permute-start.8 = (f32[2,16,1,256]{3,2,1,0:T(1,128)S(1)}, f32[2,16,1,256]{3,2,1,0:T(1,128)S(1)}, u32[]{:S(2)}, u32[]{:S(2)}) collective-permute-start(f32[2,16,1,256]{3,2,1,0:T(1,128)S(1)} %get-tuple-element.15), channel_id=1, source_target_pairs={{16,0},{32,16},{48,32},{64,48},{80,64},{96,80},{112,96},{128,112},... | collective-permute-start | bytes 98312 | tf_op jit(solution)/shard_map/ppermute | solution.py:17
  56.2 5.2 %collective-permute-start.9 = (f32[2,16,1,256]{3,2,1,0:T(1,128)S(1)}, f32[2,16,1,256]{3,2,1,0:T(1,128)S(1)}, u32[]{:S(2)}, u32[]{:S(2)}) collective-permute-start(f32[2,16,1,256]{3,2,1,0:T(1,128)S(1)} %get-tuple-element.16), channel_id=1, source_target_pairs={{0,16},{16,32},{32,48},{48,64},{64,80},{80,96},{96,112},{112,128},... | collective-permute-start | bytes 98312 | tf_op jit(solution)/shard_map/ppermute | solution.py:15
  61.8 15.0 %copy-start.15 = (f32[2,16,16,256]{3,2,1,0:T(8,128)S(1)}, f32[2,16,16,256]{3,2,1,0:T(8,128)}, u32[]{:S(2)}) copy-start(f32[2,16,16,256]{3,2,1,0:T(8,128)} %get-tuple-element.8) | copy-start | bytes 1572868
  61.8 13.8 %collective-permute-start.10 = (f32[2,16,18,1]{3,2,1,0:T(8,128)S(1)}, f32[2,16,18,1]{3,2,1,0:T(8,128)S(1)}, u32[]{:S(2)}, u32[]{:S(2)}) collective-permute-start(f32[2,16,18,1]{3,2,1,0:T(8,128)S(1)} %get-tuple-element.11), channel_id=1, source_target_pairs={{1,0},{2,1},{3,2},{4,3},{5,4},{6,5},{7,6},{8,7},{9,8},{10,9},{11,1... | collective-permute-start | bytes 6920 | tf_op jit(solution)/shard_map/ppermute | solution.py:17
  63.2 13.6 %collective-permute-start.11 = (f32[2,16,18,1]{3,2,1,0:T(8,128)S(1)}, f32[2,16,18,1]{3,2,1,0:T(8,128)S(1)}, u32[]{:S(2)}, u32[]{:S(2)}) collective-permute-start(f32[2,16,18,1]{3,2,1,0:T(8,128)S(1)} %get-tuple-element.12), channel_id=1, source_target_pairs={{0,1},{1,2},{2,3},{3,4},{4,5},{5,6},{6,7},{7,8},{8,9},{9,10},{10,1... | collective-permute-start | bytes 6920 | tf_op jit(solution)/shard_map/ppermute | solution.py:15
  78.2 23.4 %collective-permute-start.12 = (f32[16,16,256]{2,1,0:T(8,128)S(1)}, f32[16,16,256]{2,1,0:T(8,128)S(1)}, u32[]{:S(2)}, u32[]{:S(2)}) collective-permute-start(f32[16,16,256]{2,1,0:T(8,128)S(1)} %broadcast_select_fusion), channel_id=1, source_target_pairs={{0,256},{256,0},{1,257},{257,1},{2,258},{258,2},{3,259},{259,3},{4... | collective-permute-start | bytes 786440 | tf_op jit(solution)/shard_map/ppermute | solution.py:106
  185.7 32.8 %collective-permute-start.13 = (f32[16,16,256]{2,1,0:T(8,128)S(1)}, f32[16,16,256]{2,1,0:T(8,128)S(1)}, u32[]{:S(2)}, u32[]{:S(2)}) collective-permute-start(f32[16,16,256]{2,1,0:T(8,128)S(1)} %fusion.43), channel_id=1, source_target_pairs={{0,256},{256,0},{1,257},{257,1},{2,258},{258,2},{3,259},{259,3},{4... | collective-permute-start | bytes 786440 | tf_op jit(solution)/shard_map/ppermute | solution.py:119
  (13 other events, 44.9 us)
Sparse Core Ops, SparseCore 0:
  102.5 79.4 all-gather.1

commit v2 on v1

--- a/solution.py
+++ b/solution.py
@@ -81,24 +81,30 @@
     block_cols,
 ):
     layers, rows_x, cols_y = conductivity.shape
-    steps = forward_temp.shape[0]
     keep = 1.0 - fixed_mask.astype(jnp.float32)
-    heat_sens = jnp.zeros((layers, rows_x, cols_y), jnp.float32)
-    flow_x = jnp.zeros((layers, rows_x, cols_y), jnp.float32)
-    flow_y = jnp.zeros((layers, rows_x, cols_y), jnp.float32)
-    kappa_pad = extended(conductivity, (("gx", 1), ("gy", 2)), 1)
-    weights = face_weights(kappa_pad)
-    adjoint = terminal
-    for level in reversed(range(steps)):
-        padded = extended(adjoint, (("gx", 2), ("gy", 3)), 1)
-        source = well_sources(wells, misfit[level], layers, rows_x, cols_y, 0)
-        adjoint, diffusion, slope_x, slope_y = advance(
-            padded, weights, keep, velocity[0], velocity[1], source
-        )
-        temper = forward_temp[level].astype(jnp.float32)
-        heat_sens = heat_sens + jnp.sum(temper * diffusion, axis=0)
-        flow_x = flow_x + jnp.sum(temper * slope_x, axis=0)
-        flow_y = flow_y + jnp.sum(temper * slope_y, axis=0)
+    packed = jnp.concatenate([terminal, conductivity[None], velocity, keep[None]], axis=0)
+    box = extended(packed, (("gx", 2), ("gy", 3)), 2)
+    ring_velocity = box[3:5, :, 1:-1, 1:-1]
+    ring_keep = box[5, :, 1:-1, 1:-1]
+    ring_weights = face_weights(box[2])
+    weights = [w[:, 1:-1, 1:-1] for w in ring_weights]
+    ring_source = well_sources(wells, misfit[1], layers, rows_x, cols_y, 1)
+    ring_adjoint, diffusion, slope_x, slope_y = advance(
+        box[0:2], ring_weights, ring_keep, ring_velocity[0], ring_velocity[1], ring_source
+    )
+    temper = forward_temp[1].astype(jnp.float32)
+    inner = (Ellipsis, slice(1, -1), slice(1, -1))
+    heat_sens = jnp.sum(temper * diffusion[inner], axis=0)
+    flow_x = jnp.sum(temper * slope_x[inner], axis=0)
+    flow_y = jnp.sum(temper * slope_y[inner], axis=0)
+    source = well_sources(wells, misfit[0], layers, rows_x, cols_y, 0)
+    _, diffusion, slope_x, slope_y = advance(
+        ring_adjoint, weights, keep, velocity[0], velocity[1], source
+    )
+    temper = forward_temp[0].astype(jnp.float32)
+    heat_sens = heat_sens + jnp.sum(temper * diffusion, axis=0)
+    flow_x = flow_x + jnp.sum(temper * slope_x, axis=0)
+    flow_y = flow_y + jnp.sum(temper * slope_y, axis=0)
     first = lax.axis_index("sec") == 0
     mine = jnp.where(first, flow_x, flow_y)
     other = jnp.where(first, flow_y, flow_x)

time: 227 us -> 199 us (0.88)
  waiting for transfers between devices: 135 us -> 111 us
  starting transfers between devices: 55.7 us -> 38.2 us
  local copies, waits for them, and re-layouts: 7.91 us -> 21.7 us
    ppermute x6 -> x2, waiting for transfers between devices: 13.8 us -> 0.01 us  [extended(): lax.ppermute(tail, axis, [(i, (i + 1) % count) for i in range(ends)])]
    ppermute x1, waiting for transfers between devices: 10.4 us -> 23 us  [shards(): rounded = (mine + lax.ppermute(other, 'sec', partner)).astype(jnp.bfloat16)]
    all_gather x1, waiting for transfers between devices: 76.5 us -> 64.6 us  [shards(): piece = lax.all_gather(rounded, 'gy', axis=2, tiled=True)]
    ppermute x6 -> x2, waiting for transfers between devices: 14.7 us -> 3.91 us  [extended(): lax.ppermute(head, axis, [((i + 1) % count, i) for i in range(ends)])]
    ppermute x6 -> x2, starting transfers between devices: 16 us -> 6.04 us  [extended(): lax.ppermute(tail, axis, [(i, (i + 1) % count) for i in range(ends)])]
    ppermute x6 -> x2, starting transfers between devices: 14.7 us -> 4.92 us  [extended(): lax.ppermute(head, axis, [((i + 1) % count, i) for i in range(ends)])]
    unnamed x45 -> x46, local copies, waits for them, and re-layouts: 3.44 us -> 10.2 us
    ppermute x0 -> x2, local copies, waits for them, and re-layouts: none -> 3.24 us  [the longest x1 1.62 us: extended(): lax.ppermute(tail, axis, [(i, (i + 1) % count) for i in range(ends)])]
  transfers between devices with their start and end apart: 15 -> 7, of which waited for: 10 -> 5; matrix products, arithmetic and copies ran while one was open for 4% -> 4% of each run, Pallas kernels for 0% -> 0%
where the time goes in v2:
time: 199 us
  waiting for transfers between devices  111 us (56%)
  starting transfers between devices  38.2 us (19%)
  local copies, waits for them, and re-layouts  21.7 us (11%)
  between operations  14.5 us (7%)
  other arithmetic  12.1 us (6%)
    all_gather x1, waiting for transfers between devices, shards(): piece = lax.all_gather(rounded, 'gy', axis=2, tiled=True)  64.6 us
    ppermute x1, waiting for transfers between devices, shards(): rounded = (mine + lax.ppermute(other, 'sec', partner)).astype(jnp.bfloat16)  23 us
    ppermute x1, waiting for transfers between devices, shards(): sensitivity = partial_sens + lax.ppermute(partial_sens, 'sec', partner)  19.8 us
    ppermute x1, starting transfers between devices, shards(): rounded = (mine + lax.ppermute(other, 'sec', partner)).astype(jnp.bfloat16)  15.3 us
    ppermute x1, starting transfers between devices, shards(): sensitivity = partial_sens + lax.ppermute(partial_sens, 'sec', partner)  11.9 us
    unnamed x46, local copies, waits for them, and re-layouts  10.2 us
    ppermute x2, starting transfers between devices, extended(): lax.ppermute(tail, axis, [(i, (i + 1) % count) for i in range(ends)])  6.04 us
    ppermute x2, starting transfers between devices, extended(): lax.ppermute(head, axis, [((i + 1) % count, i) for i in range(ends)])  4.92 us
  transfers between devices with their start and end apart: 7, of which 5 were waited for; matrix products, arithmetic and copies ran while one was open for 4% of the time, Pallas kernels for 0%

profile of v2, /device:TPU:32, one launch (start us, length us, event | category | flops | bytes accessed | tf_op | source)
XLA Modules:
  0.0 198.6 jit_solution(4899318045097378759)
XLA Ops:
  7.2 1.4 copy.51
  8.7 1.4 copy.52
  10.5 1.9 collective-permute-start
  12.4 3.6 %collective-permute-start.1 = (f32[6,16,2,256]{3,1,2,0:T(8,128)S(1)}, f32[6,16,2,256]{3,1,2,0:T(8,128)S(1)}, u32[]{:S(2)}, u32[]{:S(2)}) collective-permute-start(f32[6,16,2,256]{3,1,2,0:T(8,128)S(1)} %get-tuple-element.24), channel_id=1, source_target_pairs={{16,0},{32,16},{48,32},{64,48},{80,64},{96,80},{112,96},{128,112},... | collective-permute-start | bytes 589832 | tf_op jit(solution)/shard_map/ppermute | solution.py:17
  16.5 2.4 %select_reduce_fusion = f32[2,16,18,258]{3,1,2,0:T(8,128)} fusion(f32[2,8]{1,0:T(2,128)S(1)} %slice_bitcast_fusion.2, pred[2,8,258]{2,1,0:T(8,128)(4,1)S(1)} %broadcast_compare_fusion, pred[2,8,16,18]{2,3,1,0:T(8,128)(4,1)S(1)} %broadcast_and_fusion), kind=kLoop, calls=%fused_computation | loop fusion | flops 3417984 | bytes 603232 | tf_op jit(solution)/shard_map/reduce_sum | solution.py:68
  20.5 1.3 fusion.47
  21.8 1.9 copy.53
  23.6 4.1 %collective-permute-start.2 = (f32[6,16,20,2]{2,1,3,0:T(8,128)S(1)}, f32[6,16,20,2]{2,1,3,0:T(8,128)}, u32[]{:S(2)}, u32[]{:S(2)}) collective-permute-start(f32[6,16,20,2]{2,1,3,0:T(8,128)S(1)} %copy.53), channel_id=1, source_target_pairs={{0,1},{1,2},{2,3},{3,4},{4,5},{5,6},{6,7},{7,8},{8,9},{9,10},{10,1... | collective-permute-start | bytes 46088 | tf_op jit(solution)/shard_map/ppermute | solution.py:15
  27.7 1.3 copy.54
  29.0 1.3 collective-permute-start.3
  31.2 1.6 copy.55
  32.8 3.6 %collective-permute-done.3 = f32[6,16,20,2]{2,1,3,0:T(8,128)} collective-permute-done((f32[6,16,20,2]{2,1,3,0:T(8,128)}, f32[6,16,20,2]{2,1,3,0:T(8,128)}, u32[]{:S(2)}, u32[]{:S(2)}) %collective-permute-start.3) | collective-permute-done | bytes 15392 | tf_op jit(solution)/shard_map/ppermute | solution.py:17
  36.4 1.6 copy.56
  38.0 3.6 %pad_maximum_fusion = f32[6,16,20,260]{3,1,2,0:T(8,128)S(1)} fusion(f32[6,16,20,2]{3,1,2,0:T(8,128)S(1)} %copy.56, f32[6,16,2,256]{3,1,2,0:T(8,128)} %copy-done.10, f32[1,16,16,256]{3,1,2,0:T(8,128)} %copy-done.3, f32[2,16,16,256]{3,1,2,0:T(8,128)S(1)} %copy.52, f32[1,16,16,256]{3,1,2,0:T(8,128)} %copy-done.5, f32[2,16,16,256]{3,1,2,0:T(8,128)S(1)} %copy.51, ...), kind=kLoop, calls=%fused_computation.1 | loop fusion | flops 3494400 | bytes 3993600 | tf_op jit(solution)/shard_map/concatenate | solution.py:13
  42.1 1.1 copy-done.1
  45.5 1.5 copy-done.2
  47.5 1.3 add_multiply_fusion
  50.8 15.3 %collective-permute-start.4 = (f32[16,16,256]{2,0,1:T(8,128)S(1)}, f32[16,16,256]{2,0,1:T(8,128)S(1)}, u32[]{:S(2)}, u32[]{:S(2)}) collective-permute-start(f32[16,16,256]{2,0,1:T(8,128)S(1)} %broadcast_select_fusion), channel_id=1, source_target_pairs={{0,256},{256,0},{1,257},{257,1},{2,258},{258,2},{3,259},{259,3},{4... | collective-permute-start | bytes 786440 | tf_op jit(solution)/shard_map/ppermute | solution.py:112
  66.1 23.0 %collective-permute-done.4 = f32[16,16,256]{2,0,1:T(8,128)S(1)} collective-permute-done((f32[16,16,256]{2,0,1:T(8,128)S(1)}, f32[16,16,256]{2,0,1:T(8,128)S(1)}, u32[]{:S(2)}, u32[]{:S(2)}) %collective-permute-start.4) | collective-permute-done | bytes 262176 | tf_op jit(solution)/shard_map/ppermute | solution.py:112
  89.8 64.6 %all-gather.2.cloned.1.call-done = bf16[16,16,4096]{2,0,1:T(8,128)(2,1)} async-done(((bf16[16,16,256]{2,0,1:T(8,128)(2,1)}), bf16[16,16,4096]{2,0,1:T(8,128)(2,1)}) %all-gather.2.cloned.1.call-update) | async-done | bytes 2097168 | tf_op jit(solution)/shard_map/all_gather | solution.py:114
  154.4 2.1 %copy.75 = bf16[32,8,32,128]{3,2,1,0:T(8,128)(2,1)S(1)} copy(bf16[32,8,32,128]{3,1,2,0:T(8,128)(2,1)} %bitcast.70) | data formatting | bytes 4194304
  158.0 11.9 %collective-permute-start.5 = (f32[16,16,256]{2,0,1:T(8,128)S(1)}, f32[16,16,256]{2,0,1:T(8,128)S(1)}, u32[]{:S(2)}, u32[]{:S(2)}) collective-permute-start(f32[16,16,256]{2,0,1:T(8,128)S(1)} %fusion.40), channel_id=1, source_target_pairs={{0,256},{256,0},{1,257},{257,1},{2,258},{258,2},{3,259},{259,3},{4... | collective-permute-start | bytes 786440 | tf_op jit(solution)/shard_map/ppermute | solution.py:125
  170.2 0.9 broadcast_in_dim_reshape.3
  171.1 19.8 %collective-permute-done.5 = f32[16,16,256]{2,0,1:T(8,128)S(1)} collective-permute-done((f32[16,16,256]{2,0,1:T(8,128)S(1)}, f32[16,16,256]{2,0,1:T(8,128)S(1)}, u32[]{:S(2)}, u32[]{:S(2)}) %collective-permute-start.5) | collective-permute-done | bytes 262176 | tf_op jit(solution)/shard_map/ppermute | solution.py:125
  (81 shorter events, 11.6 us)
Async XLA Ops:
  7.2 149.9 %copy-start = (bf16[2,7,128,128]{3,2,1,0:T(8,128)(2,1)S(1)}, bf16[2,7,128,128]{3,2,1,0:T(8,128)(2,1)}, u32[]{:S(2)}) copy-start(bf16[2,7,128,128]{3,2,1,0:T(8,128)(2,1)} %param.18) | copy-start | bytes 1376260
  7.2 2.9 %copy-start.16 = (f32[16,16,256]{2,1,0:T(8,128)S(1)}, f32[16,16,256]{2,1,0:T(8,128)}, u32[]{:S(2)}) copy-start(f32[16,16,256]{2,1,0:T(8,128)} %param.12) | copy-start | bytes 786436
  7.2 2.9 %copy-start.15 = (s32[16,16,256]{2,1,0:T(8,128)S(1)}, s32[16,16,256]{2,1,0:T(8,128)}, u32[]{:S(2)}) copy-start(s32[16,16,256]{2,1,0:T(8,128)} %param.14) | copy-start | bytes 786436
  7.2 147.2 %all-gather.2.cloned.1.call-start = ((), (), s32[]{:S(2)}) async-start(), calls=%async_computation | async-start | bytes 2228224 | tf_op jit(solution)/shard_map/all_gather | solution.py:114
  8.7 7.4 %copy-start.18 = (s32[2,8,3]{1,0,2:T(2,128)S(1)}, s32[2,8,3]{1,0,2:T(2,128)}, u32[]{:S(2)}) copy-start(s32[2,8,3]{1,0,2:T(2,128)} %param.15) | copy-start | bytes 580
  8.7 7.5 %copy-start.20 = (f32[2,2,8]{2,1,0:T(2,128)S(1)}, f32[2,2,8]{2,1,0:T(2,128)}, u32[]{:S(2)}) copy-start(f32[2,2,8]{2,1,0:T(2,128)} %param.16) | copy-start | bytes 388
  10.4 10.0 %copy-start.3 = (f32[1,16,16,256]{3,1,2,0:T(8,128)}, f32[1,16,16,256]{3,1,2,0:T(8,128)S(1)}, u32[]{:S(2)}) copy-start(f32[1,16,16,256]{3,1,2,0:T(8,128)S(1)} %get-tuple-element.36) | copy-start | bytes 786436
  10.4 10.0 %copy-start.5 = (f32[1,16,16,256]{3,1,2,0:T(8,128)}, f32[1,16,16,256]{3,1,2,0:T(8,128)S(1)}, u32[]{:S(2)}) copy-start(f32[1,16,16,256]{3,1,2,0:T(8,128)S(1)} %get-tuple-element.37) | copy-start | bytes 786436
  10.5 8.4 %collective-permute-start = (f32[6,16,2,256]{3,1,2,0:T(8,128)S(1)}, f32[6,16,2,256]{3,1,2,0:T(8,128)S(1)}, u32[]{:S(2)}, u32[]{:S(2)}) collective-permute-start(f32[6,16,2,256]{3,1,2,0:T(8,128)S(1)} %get-tuple-element.23), channel_id=1, source_target_pairs={{0,16},{16,32},{32,48},{48,64},{64,80},{80,96},{96,112},{112,128},... | collective-permute-start | bytes 589832 | tf_op jit(solution)/shard_map/ppermute | solution.py:15
  12.4 6.8 %collective-permute-start.1 = (f32[6,16,2,256]{3,1,2,0:T(8,128)S(1)}, f32[6,16,2,256]{3,1,2,0:T(8,128)S(1)}, u32[]{:S(2)}, u32[]{:S(2)}) collective-permute-start(f32[6,16,2,256]{3,1,2,0:T(8,128)S(1)} %get-tuple-element.24), channel_id=1, source_target_pairs={{16,0},{32,16},{48,32},{64,48},{80,64},{96,80},{112,96},{128,112},... | collective-permute-start | bytes 589832 | tf_op jit(solution)/shard_map/ppermute | solution.py:17
  20.4 9.9 %copy-start.14 = (bf16[2,2,16,16,256]{4,3,2,1,0:T(8,128)(2,1)S(1)}, bf16[2,2,16,16,256]{4,3,2,1,0:T(8,128)(2,1)}, u32[]{:S(2)}) copy-start(bf16[2,2,16,16,256]{4,3,2,1,0:T(8,128)(2,1)} %param.11) | copy-start | bytes 1572868
  23.6 7.6 %collective-permute-start.2 = (f32[6,16,20,2]{2,1,3,0:T(8,128)S(1)}, f32[6,16,20,2]{2,1,3,0:T(8,128)}, u32[]{:S(2)}, u32[]{:S(2)}) collective-permute-start(f32[6,16,20,2]{2,1,3,0:T(8,128)S(1)} %copy.53), channel_id=1, source_target_pairs={{0,1},{1,2},{2,3},{3,4},{4,5},{5,6},{6,7},{7,8},{8,9},{9,10},{10,1... | collective-permute-start | bytes 46088 | tf_op jit(solution)/shard_map/ppermute | solution.py:15
  29.0 7.3 %collective-permute-start.3 = (f32[6,16,20,2]{2,1,3,0:T(8,128)}, f32[6,16,20,2]{2,1,3,0:T(8,128)}, u32[]{:S(2)}, u32[]{:S(2)}) collective-permute-start(f32[6,16,20,2]{2,1,3,0:T(8,128)} %copy.54), channel_id=1, source_target_pairs={{1,0},{2,1},{3,2},{4,3},{5,4},{6,5},{7,6},{8,7},{9,8},{10,9},{11,1... | collective-permute-start | bytes 46088 | tf_op jit(solution)/shard_map/ppermute | solution.py:17
  41.6 1.6 copy-start.1
  44.0 1.0 copy-start.6
  44.0 1.1 copy-start.9
  44.0 1.1 copy-start.11
  45.2 1.8 copy-start.2
  45.2 2.4 %slice-start = ((f32[6,16,20,260]{3,1,2,0:T(8,128)}), f32[2,16,20,260]{3,1,2,0:T(8,128)S(1)}, s32[]{:S(2)}) async-start(f32[6,16,20,260]{3,1,2,0:T(8,128)} %copy-done.1), calls=%async_computation.1 | async-start | bytes 1966080 | tf_op jit(solution)/shard_map/slice | solution.py:93
  45.2 2.4 %copy-start.7 = (f32[2,16,18,258]{3,1,2,0:T(8,128)S(1)}, f32[2,16,18,258]{3,1,2,0:T(8,128)}, u32[]{:S(2)}) copy-start(f32[2,16,18,258]{3,1,2,0:T(8,128)} %select_reduce_fusion) | copy-start | bytes 1783300
  47.5 1.4 copy-start.13
  50.8 38.2 %collective-permute-start.4 = (f32[16,16,256]{2,0,1:T(8,128)S(1)}, f32[16,16,256]{2,0,1:T(8,128)S(1)}, u32[]{:S(2)}, u32[]{:S(2)}) collective-permute-start(f32[16,16,256]{2,0,1:T(8,128)S(1)} %broadcast_select_fusion), channel_id=1, source_target_pairs={{0,256},{256,0},{1,257},{257,1},{2,258},{258,2},{3,259},{259,3},{4... | collective-permute-start | bytes 786440 | tf_op jit(solution)/shard_map/ppermute | solution.py:112
  154.4 2.1 %copy-start.19 = (s32[2,7]{1,0:T(2,128)S(1)}, s32[2,7]{1,0:T(2,128)}, u32[]{:S(2)}) copy-start(s32[2,7]{1,0:T(2,128)} %param.19) | copy-start | bytes 172
  158.0 32.8 %collective-permute-start.5 = (f32[16,16,256]{2,0,1:T(8,128)S(1)}, f32[16,16,256]{2,0,1:T(8,128)S(1)}, u32[]{:S(2)}, u32[]{:S(2)}) collective-permute-start(f32[16,16,256]{2,0,1:T(8,128)S(1)} %fusion.40), channel_id=1, source_target_pairs={{0,256},{256,0},{1,257},{257,1},{2,258},{258,2},{3,259},{259,3},{4... | collective-permute-start | bytes 786440 | tf_op jit(solution)/shard_map/ppermute | solution.py:125
  (5 other events, 4.2 us)
Sparse Core Ops, SparseCore 0:
  90.0 64.4 all-gather.1

commit v3 on v2

--- a/solution.py
+++ b/solution.py
@@ -111,12 +111,27 @@
     partner = [(0, 1), (1, 0)]
     rounded = (mine + lax.ppermute(other, "sec", partner)).astype(jnp.bfloat16)
     row_blocks, per_row, block_size, _ = blocks.shape
-    piece = lax.all_gather(rounded, "gy", axis=2, tiled=True)
-    count = piece.shape[2] // block_size
-    split_rows = piece.reshape(layers, rows_x, count, block_size)
-    block_ids = jnp.arange(count, dtype=jnp.int32)
-    chosen = (block_cols[:, :, None] == block_ids[None, None, :]).astype(jnp.bfloat16)
-    portion = jnp.einsum("bkq,zxqj->bkzxj", chosen, split_rows, preferred_element_type=jnp.float32)
+    count = lax.axis_size("gy")
+    side = int(round(count ** 0.5))
+    me = lax.axis_index("gy")
+    across = [rounded]
+    for shift in range(1, side):
+        pairs = [(i, (i // side) * side + (i % side + shift) % side) for i in range(count)]
+        across.append(lax.ppermute(rounded, "gy", pairs))
+    row = jnp.stack(across)
+    along = [row]
+    for shift in range(1, side):
+        pairs = [(i, (i + side * shift) % count) for i in range(count)]
+        along.append(lax.ppermute(row, "gy", pairs))
+    halves = cols_y // block_size
+    pieces = jnp.stack(along).reshape(count, layers, rows_x, halves, block_size)
+    owner = block_cols // halves
+    slot = ((me // side - owner // side) % side) * side + (me % side - owner % side) % side
+    chosen = (
+        (slot[:, :, None, None] == jnp.arange(count, dtype=jnp.int32)[None, None, :, None])
+        & ((block_cols % halves)[:, :, None, None] == jnp.arange(halves, dtype=jnp.int32)[None, None, None, :])
+    ).astype(jnp.bfloat16)
+    portion = jnp.einsum("bkph,pzxhj->bkzxj", chosen, pieces, preferred_element_type=jnp.float32)
     picked = portion.astype(jnp.bfloat16)
     head = jnp.einsum(
         "bkzxj,bkij->zxbi", picked, blocks, preferred_element_type=jnp.float32

time: 199 us -> 162 us (0.81)
  the two profiles are of different devices: /device:TPU:32 before, /device:TPU:96 now
where the time goes in v3:
time: 162 us
  waiting for transfers between devices  66.1 us (41%)
  starting transfers between devices  57.5 us (35%)
  local copies, waits for them, and re-layouts  21.3 us (13%)
  other arithmetic  12 us (7%)
  matrix products  3.49 us (2%)
    ppermute x1, waiting for transfers between devices, shards(): rounded = (mine + lax.ppermute(other, 'sec', partner)).astype(jnp.bfloat16)  22.2 us
    ppermute x3, waiting for transfers between devices, shards(): along.append(lax.ppermute(row, 'gy', pairs))  20.8 us
    ppermute x1, waiting for transfers between devices, shards(): sensitivity = partial_sens + lax.ppermute(partial_sens, 'sec', partner)  16.2 us
    ppermute x1, starting transfers between devices, shards(): rounded = (mine + lax.ppermute(other, 'sec', partner)).astype(jnp.bfloat16)  13.5 us
    ppermute x3, starting transfers between devices, shards(): along.append(lax.ppermute(row, 'gy', pairs))  12.6 us
    ppermute x3, starting transfers between devices, shards(): across.append(lax.ppermute(rounded, 'gy', pairs))  11.2 us
    ppermute x1, starting transfers between devices, shards(): sensitivity = partial_sens + lax.ppermute(partial_sens, 'sec', partner)  9.48 us
    unnamed x45, local copies, waits for them, and re-layouts  7.85 us
  transfers between devices with their start and end apart: 12, of which 8 were waited for; matrix products, arithmetic and copies ran while one was open for 5% of the time, Pallas kernels for 0%

profile of v3, /device:TPU:96, one launch (start us, length us, event | category | flops | bytes accessed | tf_op | source)
XLA Modules:
  0.0 161.6 jit_solution(16842873337863793976)
XLA Ops:
  3.9 1.9 %collective-permute-start.1 = (f32[6,16,2,256]{3,1,2,0:T(8,128)S(1)}, f32[6,16,2,256]{3,1,2,0:T(8,128)S(1)}, u32[]{:S(2)}, u32[]{:S(2)}) collective-permute-start(f32[6,16,2,256]{3,1,2,0:T(8,128)S(1)} %get-tuple-element.24), channel_id=1, source_target_pairs={{16,0},{32,16},{48,32},{64,48},{80,64},{96,80},{112,96},{128,112},... | collective-permute-start | bytes 589832 | tf_op jit(solution)/shard_map/ppermute | solution.py:17
  5.8 2.4 %collective-permute-start = (f32[6,16,2,256]{3,1,2,0:T(8,128)S(1)}, f32[6,16,2,256]{3,1,2,0:T(8,128)S(1)}, u32[]{:S(2)}, u32[]{:S(2)}) collective-permute-start(f32[6,16,2,256]{3,1,2,0:T(8,128)S(1)} %get-tuple-element.23), channel_id=1, source_target_pairs={{0,16},{16,32},{32,48},{48,64},{64,80},{80,96},{96,112},{112,128},... | collective-permute-start | bytes 589832 | tf_op jit(solution)/shard_map/ppermute | solution.py:15
  8.7 2.4 %select_reduce_fusion = f32[2,16,18,258]{3,1,2,0:T(8,128)} fusion(f32[2,8]{1,0:T(2,128)S(1)} %slice_bitcast_fusion.2, pred[2,8,258]{2,1,0:T(8,128)(4,1)S(1)} %broadcast_compare_fusion, pred[2,8,16,18]{2,3,1,0:T(8,128)(4,1)S(1)} %broadcast_and_fusion), kind=kLoop, calls=%fused_computation | loop fusion | flops 3417984 | bytes 603232 | tf_op jit(solution)/shard_map/reduce_sum | solution.py:68
  11.1 1.7 %collective-permute-done = f32[6,16,2,256]{3,1,2,0:T(8,128)S(1)} collective-permute-done((f32[6,16,2,256]{3,1,2,0:T(8,128)S(1)}, f32[6,16,2,256]{3,1,2,0:T(8,128)S(1)}, u32[]{:S(2)}, u32[]{:S(2)}) %collective-permute-start) | collective-permute-done | bytes 196640 | tf_op jit(solution)/shard_map/ppermute | solution.py:15
  15.0 1.9 %copy.71 = f32[6,16,20,2]{2,1,3,0:T(8,128)S(1)} copy(f32[6,16,20,2]{3,1,2,0:T(8,128)} %get-tuple-element.22) | data formatting | bytes 30720 | tf_op jit(solution)/shard_map/slice | solution.py:11
  19.5 5.2 %collective-permute-start.2 = (f32[6,16,20,2]{2,1,3,0:T(8,128)}, f32[6,16,20,2]{2,1,3,0:T(8,128)}, u32[]{:S(2)}, u32[]{:S(2)}) collective-permute-start(f32[6,16,20,2]{2,1,3,0:T(8,128)} %copy.70), channel_id=1, source_target_pairs={{0,1},{1,2},{2,3},{3,4},{4,5},{5,6},{6,7},{7,8},{8,9},{9,10},{10,1... | collective-permute-start | bytes 46088 | tf_op jit(solution)/shard_map/ppermute | solution.py:15
  25.5 1.6 %copy.73 = f32[6,16,20,2]{3,1,2,0:T(8,128)S(1)} copy(f32[6,16,20,2]{2,1,3,0:T(8,128)} %collective-permute-done.3) | data formatting | bytes 30720 | tf_op jit(solution)/shard_map/ppermute | solution.py:17
  27.2 1.6 %copy.72 = f32[6,16,20,2]{3,1,2,0:T(8,128)S(1)} copy(f32[6,16,20,2]{2,1,3,0:T(8,128)} %collective-permute-done.2) | data formatting | bytes 30720 | tf_op jit(solution)/shard_map/ppermute | solution.py:15
  28.8 3.6 %pad_maximum_fusion = f32[6,16,20,260]{3,1,2,0:T(8,128)S(1)} fusion(f32[6,16,20,2]{3,1,2,0:T(8,128)S(1)} %copy.73, f32[6,16,2,256]{3,1,2,0:T(8,128)} %copy-done.8, f32[1,16,16,256]{3,1,2,0:T(8,128)} %copy-done.3, f32[2,16,16,256]{3,1,2,0:T(8,128)S(1)} %copy.69, f32[1,16,16,256]{3,1,2,0:T(8,128)} %copy-done.5, f32[2,16,16,256]{3,1,2,0:T(8,128)S(1)} %copy.68, ...), kind=kLoop, calls=%fused_computation.1 | loop fusion | flops 3494400 | bytes 3993600 | tf_op jit(solution)/shard_map/concatenate | solution.py:13
  41.6 13.5 %collective-permute-start.4 = (f32[16,16,256]{2,0,1:T(8,128)S(1)}, f32[16,16,256]{2,0,1:T(8,128)S(1)}, u32[]{:S(2)}, u32[]{:S(2)}) collective-permute-start(f32[16,16,256]{2,0,1:T(8,128)S(1)} %broadcast_select_fusion), channel_id=1, source_target_pairs={{0,256},{256,0},{1,257},{257,1},{2,258},{258,2},{3,259},{259,3},{4... | collective-permute-start | bytes 786440 | tf_op jit(solution)/shard_map/ppermute | solution.py:112
  55.1 22.2 %collective-permute-done.4 = f32[16,16,256]{2,0,1:T(8,128)S(1)} collective-permute-done((f32[16,16,256]{2,0,1:T(8,128)S(1)}, f32[16,16,256]{2,0,1:T(8,128)S(1)}, u32[]{:S(2)}, u32[]{:S(2)}) %collective-permute-start.4) | collective-permute-done | bytes 262176 | tf_op jit(solution)/shard_map/ppermute | solution.py:112
  77.4 6.5 %collective-permute-start.7 = (bf16[16,16,256]{2,0,1:T(8,128)(2,1)S(1)}, bf16[16,16,256]{2,0,1:T(8,128)(2,1)S(1)}, u32[]{:S(2)}, u32[]{:S(2)}) collective-permute-start(bf16[16,16,256]{2,0,1:T(8,128)(2,1)S(1)} %add_convert_fusion), channel_id=1, source_target_pairs={{0,3},{1,0},{2,1},{3,2},{4,7},{5,4},{6,5},{7,6},{8,11},{9,8},{10,9... | collective-permute-start | bytes 393224 | tf_op jit(solution)/shard_map/ppermute | solution.py:120
  83.9 1.9 %collective-permute-start.6 = (bf16[16,16,256]{2,0,1:T(8,128)(2,1)S(1)}, bf16[16,16,256]{2,0,1:T(8,128)(2,1)S(1)}, u32[]{:S(2)}, u32[]{:S(2)}) collective-permute-start(bf16[16,16,256]{2,0,1:T(8,128)(2,1)S(1)} %add_convert_fusion), channel_id=1, source_target_pairs={{0,2},{1,3},{2,0},{3,1},{4,6},{5,7},{6,4},{7,5},{8,10},{9,11},{10,... | collective-permute-start | bytes 393224 | tf_op jit(solution)/shard_map/ppermute | solution.py:120
  85.8 2.8 %collective-permute-start.5 = (bf16[16,16,256]{2,0,1:T(8,128)(2,1)S(1)}, bf16[16,16,256]{2,0,1:T(8,128)(2,1)S(1)}, u32[]{:S(2)}, u32[]{:S(2)}) collective-permute-start(bf16[16,16,256]{2,0,1:T(8,128)(2,1)S(1)} %add_convert_fusion), channel_id=1, source_target_pairs={{0,1},{1,2},{2,3},{3,0},{4,5},{5,6},{6,7},{7,4},{8,9},{9,10},{10,1... | collective-permute-start | bytes 393224 | tf_op jit(solution)/shard_map/ppermute | solution.py:120
  89.1 3.3 %collective-permute-done.6 = bf16[16,16,256]{2,0,1:T(8,128)(2,1)S(1)} collective-permute-done((bf16[16,16,256]{2,0,1:T(8,128)(2,1)S(1)}, bf16[16,16,256]{2,0,1:T(8,128)(2,1)S(1)}, u32[]{:S(2)}, u32[]{:S(2)}) %collective-permute-start.6) | collective-permute-done | bytes 131104 | tf_op jit(solution)/shard_map/ppermute | solution.py:120
  94.0 7.2 %collective-permute-start.10 = (bf16[4,16,16,256]{3,1,2,0:T(8,128)(2,1)S(1)}, bf16[4,16,16,256]{3,1,2,0:T(8,128)(2,1)S(1)}, u32[]{:S(2)}, u32[]{:S(2)}) collective-permute-start(bf16[4,16,16,256]{3,1,2,0:T(8,128)(2,1)S(1)} %get-tuple-element.26), channel_id=1, source_target_pairs={{0,12},{1,13},{2,14},{3,15},{4,0},{5,1},{6,2},{7,3},{8,4},{9,5},{1... | collective-permute-start | bytes 1572872 | tf_op jit(solution)/shard_map/ppermute | solution.py:125
  101.2 2.4 %collective-permute-start.9 = (bf16[4,16,16,256]{3,1,2,0:T(8,128)(2,1)S(1)}, bf16[4,16,16,256]{3,1,2,0:T(8,128)(2,1)S(1)}, u32[]{:S(2)}, u32[]{:S(2)}) collective-permute-start(bf16[4,16,16,256]{3,1,2,0:T(8,128)(2,1)S(1)} %get-tuple-element.26), channel_id=1, source_target_pairs={{0,8},{1,9},{2,10},{3,11},{4,12},{5,13},{6,14},{7,15},{8,0},{9,1},... | collective-permute-start | bytes 1572872 | tf_op jit(solution)/shard_map/ppermute | solution.py:125
  103.6 3.0 %collective-permute-start.8 = (bf16[4,16,16,256]{3,1,2,0:T(8,128)(2,1)S(1)}, bf16[4,16,16,256]{3,1,2,0:T(8,128)(2,1)S(1)}, u32[]{:S(2)}, u32[]{:S(2)}) collective-permute-start(bf16[4,16,16,256]{3,1,2,0:T(8,128)(2,1)S(1)} %get-tuple-element.26), channel_id=1, source_target_pairs={{0,4},{1,5},{2,6},{3,7},{4,8},{5,9},{6,10},{7,11},{8,12},{9,13},{1... | collective-permute-start | bytes 1572872 | tf_op jit(solution)/shard_map/ppermute | solution.py:125
  106.7 15.2 %collective-permute-done.10 = bf16[4,16,16,256]{3,1,2,0:T(8,128)(2,1)S(1)} collective-permute-done((bf16[4,16,16,256]{3,1,2,0:T(8,128)(2,1)S(1)}, bf16[4,16,16,256]{3,1,2,0:T(8,128)(2,1)S(1)}, u32[]{:S(2)}, u32[]{:S(2)}) %collective-permute-start.10) | collective-permute-done | bytes 524320 | tf_op jit(solution)/shard_map/ppermute | solution.py:125
  121.9 5.6 %collective-permute-done.8 = bf16[4,16,16,256]{3,1,2,0:T(8,128)(2,1)S(1)} collective-permute-done((bf16[4,16,16,256]{3,1,2,0:T(8,128)(2,1)S(1)}, bf16[4,16,16,256]{3,1,2,0:T(8,128)(2,1)S(1)}, u32[]{:S(2)}, u32[]{:S(2)}) %collective-permute-start.8) | collective-permute-done | bytes 524320 | tf_op jit(solution)/shard_map/ppermute | solution.py:125
  127.8 2.1 %reshape.95 = bf16[16,16,16,2,128]{4,3,1,2,0:T(2,128)(2,1)} reshape(bf16[4,4,16,16,256]{4,2,3,1,0:T(8,128)(2,1)S(1)} %pad_maximum_fusion.1) | data formatting | bytes 4194304 | tf_op jit(solution)/shard_map/reshape | solution.py:127
  129.8 3.1 %bitcast_convert_fusion = bf16[2,7,16,16,128]{4,1,3,2,0:T(8,128)(2,1)S(1)} fusion(bf16[16,16,16,2,128]{4,3,1,2,0:T(2,128)(2,1)} %reshape.95, pred[2,7,2]{1,2,0:T(4,128)(4,1)S(1)} %iota_compare_fusion.2, pred[2,7,16]{2,1,0:T(8,128)(4,1)S(1)} %iota_compare_fusion.1), kind=kOutput, calls=%fused_computation.3 | convolution fusion | flops 29819328 | bytes 3014908 | tf_op jit(solution)/shard_map/bkph,pzxhj->bkzxj/dot_general | solution.py:134
  133.9 9.5 %collective-permute-start.11 = (f32[16,16,256]{2,0,1:T(8,128)S(1)}, f32[16,16,256]{2,0,1:T(8,128)S(1)}, u32[]{:S(2)}, u32[]{:S(2)}) collective-permute-start(f32[16,16,256]{2,0,1:T(8,128)S(1)} %fusion.39), channel_id=1, source_target_pairs={{0,256},{256,0},{1,257},{257,1},{2,258},{258,2},{3,259},{259,3},{4... | collective-permute-start | bytes 786440 | tf_op jit(solution)/shard_map/ppermute | solution.py:140
  144.6 16.2 %collective-permute-done.11 = f32[16,16,256]{2,0,1:T(8,128)S(1)} collective-permute-done((f32[16,16,256]{2,0,1:T(8,128)S(1)}, f32[16,16,256]{2,0,1:T(8,128)S(1)}, u32[]{:S(2)}, u32[]{:S(2)}) %collective-permute-start.11) | collective-permute-done | bytes 262176 | tf_op jit(solution)/shard_map/ppermute | solution.py:140
  (95 shorter events, 23.8 us)
Async XLA Ops:
  0.6 132.3 %copy-start = (bf16[2,7,128,128]{3,2,1,0:T(8,128)(2,1)S(1)}, bf16[2,7,128,128]{3,2,1,0:T(8,128)(2,1)}, u32[]{:S(2)}) copy-start(bf16[2,7,128,128]{3,2,1,0:T(8,128)(2,1)} %param.18) | copy-start | bytes 1376260
  0.6 2.8 %copy-start.15 = (s32[16,16,256]{2,1,0:T(8,128)S(1)}, s32[16,16,256]{2,1,0:T(8,128)}, u32[]{:S(2)}) copy-start(s32[16,16,256]{2,1,0:T(8,128)} %param.14) | copy-start | bytes 786436
  0.7 2.8 %copy-start.16 = (f32[16,16,256]{2,1,0:T(8,128)S(1)}, f32[16,16,256]{2,1,0:T(8,128)}, u32[]{:S(2)}) copy-start(f32[16,16,256]{2,1,0:T(8,128)} %param.12) | copy-start | bytes 786436
  2.1 6.1 %copy-start.20 = (f32[2,2,8]{2,1,0:T(2,128)S(1)}, f32[2,2,8]{2,1,0:T(2,128)}, u32[]{:S(2)}) copy-start(f32[2,2,8]{2,1,0:T(2,128)} %param.16) | copy-start | bytes 388
  2.1 6.2 %copy-start.18 = (s32[2,8,3]{1,0,2:T(2,128)S(1)}, s32[2,8,3]{1,0,2:T(2,128)}, u32[]{:S(2)}) copy-start(s32[2,8,3]{1,0,2:T(2,128)} %param.15) | copy-start | bytes 580
  3.8 9.8 %copy-start.3 = (f32[1,16,16,256]{3,1,2,0:T(8,128)}, f32[1,16,16,256]{3,1,2,0:T(8,128)S(1)}, u32[]{:S(2)}) copy-start(f32[1,16,16,256]{3,1,2,0:T(8,128)S(1)} %get-tuple-element.40) | copy-start | bytes 786436
  3.8 9.8 %copy-start.5 = (f32[1,16,16,256]{3,1,2,0:T(8,128)}, f32[1,16,16,256]{3,1,2,0:T(8,128)S(1)}, u32[]{:S(2)}) copy-start(f32[1,16,16,256]{3,1,2,0:T(8,128)S(1)} %get-tuple-element.41) | copy-start | bytes 786436
  3.9 7.2 %collective-permute-start.1 = (f32[6,16,2,256]{3,1,2,0:T(8,128)S(1)}, f32[6,16,2,256]{3,1,2,0:T(8,128)S(1)}, u32[]{:S(2)}, u32[]{:S(2)}) collective-permute-start(f32[6,16,2,256]{3,1,2,0:T(8,128)S(1)} %get-tuple-element.24), channel_id=1, source_target_pairs={{16,0},{32,16},{48,32},{64,48},{80,64},{96,80},{112,96},{128,112},... | collective-permute-start | bytes 589832 | tf_op jit(solution)/shard_map/ppermute | solution.py:17
  5.8 7.0 %collective-permute-start = (f32[6,16,2,256]{3,1,2,0:T(8,128)S(1)}, f32[6,16,2,256]{3,1,2,0:T(8,128)S(1)}, u32[]{:S(2)}, u32[]{:S(2)}) collective-permute-start(f32[6,16,2,256]{3,1,2,0:T(8,128)S(1)} %get-tuple-element.23), channel_id=1, source_target_pairs={{0,16},{16,32},{32,48},{48,64},{64,80},{80,96},{96,112},{112,128},... | collective-permute-start | bytes 589832 | tf_op jit(solution)/shard_map/ppermute | solution.py:15
  13.7 11.0 %copy-start.14 = (bf16[2,2,16,16,256]{4,3,2,1,0:T(8,128)(2,1)S(1)}, bf16[2,2,16,16,256]{4,3,2,1,0:T(8,128)(2,1)}, u32[]{:S(2)}) copy-start(bf16[2,2,16,16,256]{4,3,2,1,0:T(8,128)(2,1)} %param.11) | copy-start | bytes 1572868
  16.9 8.6 %collective-permute-start.3 = (f32[6,16,20,2]{2,1,3,0:T(8,128)S(1)}, f32[6,16,20,2]{2,1,3,0:T(8,128)}, u32[]{:S(2)}, u32[]{:S(2)}) collective-permute-start(f32[6,16,20,2]{2,1,3,0:T(8,128)S(1)} %copy.71), channel_id=1, source_target_pairs={{1,0},{2,1},{3,2},{4,3},{5,4},{6,5},{7,6},{8,7},{9,8},{10,9},{11,1... | collective-permute-start | bytes 46088 | tf_op jit(solution)/shard_map/ppermute | solution.py:17
  19.5 7.7 %collective-permute-start.2 = (f32[6,16,20,2]{2,1,3,0:T(8,128)}, f32[6,16,20,2]{2,1,3,0:T(8,128)}, u32[]{:S(2)}, u32[]{:S(2)}) collective-permute-start(f32[6,16,20,2]{2,1,3,0:T(8,128)} %copy.70), channel_id=1, source_target_pairs={{0,1},{1,2},{2,3},{3,4},{4,5},{5,6},{6,7},{7,8},{8,9},{9,10},{10,1... | collective-permute-start | bytes 46088 | tf_op jit(solution)/shard_map/ppermute | solution.py:15
  35.9 1.8 %copy-start.2 = (f32[6,16,20,260]{3,1,2,0:T(8,128)S(1)}, f32[6,16,20,260]{3,1,2,0:T(8,128)}, u32[]{:S(2)}) copy-start(f32[6,16,20,260]{3,1,2,0:T(8,128)} %copy-done.1) | copy-start | bytes 5990404
  35.9 2.4 %slice-start = ((f32[6,16,20,260]{3,1,2,0:T(8,128)}), f32[2,16,20,260]{3,1,2,0:T(8,128)S(1)}, s32[]{:S(2)}) async-start(f32[6,16,20,260]{3,1,2,0:T(8,128)} %copy-done.1), calls=%async_computation | async-start | bytes 1966080 | tf_op jit(solution)/shard_map/slice | solution.py:93
  35.9 2.4 %copy-start.7 = (f32[2,16,18,258]{3,1,2,0:T(8,128)S(1)}, f32[2,16,18,258]{3,1,2,0:T(8,128)}, u32[]{:S(2)}) copy-start(f32[2,16,18,258]{3,1,2,0:T(8,128)} %select_reduce_fusion) | copy-start | bytes 1783300
  41.5 65.1 %copy-start.19 = (s32[2,7]{1,0:T(2,128)S(1)}, s32[2,7]{1,0:T(2,128)}, u32[]{:S(2)}) copy-start(s32[2,7]{1,0:T(2,128)} %param.19) | copy-start | bytes 172
  41.6 35.6 %collective-permute-start.4 = (f32[16,16,256]{2,0,1:T(8,128)S(1)}, f32[16,16,256]{2,0,1:T(8,128)S(1)}, u32[]{:S(2)}, u32[]{:S(2)}) collective-permute-start(f32[16,16,256]{2,0,1:T(8,128)S(1)} %broadcast_select_fusion), channel_id=1, source_target_pairs={{0,256},{256,0},{1,257},{257,1},{2,258},{258,2},{3,259},{259,3},{4... | collective-permute-start | bytes 786440 | tf_op jit(solution)/shard_map/ppermute | solution.py:112
  77.4 11.7 %collective-permute-start.7 = (bf16[16,16,256]{2,0,1:T(8,128)(2,1)S(1)}, bf16[16,16,256]{2,0,1:T(8,128)(2,1)S(1)}, u32[]{:S(2)}, u32[]{:S(2)}) collective-permute-start(bf16[16,16,256]{2,0,1:T(8,128)(2,1)S(1)} %add_convert_fusion), channel_id=1, source_target_pairs={{0,3},{1,0},{2,1},{3,2},{4,7},{5,4},{6,5},{7,6},{8,11},{9,8},{10,9... | collective-permute-start | bytes 393224 | tf_op jit(solution)/shard_map/ppermute | solution.py:120
  83.9 8.5 %collective-permute-start.6 = (bf16[16,16,256]{2,0,1:T(8,128)(2,1)S(1)}, bf16[16,16,256]{2,0,1:T(8,128)(2,1)S(1)}, u32[]{:S(2)}, u32[]{:S(2)}) collective-permute-start(bf16[16,16,256]{2,0,1:T(8,128)(2,1)S(1)} %add_convert_fusion), channel_id=1, source_target_pairs={{0,2},{1,3},{2,0},{3,1},{4,6},{5,7},{6,4},{7,5},{8,10},{9,11},{10,... | collective-permute-start | bytes 393224 | tf_op jit(solution)/shard_map/ppermute | solution.py:120
  85.8 8.1 %collective-permute-start.5 = (bf16[16,16,256]{2,0,1:T(8,128)(2,1)S(1)}, bf16[16,16,256]{2,0,1:T(8,128)(2,1)S(1)}, u32[]{:S(2)}, u32[]{:S(2)}) collective-permute-start(bf16[16,16,256]{2,0,1:T(8,128)(2,1)S(1)} %add_convert_fusion), channel_id=1, source_target_pairs={{0,1},{1,2},{2,3},{3,0},{4,5},{5,6},{6,7},{7,4},{8,9},{9,10},{10,1... | collective-permute-start | bytes 393224 | tf_op jit(solution)/shard_map/ppermute | solution.py:120
  94.0 27.9 %collective-permute-start.10 = (bf16[4,16,16,256]{3,1,2,0:T(8,128)(2,1)S(1)}, bf16[4,16,16,256]{3,1,2,0:T(8,128)(2,1)S(1)}, u32[]{:S(2)}, u32[]{:S(2)}) collective-permute-start(bf16[4,16,16,256]{3,1,2,0:T(8,128)(2,1)S(1)} %get-tuple-element.26), channel_id=1, source_target_pairs={{0,12},{1,13},{2,14},{3,15},{4,0},{5,1},{6,2},{7,3},{8,4},{9,5},{1... | collective-permute-start | bytes 1572872 | tf_op jit(solution)/shard_map/ppermute | solution.py:125
  101.2 20.7 %collective-permute-start.9 = (bf16[4,16,16,256]{3,1,2,0:T(8,128)(2,1)S(1)}, bf16[4,16,16,256]{3,1,2,0:T(8,128)(2,1)S(1)}, u32[]{:S(2)}, u32[]{:S(2)}) collective-permute-start(bf16[4,16,16,256]{3,1,2,0:T(8,128)(2,1)S(1)} %get-tuple-element.26), channel_id=1, source_target_pairs={{0,8},{1,9},{2,10},{3,11},{4,12},{5,13},{6,14},{7,15},{8,0},{9,1},... | collective-permute-start | bytes 1572872 | tf_op jit(solution)/shard_map/ppermute | solution.py:125
  103.6 23.9 %collective-permute-start.8 = (bf16[4,16,16,256]{3,1,2,0:T(8,128)(2,1)S(1)}, bf16[4,16,16,256]{3,1,2,0:T(8,128)(2,1)S(1)}, u32[]{:S(2)}, u32[]{:S(2)}) collective-permute-start(bf16[4,16,16,256]{3,1,2,0:T(8,128)(2,1)S(1)} %get-tuple-element.26), channel_id=1, source_target_pairs={{0,4},{1,5},{2,6},{3,7},{4,8},{5,9},{6,10},{7,11},{8,12},{9,13},{1... | collective-permute-start | bytes 1572872 | tf_op jit(solution)/shard_map/ppermute | solution.py:125
  133.9 26.8 %collective-permute-start.11 = (f32[16,16,256]{2,0,1:T(8,128)S(1)}, f32[16,16,256]{2,0,1:T(8,128)S(1)}, u32[]{:S(2)}, u32[]{:S(2)}) collective-permute-start(f32[16,16,256]{2,0,1:T(8,128)S(1)} %fusion.39), channel_id=1, source_target_pairs={{0,256},{256,0},{1,257},{257,1},{2,258},{258,2},{3,259},{259,3},{4... | collective-permute-start | bytes 786440 | tf_op jit(solution)/shard_map/ppermute | solution.py:140
  (10 other events, 11.4 us)

commit v4 on v2

--- a/solution.py
+++ b/solution.py
@@ -68,6 +68,40 @@
     return jnp.sum(jnp.where(matches, misfit_level[:, :, None, None, None], 0.0), axis=1)
 
 
+def head_chunk(mine, other, heat_sens, gradient, blocks, block_cols):
+    partner = [(0, 1), (1, 0)]
+    layers, rows_x, cols_y = mine.shape
+    rounded = (mine + lax.ppermute(other, "sec", partner)).astype(jnp.bfloat16)
+    row_blocks, per_row, block_size, _ = blocks.shape
+    count = lax.axis_size("gy")
+    side = int(round(count ** 0.5))
+    me = lax.axis_index("gy")
+    across = [rounded]
+    for shift in range(1, side):
+        pairs = [(i, (i // side) * side + (i % side + shift) % side) for i in range(count)]
+        across.append(lax.ppermute(rounded, "gy", pairs))
+    row = jnp.stack(across)
+    along = [row]
+    for shift in range(1, side):
+        pairs = [(i, (i + side * shift) % count) for i in range(count)]
+        along.append(lax.ppermute(row, "gy", pairs))
+    halves = cols_y // block_size
+    pieces = jnp.stack(along).reshape(count, layers, rows_x, halves, block_size)
+    owner = block_cols // halves
+    slot = ((me // side - owner // side) % side) * side + (me % side - owner % side) % side
+    chosen = (
+        (slot[:, :, None, None] == jnp.arange(count, dtype=jnp.int32)[None, None, :, None])
+        & ((block_cols % halves)[:, :, None, None] == jnp.arange(halves, dtype=jnp.int32)[None, None, None, :])
+    ).astype(jnp.bfloat16)
+    portion = jnp.einsum("bkph,pzxhj->bkzxj", chosen, pieces, preferred_element_type=jnp.float32)
+    picked = portion.astype(jnp.bfloat16)
+    head = jnp.einsum(
+        "bkzxj,bkij->zxbi", picked, blocks, preferred_element_type=jnp.float32
+    ).reshape(layers, rows_x, cols_y)
+    partial_sens = heat_sens + head * gradient
+    return head, partial_sens + lax.ppermute(partial_sens, "sec", partner)
+
+
 def shards(
     terminal,
     forward_temp,
@@ -108,21 +142,19 @@
     first = lax.axis_index("sec") == 0
     mine = jnp.where(first, flow_x, flow_y)
     other = jnp.where(first, flow_y, flow_x)
-    partner = [(0, 1), (1, 0)]
-    rounded = (mine + lax.ppermute(other, "sec", partner)).astype(jnp.bfloat16)
-    row_blocks, per_row, block_size, _ = blocks.shape
-    piece = lax.all_gather(rounded, "gy", axis=2, tiled=True)
-    count = piece.shape[2] // block_size
-    split_rows = piece.reshape(layers, rows_x, count, block_size)
-    block_ids = jnp.arange(count, dtype=jnp.int32)
-    chosen = (block_cols[:, :, None] == block_ids[None, None, :]).astype(jnp.bfloat16)
-    portion = jnp.einsum("bkq,zxqj->bkzxj", chosen, split_rows, preferred_element_type=jnp.float32)
-    picked = portion.astype(jnp.bfloat16)
-    head = jnp.einsum(
-        "bkzxj,bkij->zxbi", picked, blocks, preferred_element_type=jnp.float32
-    ).reshape(layers, rows_x, cols_y)
-    partial_sens = heat_sens + head * head_gradient[0].astype(jnp.float32)
-    sensitivity = partial_sens + lax.ppermute(partial_sens, "sec", partner)
+    gradient = head_gradient[0].astype(jnp.float32)
+    chunks = 2
+    depth = layers // chunks
+    heads, sens = [], []
+    for part in range(chunks):
+        cut = slice(part * depth, (part + 1) * depth)
+        head, total = head_chunk(
+            mine[cut], other[cut], heat_sens[cut], gradient[cut], blocks, block_cols
+        )
+        heads.append(head)
+        sens.append(total)
+    head = jnp.concatenate(heads, axis=0)
+    sensitivity = jnp.concatenate(sens, axis=0)
     return (head[None], sensitivity)
 
 

time: 199 us -> 173 us (0.87)
  the two profiles are of different devices: /device:TPU:32 before, /device:TPU:1 now
where the time goes in v4:
time: 173 us; the launch traced here: 172 us
  starting transfers between devices  90.4 us (52%)
  waiting for transfers between devices  46.3 us (27%)
  local copies, waits for them, and re-layouts  15.9 us (9%)
  other arithmetic  15.6 us (9%)
  matrix products  2.23 us (1%)
    ppermute x6, starting transfers between devices, head_chunk(): across.append(lax.ppermute(rounded, 'gy', pairs))  24.7 us
    ppermute x6, starting transfers between devices, head_chunk(): along.append(lax.ppermute(row, 'gy', pairs))  21.1 us
    ppermute x2, waiting for transfers between devices, head_chunk(): return (head, partial_sens + lax.ppermute(partial_sens, 'sec', partner))  19 us
    ppermute x2, waiting for transfers between devices, head_chunk(): rounded = (mine + lax.ppermute(other, 'sec', partner)).astype(jnp.bfloat16)  17.7 us
    ppermute x2, starting transfers between devices, head_chunk(): rounded = (mine + lax.ppermute(other, 'sec', partner)).astype(jnp.bfloat16)  14 us
    ppermute x2, starting transfers between devices, head_chunk(): return (head, partial_sens + lax.ppermute(partial_sens, 'sec', partner))  14 us
    ppermute x2, starting transfers between devices, extended(): lax.ppermute(head, axis, [((i + 1) % count, i) for i in range(ends)])  10.1 us
    ppermute x6, waiting for transfers between devices, head_chunk(): along.append(lax.ppermute(row, 'gy', pairs))  9.6 us
  transfers between devices with their start and end apart: 20, of which 7 were waited for; matrix products, arithmetic and copies ran while one was open for 5% of the time, Pallas kernels for 0%

profile of v4, /device:TPU:1, one launch (start us, length us, event | category | flops | bytes accessed | tf_op | source)
XLA Modules:
  0.0 171.8 jit_solution(8382031487553324909)
XLA Ops:
  4.9 8.8 %collective-permute-start.1 = (f32[6,16,2,256]{3,1,2,0:T(8,128)S(1)}, f32[6,16,2,256]{3,1,2,0:T(8,128)S(1)}, u32[]{:S(2)}, u32[]{:S(2)}) collective-permute-start(f32[6,16,2,256]{3,1,2,0:T(8,128)S(1)} %get-tuple-element.24), channel_id=1, source_target_pairs={{16,0},{32,16},{48,32},{64,48},{80,64},{96,80},{112,96},{128,112},... | collective-permute-start | bytes 589832 | tf_op jit(solution)/shard_map/ppermute | solution.py:17
  16.0 2.4 %select_reduce_fusion = f32[2,16,18,258]{3,1,2,0:T(8,128)} fusion(f32[2,8]{1,0:T(2,128)S(1)} %slice_bitcast_fusion.4, pred[2,8,258]{2,1,0:T(8,128)(4,1)S(1)} %broadcast_compare_fusion, pred[2,8,16,18]{2,3,1,0:T(8,128)(4,1)S(1)} %broadcast_and_fusion), kind=kLoop, calls=%fused_computation | loop fusion | flops 3417984 | bytes 603232 | tf_op jit(solution)/shard_map/reduce_sum | solution.py:68
  26.0 4.6 %collective-permute-start.2 = (f32[6,16,20,2]{2,1,3,0:T(8,128)S(1)}, f32[6,16,20,2]{2,1,3,0:T(8,128)}, u32[]{:S(2)}, u32[]{:S(2)}) collective-permute-start(f32[6,16,20,2]{2,1,3,0:T(8,128)S(1)} %copy.77), channel_id=1, source_target_pairs={{0,1},{1,2},{2,3},{3,4},{4,5},{5,6},{6,7},{7,8},{8,9},{9,10},{10,1... | collective-permute-start | bytes 46088 | tf_op jit(solution)/shard_map/ppermute | solution.py:15
  33.8 3.6 %pad_maximum_fusion = f32[6,16,20,260]{3,1,2,0:T(8,128)S(1)} fusion(f32[6,16,20,2]{3,1,2,0:T(8,128)S(1)} %copy.80, f32[6,16,2,256]{3,1,2,0:T(8,128)} %copy-done.8, f32[1,16,16,256]{3,1,2,0:T(8,128)} %copy-done.3, f32[2,16,16,256]{3,1,2,0:T(8,128)S(1)} %copy.76, f32[1,16,16,256]{3,1,2,0:T(8,128)} %copy-done.5, f32[2,16,16,256]{3,1,2,0:T(8,128)S(1)} %copy.75, ...), kind=kLoop, calls=%fused_computation.1 | loop fusion | flops 3494400 | bytes 3993600 | tf_op jit(solution)/shard_map/concatenate | solution.py:13
  45.1 11.4 %collective-permute-start.4 = (f32[8,16,256]{2,0,1:T(8,128)S(1)}, f32[8,16,256]{2,0,1:T(8,128)S(1)}, u32[]{:S(2)}, u32[]{:S(2)}) collective-permute-start(f32[8,16,256]{2,0,1:T(8,128)S(1)} %get-tuple-element.41), channel_id=1, source_target_pairs={{0,256},{256,0},{1,257},{257,1},{2,258},{258,2},{3,259},{259,3},{4... | collective-permute-start | bytes 393224 | tf_op jit(solution)/shard_map/ppermute | solution.py:74
  56.5 2.6 %collective-permute-start.11 = (f32[8,16,256]{2,0,1:T(8,128)S(1)}, f32[8,16,256]{2,0,1:T(8,128)S(1)}, u32[]{:S(2)}, u32[]{:S(2)}) collective-permute-start(f32[8,16,256]{2,0,1:T(8,128)S(1)} %get-tuple-element.42), channel_id=1, source_target_pairs={{0,256},{256,0},{1,257},{257,1},{2,258},{258,2},{3,259},{259,3},{4... | collective-permute-start | bytes 393224 | tf_op jit(solution)/shard_map/ppermute | solution.py:74
  60.2 16.6 %collective-permute-done.11 = f32[8,16,256]{2,0,1:T(8,128)S(1)} collective-permute-done((f32[8,16,256]{2,0,1:T(8,128)S(1)}, f32[8,16,256]{2,0,1:T(8,128)S(1)}, u32[]{:S(2)}, u32[]{:S(2)}) %collective-permute-start.11) | collective-permute-done | bytes 131104 | tf_op jit(solution)/shard_map/ppermute | solution.py:74
  76.9 10.8 %collective-permute-start.14 = (bf16[8,16,256]{2,0,1:T(8,128)(2,1)S(1)}, bf16[8,16,256]{2,0,1:T(8,128)(2,1)S(1)}, u32[]{:S(2)}, u32[]{:S(2)}) collective-permute-start(bf16[8,16,256]{2,0,1:T(8,128)(2,1)S(1)} %get-tuple-element.40), channel_id=1, source_target_pairs={{0,3},{1,0},{2,1},{3,2},{4,7},{5,4},{6,5},{7,6},{8,11},{9,8},{10,9... | collective-permute-start | bytes 196616 | tf_op jit(solution)/shard_map/ppermute | solution.py:82
  87.6 1.9 %collective-permute-start.13 = (bf16[8,16,256]{2,0,1:T(8,128)(2,1)S(1)}, bf16[8,16,256]{2,0,1:T(8,128)(2,1)S(1)}, u32[]{:S(2)}, u32[]{:S(2)}) collective-permute-start(bf16[8,16,256]{2,0,1:T(8,128)(2,1)S(1)} %get-tuple-element.40), channel_id=1, source_target_pairs={{0,2},{1,3},{2,0},{3,1},{4,6},{5,7},{6,4},{7,5},{8,10},{9,11},{10,... | collective-permute-start | bytes 196616 | tf_op jit(solution)/shard_map/ppermute | solution.py:82
  89.6 2.5 %collective-permute-start.12 = (bf16[8,16,256]{2,0,1:T(8,128)(2,1)S(1)}, bf16[8,16,256]{2,0,1:T(8,128)(2,1)S(1)}, u32[]{:S(2)}, u32[]{:S(2)}) collective-permute-start(bf16[8,16,256]{2,0,1:T(8,128)(2,1)S(1)} %get-tuple-element.40), channel_id=1, source_target_pairs={{0,1},{1,2},{2,3},{3,0},{4,5},{5,6},{6,7},{7,4},{8,9},{9,10},{10,1... | collective-permute-start | bytes 196616 | tf_op jit(solution)/shard_map/ppermute | solution.py:82
  92.1 4.0 %collective-permute-start.7 = (bf16[8,16,256]{2,0,1:T(8,128)(2,1)S(1)}, bf16[8,16,256]{2,0,1:T(8,128)(2,1)S(1)}, u32[]{:S(2)}, u32[]{:S(2)}) collective-permute-start(bf16[8,16,256]{2,0,1:T(8,128)(2,1)S(1)} %get-tuple-element.39), channel_id=1, source_target_pairs={{0,3},{1,0},{2,1},{3,2},{4,7},{5,4},{6,5},{7,6},{8,11},{9,8},{10,9... | collective-permute-start | bytes 196616 | tf_op jit(solution)/shard_map/ppermute | solution.py:82
  96.1 3.7 %collective-permute-start.6 = (bf16[8,16,256]{2,0,1:T(8,128)(2,1)S(1)}, bf16[8,16,256]{2,0,1:T(8,128)(2,1)S(1)}, u32[]{:S(2)}, u32[]{:S(2)}) collective-permute-start(bf16[8,16,256]{2,0,1:T(8,128)(2,1)S(1)} %get-tuple-element.39), channel_id=1, source_target_pairs={{0,2},{1,3},{2,0},{3,1},{4,6},{5,7},{6,4},{7,5},{8,10},{9,11},{10,... | collective-permute-start | bytes 196616 | tf_op jit(solution)/shard_map/ppermute | solution.py:82
  101.8 6.9 %collective-permute-start.17 = (bf16[4,8,16,256]{3,1,2,0:T(8,128)(2,1)S(1)}, bf16[4,8,16,256]{3,1,2,0:T(8,128)(2,1)S(1)}, u32[]{:S(2)}, u32[]{:S(2)}) collective-permute-start(bf16[4,8,16,256]{3,1,2,0:T(8,128)(2,1)S(1)} %get-tuple-element.44), channel_id=1, source_target_pairs={{0,12},{1,13},{2,14},{3,15},{4,0},{5,1},{6,2},{7,3},{8,4},{9,5},{1... | collective-permute-start | bytes 786440 | tf_op jit(solution)/shard_map/ppermute | solution.py:87
  108.7 2.1 %collective-permute-start.16 = (bf16[4,8,16,256]{3,1,2,0:T(8,128)(2,1)S(1)}, bf16[4,8,16,256]{3,1,2,0:T(8,128)(2,1)S(1)}, u32[]{:S(2)}, u32[]{:S(2)}) collective-permute-start(bf16[4,8,16,256]{3,1,2,0:T(8,128)(2,1)S(1)} %get-tuple-element.44), channel_id=1, source_target_pairs={{0,8},{1,9},{2,10},{3,11},{4,12},{5,13},{6,14},{7,15},{8,0},{9,1},... | collective-permute-start | bytes 786440 | tf_op jit(solution)/shard_map/ppermute | solution.py:87
  110.9 2.5 %collective-permute-start.15 = (bf16[4,8,16,256]{3,1,2,0:T(8,128)(2,1)S(1)}, bf16[4,8,16,256]{3,1,2,0:T(8,128)(2,1)S(1)}, u32[]{:S(2)}, u32[]{:S(2)}) collective-permute-start(bf16[4,8,16,256]{3,1,2,0:T(8,128)(2,1)S(1)} %get-tuple-element.44), channel_id=1, source_target_pairs={{0,4},{1,5},{2,6},{3,7},{4,8},{5,9},{6,10},{7,11},{8,12},{9,13},{1... | collective-permute-start | bytes 786440 | tf_op jit(solution)/shard_map/ppermute | solution.py:87
  113.5 4.2 %collective-permute-start.10 = (bf16[4,8,16,256]{3,1,2,0:T(8,128)(2,1)S(1)}, bf16[4,8,16,256]{3,1,2,0:T(8,128)(2,1)}, u32[]{:S(2)}, u32[]{:S(2)}) collective-permute-start(bf16[4,8,16,256]{3,1,2,0:T(8,128)(2,1)S(1)} %get-tuple-element.38), channel_id=1, source_target_pairs={{0,12},{1,13},{2,14},{3,15},{4,0},{5,1},{6,2},{7,3},{8,4},{9,5},{1... | collective-permute-start | bytes 786440 | tf_op jit(solution)/shard_map/ppermute | solution.py:87
  117.7 3.4 %collective-permute-start.9 = (bf16[4,8,16,256]{3,1,2,0:T(8,128)(2,1)S(1)}, bf16[4,8,16,256]{3,1,2,0:T(8,128)(2,1)}, u32[]{:S(2)}, u32[]{:S(2)}) collective-permute-start(bf16[4,8,16,256]{3,1,2,0:T(8,128)(2,1)S(1)} %get-tuple-element.38), channel_id=1, source_target_pairs={{0,8},{1,9},{2,10},{3,11},{4,12},{5,13},{6,14},{7,15},{8,0},{9,1},... | collective-permute-start | bytes 786440 | tf_op jit(solution)/shard_map/ppermute | solution.py:87
  121.2 1.9 %collective-permute-start.8 = (bf16[4,8,16,256]{3,1,2,0:T(8,128)(2,1)S(1)}, bf16[4,8,16,256]{3,1,2,0:T(8,128)(2,1)}, u32[]{:S(2)}, u32[]{:S(2)}) collective-permute-start(bf16[4,8,16,256]{3,1,2,0:T(8,128)(2,1)S(1)} %get-tuple-element.38), channel_id=1, source_target_pairs={{0,4},{1,5},{2,6},{3,7},{4,8},{5,9},{6,10},{7,11},{8,12},{9,13},{1... | collective-permute-start | bytes 786440 | tf_op jit(solution)/shard_map/ppermute | solution.py:87
  124.7 2.7 %collective-permute-done.10 = bf16[4,8,16,256]{3,1,2,0:T(8,128)(2,1)} collective-permute-done((bf16[4,8,16,256]{3,1,2,0:T(8,128)(2,1)S(1)}, bf16[4,8,16,256]{3,1,2,0:T(8,128)(2,1)}, u32[]{:S(2)}, u32[]{:S(2)}) %collective-permute-start.10) | collective-permute-done | bytes 262176 | tf_op jit(solution)/shard_map/ppermute | solution.py:87
  129.3 5.0 %collective-permute-done.8 = bf16[4,8,16,256]{3,1,2,0:T(8,128)(2,1)} collective-permute-done((bf16[4,8,16,256]{3,1,2,0:T(8,128)(2,1)S(1)}, bf16[4,8,16,256]{3,1,2,0:T(8,128)(2,1)}, u32[]{:S(2)}, u32[]{:S(2)}) %collective-permute-start.8) | collective-permute-done | bytes 262176 | tf_op jit(solution)/shard_map/ppermute | solution.py:87
  137.2 9.7 %collective-permute-start.19 = (f32[8,16,256]{2,0,1:T(8,128)S(1)}, f32[8,16,256]{2,0,1:T(8,128)S(1)}, u32[]{:S(2)}, u32[]{:S(2)}) collective-permute-start(f32[8,16,256]{2,0,1:T(8,128)S(1)} %get-tuple-element.28), channel_id=1, source_target_pairs={{0,256},{256,0},{1,257},{257,1},{2,258},{258,2},{3,259},{259,3},{4... | collective-permute-start | bytes 393224 | tf_op jit(solution)/shard_map/ppermute | solution.py:102
  146.9 4.3 %collective-permute-start.18 = (f32[8,16,256]{2,0,1:T(8,128)S(1)}, f32[8,16,256]{2,0,1:T(8,128)S(1)}, u32[]{:S(2)}, u32[]{:S(2)}) collective-permute-start(f32[8,16,256]{2,0,1:T(8,128)S(1)} %get-tuple-element.27), channel_id=1, source_target_pairs={{0,256},{256,0},{1,257},{257,1},{2,258},{258,2},{3,259},{259,3},{4... | collective-permute-start | bytes 393224 | tf_op jit(solution)/shard_map/ppermute | solution.py:102
  151.9 16.2 %collective-permute-done.19 = f32[8,16,256]{2,0,1:T(8,128)S(1)} collective-permute-done((f32[8,16,256]{2,0,1:T(8,128)S(1)}, f32[8,16,256]{2,0,1:T(8,128)S(1)}, u32[]{:S(2)}, u32[]{:S(2)}) %collective-permute-start.19) | collective-permute-done | bytes 131104 | tf_op jit(solution)/shard_map/ppermute | solution.py:102
  168.1 2.8 %collective-permute-done.18 = f32[8,16,256]{2,0,1:T(8,128)S(1)} collective-permute-done((f32[8,16,256]{2,0,1:T(8,128)S(1)}, f32[8,16,256]{2,0,1:T(8,128)S(1)}, u32[]{:S(2)}, u32[]{:S(2)}) %collective-permute-start.18) | collective-permute-done | bytes 131104 | tf_op jit(solution)/shard_map/ppermute | solution.py:102
  (118 shorter events, 35.8 us)
Async XLA Ops:
  0.6 123.7 %copy-start = (bf16[2,7,128,128]{3,2,1,0:T(8,128)(2,1)S(1)}, bf16[2,7,128,128]{3,2,1,0:T(8,128)(2,1)}, u32[]{:S(2)}) copy-start(bf16[2,7,128,128]{3,2,1,0:T(8,128)(2,1)} %param.18) | copy-start | bytes 1376260
  0.7 17.8 %copy-start.15 = (bf16[2,2,16,16,256]{4,3,2,1,0:T(8,128)(2,1)S(1)}, bf16[2,2,16,16,256]{4,3,2,1,0:T(8,128)(2,1)}, u32[]{:S(2)}) copy-start(bf16[2,2,16,16,256]{4,3,2,1,0:T(8,128)(2,1)} %param.11) | copy-start | bytes 1572868
  4.8 16.0 %copy-start.3 = (f32[1,16,16,256]{3,1,2,0:T(8,128)}, f32[1,16,16,256]{3,1,2,0:T(8,128)S(1)}, u32[]{:S(2)}) copy-start(f32[1,16,16,256]{3,1,2,0:T(8,128)S(1)} %get-tuple-element.50) | copy-start | bytes 786436
  4.8 16.0 %copy-start.5 = (f32[1,16,16,256]{3,1,2,0:T(8,128)}, f32[1,16,16,256]{3,1,2,0:T(8,128)S(1)}, u32[]{:S(2)}) copy-start(f32[1,16,16,256]{3,1,2,0:T(8,128)S(1)} %get-tuple-element.51) | copy-start | bytes 786436
  4.9 14.4 %collective-permute-start.1 = (f32[6,16,2,256]{3,1,2,0:T(8,128)S(1)}, f32[6,16,2,256]{3,1,2,0:T(8,128)S(1)}, u32[]{:S(2)}, u32[]{:S(2)}) collective-permute-start(f32[6,16,2,256]{3,1,2,0:T(8,128)S(1)} %get-tuple-element.24), channel_id=1, source_target_pairs={{16,0},{32,16},{48,32},{64,48},{80,64},{96,80},{112,96},{128,112},... | collective-permute-start | bytes 589832 | tf_op jit(solution)/shard_map/ppermute | solution.py:17
  13.7 5.6 %collective-permute-start = (f32[6,16,2,256]{3,1,2,0:T(8,128)S(1)}, f32[6,16,2,256]{3,1,2,0:T(8,128)S(1)}, u32[]{:S(2)}, u32[]{:S(2)}) collective-permute-start(f32[6,16,2,256]{3,1,2,0:T(8,128)S(1)} %get-tuple-element.23), channel_id=1, source_target_pairs={{0,16},{16,32},{32,48},{48,64},{64,80},{80,96},{96,112},{112,128},... | collective-permute-start | bytes 589832 | tf_op jit(solution)/shard_map/ppermute | solution.py:15
  24.0 7.4 %collective-permute-start.3 = (f32[6,16,20,2]{2,1,3,0:T(8,128)S(1)}, f32[6,16,20,2]{2,1,3,0:T(8,128)S(1)}, u32[]{:S(2)}, u32[]{:S(2)}) collective-permute-start(f32[6,16,20,2]{2,1,3,0:T(8,128)S(1)} %copy.78), channel_id=1, source_target_pairs={{1,0},{2,1},{3,2},{4,3},{5,4},{6,5},{7,6},{8,7},{9,8},{10,9},{11,1... | collective-permute-start | bytes 46088 | tf_op jit(solution)/shard_map/ppermute | solution.py:17
  26.0 6.1 %collective-permute-start.2 = (f32[6,16,20,2]{2,1,3,0:T(8,128)S(1)}, f32[6,16,20,2]{2,1,3,0:T(8,128)}, u32[]{:S(2)}, u32[]{:S(2)}) collective-permute-start(f32[6,16,20,2]{2,1,3,0:T(8,128)S(1)} %copy.77), channel_id=1, source_target_pairs={{0,1},{1,2},{2,3},{3,4},{4,5},{5,6},{6,7},{7,8},{8,9},{9,10},{10,1... | collective-permute-start | bytes 46088 | tf_op jit(solution)/shard_map/ppermute | solution.py:15
  45.1 15.2 %collective-permute-start.4 = (f32[8,16,256]{2,0,1:T(8,128)S(1)}, f32[8,16,256]{2,0,1:T(8,128)S(1)}, u32[]{:S(2)}, u32[]{:S(2)}) collective-permute-start(f32[8,16,256]{2,0,1:T(8,128)S(1)} %get-tuple-element.41), channel_id=1, source_target_pairs={{0,256},{256,0},{1,257},{257,1},{2,258},{258,2},{3,259},{259,3},{4... | collective-permute-start | bytes 393224 | tf_op jit(solution)/shard_map/ppermute | solution.py:74
  56.5 20.3 %collective-permute-start.11 = (f32[8,16,256]{2,0,1:T(8,128)S(1)}, f32[8,16,256]{2,0,1:T(8,128)S(1)}, u32[]{:S(2)}, u32[]{:S(2)}) collective-permute-start(f32[8,16,256]{2,0,1:T(8,128)S(1)} %get-tuple-element.42), channel_id=1, source_target_pairs={{0,256},{256,0},{1,257},{257,1},{2,258},{258,2},{3,259},{259,3},{4... | collective-permute-start | bytes 393224 | tf_op jit(solution)/shard_map/ppermute | solution.py:74
  76.9 22.9 %collective-permute-start.14 = (bf16[8,16,256]{2,0,1:T(8,128)(2,1)S(1)}, bf16[8,16,256]{2,0,1:T(8,128)(2,1)S(1)}, u32[]{:S(2)}, u32[]{:S(2)}) collective-permute-start(bf16[8,16,256]{2,0,1:T(8,128)(2,1)S(1)} %get-tuple-element.40), channel_id=1, source_target_pairs={{0,3},{1,0},{2,1},{3,2},{4,7},{5,4},{6,5},{7,6},{8,11},{9,8},{10,9... | collective-permute-start | bytes 196616 | tf_op jit(solution)/shard_map/ppermute | solution.py:82
  87.6 14.1 %collective-permute-start.13 = (bf16[8,16,256]{2,0,1:T(8,128)(2,1)S(1)}, bf16[8,16,256]{2,0,1:T(8,128)(2,1)S(1)}, u32[]{:S(2)}, u32[]{:S(2)}) collective-permute-start(bf16[8,16,256]{2,0,1:T(8,128)(2,1)S(1)} %get-tuple-element.40), channel_id=1, source_target_pairs={{0,2},{1,3},{2,0},{3,1},{4,6},{5,7},{6,4},{7,5},{8,10},{9,11},{10,... | collective-permute-start | bytes 196616 | tf_op jit(solution)/shard_map/ppermute | solution.py:82
  89.6 12.2 %collective-permute-start.12 = (bf16[8,16,256]{2,0,1:T(8,128)(2,1)S(1)}, bf16[8,16,256]{2,0,1:T(8,128)(2,1)S(1)}, u32[]{:S(2)}, u32[]{:S(2)}) collective-permute-start(bf16[8,16,256]{2,0,1:T(8,128)(2,1)S(1)} %get-tuple-element.40), channel_id=1, source_target_pairs={{0,1},{1,2},{2,3},{3,0},{4,5},{5,6},{6,7},{7,4},{8,9},{9,10},{10,1... | collective-permute-start | bytes 196616 | tf_op jit(solution)/shard_map/ppermute | solution.py:82
  92.1 18.7 %collective-permute-start.7 = (bf16[8,16,256]{2,0,1:T(8,128)(2,1)S(1)}, bf16[8,16,256]{2,0,1:T(8,128)(2,1)S(1)}, u32[]{:S(2)}, u32[]{:S(2)}) collective-permute-start(bf16[8,16,256]{2,0,1:T(8,128)(2,1)S(1)} %get-tuple-element.39), channel_id=1, source_target_pairs={{0,3},{1,0},{2,1},{3,2},{4,7},{5,4},{6,5},{7,6},{8,11},{9,8},{10,9... | collective-permute-start | bytes 196616 | tf_op jit(solution)/shard_map/ppermute | solution.py:82
  96.1 17.3 %collective-permute-start.6 = (bf16[8,16,256]{2,0,1:T(8,128)(2,1)S(1)}, bf16[8,16,256]{2,0,1:T(8,128)(2,1)S(1)}, u32[]{:S(2)}, u32[]{:S(2)}) collective-permute-start(bf16[8,16,256]{2,0,1:T(8,128)(2,1)S(1)} %get-tuple-element.39), channel_id=1, source_target_pairs={{0,2},{1,3},{2,0},{3,1},{4,6},{5,7},{6,4},{7,5},{8,10},{9,11},{10,... | collective-permute-start | bytes 196616 | tf_op jit(solution)/shard_map/ppermute | solution.py:82
  99.8 13.7 %collective-permute-start.5 = (bf16[8,16,256]{2,0,1:T(8,128)(2,1)S(1)}, bf16[8,16,256]{2,0,1:T(8,128)(2,1)S(1)}, u32[]{:S(2)}, u32[]{:S(2)}) collective-permute-start(bf16[8,16,256]{2,0,1:T(8,128)(2,1)S(1)} %get-tuple-element.39), channel_id=1, source_target_pairs={{0,1},{1,2},{2,3},{3,0},{4,5},{5,6},{6,7},{7,4},{8,9},{9,10},{10,1... | collective-permute-start | bytes 196616 | tf_op jit(solution)/shard_map/ppermute | solution.py:82
  101.8 19.3 %collective-permute-start.17 = (bf16[4,8,16,256]{3,1,2,0:T(8,128)(2,1)S(1)}, bf16[4,8,16,256]{3,1,2,0:T(8,128)(2,1)S(1)}, u32[]{:S(2)}, u32[]{:S(2)}) collective-permute-start(bf16[4,8,16,256]{3,1,2,0:T(8,128)(2,1)S(1)} %get-tuple-element.44), channel_id=1, source_target_pairs={{0,12},{1,13},{2,14},{3,15},{4,0},{5,1},{6,2},{7,3},{8,4},{9,5},{1... | collective-permute-start | bytes 786440 | tf_op jit(solution)/shard_map/ppermute | solution.py:87
  108.7 14.4 %collective-permute-start.16 = (bf16[4,8,16,256]{3,1,2,0:T(8,128)(2,1)S(1)}, bf16[4,8,16,256]{3,1,2,0:T(8,128)(2,1)S(1)}, u32[]{:S(2)}, u32[]{:S(2)}) collective-permute-start(bf16[4,8,16,256]{3,1,2,0:T(8,128)(2,1)S(1)} %get-tuple-element.44), channel_id=1, source_target_pairs={{0,8},{1,9},{2,10},{3,11},{4,12},{5,13},{6,14},{7,15},{8,0},{9,1},... | collective-permute-start | bytes 786440 | tf_op jit(solution)/shard_map/ppermute | solution.py:87
  110.9 12.2 %collective-permute-start.15 = (bf16[4,8,16,256]{3,1,2,0:T(8,128)(2,1)S(1)}, bf16[4,8,16,256]{3,1,2,0:T(8,128)(2,1)S(1)}, u32[]{:S(2)}, u32[]{:S(2)}) collective-permute-start(bf16[4,8,16,256]{3,1,2,0:T(8,128)(2,1)S(1)} %get-tuple-element.44), channel_id=1, source_target_pairs={{0,4},{1,5},{2,6},{3,7},{4,8},{5,9},{6,10},{7,11},{8,12},{9,13},{1... | collective-permute-start | bytes 786440 | tf_op jit(solution)/shard_map/ppermute | solution.py:87
  113.5 13.9 %collective-permute-start.10 = (bf16[4,8,16,256]{3,1,2,0:T(8,128)(2,1)S(1)}, bf16[4,8,16,256]{3,1,2,0:T(8,128)(2,1)}, u32[]{:S(2)}, u32[]{:S(2)}) collective-permute-start(bf16[4,8,16,256]{3,1,2,0:T(8,128)(2,1)S(1)} %get-tuple-element.38), channel_id=1, source_target_pairs={{0,12},{1,13},{2,14},{3,15},{4,0},{5,1},{6,2},{7,3},{8,4},{9,5},{1... | collective-permute-start | bytes 786440 | tf_op jit(solution)/shard_map/ppermute | solution.py:87
  117.7 11.6 %collective-permute-start.9 = (bf16[4,8,16,256]{3,1,2,0:T(8,128)(2,1)S(1)}, bf16[4,8,16,256]{3,1,2,0:T(8,128)(2,1)}, u32[]{:S(2)}, u32[]{:S(2)}) collective-permute-start(bf16[4,8,16,256]{3,1,2,0:T(8,128)(2,1)S(1)} %get-tuple-element.38), channel_id=1, source_target_pairs={{0,8},{1,9},{2,10},{3,11},{4,12},{5,13},{6,14},{7,15},{8,0},{9,1},... | collective-permute-start | bytes 786440 | tf_op jit(solution)/shard_map/ppermute | solution.py:87
  121.2 13.1 %collective-permute-start.8 = (bf16[4,8,16,256]{3,1,2,0:T(8,128)(2,1)S(1)}, bf16[4,8,16,256]{3,1,2,0:T(8,128)(2,1)}, u32[]{:S(2)}, u32[]{:S(2)}) collective-permute-start(bf16[4,8,16,256]{3,1,2,0:T(8,128)(2,1)S(1)} %get-tuple-element.38), channel_id=1, source_target_pairs={{0,4},{1,5},{2,6},{3,7},{4,8},{5,9},{6,10},{7,11},{8,12},{9,13},{1... | collective-permute-start | bytes 786440 | tf_op jit(solution)/shard_map/ppermute | solution.py:87
  137.2 30.9 %collective-permute-start.19 = (f32[8,16,256]{2,0,1:T(8,128)S(1)}, f32[8,16,256]{2,0,1:T(8,128)S(1)}, u32[]{:S(2)}, u32[]{:S(2)}) collective-permute-start(f32[8,16,256]{2,0,1:T(8,128)S(1)} %get-tuple-element.28), channel_id=1, source_target_pairs={{0,256},{256,0},{1,257},{257,1},{2,258},{258,2},{3,259},{259,3},{4... | collective-permute-start | bytes 393224 | tf_op jit(solution)/shard_map/ppermute | solution.py:102
  146.9 24.0 %collective-permute-start.18 = (f32[8,16,256]{2,0,1:T(8,128)S(1)}, f32[8,16,256]{2,0,1:T(8,128)S(1)}, u32[]{:S(2)}, u32[]{:S(2)}) collective-permute-start(f32[8,16,256]{2,0,1:T(8,128)S(1)} %get-tuple-element.27), channel_id=1, source_target_pairs={{0,256},{256,0},{1,257},{257,1},{2,258},{258,2},{3,259},{259,3},{4... | collective-permute-start | bytes 393224 | tf_op jit(solution)/shard_map/ppermute | solution.py:102
  (17 other events, 76.6 us)

commit v5 on v3

--- a/solution.py
+++ b/solution.py
@@ -114,19 +114,27 @@
     count = lax.axis_size("gy")
     side = int(round(count ** 0.5))
     me = lax.axis_index("gy")
-    across = [rounded]
-    for shift in range(1, side):
-        pairs = [(i, (i // side) * side + (i % side + shift) % side) for i in range(count)]
-        across.append(lax.ppermute(rounded, "gy", pairs))
-    row = jnp.stack(across)
-    along = [row]
-    for shift in range(1, side):
-        pairs = [(i, (i + side * shift) % count) for i in range(count)]
-        along.append(lax.ppermute(row, "gy", pairs))
+    def inner(shift):
+        return [(i, (i // side) * side + (i % side + shift) % side) for i in range(count)]
+
+    def outer(shift):
+        return [(i, (i + side * shift) % count) for i in range(count)]
+
+    def gather(value, first, second):
+        row = jnp.stack([value] + [lax.ppermute(value, "gy", first(t)) for t in range(1, side)])
+        return jnp.stack([row] + [lax.ppermute(row, "gy", second(t)) for t in range(1, side)])
+
     halves = cols_y // block_size
-    pieces = jnp.stack(along).reshape(count, layers, rows_x, halves, block_size)
+    front = gather(rounded[..., :block_size], inner, outer)
+    back = gather(rounded[..., block_size:], outer, inner)
+    pieces = jnp.stack(
+        [front.reshape(count, layers, rows_x, block_size), back.reshape(count, layers, rows_x, block_size)],
+        axis=3,
+    )
     owner = block_cols // halves
-    slot = ((me // side - owner // side) % side) * side + (me % side - owner % side) % side
+    step_x = (me // side - owner // side) % side
+    step_y = (me % side - owner % side) % side
+    slot = jnp.where(block_cols % halves == 0, step_x * side + step_y, step_y * side + step_x)
     chosen = (
         (slot[:, :, None, None] == jnp.arange(count, dtype=jnp.int32)[None, None, :, None])
         & ((block_cols % halves)[:, :, None, None] == jnp.arange(halves, dtype=jnp.int32)[None, None, None, :])

time: 162 us -> 163 us (level)
  the two profiles are of different devices: /device:TPU:96 before, /device:TPU:32 now
where the time goes in v5:
time: 163 us; the launch traced here: 162 us
  starting transfers between devices  77.9 us (48%)
  waiting for transfers between devices  49.7 us (30%)
  local copies, waits for them, and re-layouts  19.2 us (12%)
  other arithmetic  13 us (8%)
    ppermute x1, waiting for transfers between devices, shards(): rounded = (mine + lax.ppermute(other, 'sec', partner)).astype(jnp.bfloat16)  22 us
    ppermute x6, starting transfers between devices, gather(): lax.ppermute(value, 'gy', first(t))  21.1 us
    ppermute x6, starting transfers between devices, gather(): lax.ppermute(row, 'gy', second(t))  19.5 us
    ppermute x1, waiting for transfers between devices, shards(): sensitivity = partial_sens + lax.ppermute(partial_sens, 'sec', partner)  15.3 us
    ppermute x1, starting transfers between devices, shards(): sensitivity = partial_sens + lax.ppermute(partial_sens, 'sec', partner)  15 us
    ppermute x1, starting transfers between devices, shards(): rounded = (mine + lax.ppermute(other, 'sec', partner)).astype(jnp.bfloat16)  11.4 us
    ppermute x2, starting transfers between devices, extended(): lax.ppermute(tail, axis, [(i, (i + 1) % count) for i in range(ends)])  7.58 us
    ppermute x6, waiting for transfers between devices, gather(): lax.ppermute(row, 'gy', second(t))  6.88 us
  transfers between devices with their start and end apart: 18, of which 6 were waited for; matrix products, arithmetic and copies ran while one was open for 5% of the time, Pallas kernels for 0%

profile of v5, /device:TPU:32, one launch (start us, length us, event | category | flops | bytes accessed | tf_op | source)
XLA Modules:
  0.0 162.3 jit_solution(7039055075051603481)
XLA Ops:
  4.8 1.9 %collective-permute-start.1 = (f32[6,16,2,256]{3,1,2,0:T(8,128)S(1)}, f32[6,16,2,256]{3,1,2,0:T(8,128)S(1)}, u32[]{:S(2)}, u32[]{:S(2)}) collective-permute-start(f32[6,16,2,256]{3,1,2,0:T(8,128)S(1)} %get-tuple-element.26), channel_id=1, source_target_pairs={{16,0},{32,16},{48,32},{64,48},{80,64},{96,80},{112,96},{128,112},... | collective-permute-start | bytes 589832 | tf_op jit(solution)/shard_map/ppermute | solution.py:17
  6.8 2.4 %collective-permute-start = (f32[6,16,2,256]{3,1,2,0:T(8,128)S(1)}, f32[6,16,2,256]{3,1,2,0:T(8,128)S(1)}, u32[]{:S(2)}, u32[]{:S(2)}) collective-permute-start(f32[6,16,2,256]{3,1,2,0:T(8,128)S(1)} %get-tuple-element.25), channel_id=1, source_target_pairs={{0,16},{16,32},{32,48},{48,64},{64,80},{80,96},{96,112},{112,128},... | collective-permute-start | bytes 589832 | tf_op jit(solution)/shard_map/ppermute | solution.py:15
  9.6 2.4 %select_reduce_fusion = f32[2,16,18,258]{3,1,2,0:T(8,128)} fusion(f32[2,8]{1,0:T(2,128)S(1)} %slice_bitcast_fusion.2, pred[2,8,258]{2,1,0:T(8,128)(4,1)S(1)} %broadcast_compare_fusion, pred[2,8,16,18]{2,3,1,0:T(8,128)(4,1)S(1)} %broadcast_and_fusion), kind=kLoop, calls=%fused_computation | loop fusion | flops 3417984 | bytes 603232 | tf_op jit(solution)/shard_map/reduce_sum | solution.py:68
  12.0 5.6 %collective-permute-done = f32[6,16,2,256]{3,1,2,0:T(8,128)S(1)} collective-permute-done((f32[6,16,2,256]{3,1,2,0:T(8,128)S(1)}, f32[6,16,2,256]{3,1,2,0:T(8,128)S(1)}, u32[]{:S(2)}, u32[]{:S(2)}) %collective-permute-start) | collective-permute-done | bytes 196640 | tf_op jit(solution)/shard_map/ppermute | solution.py:15
  24.3 5.2 %collective-permute-start.2 = (f32[6,16,20,2]{2,1,3,0:T(8,128)}, f32[6,16,20,2]{2,1,3,0:T(8,128)}, u32[]{:S(2)}, u32[]{:S(2)}) collective-permute-start(f32[6,16,20,2]{2,1,3,0:T(8,128)} %copy.80), channel_id=1, source_target_pairs={{0,1},{1,2},{2,3},{3,4},{4,5},{5,6},{6,7},{7,8},{8,9},{9,10},{10,1... | collective-permute-start | bytes 46088 | tf_op jit(solution)/shard_map/ppermute | solution.py:15
  33.5 3.6 %pad_maximum_fusion = f32[6,16,20,260]{3,1,2,0:T(8,128)S(1)} fusion(f32[6,16,20,2]{3,1,2,0:T(8,128)S(1)} %copy.83, f32[6,16,2,256]{3,1,2,0:T(8,128)} %copy-done.8, f32[1,16,16,256]{3,1,2,0:T(8,128)} %copy-done.3, f32[2,16,16,256]{3,1,2,0:T(8,128)S(1)} %copy.79, f32[1,16,16,256]{3,1,2,0:T(8,128)} %copy-done.5, f32[2,16,16,256]{3,1,2,0:T(8,128)S(1)} %copy.78, ...), kind=kLoop, calls=%fused_computation.1 | loop fusion | flops 3494400 | bytes 3993600 | tf_op jit(solution)/shard_map/concatenate | solution.py:13
  44.8 11.4 %collective-permute-start.4 = (f32[16,16,256]{2,0,1:T(8,128)S(1)}, f32[16,16,256]{2,0,1:T(8,128)S(1)}, u32[]{:S(2)}, u32[]{:S(2)}) collective-permute-start(f32[16,16,256]{2,0,1:T(8,128)S(1)} %broadcast_select_fusion), channel_id=1, source_target_pairs={{0,256},{256,0},{1,257},{257,1},{2,258},{258,2},{3,259},{259,3},{4... | collective-permute-start | bytes 786440 | tf_op jit(solution)/shard_map/ppermute | solution.py:112
  56.3 22.0 %collective-permute-done.4 = f32[16,16,256]{2,0,1:T(8,128)S(1)} collective-permute-done((f32[16,16,256]{2,0,1:T(8,128)S(1)}, f32[16,16,256]{2,0,1:T(8,128)S(1)}, u32[]{:S(2)}, u32[]{:S(2)}) %collective-permute-start.4) | collective-permute-done | bytes 262176 | tf_op jit(solution)/shard_map/ppermute | solution.py:112
  78.4 1.9 %collective-permute-start.13 = (bf16[16,16,128]{2,0,1:T(8,128)(2,1)S(1)}, bf16[16,16,128]{2,0,1:T(8,128)(2,1)S(1)}, u32[]{:S(2)}, u32[]{:S(2)}) collective-permute-start(bf16[16,16,128]{2,0,1:T(8,128)(2,1)S(1)} %get-tuple-element.41), channel_id=1, source_target_pairs={{0,12},{1,13},{2,14},{3,15},{4,0},{5,1},{6,2},{7,3},{8,4},{9,5},{1... | collective-permute-start | bytes 196616 | tf_op jit(solution)/shard_map/ppermute | solution.py:124
  80.3 1.9 %collective-permute-start.12 = (bf16[16,16,128]{2,0,1:T(8,128)(2,1)S(1)}, bf16[16,16,128]{2,0,1:T(8,128)(2,1)S(1)}, u32[]{:S(2)}, u32[]{:S(2)}) collective-permute-start(bf16[16,16,128]{2,0,1:T(8,128)(2,1)S(1)} %get-tuple-element.41), channel_id=1, source_target_pairs={{0,8},{1,9},{2,10},{3,11},{4,12},{5,13},{6,14},{7,15},{8,0},{9,1},... | collective-permute-start | bytes 196616 | tf_op jit(solution)/shard_map/ppermute | solution.py:124
  82.3 3.9 %collective-permute-start.11 = (bf16[16,16,128]{2,0,1:T(8,128)(2,1)S(1)}, bf16[16,16,128]{2,0,1:T(8,128)(2,1)S(1)}, u32[]{:S(2)}, u32[]{:S(2)}) collective-permute-start(bf16[16,16,128]{2,0,1:T(8,128)(2,1)S(1)} %get-tuple-element.41), channel_id=1, source_target_pairs={{0,4},{1,5},{2,6},{3,7},{4,8},{5,9},{6,10},{7,11},{8,12},{9,13},{1... | collective-permute-start | bytes 196616 | tf_op jit(solution)/shard_map/ppermute | solution.py:124
  86.2 8.7 %collective-permute-start.7 = (bf16[16,16,128]{2,0,1:T(8,128)(2,1)S(1)}, bf16[16,16,128]{2,0,1:T(8,128)(2,1)S(1)}, u32[]{:S(2)}, u32[]{:S(2)}) collective-permute-start(bf16[16,16,128]{2,0,1:T(8,128)(2,1)S(1)} %get-tuple-element.42), channel_id=1, source_target_pairs={{0,3},{1,0},{2,1},{3,2},{4,7},{5,4},{6,5},{7,6},{8,11},{9,8},{10,9... | collective-permute-start | bytes 196616 | tf_op jit(solution)/shard_map/ppermute | solution.py:124
  94.9 1.9 %collective-permute-start.6 = (bf16[16,16,128]{2,0,1:T(8,128)(2,1)S(1)}, bf16[16,16,128]{2,0,1:T(8,128)(2,1)S(1)}, u32[]{:S(2)}, u32[]{:S(2)}) collective-permute-start(bf16[16,16,128]{2,0,1:T(8,128)(2,1)S(1)} %get-tuple-element.42), channel_id=1, source_target_pairs={{0,2},{1,3},{2,0},{3,1},{4,6},{5,7},{6,4},{7,5},{8,10},{9,11},{10,... | collective-permute-start | bytes 196616 | tf_op jit(solution)/shard_map/ppermute | solution.py:124
  96.9 2.8 %collective-permute-start.5 = (bf16[16,16,128]{2,0,1:T(8,128)(2,1)S(1)}, bf16[16,16,128]{2,0,1:T(8,128)(2,1)S(1)}, u32[]{:S(2)}, u32[]{:S(2)}) collective-permute-start(bf16[16,16,128]{2,0,1:T(8,128)(2,1)S(1)} %get-tuple-element.42), channel_id=1, source_target_pairs={{0,1},{1,2},{2,3},{3,0},{4,5},{5,6},{6,7},{7,4},{8,9},{9,10},{10,1... | collective-permute-start | bytes 196616 | tf_op jit(solution)/shard_map/ppermute | solution.py:124
  99.7 4.3 %collective-permute-start.16 = (bf16[4,16,16,128]{3,1,2,0:T(8,128)(2,1)S(1)}, bf16[4,16,16,128]{3,1,2,0:T(8,128)(2,1)S(1)}, u32[]{:S(2)}, u32[]{:S(2)}) collective-permute-start(bf16[4,16,16,128]{3,1,2,0:T(8,128)(2,1)S(1)} %get-tuple-element.38), channel_id=1, source_target_pairs={{0,3},{1,0},{2,1},{3,2},{4,7},{5,4},{6,5},{7,6},{8,11},{9,8},{10,9... | collective-permute-start | bytes 786440 | tf_op jit(solution)/shard_map/ppermute | solution.py:125
  104.1 4.2 %collective-permute-start.15 = (bf16[4,16,16,128]{3,1,2,0:T(8,128)(2,1)S(1)}, bf16[4,16,16,128]{3,1,2,0:T(8,128)(2,1)S(1)}, u32[]{:S(2)}, u32[]{:S(2)}) collective-permute-start(bf16[4,16,16,128]{3,1,2,0:T(8,128)(2,1)S(1)} %get-tuple-element.38), channel_id=1, source_target_pairs={{0,2},{1,3},{2,0},{3,1},{4,6},{5,7},{6,4},{7,5},{8,10},{9,11},{10,... | collective-permute-start | bytes 786440 | tf_op jit(solution)/shard_map/ppermute | solution.py:125
  108.3 1.9 %collective-permute-start.14 = (bf16[4,16,16,128]{3,1,2,0:T(8,128)(2,1)S(1)}, bf16[4,16,16,128]{3,1,2,0:T(8,128)(2,1)S(1)}, u32[]{:S(2)}, u32[]{:S(2)}) collective-permute-start(bf16[4,16,16,128]{3,1,2,0:T(8,128)(2,1)S(1)} %get-tuple-element.38), channel_id=1, source_target_pairs={{0,1},{1,2},{2,3},{3,0},{4,5},{5,6},{6,7},{7,4},{8,9},{9,10},{10,1... | collective-permute-start | bytes 786440 | tf_op jit(solution)/shard_map/ppermute | solution.py:125
  110.3 4.4 %collective-permute-start.10 = (bf16[4,16,16,128]{3,1,2,0:T(8,128)(2,1)S(1)}, bf16[4,16,16,128]{3,1,2,0:T(8,128)(2,1)S(1)}, u32[]{:S(2)}, u32[]{:S(2)}) collective-permute-start(bf16[4,16,16,128]{3,1,2,0:T(8,128)(2,1)S(1)} %get-tuple-element.36), channel_id=1, source_target_pairs={{0,12},{1,13},{2,14},{3,15},{4,0},{5,1},{6,2},{7,3},{8,4},{9,5},{1... | collective-permute-start | bytes 786440 | tf_op jit(solution)/shard_map/ppermute | solution.py:125
  114.8 1.9 %collective-permute-start.9 = (bf16[4,16,16,128]{3,1,2,0:T(8,128)(2,1)S(1)}, bf16[4,16,16,128]{3,1,2,0:T(8,128)(2,1)S(1)}, u32[]{:S(2)}, u32[]{:S(2)}) collective-permute-start(bf16[4,16,16,128]{3,1,2,0:T(8,128)(2,1)S(1)} %get-tuple-element.36), channel_id=1, source_target_pairs={{0,8},{1,9},{2,10},{3,11},{4,12},{5,13},{6,14},{7,15},{8,0},{9,1},... | collective-permute-start | bytes 786440 | tf_op jit(solution)/shard_map/ppermute | solution.py:125
  116.7 2.8 %collective-permute-start.8 = (bf16[4,16,16,128]{3,1,2,0:T(8,128)(2,1)S(1)}, bf16[4,16,16,128]{3,1,2,0:T(8,128)(2,1)S(1)}, u32[]{:S(2)}, u32[]{:S(2)}) collective-permute-start(bf16[4,16,16,128]{3,1,2,0:T(8,128)(2,1)S(1)} %get-tuple-element.36), channel_id=1, source_target_pairs={{0,4},{1,5},{2,6},{3,7},{4,8},{5,9},{6,10},{7,11},{8,12},{9,13},{1... | collective-permute-start | bytes 786440 | tf_op jit(solution)/shard_map/ppermute | solution.py:125
  121.3 3.3 %collective-permute-done.9 = bf16[4,16,16,128]{3,1,2,0:T(8,128)(2,1)S(1)} collective-permute-done((bf16[4,16,16,128]{3,1,2,0:T(8,128)(2,1)S(1)}, bf16[4,16,16,128]{3,1,2,0:T(8,128)(2,1)S(1)}, u32[]{:S(2)}, u32[]{:S(2)}) %collective-permute-start.9) | collective-permute-done | bytes 262176 | tf_op jit(solution)/shard_map/ppermute | solution.py:125
  124.6 2.7 %collective-permute-done.8 = bf16[4,16,16,128]{3,1,2,0:T(8,128)(2,1)S(1)} collective-permute-done((bf16[4,16,16,128]{3,1,2,0:T(8,128)(2,1)S(1)}, bf16[4,16,16,128]{3,1,2,0:T(8,128)(2,1)S(1)}, u32[]{:S(2)}, u32[]{:S(2)}) %collective-permute-start.8) | collective-permute-done | bytes 262176 | tf_op jit(solution)/shard_map/ppermute | solution.py:125
  130.0 15.0 %collective-permute-start.17 = (f32[16,16,256]{2,0,1:T(8,128)S(1)}, f32[16,16,256]{2,0,1:T(8,128)S(1)}, u32[]{:S(2)}, u32[]{:S(2)}) collective-permute-start(f32[16,16,256]{2,0,1:T(8,128)S(1)} %fusion.37), channel_id=1, source_target_pairs={{0,256},{256,0},{1,257},{257,1},{2,258},{258,2},{3,259},{259,3},{4... | collective-permute-start | bytes 786440 | tf_op jit(solution)/shard_map/ppermute | solution.py:148
  146.1 15.3 %collective-permute-done.17 = f32[16,16,256]{2,0,1:T(8,128)S(1)} collective-permute-done((f32[16,16,256]{2,0,1:T(8,128)S(1)}, f32[16,16,256]{2,0,1:T(8,128)S(1)}, u32[]{:S(2)}, u32[]{:S(2)}) %collective-permute-start.17) | collective-permute-done | bytes 262176 | tf_op jit(solution)/shard_map/ppermute | solution.py:148
  (107 shorter events, 29.4 us)
Async XLA Ops:
  0.6 128.4 %copy-start = (bf16[2,7,128,128]{3,2,1,0:T(8,128)(2,1)S(1)}, bf16[2,7,128,128]{3,2,1,0:T(8,128)(2,1)}, u32[]{:S(2)}) copy-start(bf16[2,7,128,128]{3,2,1,0:T(8,128)(2,1)} %param.18) | copy-start | bytes 1376260
  0.7 8.6 %copy-start.16 = (s32[2,8,3]{1,0,2:T(2,128)S(1)}, s32[2,8,3]{1,0,2:T(2,128)}, u32[]{:S(2)}) copy-start(s32[2,8,3]{1,0,2:T(2,128)} %param.15) | copy-start | bytes 580
  4.8 13.7 %copy-start.3 = (f32[1,16,16,256]{3,1,2,0:T(8,128)}, f32[1,16,16,256]{3,1,2,0:T(8,128)S(1)}, u32[]{:S(2)}) copy-start(f32[1,16,16,256]{3,1,2,0:T(8,128)S(1)} %get-tuple-element.46) | copy-start | bytes 786436
  4.8 13.7 %copy-start.5 = (f32[1,16,16,256]{3,1,2,0:T(8,128)}, f32[1,16,16,256]{3,1,2,0:T(8,128)S(1)}, u32[]{:S(2)}) copy-start(f32[1,16,16,256]{3,1,2,0:T(8,128)S(1)} %get-tuple-element.47) | copy-start | bytes 786436
  4.8 7.2 %collective-permute-start.1 = (f32[6,16,2,256]{3,1,2,0:T(8,128)S(1)}, f32[6,16,2,256]{3,1,2,0:T(8,128)S(1)}, u32[]{:S(2)}, u32[]{:S(2)}) collective-permute-start(f32[6,16,2,256]{3,1,2,0:T(8,128)S(1)} %get-tuple-element.26), channel_id=1, source_target_pairs={{16,0},{32,16},{48,32},{64,48},{80,64},{96,80},{112,96},{128,112},... | collective-permute-start | bytes 589832 | tf_op jit(solution)/shard_map/ppermute | solution.py:17
  6.8 10.8 %collective-permute-start = (f32[6,16,2,256]{3,1,2,0:T(8,128)S(1)}, f32[6,16,2,256]{3,1,2,0:T(8,128)S(1)}, u32[]{:S(2)}, u32[]{:S(2)}) collective-permute-start(f32[6,16,2,256]{3,1,2,0:T(8,128)S(1)} %get-tuple-element.25), channel_id=1, source_target_pairs={{0,16},{16,32},{32,48},{48,64},{64,80},{80,96},{96,112},{112,128},... | collective-permute-start | bytes 589832 | tf_op jit(solution)/shard_map/ppermute | solution.py:15
  18.5 10.9 %copy-start.14 = (bf16[2,2,16,16,256]{4,3,2,1,0:T(8,128)(2,1)S(1)}, bf16[2,2,16,16,256]{4,3,2,1,0:T(8,128)(2,1)}, u32[]{:S(2)}) copy-start(bf16[2,2,16,16,256]{4,3,2,1,0:T(8,128)(2,1)} %param.11) | copy-start | bytes 1572868
  21.7 8.6 %collective-permute-start.3 = (f32[6,16,20,2]{2,1,3,0:T(8,128)S(1)}, f32[6,16,20,2]{2,1,3,0:T(8,128)}, u32[]{:S(2)}, u32[]{:S(2)}) collective-permute-start(f32[6,16,20,2]{2,1,3,0:T(8,128)S(1)} %copy.81), channel_id=1, source_target_pairs={{1,0},{2,1},{3,2},{4,3},{5,4},{6,5},{7,6},{8,7},{9,8},{10,9},{11,1... | collective-permute-start | bytes 46088 | tf_op jit(solution)/shard_map/ppermute | solution.py:17
  24.3 7.6 %collective-permute-start.2 = (f32[6,16,20,2]{2,1,3,0:T(8,128)}, f32[6,16,20,2]{2,1,3,0:T(8,128)}, u32[]{:S(2)}, u32[]{:S(2)}) collective-permute-start(f32[6,16,20,2]{2,1,3,0:T(8,128)} %copy.80), channel_id=1, source_target_pairs={{0,1},{1,2},{2,3},{3,4},{4,5},{5,6},{6,7},{7,8},{8,9},{9,10},{10,1... | collective-permute-start | bytes 46088 | tf_op jit(solution)/shard_map/ppermute | solution.py:15
  44.7 41.5 %copy-start.17 = (s32[2,7]{1,0:T(2,128)S(1)}, s32[2,7]{1,0:T(2,128)}, u32[]{:S(2)}) copy-start(s32[2,7]{1,0:T(2,128)} %param.19) | copy-start | bytes 172
  44.8 33.4 %collective-permute-start.4 = (f32[16,16,256]{2,0,1:T(8,128)S(1)}, f32[16,16,256]{2,0,1:T(8,128)S(1)}, u32[]{:S(2)}, u32[]{:S(2)}) collective-permute-start(f32[16,16,256]{2,0,1:T(8,128)S(1)} %broadcast_select_fusion), channel_id=1, source_target_pairs={{0,256},{256,0},{1,257},{257,1},{2,258},{258,2},{3,259},{259,3},{4... | collective-permute-start | bytes 786440 | tf_op jit(solution)/shard_map/ppermute | solution.py:112
  78.4 18.5 %collective-permute-start.13 = (bf16[16,16,128]{2,0,1:T(8,128)(2,1)S(1)}, bf16[16,16,128]{2,0,1:T(8,128)(2,1)S(1)}, u32[]{:S(2)}, u32[]{:S(2)}) collective-permute-start(bf16[16,16,128]{2,0,1:T(8,128)(2,1)S(1)} %get-tuple-element.41), channel_id=1, source_target_pairs={{0,12},{1,13},{2,14},{3,15},{4,0},{5,1},{6,2},{7,3},{8,4},{9,5},{1... | collective-permute-start | bytes 196616 | tf_op jit(solution)/shard_map/ppermute | solution.py:124
  80.3 19.3 %collective-permute-start.12 = (bf16[16,16,128]{2,0,1:T(8,128)(2,1)S(1)}, bf16[16,16,128]{2,0,1:T(8,128)(2,1)S(1)}, u32[]{:S(2)}, u32[]{:S(2)}) collective-permute-start(bf16[16,16,128]{2,0,1:T(8,128)(2,1)S(1)} %get-tuple-element.41), channel_id=1, source_target_pairs={{0,8},{1,9},{2,10},{3,11},{4,12},{5,13},{6,14},{7,15},{8,0},{9,1},... | collective-permute-start | bytes 196616 | tf_op jit(solution)/shard_map/ppermute | solution.py:124
  82.3 17.4 %collective-permute-start.11 = (bf16[16,16,128]{2,0,1:T(8,128)(2,1)S(1)}, bf16[16,16,128]{2,0,1:T(8,128)(2,1)S(1)}, u32[]{:S(2)}, u32[]{:S(2)}) collective-permute-start(bf16[16,16,128]{2,0,1:T(8,128)(2,1)S(1)} %get-tuple-element.41), channel_id=1, source_target_pairs={{0,4},{1,5},{2,6},{3,7},{4,8},{5,9},{6,10},{7,11},{8,12},{9,13},{1... | collective-permute-start | bytes 196616 | tf_op jit(solution)/shard_map/ppermute | solution.py:124
  86.2 22.1 %collective-permute-start.7 = (bf16[16,16,128]{2,0,1:T(8,128)(2,1)S(1)}, bf16[16,16,128]{2,0,1:T(8,128)(2,1)S(1)}, u32[]{:S(2)}, u32[]{:S(2)}) collective-permute-start(bf16[16,16,128]{2,0,1:T(8,128)(2,1)S(1)} %get-tuple-element.42), channel_id=1, source_target_pairs={{0,3},{1,0},{2,1},{3,2},{4,7},{5,4},{6,5},{7,6},{8,11},{9,8},{10,9... | collective-permute-start | bytes 196616 | tf_op jit(solution)/shard_map/ppermute | solution.py:124
  94.9 15.3 %collective-permute-start.6 = (bf16[16,16,128]{2,0,1:T(8,128)(2,1)S(1)}, bf16[16,16,128]{2,0,1:T(8,128)(2,1)S(1)}, u32[]{:S(2)}, u32[]{:S(2)}) collective-permute-start(bf16[16,16,128]{2,0,1:T(8,128)(2,1)S(1)} %get-tuple-element.42), channel_id=1, source_target_pairs={{0,2},{1,3},{2,0},{3,1},{4,6},{5,7},{6,4},{7,5},{8,10},{9,11},{10,... | collective-permute-start | bytes 196616 | tf_op jit(solution)/shard_map/ppermute | solution.py:124
  96.9 13.4 %collective-permute-start.5 = (bf16[16,16,128]{2,0,1:T(8,128)(2,1)S(1)}, bf16[16,16,128]{2,0,1:T(8,128)(2,1)S(1)}, u32[]{:S(2)}, u32[]{:S(2)}) collective-permute-start(bf16[16,16,128]{2,0,1:T(8,128)(2,1)S(1)} %get-tuple-element.42), channel_id=1, source_target_pairs={{0,1},{1,2},{2,3},{3,0},{4,5},{5,6},{6,7},{7,4},{8,9},{9,10},{10,1... | collective-permute-start | bytes 196616 | tf_op jit(solution)/shard_map/ppermute | solution.py:124
  99.7 17.0 %collective-permute-start.16 = (bf16[4,16,16,128]{3,1,2,0:T(8,128)(2,1)S(1)}, bf16[4,16,16,128]{3,1,2,0:T(8,128)(2,1)S(1)}, u32[]{:S(2)}, u32[]{:S(2)}) collective-permute-start(bf16[4,16,16,128]{3,1,2,0:T(8,128)(2,1)S(1)} %get-tuple-element.38), channel_id=1, source_target_pairs={{0,3},{1,0},{2,1},{3,2},{4,7},{5,4},{6,5},{7,6},{8,11},{9,8},{10,9... | collective-permute-start | bytes 786440 | tf_op jit(solution)/shard_map/ppermute | solution.py:125
  104.1 15.4 %collective-permute-start.15 = (bf16[4,16,16,128]{3,1,2,0:T(8,128)(2,1)S(1)}, bf16[4,16,16,128]{3,1,2,0:T(8,128)(2,1)S(1)}, u32[]{:S(2)}, u32[]{:S(2)}) collective-permute-start(bf16[4,16,16,128]{3,1,2,0:T(8,128)(2,1)S(1)} %get-tuple-element.38), channel_id=1, source_target_pairs={{0,2},{1,3},{2,0},{3,1},{4,6},{5,7},{6,4},{7,5},{8,10},{9,11},{10,... | collective-permute-start | bytes 786440 | tf_op jit(solution)/shard_map/ppermute | solution.py:125
  108.3 11.2 %collective-permute-start.14 = (bf16[4,16,16,128]{3,1,2,0:T(8,128)(2,1)S(1)}, bf16[4,16,16,128]{3,1,2,0:T(8,128)(2,1)S(1)}, u32[]{:S(2)}, u32[]{:S(2)}) collective-permute-start(bf16[4,16,16,128]{3,1,2,0:T(8,128)(2,1)S(1)} %get-tuple-element.38), channel_id=1, source_target_pairs={{0,1},{1,2},{2,3},{3,0},{4,5},{5,6},{6,7},{7,4},{8,9},{9,10},{10,1... | collective-permute-start | bytes 786440 | tf_op jit(solution)/shard_map/ppermute | solution.py:125
  110.3 11.0 %collective-permute-start.10 = (bf16[4,16,16,128]{3,1,2,0:T(8,128)(2,1)S(1)}, bf16[4,16,16,128]{3,1,2,0:T(8,128)(2,1)S(1)}, u32[]{:S(2)}, u32[]{:S(2)}) collective-permute-start(bf16[4,16,16,128]{3,1,2,0:T(8,128)(2,1)S(1)} %get-tuple-element.36), channel_id=1, source_target_pairs={{0,12},{1,13},{2,14},{3,15},{4,0},{5,1},{6,2},{7,3},{8,4},{9,5},{1... | collective-permute-start | bytes 786440 | tf_op jit(solution)/shard_map/ppermute | solution.py:125
  114.8 9.9 %collective-permute-start.9 = (bf16[4,16,16,128]{3,1,2,0:T(8,128)(2,1)S(1)}, bf16[4,16,16,128]{3,1,2,0:T(8,128)(2,1)S(1)}, u32[]{:S(2)}, u32[]{:S(2)}) collective-permute-start(bf16[4,16,16,128]{3,1,2,0:T(8,128)(2,1)S(1)} %get-tuple-element.36), channel_id=1, source_target_pairs={{0,8},{1,9},{2,10},{3,11},{4,12},{5,13},{6,14},{7,15},{8,0},{9,1},... | collective-permute-start | bytes 786440 | tf_op jit(solution)/shard_map/ppermute | solution.py:125
  116.7 10.6 %collective-permute-start.8 = (bf16[4,16,16,128]{3,1,2,0:T(8,128)(2,1)S(1)}, bf16[4,16,16,128]{3,1,2,0:T(8,128)(2,1)S(1)}, u32[]{:S(2)}, u32[]{:S(2)}) collective-permute-start(bf16[4,16,16,128]{3,1,2,0:T(8,128)(2,1)S(1)} %get-tuple-element.36), channel_id=1, source_target_pairs={{0,4},{1,5},{2,6},{3,7},{4,8},{5,9},{6,10},{7,11},{8,12},{9,13},{1... | collective-permute-start | bytes 786440 | tf_op jit(solution)/shard_map/ppermute | solution.py:125
  130.0 31.4 %collective-permute-start.17 = (f32[16,16,256]{2,0,1:T(8,128)S(1)}, f32[16,16,256]{2,0,1:T(8,128)S(1)}, u32[]{:S(2)}, u32[]{:S(2)}) collective-permute-start(f32[16,16,256]{2,0,1:T(8,128)S(1)} %fusion.37), channel_id=1, source_target_pairs={{0,256},{256,0},{1,257},{257,1},{2,258},{258,2},{3,259},{259,3},{4... | collective-permute-start | bytes 786440 | tf_op jit(solution)/shard_map/ppermute | solution.py:148
  (14 other events, 35.5 us)

commit v6 on v2

--- a/solution.py
+++ b/solution.py
@@ -111,12 +111,16 @@
     partner = [(0, 1), (1, 0)]
     rounded = (mine + lax.ppermute(other, "sec", partner)).astype(jnp.bfloat16)
     row_blocks, per_row, block_size, _ = blocks.shape
-    piece = lax.all_gather(rounded, "gy", axis=2, tiled=True)
-    count = piece.shape[2] // block_size
-    split_rows = piece.reshape(layers, rows_x, count, block_size)
-    block_ids = jnp.arange(count, dtype=jnp.int32)
-    chosen = (block_cols[:, :, None] == block_ids[None, None, :]).astype(jnp.bfloat16)
-    portion = jnp.einsum("bkq,zxqj->bkzxj", chosen, split_rows, preferred_element_type=jnp.float32)
+    count = lax.axis_size("gy")
+    halves = cols_y // block_size
+    copies = jnp.broadcast_to(rounded[None], (count,) + rounded.shape)
+    gathered = lax.all_to_all(copies, "gy", 0, 0, tiled=False)
+    pieces = gathered.reshape(count, layers, rows_x, halves, block_size)
+    chosen = (
+        ((block_cols // halves)[:, :, None, None] == jnp.arange(count, dtype=jnp.int32)[None, None, :, None])
+        & ((block_cols % halves)[:, :, None, None] == jnp.arange(halves, dtype=jnp.int32)[None, None, None, :])
+    ).astype(jnp.bfloat16)
+    portion = jnp.einsum("bkph,pzxhj->bkzxj", chosen, pieces, preferred_element_type=jnp.float32)
     picked = portion.astype(jnp.bfloat16)
     head = jnp.einsum(
         "bkzxj,bkij->zxbi", picked, blocks, preferred_element_type=jnp.float32

time: 199 us -> 154 us (0.77)
  waiting for transfers between devices: 111 us -> 68.7 us
  between operations: 14.5 us -> 1.12 us
  starting transfers between devices: 38.2 us -> 45.5 us
  matrix products: 0.91 us -> 3.49 us
    all_gather x1 -> x0, waiting for transfers between devices: 64.6 us -> none  [shards(): piece = lax.all_gather(rounded, 'gy', axis=2, tiled=True)]
    all_to_all x0 -> x1, waiting for transfers between devices: none -> 29 us  [shards(): gathered = lax.all_to_all(copies, 'gy', 0, 0, tiled=False)]
    all_to_all x0 -> x1, starting transfers between devices: none -> 7.75 us  [shards(): gathered = lax.all_to_all(copies, 'gy', 0, 0, tiled=False)]
    ppermute x1, waiting for transfers between devices: 19.8 us -> 12.7 us  [shards(): sensitivity = partial_sens + lax.ppermute(partial_sens, 'sec', partner)]
    dot_general x1, matrix products: 0.5 us -> 3.08 us  [shards(): jnp.einsum('bkph,pzxhj->bkzxj', chosen, pieces, preferred_element_type=jn...]
    unnamed x46 -> x45, local copies, waits for them, and re-layouts: 10.2 us -> 8.18 us
    reshape x0 -> x1, local copies, waits for them, and re-layouts: none -> 2.06 us  [shards(): pieces = gathered.reshape(count, layers, rows_x, halves, block_size)]
  transfers between devices with their start and end apart: 7 -> 7, of which waited for: 5 -> 5; matrix products, arithmetic and copies ran while one was open for 4% -> 5% of each run, Pallas kernels for 0% -> 0%
where the time goes in v6:
time: 154 us
  waiting for transfers between devices  68.7 us (45%)
  starting transfers between devices  45.5 us (30%)
  local copies, waits for them, and re-layouts  23.2 us (15%)
  other arithmetic  11.6 us (8%)
  matrix products  3.49 us (2%)
    all_to_all x1, waiting for transfers between devices, shards(): gathered = lax.all_to_all(copies, 'gy', 0, 0, tiled=False)  29 us
    ppermute x1, waiting for transfers between devices, shards(): rounded = (mine + lax.ppermute(other, 'sec', partner)).astype(jnp.bfloat16)  23.2 us
    ppermute x1, starting transfers between devices, shards(): rounded = (mine + lax.ppermute(other, 'sec', partner)).astype(jnp.bfloat16)  15.1 us
    ppermute x1, waiting for transfers between devices, shards(): sensitivity = partial_sens + lax.ppermute(partial_sens, 'sec', partner)  12.7 us
    ppermute x1, starting transfers between devices, shards(): sensitivity = partial_sens + lax.ppermute(partial_sens, 'sec', partner)  11.7 us
    unnamed x45, local copies, waits for them, and re-layouts  8.18 us
    all_to_all x1, starting transfers between devices, shards(): gathered = lax.all_to_all(copies, 'gy', 0, 0, tiled=False)  7.75 us
    ppermute x2, starting transfers between devices, extended(): lax.ppermute(tail, axis, [(i, (i + 1) % count) for i in range(ends)])  6.04 us
  transfers between devices with their start and end apart: 7, of which 5 were waited for; matrix products, arithmetic and copies ran while one was open for 5% of the time, Pallas kernels for 0%

profile of v6, /device:TPU:32, one launch (start us, length us, event | category | flops | bytes accessed | tf_op | source)
XLA Modules:
  0.0 153.7 jit_solution(8732108871894476685)
XLA Ops:
  0.7 1.4 copy.68
  2.1 1.4 copy.69
  3.9 1.9 %collective-permute-start = (f32[6,16,2,256]{3,1,2,0:T(8,128)S(1)}, f32[6,16,2,256]{3,1,2,0:T(8,128)S(1)}, u32[]{:S(2)}, u32[]{:S(2)}) collective-permute-start(f32[6,16,2,256]{3,1,2,0:T(8,128)S(1)} %get-tuple-element.23), channel_id=1, source_target_pairs={{0,16},{16,32},{32,48},{48,64},{64,80},{80,96},{96,112},{112,128},... | collective-permute-start | bytes 589832 | tf_op jit(solution)/shard_map/ppermute | solution.py:15
  5.8 3.6 %collective-permute-start.1 = (f32[6,16,2,256]{3,1,2,0:T(8,128)S(1)}, f32[6,16,2,256]{3,1,2,0:T(8,128)S(1)}, u32[]{:S(2)}, u32[]{:S(2)}) collective-permute-start(f32[6,16,2,256]{3,1,2,0:T(8,128)S(1)} %get-tuple-element.24), channel_id=1, source_target_pairs={{16,0},{32,16},{48,32},{64,48},{80,64},{96,80},{112,96},{128,112},... | collective-permute-start | bytes 589832 | tf_op jit(solution)/shard_map/ppermute | solution.py:17
  9.9 2.4 %select_reduce_fusion = f32[2,16,18,258]{3,1,2,0:T(8,128)} fusion(f32[2,8]{1,0:T(2,128)S(1)} %slice_bitcast_fusion.2, pred[2,8,258]{2,1,0:T(8,128)(4,1)S(1)} %broadcast_compare_fusion, pred[2,8,16,18]{2,3,1,0:T(8,128)(4,1)S(1)} %broadcast_and_fusion), kind=kLoop, calls=%fused_computation | loop fusion | flops 3417984 | bytes 603232 | tf_op jit(solution)/shard_map/reduce_sum | solution.py:68
  13.9 1.3 fusion.47
  15.2 1.9 %copy.70 = f32[6,16,20,2]{2,1,3,0:T(8,128)S(1)} copy(f32[6,16,20,2]{3,1,2,0:T(8,128)} %get-tuple-element.21) | data formatting | bytes 30720 | tf_op jit(solution)/shard_map/slice | solution.py:12
  17.0 4.1 %collective-permute-start.2 = (f32[6,16,20,2]{2,1,3,0:T(8,128)S(1)}, f32[6,16,20,2]{2,1,3,0:T(8,128)}, u32[]{:S(2)}, u32[]{:S(2)}) collective-permute-start(f32[6,16,20,2]{2,1,3,0:T(8,128)S(1)} %copy.70), channel_id=1, source_target_pairs={{0,1},{1,2},{2,3},{3,4},{4,5},{5,6},{6,7},{7,8},{8,9},{9,10},{10,1... | collective-permute-start | bytes 46088 | tf_op jit(solution)/shard_map/ppermute | solution.py:15
  21.2 1.3 copy.71
  24.6 1.6 %copy.72 = f32[6,16,20,2]{3,1,2,0:T(8,128)S(1)} copy(f32[6,16,20,2]{2,1,3,0:T(8,128)} %collective-permute-done.2) | data formatting | bytes 30720 | tf_op jit(solution)/shard_map/ppermute | solution.py:15
  26.2 3.6 %collective-permute-done.3 = f32[6,16,20,2]{2,1,3,0:T(8,128)} collective-permute-done((f32[6,16,20,2]{2,1,3,0:T(8,128)}, f32[6,16,20,2]{2,1,3,0:T(8,128)}, u32[]{:S(2)}, u32[]{:S(2)}) %collective-permute-start.3) | collective-permute-done | bytes 15392 | tf_op jit(solution)/shard_map/ppermute | solution.py:17
  29.8 1.6 %copy.73 = f32[6,16,20,2]{3,1,2,0:T(8,128)S(1)} copy(f32[6,16,20,2]{2,1,3,0:T(8,128)} %collective-permute-done.3) | data formatting | bytes 30720 | tf_op jit(solution)/shard_map/ppermute | solution.py:17
  31.4 3.6 %pad_maximum_fusion = f32[6,16,20,260]{3,1,2,0:T(8,128)S(1)} fusion(f32[6,16,20,2]{3,1,2,0:T(8,128)S(1)} %copy.73, f32[6,16,2,256]{3,1,2,0:T(8,128)} %copy-done.10, f32[1,16,16,256]{3,1,2,0:T(8,128)} %copy-done.3, f32[2,16,16,256]{3,1,2,0:T(8,128)S(1)} %copy.69, f32[1,16,16,256]{3,1,2,0:T(8,128)} %copy-done.5, f32[2,16,16,256]{3,1,2,0:T(8,128)S(1)} %copy.68, ...), kind=kLoop, calls=%fused_computation.1 | loop fusion | flops 3494400 | bytes 3993600 | tf_op jit(solution)/shard_map/concatenate | solution.py:13
  38.9 1.5 copy-done.2
  40.9 1.3 add_multiply_fusion
  44.2 15.1 %collective-permute-start.4 = (f32[16,16,256]{2,0,1:T(8,128)S(1)}, f32[16,16,256]{2,0,1:T(8,128)S(1)}, u32[]{:S(2)}, u32[]{:S(2)}) collective-permute-start(f32[16,16,256]{2,0,1:T(8,128)S(1)} %broadcast_select_fusion), channel_id=1, source_target_pairs={{0,256},{256,0},{1,257},{257,1},{2,258},{258,2},{3,259},{259,3},{4... | collective-permute-start | bytes 786440 | tf_op jit(solution)/shard_map/ppermute | solution.py:112
  59.3 23.2 %collective-permute-done.4 = f32[16,16,256]{2,0,1:T(8,128)S(1)} collective-permute-done((f32[16,16,256]{2,0,1:T(8,128)S(1)}, f32[16,16,256]{2,0,1:T(8,128)S(1)}, u32[]{:S(2)}, u32[]{:S(2)}) %collective-permute-start.4) | collective-permute-done | bytes 262176 | tf_op jit(solution)/shard_map/ppermute | solution.py:112
  82.7 1.5 broadcast_in_dim.57
  84.2 7.8 %all-to-all-start = ((bf16[16,16,16,256]{3,2,1,0:T(8,128)(2,1)}), bf16[16,16,16,256]{3,2,1,0:T(8,128)(2,1)S(1)}, u32[]{:S(2)}, u32[]{:S(2)}) async-start(bf16[16,16,16,256]{3,2,1,0:T(8,128)(2,1)} %broadcast_in_dim.57), calls=%async_computation | async-start | bytes 4194304 | tf_op jit(solution)/shard_map/all_to_all | solution.py:117
  92.1 29.0 %all-to-all-done = bf16[16,16,16,256]{3,2,1,0:T(8,128)(2,1)S(1)} async-done(((bf16[16,16,16,256]{3,2,1,0:T(8,128)(2,1)}), bf16[16,16,16,256]{3,2,1,0:T(8,128)(2,1)S(1)}, u32[]{:S(2)}, u32[]{:S(2)}) %all-to-all-start) | async-done | bytes 2097184 | tf_op jit(solution)/shard_map/all_to_all | solution.py:117
  121.1 2.1 %reshape.86 = bf16[16,16,16,2,128]{4,3,2,1,0:T(2,128)(2,1)} reshape(bf16[16,16,16,256]{3,2,1,0:T(8,128)(2,1)S(1)} %all-to-all-done) | data formatting | bytes 4194304 | tf_op jit(solution)/shard_map/reshape | solution.py:118
  123.2 3.1 %bitcast_convert_fusion = bf16[2,7,16,16,128]{4,1,3,2,0:T(8,128)(2,1)S(1)} fusion(bf16[16,16,16,2,128]{4,3,2,1,0:T(2,128)(2,1)} %reshape.86, pred[2,7,2]{1,2,0:T(4,128)(4,1)S(1)} %iota_compare_fusion.2, pred[2,7,16]{2,1,0:T(8,128)(4,1)S(1)} %iota_compare_fusion.1), kind=kOutput, calls=%fused_computation.2 | convolution fusion | flops 29819328 | bytes 3014908 | tf_op jit(solution)/shard_map/bkph,pzxhj->bkzxj/dot_general | solution.py:123
  127.3 11.7 %collective-permute-start.5 = (f32[16,16,256]{2,0,1:T(8,128)S(1)}, f32[16,16,256]{2,0,1:T(8,128)S(1)}, u32[]{:S(2)}, u32[]{:S(2)}) collective-permute-start(f32[16,16,256]{2,0,1:T(8,128)S(1)} %fusion.39), channel_id=1, source_target_pairs={{0,256},{256,0},{1,257},{257,1},{2,258},{258,2},{3,259},{259,3},{4... | collective-permute-start | bytes 786440 | tf_op jit(solution)/shard_map/ppermute | solution.py:129
  140.1 12.7 %collective-permute-done.5 = f32[16,16,256]{2,0,1:T(8,128)S(1)} collective-permute-done((f32[16,16,256]{2,0,1:T(8,128)S(1)}, f32[16,16,256]{2,0,1:T(8,128)S(1)}, u32[]{:S(2)}, u32[]{:S(2)}) %collective-permute-start.5) | collective-permute-done | bytes 262176 | tf_op jit(solution)/shard_map/ppermute | solution.py:129
  (85 shorter events, 13.9 us)
Async XLA Ops:
  0.6 125.6 %copy-start = (bf16[2,7,128,128]{3,2,1,0:T(8,128)(2,1)S(1)}, bf16[2,7,128,128]{3,2,1,0:T(8,128)(2,1)}, u32[]{:S(2)}) copy-start(bf16[2,7,128,128]{3,2,1,0:T(8,128)(2,1)} %param.18) | copy-start | bytes 1376260
  0.6 2.8 %copy-start.16 = (f32[16,16,256]{2,1,0:T(8,128)S(1)}, f32[16,16,256]{2,1,0:T(8,128)}, u32[]{:S(2)}) copy-start(f32[16,16,256]{2,1,0:T(8,128)} %param.12) | copy-start | bytes 786436
  0.7 2.8 %copy-start.15 = (s32[16,16,256]{2,1,0:T(8,128)S(1)}, s32[16,16,256]{2,1,0:T(8,128)}, u32[]{:S(2)}) copy-start(s32[16,16,256]{2,1,0:T(8,128)} %param.14) | copy-start | bytes 786436
  2.1 7.4 %copy-start.18 = (s32[2,8,3]{1,0,2:T(2,128)S(1)}, s32[2,8,3]{1,0,2:T(2,128)}, u32[]{:S(2)}) copy-start(s32[2,8,3]{1,0,2:T(2,128)} %param.15) | copy-start | bytes 580
  2.1 7.5 %copy-start.20 = (f32[2,2,8]{2,1,0:T(2,128)S(1)}, f32[2,2,8]{2,1,0:T(2,128)}, u32[]{:S(2)}) copy-start(f32[2,2,8]{2,1,0:T(2,128)} %param.16) | copy-start | bytes 388
  3.8 10.0 %copy-start.3 = (f32[1,16,16,256]{3,1,2,0:T(8,128)}, f32[1,16,16,256]{3,1,2,0:T(8,128)S(1)}, u32[]{:S(2)}) copy-start(f32[1,16,16,256]{3,1,2,0:T(8,128)S(1)} %get-tuple-element.38) | copy-start | bytes 786436
  3.8 10.0 %copy-start.5 = (f32[1,16,16,256]{3,1,2,0:T(8,128)}, f32[1,16,16,256]{3,1,2,0:T(8,128)S(1)}, u32[]{:S(2)}) copy-start(f32[1,16,16,256]{3,1,2,0:T(8,128)S(1)} %get-tuple-element.39) | copy-start | bytes 786436
  3.9 8.4 %collective-permute-start = (f32[6,16,2,256]{3,1,2,0:T(8,128)S(1)}, f32[6,16,2,256]{3,1,2,0:T(8,128)S(1)}, u32[]{:S(2)}, u32[]{:S(2)}) collective-permute-start(f32[6,16,2,256]{3,1,2,0:T(8,128)S(1)} %get-tuple-element.23), channel_id=1, source_target_pairs={{0,16},{16,32},{32,48},{48,64},{64,80},{80,96},{96,112},{112,128},... | collective-permute-start | bytes 589832 | tf_op jit(solution)/shard_map/ppermute | solution.py:15
  5.8 6.8 %collective-permute-start.1 = (f32[6,16,2,256]{3,1,2,0:T(8,128)S(1)}, f32[6,16,2,256]{3,1,2,0:T(8,128)S(1)}, u32[]{:S(2)}, u32[]{:S(2)}) collective-permute-start(f32[6,16,2,256]{3,1,2,0:T(8,128)S(1)} %get-tuple-element.24), channel_id=1, source_target_pairs={{16,0},{32,16},{48,32},{64,48},{80,64},{96,80},{112,96},{128,112},... | collective-permute-start | bytes 589832 | tf_op jit(solution)/shard_map/ppermute | solution.py:17
  13.9 9.9 %copy-start.14 = (bf16[2,2,16,16,256]{4,3,2,1,0:T(8,128)(2,1)S(1)}, bf16[2,2,16,16,256]{4,3,2,1,0:T(8,128)(2,1)}, u32[]{:S(2)}) copy-start(bf16[2,2,16,16,256]{4,3,2,1,0:T(8,128)(2,1)} %param.11) | copy-start | bytes 1572868
  17.0 7.6 %collective-permute-start.2 = (f32[6,16,20,2]{2,1,3,0:T(8,128)S(1)}, f32[6,16,20,2]{2,1,3,0:T(8,128)}, u32[]{:S(2)}, u32[]{:S(2)}) collective-permute-start(f32[6,16,20,2]{2,1,3,0:T(8,128)S(1)} %copy.70), channel_id=1, source_target_pairs={{0,1},{1,2},{2,3},{3,4},{4,5},{5,6},{6,7},{7,8},{8,9},{9,10},{10,1... | collective-permute-start | bytes 46088 | tf_op jit(solution)/shard_map/ppermute | solution.py:15
  22.5 7.3 %collective-permute-start.3 = (f32[6,16,20,2]{2,1,3,0:T(8,128)}, f32[6,16,20,2]{2,1,3,0:T(8,128)}, u32[]{:S(2)}, u32[]{:S(2)}) collective-permute-start(f32[6,16,20,2]{2,1,3,0:T(8,128)} %copy.71), channel_id=1, source_target_pairs={{1,0},{2,1},{3,2},{4,3},{5,4},{6,5},{7,6},{8,7},{9,8},{10,9},{11,1... | collective-permute-start | bytes 46088 | tf_op jit(solution)/shard_map/ppermute | solution.py:17
  35.1 1.6 %copy-start.1 = (f32[6,16,20,260]{3,1,2,0:T(8,128)}, f32[6,16,20,260]{3,1,2,0:T(8,128)S(1)}, u32[]{:S(2)}) copy-start(f32[6,16,20,260]{3,1,2,0:T(8,128)S(1)} %pad_maximum_fusion) | copy-start | bytes 5990404
  37.4 1.0 copy-start.6
  37.5 1.1 copy-start.9
  37.5 1.1 copy-start.11
  38.6 1.8 %copy-start.2 = (f32[6,16,20,260]{3,1,2,0:T(8,128)S(1)}, f32[6,16,20,260]{3,1,2,0:T(8,128)}, u32[]{:S(2)}) copy-start(f32[6,16,20,260]{3,1,2,0:T(8,128)} %copy-done.1) | copy-start | bytes 5990404
  38.6 2.4 %slice-start = ((f32[6,16,20,260]{3,1,2,0:T(8,128)}), f32[2,16,20,260]{3,1,2,0:T(8,128)S(1)}, s32[]{:S(2)}) async-start(f32[6,16,20,260]{3,1,2,0:T(8,128)} %copy-done.1), calls=%async_computation.1 | async-start | bytes 1966080 | tf_op jit(solution)/shard_map/slice | solution.py:93
  38.6 2.4 %copy-start.7 = (f32[2,16,18,258]{3,1,2,0:T(8,128)S(1)}, f32[2,16,18,258]{3,1,2,0:T(8,128)}, u32[]{:S(2)}) copy-start(f32[2,16,18,258]{3,1,2,0:T(8,128)} %select_reduce_fusion) | copy-start | bytes 1783300
  40.9 1.4 copy-start.13
  44.2 38.2 %collective-permute-start.4 = (f32[16,16,256]{2,0,1:T(8,128)S(1)}, f32[16,16,256]{2,0,1:T(8,128)S(1)}, u32[]{:S(2)}, u32[]{:S(2)}) collective-permute-start(f32[16,16,256]{2,0,1:T(8,128)S(1)} %broadcast_select_fusion), channel_id=1, source_target_pairs={{0,256},{256,0},{1,257},{257,1},{2,258},{258,2},{3,259},{259,3},{4... | collective-permute-start | bytes 786440 | tf_op jit(solution)/shard_map/ppermute | solution.py:112
  84.2 7.8 %copy-start.19 = (s32[2,7]{1,0:T(2,128)S(1)}, s32[2,7]{1,0:T(2,128)}, u32[]{:S(2)}) copy-start(s32[2,7]{1,0:T(2,128)} %param.19) | copy-start | bytes 172
  84.2 36.9 %all-to-all-start = ((bf16[16,16,16,256]{3,2,1,0:T(8,128)(2,1)}), bf16[16,16,16,256]{3,2,1,0:T(8,128)(2,1)S(1)}, u32[]{:S(2)}, u32[]{:S(2)}) async-start(bf16[16,16,16,256]{3,2,1,0:T(8,128)(2,1)} %broadcast_in_dim.57), calls=%async_computation | async-start | bytes 4194304 | tf_op jit(solution)/shard_map/all_to_all | solution.py:117
  127.3 25.5 %collective-permute-start.5 = (f32[16,16,256]{2,0,1:T(8,128)S(1)}, f32[16,16,256]{2,0,1:T(8,128)S(1)}, u32[]{:S(2)}, u32[]{:S(2)}) collective-permute-start(f32[16,16,256]{2,0,1:T(8,128)S(1)} %fusion.39), channel_id=1, source_target_pairs={{0,256},{256,0},{1,257},{257,1},{2,258},{258,2},{3,259},{259,3},{4... | collective-permute-start | bytes 786440 | tf_op jit(solution)/shard_map/ppermute | solution.py:129
  (5 other events, 4.2 us)

commit v7 on v6

--- a/solution.py
+++ b/solution.py
@@ -2,6 +2,8 @@
 import jax.numpy as jnp
 from jax import lax
 from jax.sharding import PartitionSpec as P
+from jax.experimental import pallas as pl
+from jax.experimental.pallas import tpu as pltpu
 
 
 def extended(cells, sides, width):
@@ -68,6 +70,42 @@
     return jnp.sum(jnp.where(matches, misfit_level[:, :, None, None, None], 0.0), axis=1)
 
 
+def head_kernel(cols_ref, gathered_ref, blocks_ref, heat_ref, grad_ref, head_ref, part_ref):
+    row_blocks, per_row, size, _ = blocks_ref.shape
+    halves = gathered_ref.shape[2] // size
+    for row in range(row_blocks):
+        total = jnp.zeros((gathered_ref.shape[1], size), jnp.float32)
+        for k in range(per_row):
+            col = cols_ref[row, k]
+            start = pl.multiple_of((col % halves) * size, size)
+            slab = gathered_ref[col // halves, :, pl.ds(start, size)]
+            total = total + lax.dot_general(
+                slab, blocks_ref[row, k], (((1,), (1,)), ((), ())), preferred_element_type=jnp.float32
+            )
+        out = slice(row * size, (row + 1) * size)
+        head_ref[:, out] = total
+        part_ref[:, out] = heat_ref[:, out] + total * grad_ref[:, out].astype(jnp.float32)
+
+
+def apply_head(block_cols, gathered, blocks, heat, grad):
+    cells, width = heat.shape
+    vmem = pltpu.VMEM
+    return pl.pallas_call(
+        head_kernel,
+        out_shape=(
+            jax.ShapeDtypeStruct((cells, width), jnp.float32),
+            jax.ShapeDtypeStruct((cells, width), jnp.float32),
+        ),
+        in_specs=[pl.BlockSpec(memory_space=pltpu.SMEM)] + [pl.BlockSpec(memory_space=vmem)] * 4,
+        out_specs=(pl.BlockSpec(memory_space=vmem), pl.BlockSpec(memory_space=vmem)),
+        cost_estimate=pl.CostEstimate(
+            flops=2 * cells * width * blocks.shape[1] * blocks.shape[2],
+            bytes_accessed=gathered.size * 2 + blocks.size * 2 + cells * width * 14,
+            transcendentals=0,
+        ),
+    )(block_cols, gathered, blocks, heat, grad)
+
+
 def shards(
     terminal,
     forward_temp,
@@ -112,20 +150,18 @@
     rounded = (mine + lax.ppermute(other, "sec", partner)).astype(jnp.bfloat16)
     row_blocks, per_row, block_size, _ = blocks.shape
     count = lax.axis_size("gy")
-    halves = cols_y // block_size
     copies = jnp.broadcast_to(rounded[None], (count,) + rounded.shape)
     gathered = lax.all_to_all(copies, "gy", 0, 0, tiled=False)
-    pieces = gathered.reshape(count, layers, rows_x, halves, block_size)
-    chosen = (
-        ((block_cols // halves)[:, :, None, None] == jnp.arange(count, dtype=jnp.int32)[None, None, :, None])
-        & ((block_cols % halves)[:, :, None, None] == jnp.arange(halves, dtype=jnp.int32)[None, None, None, :])
-    ).astype(jnp.bfloat16)
-    portion = jnp.einsum("bkph,pzxhj->bkzxj", chosen, pieces, preferred_element_type=jnp.float32)
-    picked = portion.astype(jnp.bfloat16)
-    head = jnp.einsum(
-        "bkzxj,bkij->zxbi", picked, blocks, preferred_element_type=jnp.float32
-    ).reshape(layers, rows_x, cols_y)
-    partial_sens = heat_sens + head * head_gradient[0].astype(jnp.float32)
+    cells = layers * rows_x
+    head, partial_sens = apply_head(
+        block_cols,
+        gathered.reshape(count, cells, cols_y),
+        blocks,
+        heat_sens.reshape(cells, cols_y),
+        head_gradient[0].reshape(cells, cols_y),
+    )
+    head = head.reshape(layers, rows_x, cols_y)
+    partial_sens = partial_sens.reshape(layers, rows_x, cols_y)
     sensitivity = partial_sens + lax.ppermute(partial_sens, "sec", partner)
     return (head[None], sensitivity)
 

time: 154 us -> 150 us (0.974)
  local copies, waits for them, and re-layouts: 23.2 us -> 17.1 us
  matrix products: 3.49 us -> 0 us
  Pallas kernels: 0 us -> 2.94 us
  other arithmetic: 11.6 us -> 14 us
    dot_general x2 -> x0, matrix products: 3.49 us -> none  [the longest x1 3.08 us: shards(): jnp.einsum('bkph,pzxhj->bkzxj', chosen, pieces, preferred_element_type=jn...]
    pallas_call x0 -> x1, Pallas kernels: none -> 2.94 us  [apply_head(): pl.pallas_call(head_kernel, out_shape=(jax.ShapeDtypeStruct((cells, width...]
    reshape x3 -> x0, local copies, waits for them, and re-layouts: 2.48 us -> none  [the longest x1 2.06 us: shards(): pieces = gathered.reshape(count, layers, rows_x, halves, block_size)]
    add x1, other arithmetic: 0.04 us -> 1.69 us  [shards(): sensitivity = partial_sens + lax.ppermute(partial_sens, 'sec', partner)]
    unnamed x45 -> x26, local copies, waits for them, and re-layouts: 8.18 us -> 7.04 us
where the time goes in v7:
time: 150 us
  waiting for transfers between devices  69.2 us (46%)
  starting transfers between devices  45.3 us (30%)
  local copies, waits for them, and re-layouts  17.1 us (11%)
  other arithmetic  14 us (9%)
  Pallas kernels  2.94 us (2%)
    all_to_all x1, waiting for transfers between devices, shards(): gathered = lax.all_to_all(copies, 'gy', 0, 0, tiled=False)  28.3 us
    ppermute x1, waiting for transfers between devices, shards(): rounded = (mine + lax.ppermute(other, 'sec', partner)).astype(jnp.bfloat16)  23.2 us
    ppermute x1, starting transfers between devices, shards(): rounded = (mine + lax.ppermute(other, 'sec', partner)).astype(jnp.bfloat16)  15.2 us
    ppermute x1, waiting for transfers between devices, shards(): sensitivity = partial_sens + lax.ppermute(partial_sens, 'sec', partner)  14.2 us
    ppermute x1, starting transfers between devices, shards(): sensitivity = partial_sens + lax.ppermute(partial_sens, 'sec', partner)  11.6 us
    all_to_all x1, starting transfers between devices, shards(): gathered = lax.all_to_all(copies, 'gy', 0, 0, tiled=False)  8.24 us
    unnamed x26, local copies, waits for them, and re-layouts  7.04 us
    ppermute x2, starting transfers between devices, extended(): lax.ppermute(tail, axis, [(i, (i + 1) % count) for i in range(ends)])  5.39 us
  transfers between devices with their start and end apart: 7, of which 5 were waited for; matrix products, arithmetic and copies ran while one was open for 5% of the time, Pallas kernels for 0%

profile of v7, /device:TPU:32, one launch (start us, length us, event | category | flops | bytes accessed | tf_op | source)
XLA Modules:
  0.0 149.6 jit_solution(17609329315865030259)
XLA Ops:
  0.6 1.4 copy.41
  2.0 1.4 copy.42
  3.4 1.4 fusion.33
  4.8 1.9 %collective-permute-start = (f32[6,16,2,256]{3,1,2,0:T(8,128)S(1)}, f32[6,16,2,256]{3,1,2,0:T(8,128)S(1)}, u32[]{:S(2)}, u32[]{:S(2)}) collective-permute-start(f32[6,16,2,256]{3,1,2,0:T(8,128)S(1)} %get-tuple-element.23), channel_id=1, source_target_pairs={{0,16},{16,32},{32,48},{48,64},{64,80},{80,96},{96,112},{112,128},... | collective-permute-start | bytes 589832 | tf_op jit(solution)/shard_map/ppermute | solution.py:17
  6.7 3.6 %collective-permute-start.1 = (f32[6,16,2,256]{3,1,2,0:T(8,128)S(1)}, f32[6,16,2,256]{3,1,2,0:T(8,128)S(1)}, u32[]{:S(2)}, u32[]{:S(2)}) collective-permute-start(f32[6,16,2,256]{3,1,2,0:T(8,128)S(1)} %get-tuple-element.24), channel_id=1, source_target_pairs={{16,0},{32,16},{48,32},{64,48},{80,64},{96,80},{112,96},{128,112},... | collective-permute-start | bytes 589832 | tf_op jit(solution)/shard_map/ppermute | solution.py:19
  10.8 2.4 %select_reduce_fusion = f32[2,16,18,258]{3,1,2,0:T(8,128)} fusion(f32[2,8]{1,0:T(2,128)S(1)} %slice_bitcast_fusion.2, pred[2,8,258]{2,1,0:T(8,128)(4,1)S(1)} %broadcast_compare_fusion, pred[2,8,16,18]{2,3,1,0:T(8,128)(4,1)S(1)} %broadcast_and_fusion), kind=kLoop, calls=%fused_computation | loop fusion | flops 3417984 | bytes 603232 | tf_op jit(solution)/shard_map/reduce_sum | solution.py:70
  15.0 1.3 copy.43
  16.3 3.5 %collective-permute-start.2 = (f32[6,16,20,2]{2,1,3,0:T(8,128)}, f32[6,16,20,2]{2,1,3,0:T(8,128)S(1)}, u32[]{:S(2)}, u32[]{:S(2)}) collective-permute-start(f32[6,16,20,2]{2,1,3,0:T(8,128)} %copy.43), channel_id=1, source_target_pairs={{0,1},{1,2},{2,3},{3,4},{4,5},{5,6},{6,7},{7,8},{8,9},{9,10},{10,1... | collective-permute-start | bytes 46088 | tf_op jit(solution)/shard_map/ppermute | solution.py:17
  21.8 1.9 %fusion.36 = (bf16[1,2,16,16,256]{4,3,2,1,0:T(8,128)(2,1)}, bf16[1,2,16,16,256]{4,3,2,1,0:T(8,128)(2,1)}) fusion(bf16[2,2,16,16,256]{4,3,2,1,0:T(8,128)(2,1)} %param.11), kind=kLoop, calls=%fused_computation.96 | loop fusion | bytes 1048576 | tf_op jit(solution)/shard_map/slice | solution.py:142
  24.4 3.2 %collective-permute-done.3 = f32[6,16,20,2]{2,1,3,0:T(8,128)} collective-permute-done((f32[6,16,20,2]{2,1,3,0:T(8,128)S(1)}, f32[6,16,20,2]{2,1,3,0:T(8,128)}, u32[]{:S(2)}, u32[]{:S(2)}) %collective-permute-start.3) | collective-permute-done | bytes 15392 | tf_op jit(solution)/shard_map/ppermute | solution.py:19
  27.5 1.6 %copy.46 = f32[6,16,20,2]{3,1,2,0:T(8,128)S(1)} copy(f32[6,16,20,2]{2,1,3,0:T(8,128)} %collective-permute-done.3) | data formatting | bytes 30720 | tf_op jit(solution)/shard_map/ppermute | solution.py:19
  29.1 3.5 %pad_maximum_fusion = f32[6,16,20,260]{3,1,2,0:T(8,128)S(1)} fusion(f32[6,16,20,2]{3,1,2,0:T(8,128)S(1)} %copy.46, f32[6,16,2,256]{3,1,2,0:T(8,128)} %copy-done.6, f32[1,16,16,256]{3,1,2,0:T(8,128)S(1)} %get-tuple-element.36, f32[2,16,16,256]{3,1,2,0:T(8,128)S(1)} %copy.42, f32[1,16,16,256]{3,1,2,0:T(8,128)S(1)} %get-tuple-element.37, ...), kind=kLoop, calls=%fused_computation.1 | loop fusion | flops 3494400 | bytes 3993600 | tf_op jit(solution)/shard_map/concatenate | solution.py:15
  35.4 1.5 %copy-done.1 = f32[6,16,20,260]{3,1,2,0:T(8,128)S(1)} copy-done((f32[6,16,20,260]{3,1,2,0:T(8,128)S(1)}, f32[6,16,20,260]{3,1,2,0:T(8,128)}, u32[]{:S(2)}) %copy-start.1) | copy-done | bytes 1996824
  37.5 1.3 add_multiply_fusion
  40.3 15.2 %collective-permute-start.4 = (f32[16,16,256]{2,0,1:T(8,128)S(1)}, f32[16,16,256]{2,0,1:T(8,128)S(1)}, u32[]{:S(2)}, u32[]{:S(2)}) collective-permute-start(f32[16,16,256]{2,0,1:T(8,128)S(1)} %broadcast_select_fusion), channel_id=1, source_target_pairs={{0,256},{256,0},{1,257},{257,1},{2,258},{258,2},{3,259},{259,3},{4... | collective-permute-start | bytes 786440 | tf_op jit(solution)/shard_map/ppermute | solution.py:150
  55.5 23.2 %collective-permute-done.4 = f32[16,16,256]{2,0,1:T(8,128)S(1)} collective-permute-done((f32[16,16,256]{2,0,1:T(8,128)S(1)}, f32[16,16,256]{2,0,1:T(8,128)S(1)}, u32[]{:S(2)}, u32[]{:S(2)}) %collective-permute-start.4) | collective-permute-done | bytes 262176 | tf_op jit(solution)/shard_map/ppermute | solution.py:150
  78.9 1.5 %broadcast_in_dim.53 = bf16[16,16,16,256]{3,2,1,0:T(8,128)(2,1)} broadcast(bf16[16,16,256]{2,1,0:T(8,128)(2,1)S(1)} %copy.50), dimensions={1,2,3} | broadcast | bytes 2228224 | tf_op jit(solution)/shard_map/broadcast_in_dim | solution.py:153
  80.4 8.2 %all-to-all-start = ((bf16[16,16,16,256]{3,2,1,0:T(8,128)(2,1)}), bf16[16,16,16,256]{3,2,1,0:T(8,128)(2,1)S(1)}, u32[]{:S(2)}, u32[]{:S(2)}) async-start(bf16[16,16,16,256]{3,2,1,0:T(8,128)(2,1)} %broadcast_in_dim.53), calls=%async_computation | async-start | bytes 4194304 | tf_op jit(solution)/shard_map/all_to_all | solution.py:154
  89.6 28.3 %all-to-all-done = bf16[16,16,16,256]{3,2,1,0:T(8,128)(2,1)S(1)} async-done(((bf16[16,16,16,256]{3,2,1,0:T(8,128)(2,1)}), bf16[16,16,16,256]{3,2,1,0:T(8,128)(2,1)S(1)}, u32[]{:S(2)}, u32[]{:S(2)}) %all-to-all-start) | async-done | bytes 2097184 | tf_op jit(solution)/shard_map/all_to_all | solution.py:154
  117.9 1.3 copy-done.2
  119.2 2.9 %shard_map.113 = (f32[256,256]{1,0:T(8,128)}, f32[256,256]{1,0:T(8,128)}) custom-call(s32[2,7]{1,0:T(2,128)} %cols_ref.1, bf16[16,256,256]{2,1,0:T(8,128)(2,1)} %bitcast.43, bf16[2,7,128,128]{3,2,1,0:T(8,128)(2,1)} %blocks_ref.1, f32[256,256]{1,0:T(8,128)} %bitcast.44, bf16[256,256]{1,0:T(8,128)(2,1)} %bitcast.47), custom_call_target="tpu_custom_call" | custom-call | flops 117440512 | bytes 3473408 | tf_op jit(solution)/shard_map/pallas_call | solution.py:93
  122.2 11.6 %collective-permute-start.5 = (f32[16,16,256]{2,1,0:T(8,128)}, f32[16,16,256]{2,1,0:T(8,128)S(1)}, u32[]{:S(2)}, u32[]{:S(2)}) collective-permute-start(f32[16,16,256]{2,1,0:T(8,128)} %bitcast.45), channel_id=1, source_target_pairs={{0,256},{256,0},{1,257},{257,1},{2,258},{258,2},{3,259},{259,3},{4... | collective-permute-start | bytes 786440 | tf_op jit(solution)/shard_map/ppermute | solution.py:165
  133.7 14.2 %collective-permute-done.5 = f32[16,16,256]{2,1,0:T(8,128)S(1)} collective-permute-done((f32[16,16,256]{2,1,0:T(8,128)}, f32[16,16,256]{2,1,0:T(8,128)S(1)}, u32[]{:S(2)}, u32[]{:S(2)}) %collective-permute-start.5) | collective-permute-done | bytes 262176 | tf_op jit(solution)/shard_map/ppermute | solution.py:165
  147.9 1.7 %add.142 = f32[16,16,256]{2,1,0:T(8,128)} add(f32[16,16,256]{2,1,0:T(8,128)} %bitcast.46, f32[16,16,256]{2,1,0:T(8,128)S(1)} %collective-permute-done.5) | non-fusion elementwise | flops 65536 | bytes 786432 | tf_op jit(solution)/shard_map/add | solution.py:165
  (58 shorter events, 10.7 us)
Async XLA Ops:
  0.6 9.7 %copy-start.10 = (s32[2,8,3]{1,0,2:T(2,128)S(1)}, s32[2,8,3]{1,0,2:T(2,128)}, u32[]{:S(2)}) copy-start(s32[2,8,3]{1,0,2:T(2,128)} %param.15) | copy-start | bytes 580
  0.6 9.8 %copy-start.11 = (f32[2,2,8]{2,1,0:T(2,128)S(1)}, f32[2,2,8]{2,1,0:T(2,128)}, u32[]{:S(2)}) copy-start(f32[2,2,8]{2,1,0:T(2,128)} %param.16) | copy-start | bytes 388
  4.8 8.4 %collective-permute-start = (f32[6,16,2,256]{3,1,2,0:T(8,128)S(1)}, f32[6,16,2,256]{3,1,2,0:T(8,128)S(1)}, u32[]{:S(2)}, u32[]{:S(2)}) collective-permute-start(f32[6,16,2,256]{3,1,2,0:T(8,128)S(1)} %get-tuple-element.23), channel_id=1, source_target_pairs={{0,16},{16,32},{32,48},{48,64},{64,80},{80,96},{96,112},{112,128},... | collective-permute-start | bytes 589832 | tf_op jit(solution)/shard_map/ppermute | solution.py:17
  6.7 6.8 %collective-permute-start.1 = (f32[6,16,2,256]{3,1,2,0:T(8,128)S(1)}, f32[6,16,2,256]{3,1,2,0:T(8,128)S(1)}, u32[]{:S(2)}, u32[]{:S(2)}) collective-permute-start(f32[6,16,2,256]{3,1,2,0:T(8,128)S(1)} %get-tuple-element.24), channel_id=1, source_target_pairs={{16,0},{32,16},{48,32},{64,48},{80,64},{96,80},{112,96},{128,112},... | collective-permute-start | bytes 589832 | tf_op jit(solution)/shard_map/ppermute | solution.py:19
  13.1 0.7 copy-start.4
  13.8 0.7 copy-start.6
  16.3 7.3 %collective-permute-start.2 = (f32[6,16,20,2]{2,1,3,0:T(8,128)}, f32[6,16,20,2]{2,1,3,0:T(8,128)S(1)}, u32[]{:S(2)}, u32[]{:S(2)}) collective-permute-start(f32[6,16,20,2]{2,1,3,0:T(8,128)} %copy.43), channel_id=1, source_target_pairs={{0,1},{1,2},{2,3},{3,4},{4,5},{5,6},{6,7},{7,8},{8,9},{9,10},{10,1... | collective-permute-start | bytes 46088 | tf_op jit(solution)/shard_map/ppermute | solution.py:17
  20.5 7.1 %collective-permute-start.3 = (f32[6,16,20,2]{2,1,3,0:T(8,128)S(1)}, f32[6,16,20,2]{2,1,3,0:T(8,128)}, u32[]{:S(2)}, u32[]{:S(2)}) collective-permute-start(f32[6,16,20,2]{2,1,3,0:T(8,128)S(1)} %copy.44), channel_id=1, source_target_pairs={{1,0},{2,1},{3,2},{4,3},{5,4},{6,5},{7,6},{8,7},{9,8},{10,9},{11,1... | collective-permute-start | bytes 46088 | tf_op jit(solution)/shard_map/ppermute | solution.py:19
  32.7 1.6 %copy-start = (f32[6,16,20,260]{3,1,2,0:T(8,128)}, f32[6,16,20,260]{3,1,2,0:T(8,128)S(1)}, u32[]{:S(2)}) copy-start(f32[6,16,20,260]{3,1,2,0:T(8,128)S(1)} %pad_maximum_fusion) | copy-start | bytes 5990404
  33.1 2.0 %copy-start.5 = (f32[6,16,2,256]{3,1,2,0:T(8,128)S(1)}, f32[6,16,2,256]{3,1,2,0:T(8,128)}, u32[]{:S(2)}) copy-start(f32[6,16,2,256]{3,1,2,0:T(8,128)} %copy-done.4) | copy-start | bytes 589828
  33.1 2.0 %copy-start.7 = (f32[6,16,2,256]{3,1,2,0:T(8,128)S(1)}, f32[6,16,2,256]{3,1,2,0:T(8,128)}, u32[]{:S(2)}) copy-start(f32[6,16,2,256]{3,1,2,0:T(8,128)} %copy-done.6) | copy-start | bytes 589828
  35.1 1.9 %copy-start.1 = (f32[6,16,20,260]{3,1,2,0:T(8,128)S(1)}, f32[6,16,20,260]{3,1,2,0:T(8,128)}, u32[]{:S(2)}) copy-start(f32[6,16,20,260]{3,1,2,0:T(8,128)} %copy-done) | copy-start | bytes 5990404
  35.1 2.2 %slice-start = ((f32[6,16,20,260]{3,1,2,0:T(8,128)}), f32[2,16,20,260]{3,1,2,0:T(8,128)S(1)}, s32[]{:S(2)}) async-start(f32[6,16,20,260]{3,1,2,0:T(8,128)} %copy-done), calls=%async_computation.1 | async-start | bytes 1966080 | tf_op jit(solution)/shard_map/slice | solution.py:131
  35.1 2.3 %copy-start.3 = (f32[2,16,18,258]{3,1,2,0:T(8,128)S(1)}, f32[2,16,18,258]{3,1,2,0:T(8,128)}, u32[]{:S(2)}) copy-start(f32[2,16,18,258]{3,1,2,0:T(8,128)} %select_reduce_fusion) | copy-start | bytes 1783300
  37.4 1.3 copy-start.9
  37.4 1.8 %copy-start.8 = (bf16[1,2,16,16,256]{4,3,2,1,0:T(8,128)(2,1)S(1)}, bf16[1,2,16,16,256]{4,3,2,1,0:T(8,128)(2,1)}, u32[]{:S(2)}) copy-start(bf16[1,2,16,16,256]{4,3,2,1,0:T(8,128)(2,1)} %get-tuple-element.25) | copy-start | bytes 786436
  40.3 38.4 %collective-permute-start.4 = (f32[16,16,256]{2,0,1:T(8,128)S(1)}, f32[16,16,256]{2,0,1:T(8,128)S(1)}, u32[]{:S(2)}, u32[]{:S(2)}) collective-permute-start(f32[16,16,256]{2,0,1:T(8,128)S(1)} %broadcast_select_fusion), channel_id=1, source_target_pairs={{0,256},{256,0},{1,257},{257,1},{2,258},{258,2},{3,259},{259,3},{4... | collective-permute-start | bytes 786440 | tf_op jit(solution)/shard_map/ppermute | solution.py:150
  80.4 37.5 %all-to-all-start = ((bf16[16,16,16,256]{3,2,1,0:T(8,128)(2,1)}), bf16[16,16,16,256]{3,2,1,0:T(8,128)(2,1)S(1)}, u32[]{:S(2)}, u32[]{:S(2)}) async-start(bf16[16,16,16,256]{3,2,1,0:T(8,128)(2,1)} %broadcast_in_dim.53), calls=%async_computation | async-start | bytes 4194304 | tf_op jit(solution)/shard_map/all_to_all | solution.py:154
  117.9 1.3 copy-start.2
  122.2 25.7 %collective-permute-start.5 = (f32[16,16,256]{2,1,0:T(8,128)}, f32[16,16,256]{2,1,0:T(8,128)S(1)}, u32[]{:S(2)}, u32[]{:S(2)}) collective-permute-start(f32[16,16,256]{2,1,0:T(8,128)} %bitcast.45), channel_id=1, source_target_pairs={{0,256},{256,0},{1,257},{257,1},{2,258},{258,2},{3,259},{259,3},{4... | collective-permute-start | bytes 786440 | tf_op jit(solution)/shard_map/ppermute | solution.py:165

commit v8 on v7

--- a/solution.py
+++ b/solution.py
@@ -68,6 +68,127 @@
     well_y = wells[:, :, 2][:, :, None, None, None]
     matches = (coord_z == well_z) & (coord_x == well_x) & (coord_y == well_y)
     return jnp.sum(jnp.where(matches, misfit_level[:, :, None, None, None], 0.0), axis=1)
+
+
+def conductance(centre, other):
+    return 2.0 * centre * other / jnp.where(centre + other > 0.0, centre + other, 1.0)
+
+
+def heat_kernel(offs_ref, wells_ref, misfit_ref, box_ref, temp_ref, heat_ref, fx_ref, fy_ref, adj_ref, w_ref):
+    tests, layers, rows, cols = adj_ref.shape
+    tile_x, tile_y = heat_ref.shape[1], heat_ref.shape[2]
+    zero = jnp.zeros((rows, cols), jnp.float32)
+
+    def plane(ref, lead, z):
+        above = jnp.where(z + 1 < layers, ref[lead, jnp.minimum(z + 1, layers - 1)], zero)
+        below = jnp.where(z > 0, ref[lead, jnp.maximum(z - 1, 0)], zero)
+        return ref[lead, z], above, below
+
+    def faces(value, above, below):
+        return [
+            above,
+            below,
+            pltpu.roll(value, rows - 1, 0),
+            pltpu.roll(value, 1, 0),
+            pltpu.roll(value, cols - 1, 1),
+            pltpu.roll(value, 1, 1),
+        ]
+
+    def weigh(z, carry):
+        centre, above, below = plane(box_ref, 2, z)
+        for face, other in enumerate(faces(centre, above, below)):
+            w_ref[face, z] = conductance(centre, other)
+        return carry
+
+    lax.fori_loop(0, layers, weigh, 0)
+
+    def advance(source_ref, level, store):
+        def body(z, carry):
+            speed_x = box_ref[3, z]
+            speed_y = box_ref[4, z]
+            keep = box_ref[5, z]
+            heat = fx = fy = None
+            for test in range(tests):
+                centre, above, below = plane(source_ref, test, z)
+                beside = faces(centre, above, below)
+                diffusion = w_ref[0, z] * (beside[0] - centre)
+                for face in range(1, 6):
+                    diffusion = diffusion + w_ref[face, z] * (beside[face] - centre)
+                slope_x = 0.5 * (beside[2] - beside[3])
+                slope_y = 0.5 * (beside[4] - beside[5])
+                updated = keep * (centre + diffusion + speed_x * slope_x + speed_y * slope_y)
+                if store:
+                    adj_ref[test, z] = updated
+                temper = temp_ref[level, test, z].astype(jnp.float32)
+                terms = [temper * v[:tile_x, :tile_y] for v in (diffusion, slope_x, slope_y)]
+                if heat is None:
+                    heat, fx, fy = terms
+                else:
+                    heat, fx, fy = heat + terms[0], fx + terms[1], fy + terms[2]
+            if store:
+                heat_ref[z], fx_ref[z], fy_ref[z] = heat, fx, fy
+            else:
+                heat_ref[z] = heat_ref[z] + heat
+                fx_ref[z] = fx_ref[z] + fx
+                fy_ref[z] = fy_ref[z] + fy
+            return carry
+
+        lax.fori_loop(0, layers, body, 0)
+
+    advance(box_ref, 1, True)
+    row_ids = lax.broadcasted_iota(jnp.int32, (rows, cols), 0)
+    col_ids = lax.broadcasted_iota(jnp.int32, (rows, cols), 1)
+    for test in range(tests):
+        for well in range(wells_ref.shape[1]):
+            depth = wells_ref[test, well, 0]
+            at_x = wells_ref[test, well, 1] - offs_ref[0]
+            at_y = wells_ref[test, well, 2] - offs_ref[1]
+            inside = (at_x >= -2) & (at_x < tile_x + 2) & (at_y >= -2) & (at_y < tile_y + 2)
+            amount = jnp.where(inside, misfit_ref[1, test, well], 0.0)
+            hit = (row_ids == jnp.where(at_x < 0, at_x + rows, at_x)) & (
+                col_ids == jnp.where(at_y < 0, at_y + cols, at_y)
+            )
+            adj_ref[test, depth] = adj_ref[test, depth] + jnp.where(hit, box_ref[5, depth] * amount, 0.0)
+    advance(adj_ref, 0, False)
+
+
+def heat_phase(offs, wells, misfit, box, temp):
+    channels, layers, rows, cols = box.shape
+    tests = temp.shape[1]
+    tile = temp.shape[3:]
+    smem = pl.BlockSpec(memory_space=pltpu.SMEM)
+    vmem = pl.BlockSpec(memory_space=pltpu.VMEM)
+    out = jax.ShapeDtypeStruct((layers,) + tile, jnp.float32)
+    return pl.pallas_call(
+        heat_kernel,
+        out_shape=(out, out, out),
+        in_specs=[smem, smem, smem, vmem, vmem],
+        out_specs=(vmem, vmem, vmem),
+        scratch_shapes=[
+            pltpu.VMEM((tests, layers, rows, cols), jnp.float32),
+            pltpu.VMEM((6, layers, rows, cols), jnp.float32),
+        ],
+    )(offs, wells, misfit, box, temp)
+
+
+def circular(cells, sides, width, sizes):
+    for (axis, dim), size in zip(sides, sizes):
+        ends = lax.axis_size(axis) - 1
+        length = cells.shape[dim]
+        head = lax.slice_in_dim(cells, 0, width, axis=dim)
+        tail = lax.slice_in_dim(cells, length - width, length, axis=dim)
+        gap = list(cells.shape)
+        gap[dim] = size - length - 2 * width
+        cells = jnp.concatenate(
+            [
+                cells,
+                lax.ppermute(head, axis, [(i + 1, i) for i in range(ends)]),
+                jnp.zeros(gap, cells.dtype),
+                lax.ppermute(tail, axis, [(i, i + 1) for i in range(ends)]),
+            ],
+            axis=dim,
+        )
+    return cells
 
 
 def head_kernel(cols_ref, gathered_ref, blocks_ref, heat_ref, grad_ref, head_ref, part_ref):
@@ -121,28 +242,11 @@
     layers, rows_x, cols_y = conductivity.shape
     keep = 1.0 - fixed_mask.astype(jnp.float32)
     packed = jnp.concatenate([terminal, conductivity[None], velocity, keep[None]], axis=0)
-    box = extended(packed, (("gx", 2), ("gy", 3)), 2)
-    ring_velocity = box[3:5, :, 1:-1, 1:-1]
-    ring_keep = box[5, :, 1:-1, 1:-1]
-    ring_weights = face_weights(box[2])
-    weights = [w[:, 1:-1, 1:-1] for w in ring_weights]
-    ring_source = well_sources(wells, misfit[1], layers, rows_x, cols_y, 1)
-    ring_adjoint, diffusion, slope_x, slope_y = advance(
-        box[0:2], ring_weights, ring_keep, ring_velocity[0], ring_velocity[1], ring_source
-    )
-    temper = forward_temp[1].astype(jnp.float32)
-    inner = (Ellipsis, slice(1, -1), slice(1, -1))
-    heat_sens = jnp.sum(temper * diffusion[inner], axis=0)
-    flow_x = jnp.sum(temper * slope_x[inner], axis=0)
-    flow_y = jnp.sum(temper * slope_y[inner], axis=0)
-    source = well_sources(wells, misfit[0], layers, rows_x, cols_y, 0)
-    _, diffusion, slope_x, slope_y = advance(
-        ring_adjoint, weights, keep, velocity[0], velocity[1], source
-    )
-    temper = forward_temp[0].astype(jnp.float32)
-    heat_sens = heat_sens + jnp.sum(temper * diffusion, axis=0)
-    flow_x = flow_x + jnp.sum(temper * slope_x, axis=0)
-    flow_y = flow_y + jnp.sum(temper * slope_y, axis=0)
+    width = 2
+    sizes = (-(-(rows_x + 2 * width) // 8) * 8, -(-(cols_y + 2 * width) // 128) * 128)
+    box = circular(packed, (("gx", 2), ("gy", 3)), width, sizes)
+    offs = jnp.stack([lax.axis_index("gx") * rows_x, lax.axis_index("gy") * cols_y]).astype(jnp.int32)
+    heat_sens, flow_x, flow_y = heat_phase(offs, wells, misfit, box, forward_temp)
     first = lax.axis_index("sec") == 0
     mine = jnp.where(first, flow_x, flow_y)
     other = jnp.where(first, flow_y, flow_x)

time: 150 us -> 149 us (level)
  the two profiles are of different devices: /device:TPU:32 before, /device:TPU:1 now
where the time goes in v8:
time: 149 us
  starting transfers between devices  50.2 us (34%)
  blocking collectives  35.1 us (24%)
  waiting for transfers between devices  34.8 us (23%)
  Pallas kernels  11.3 us (8%)
  other arithmetic  10.6 us (7%)
  local copies, waits for them, and re-layouts  5.79 us (4%)
    all_to_all x1, blocking collectives, shards(): gathered = lax.all_to_all(copies, 'gy', 0, 0, tiled=False)  35.1 us
    ppermute x1, starting transfers between devices, shards(): sensitivity = partial_sens + lax.ppermute(partial_sens, 'sec', partner)  22.4 us
    ppermute x1, waiting for transfers between devices, shards(): sensitivity = partial_sens + lax.ppermute(partial_sens, 'sec', partner)  19.6 us
    ppermute x1, waiting for transfers between devices, shards(): rounded = (mine + lax.ppermute(other, 'sec', partner)).astype(jnp.bfloat16)  12.6 us
    ppermute x1, starting transfers between devices, shards(): rounded = (mine + lax.ppermute(other, 'sec', partner)).astype(jnp.bfloat16)  11.1 us
    ppermute x2, starting transfers between devices, circular(): lax.ppermute(head, axis, [(i + 1, i) for i in range(ends)])  10.1 us
    pallas_call x1, Pallas kernels, heat_phase(): pl.pallas_call(heat_kernel, out_shape=(out, out, out), in_specs=[smem, sm...  8.34 us
    ppermute x2, starting transfers between devices, circular(): lax.ppermute(tail, axis, [(i, i + 1) for i in range(ends)])  6.57 us
  transfers between devices with their start and end apart: 6, of which 3 were waited for; matrix products, arithmetic and copies ran while one was open for 2% of the time, Pallas kernels for 0%

profile of v8, /device:TPU:1, one launch (start us, length us, event | category | flops | bytes accessed | tf_op | source)
XLA Modules:
  0.0 148.6 jit_solution(14131566862945801272)
XLA Ops:
  0.7 1.1 subtract_bitcast_fusion
  1.8 1.5 %pad_maximum_fusion.5 = (f32[6,16,2,256]{3,2,1,0:T(2,128)S(1)}, f32[6,16,2,256]{3,2,1,0:T(2,128)S(1)}) fusion(f32[1,16,16,256]{3,2,1,0:T(8,128)S(1)} %subtract_bitcast_fusion, f32[2,16,16,256]{3,2,1,0:T(8,128)} %param.13, f32[1,16,16,256]{3,2,1,0:T(8,128)} %bitcast.11, f32[2,16,16,256]{3,2,1,0:T(8,128)} %param.10), kind=kLoop, calls=%fused_computation.7 | loop fusion | flops 294912 | bytes 1966080 | tf_op jit(solution)/shard_map/slice | solution.py:178
  3.3 8.8 %collective-permute-start = (f32[6,16,2,256]{3,2,1,0:T(2,128)S(1)}, f32[6,16,2,256]{3,2,1,0:T(2,128)S(1)}, u32[]{:S(2)}, u32[]{:S(2)}) collective-permute-start(f32[6,16,2,256]{3,2,1,0:T(2,128)S(1)} %get-tuple-element.14), channel_id=1, source_target_pairs={{16,0},{32,16},{48,32},{64,48},{80,64},{96,80},{112,96},{128,112},... | collective-permute-start | bytes 589832 | tf_op jit(solution)/shard_map/ppermute | solution.py:185
  12.1 1.9 %collective-permute-start.1 = (f32[6,16,2,256]{3,2,1,0:T(2,128)S(1)}, f32[6,16,2,256]{3,2,1,0:T(2,128)S(1)}, u32[]{:S(2)}, u32[]{:S(2)}) collective-permute-start(f32[6,16,2,256]{3,2,1,0:T(2,128)S(1)} %get-tuple-element.15), channel_id=1, source_target_pairs={{0,16},{16,32},{32,48},{48,64},{64,80},{80,96},{96,112},{112,128},... | collective-permute-start | bytes 589832 | tf_op jit(solution)/shard_map/ppermute | solution.py:187
  14.0 2.6 %collective-permute-done.1 = f32[6,16,2,256]{3,2,1,0:T(2,128)S(1)} collective-permute-done((f32[6,16,2,256]{3,2,1,0:T(2,128)S(1)}, f32[6,16,2,256]{3,2,1,0:T(2,128)S(1)}, u32[]{:S(2)}, u32[]{:S(2)}) %collective-permute-start.1) | collective-permute-done | bytes 196640 | tf_op jit(solution)/shard_map/ppermute | solution.py:187
  16.7 0.6 copy-done.6
  18.4 0.6 copy.13
  19.1 1.3 collective-permute-start.2
  20.4 0.6 copy.14
  21.0 4.6 %collective-permute-start.3 = (f32[6,16,24,2]{2,1,3,0:T(8,128)S(1)}, f32[6,16,24,2]{2,1,3,0:T(8,128)}, u32[]{:S(2)}, u32[]{:S(2)}) collective-permute-start(f32[6,16,24,2]{2,1,3,0:T(8,128)S(1)} %copy.14), channel_id=1, source_target_pairs={{0,1},{1,2},{2,3},{3,4},{4,5},{5,6},{6,7},{7,8},{8,9},{9,10},{10,1... | collective-permute-start | bytes 55304 | tf_op jit(solution)/shard_map/ppermute | solution.py:187
  26.2 0.7 copy.17.wells_ref
  27.0 0.6 copy.15
  27.6 1.5 %copy.16 = f32[6,16,24,2]{3,2,1,0:T(8,128)S(1)} copy(f32[6,16,24,2]{2,1,3,0:T(8,128)} %collective-permute-done.3) | data formatting | bytes 36864 | tf_op jit(solution)/shard_map/ppermute | solution.py:187
  29.1 3.4 %pad_maximum_fusion.box_ref = f32[6,16,24,384]{3,2,1,0:T(8,128)} fusion(f32[6,16,24,2]{3,2,1,0:T(8,128)S(1)} %copy.16, f32[6,16,24,2]{3,2,1,0:T(8,128)S(1)} %copy.15, f32[6,16,2,256]{3,2,1,0:T(2,128)} %copy-done.6, f32[6,16,4,256]{3,2,1,0:T(4,128)} %copy-done.3, f32[6,16,2,256]{3,2,1,0:T(2,128)} %copy-done.5, f32[1,16,16,256]{3,2,1,0:T(8,128)} %copy-done.2, ...), kind=kLoop, calls=%fused_computation | loop fusion | flops 7962624 | bytes 5936640 | tf_op jit(solution)/shard_map/concatenate | solution.py:182
  32.5 8.3 %shard_map.113 = (f32[16,16,256]{2,1,0:T(8,128)}, f32[16,16,256]{2,1,0:T(8,128)}, f32[16,16,256]{2,1,0:T(8,128)}) custom-call(s32[2]{0:T(128)} %pad_add_fusion.offs_ref, s32[2,8,3]{2,1,0:T(8,128)} %copy.17.wells_ref, f32[2,2,8]{2,1,0:T(2,128)} %misfit_ref.1, f32[6,16,24,384]{3,2,1,0:T(8,128)} %pad_maximum_fusion.box_ref, bf16[2,2,16,16,256]{4,3,2,1,0:T(8,128)(2,1)} %temp_ref.1), custom_call_target="tpu_custom_call" | custom-call | tf_op jit(solution)/shard_map/pallas_call | solution.py:162
  40.9 1.0 broadcast_select_fusion
  41.9 11.1 %collective-permute-start.4 = (f32[16,16,256]{2,1,0:T(8,128)S(1)}, f32[16,16,256]{2,1,0:T(8,128)S(1)}, u32[]{:S(2)}, u32[]{:S(2)}) collective-permute-start(f32[16,16,256]{2,1,0:T(8,128)S(1)} %broadcast_select_fusion), channel_id=1, source_target_pairs={{0,256},{256,0},{1,257},{257,1},{2,258},{258,2},{3,259},{259,3},{4... | collective-permute-start | bytes 786440 | tf_op jit(solution)/shard_map/ppermute | solution.py:254
  53.0 12.6 %collective-permute-done.4 = f32[16,16,256]{2,1,0:T(8,128)S(1)} collective-permute-done((f32[16,16,256]{2,1,0:T(8,128)S(1)}, f32[16,16,256]{2,1,0:T(8,128)S(1)}, u32[]{:S(2)}, u32[]{:S(2)}) %collective-permute-start.4) | collective-permute-done | bytes 262176 | tf_op jit(solution)/shard_map/ppermute | solution.py:254
  65.6 1.0 add_convert_fusion
  66.8 35.1 %all_to_all.5 = bf16[16,16,16,256]{3,2,1,0:T(8,128)(2,1)} all-to-all(bf16[16,16,16,256]{3,2,1,0:T(8,128)(2,1)S(1)} %broadcast_in_dim.22), channel_id=1, replica_groups=mesh['sec'=2,'gx'=16,'gy'=16] {'gy'}, dimensions={0} | all-to-all | bytes 4194304 | tf_op jit(solution)/shard_map/all_to_all | solution.py:258
  101.9 3.0 %shard_map.114 = (f32[256,256]{1,0:T(8,128)}, f32[256,256]{1,0:T(8,128)}) custom-call(s32[2,7]{1,0:T(2,128)} %cols_ref.1, bf16[16,256,256]{2,1,0:T(8,128)(2,1)} %bitcast.10, bf16[2,7,128,128]{3,2,1,0:T(8,128)(2,1)} %blocks_ref.1, f32[256,256]{1,0:T(8,128)} %bitcast.16, bf16[256,256]{1,0:T(8,128)(2,1)} %bitcast.17), custom_call_target="tpu_custom_call" | custom-call | flops 117440512 | bytes 3473408 | tf_op jit(solution)/shard_map/pallas_call | solution.py:214
  104.9 22.4 %collective-permute-start.5 = (f32[16,16,256]{2,1,0:T(8,128)}, f32[16,16,256]{2,1,0:T(8,128)S(1)}, u32[]{:S(2)}, u32[]{:S(2)}) collective-permute-start(f32[16,16,256]{2,1,0:T(8,128)} %bitcast.14), channel_id=1, source_target_pairs={{0,256},{256,0},{1,257},{257,1},{2,258},{258,2},{3,259},{259,3},{4... | collective-permute-start | bytes 786440 | tf_op jit(solution)/shard_map/ppermute | solution.py:269
  127.3 19.6 %collective-permute-done.5 = f32[16,16,256]{2,1,0:T(8,128)S(1)} collective-permute-done((f32[16,16,256]{2,1,0:T(8,128)}, f32[16,16,256]{2,1,0:T(8,128)S(1)}, u32[]{:S(2)}, u32[]{:S(2)}) %collective-permute-start.5) | collective-permute-done | bytes 262176 | tf_op jit(solution)/shard_map/ppermute | solution.py:269
  146.9 1.7 %add.7 = f32[16,16,256]{2,1,0:T(8,128)} add(f32[16,16,256]{2,1,0:T(8,128)} %bitcast.15, f32[16,16,256]{2,1,0:T(8,128)S(1)} %collective-permute-done.5) | non-fusion elementwise | flops 65536 | bytes 786432 | tf_op jit(solution)/shard_map/add | solution.py:269
  (25 shorter events, 2.1 us)
Async XLA Ops:
  0.6 16.6 %copy-start.4 = (f32[16,16,256]{2,1,0:T(8,128)S(1)}, f32[16,16,256]{2,1,0:T(8,128)}, u32[]{:S(2)}) copy-start(f32[16,16,256]{2,1,0:T(8,128)} %param.12) | copy-start | bytes 786436
  0.6 16.6 %copy-start.1 = (f32[2,16,16,256]{3,2,1,0:T(8,128)S(1)}, f32[2,16,16,256]{3,2,1,0:T(8,128)}, u32[]{:S(2)}) copy-start(f32[2,16,16,256]{3,2,1,0:T(8,128)} %param.10) | copy-start | bytes 1572868
  0.7 16.6 %copy-start = (f32[2,16,16,256]{3,2,1,0:T(8,128)S(1)}, f32[2,16,16,256]{3,2,1,0:T(8,128)}, u32[]{:S(2)}) copy-start(f32[2,16,16,256]{3,2,1,0:T(8,128)} %param.13) | copy-start | bytes 1572868
  1.7 14.9 %copy-start.2 = (f32[1,16,16,256]{3,2,1,0:T(8,128)}, f32[1,16,16,256]{3,2,1,0:T(8,128)S(1)}, u32[]{:S(2)}) copy-start(f32[1,16,16,256]{3,2,1,0:T(8,128)S(1)} %subtract_bitcast_fusion) | copy-start | bytes 786436
  3.3 10.7 %collective-permute-start = (f32[6,16,2,256]{3,2,1,0:T(2,128)S(1)}, f32[6,16,2,256]{3,2,1,0:T(2,128)S(1)}, u32[]{:S(2)}, u32[]{:S(2)}) collective-permute-start(f32[6,16,2,256]{3,2,1,0:T(2,128)S(1)} %get-tuple-element.14), channel_id=1, source_target_pairs={{16,0},{32,16},{48,32},{64,48},{80,64},{96,80},{112,96},{128,112},... | collective-permute-start | bytes 589832 | tf_op jit(solution)/shard_map/ppermute | solution.py:185
  12.1 4.5 %collective-permute-start.1 = (f32[6,16,2,256]{3,2,1,0:T(2,128)S(1)}, f32[6,16,2,256]{3,2,1,0:T(2,128)S(1)}, u32[]{:S(2)}, u32[]{:S(2)}) collective-permute-start(f32[6,16,2,256]{3,2,1,0:T(2,128)S(1)} %get-tuple-element.15), channel_id=1, source_target_pairs={{0,16},{16,32},{32,48},{48,64},{64,80},{80,96},{96,112},{112,128},... | collective-permute-start | bytes 589832 | tf_op jit(solution)/shard_map/ppermute | solution.py:187
  14.0 2.6 %copy-start.5 = (f32[6,16,2,256]{3,2,1,0:T(2,128)}, f32[6,16,2,256]{3,2,1,0:T(2,128)S(1)}, u32[]{:S(2)}) copy-start(f32[6,16,2,256]{3,2,1,0:T(2,128)S(1)} %collective-permute-done) | copy-start | bytes 589828
  16.6 0.7 copy-start.6
  17.3 0.8 copy-start.3
  18.4 7.8 %copy-start.7 = (s32[2,8,3]{1,0,2:T(2,128)S(1)}, s32[2,8,3]{1,0,2:T(2,128)}, u32[]{:S(2)}) copy-start(s32[2,8,3]{1,0,2:T(2,128)} %param.15) | copy-start | bytes 580
  19.1 7.9 %collective-permute-start.2 = (f32[6,16,24,2]{2,1,3,0:T(8,128)S(1)}, f32[6,16,24,2]{2,1,3,0:T(8,128)S(1)}, u32[]{:S(2)}, u32[]{:S(2)}) collective-permute-start(f32[6,16,24,2]{2,1,3,0:T(8,128)S(1)} %copy.13), channel_id=1, source_target_pairs={{1,0},{2,1},{3,2},{4,3},{5,4},{6,5},{7,6},{8,7},{9,8},{10,9},{11,1... | collective-permute-start | bytes 55304 | tf_op jit(solution)/shard_map/ppermute | solution.py:185
  21.0 6.6 %collective-permute-start.3 = (f32[6,16,24,2]{2,1,3,0:T(8,128)S(1)}, f32[6,16,24,2]{2,1,3,0:T(8,128)}, u32[]{:S(2)}, u32[]{:S(2)}) collective-permute-start(f32[6,16,24,2]{2,1,3,0:T(8,128)S(1)} %copy.14), channel_id=1, source_target_pairs={{0,1},{1,2},{2,3},{3,4},{4,5},{5,6},{6,7},{7,8},{8,9},{9,10},{10,1... | collective-permute-start | bytes 55304 | tf_op jit(solution)/shard_map/ppermute | solution.py:187
  41.9 23.7 %collective-permute-start.4 = (f32[16,16,256]{2,1,0:T(8,128)S(1)}, f32[16,16,256]{2,1,0:T(8,128)S(1)}, u32[]{:S(2)}, u32[]{:S(2)}) collective-permute-start(f32[16,16,256]{2,1,0:T(8,128)S(1)} %broadcast_select_fusion), channel_id=1, source_target_pairs={{0,256},{256,0},{1,257},{257,1},{2,258},{258,2},{3,259},{259,3},{4... | collective-permute-start | bytes 786440 | tf_op jit(solution)/shard_map/ppermute | solution.py:254
  104.9 42.0 %collective-permute-start.5 = (f32[16,16,256]{2,1,0:T(8,128)}, f32[16,16,256]{2,1,0:T(8,128)S(1)}, u32[]{:S(2)}, u32[]{:S(2)}) collective-permute-start(f32[16,16,256]{2,1,0:T(8,128)} %bitcast.14), channel_id=1, source_target_pairs={{0,256},{256,0},{1,257},{257,1},{2,258},{258,2},{3,259},{259,3},{4... | collective-permute-start | bytes 786440 | tf_op jit(solution)/shard_map/ppermute | solution.py:269

commit v9 on v8

--- a/solution.py
+++ b/solution.py
@@ -227,6 +227,26 @@
     )(block_cols, gathered, blocks, heat, grad)
 
 
+def head_chunk(mine, other, heat_sens, gradient, blocks, block_cols):
+    partner = [(0, 1), (1, 0)]
+    layers, rows_x, cols_y = mine.shape
+    rounded = (mine + lax.ppermute(other, "sec", partner)).astype(jnp.bfloat16)
+    count = lax.axis_size("gy")
+    copies = jnp.broadcast_to(rounded[None], (count,) + rounded.shape)
+    gathered = lax.all_to_all(copies, "gy", 0, 0, tiled=False)
+    cells = layers * rows_x
+    head, partial_sens = apply_head(
+        block_cols,
+        gathered.reshape(count, cells, cols_y),
+        blocks,
+        heat_sens.reshape(cells, cols_y),
+        gradient.reshape(cells, cols_y),
+    )
+    head = head.reshape(layers, rows_x, cols_y)
+    partial_sens = partial_sens.reshape(layers, rows_x, cols_y)
+    return head, partial_sens + lax.ppermute(partial_sens, "sec", partner)
+
+
 def shards(
     terminal,
     forward_temp,
@@ -250,23 +270,18 @@
     first = lax.axis_index("sec") == 0
     mine = jnp.where(first, flow_x, flow_y)
     other = jnp.where(first, flow_y, flow_x)
-    partner = [(0, 1), (1, 0)]
-    rounded = (mine + lax.ppermute(other, "sec", partner)).astype(jnp.bfloat16)
-    row_blocks, per_row, block_size, _ = blocks.shape
-    count = lax.axis_size("gy")
-    copies = jnp.broadcast_to(rounded[None], (count,) + rounded.shape)
-    gathered = lax.all_to_all(copies, "gy", 0, 0, tiled=False)
-    cells = layers * rows_x
-    head, partial_sens = apply_head(
-        block_cols,
-        gathered.reshape(count, cells, cols_y),
-        blocks,
-        heat_sens.reshape(cells, cols_y),
-        head_gradient[0].reshape(cells, cols_y),
-    )
-    head = head.reshape(layers, rows_x, cols_y)
-    partial_sens = partial_sens.reshape(layers, rows_x, cols_y)
-    sensitivity = partial_sens + lax.ppermute(partial_sens, "sec", partner)
+    chunks = 2
+    depth = layers // chunks
+    heads, sens = [], []
+    for part in range(chunks):
+        cut = slice(part * depth, (part + 1) * depth)
+        head, total = head_chunk(
+            mine[cut], other[cut], heat_sens[cut], head_gradient[0, cut], blocks, block_cols
+        )
+        heads.append(head)
+        sens.append(total)
+    head = jnp.concatenate(heads, axis=0)
+    sensitivity = jnp.concatenate(sens, axis=0)
     return (head[None], sensitivity)
 
 

time: 149 us -> 150 us (level)
  the two profiles are of different devices: /device:TPU:1 before, /device:TPU:11 now
where the time goes in v9:
time: 150 us
  waiting for transfers between devices  47.2 us (31%)
  starting transfers between devices  45.6 us (30%)
  blocking collectives  20.9 us (14%)
  Pallas kernels  13.4 us (9%)
  other arithmetic  12.4 us (8%)
  local copies, waits for them, and re-layouts  9.17 us (6%)
    ppermute x2, waiting for transfers between devices, head_chunk(): rounded = (mine + lax.ppermute(other, 'sec', partner)).astype(jnp.bfloat16)  26.1 us
    all_to_all x1, blocking collectives, head_chunk(): gathered = lax.all_to_all(copies, 'gy', 0, 0, tiled=False)  20.9 us
    ppermute x2, starting transfers between devices, head_chunk(): rounded = (mine + lax.ppermute(other, 'sec', partner)).astype(jnp.bfloat16)  16.9 us
    ppermute x2, waiting for transfers between devices, head_chunk(): return (head, partial_sens + lax.ppermute(partial_sens, 'sec', partner))  14.1 us
    ppermute x2, starting transfers between devices, head_chunk(): return (head, partial_sens + lax.ppermute(partial_sens, 'sec', partner))  11 us
    pallas_call x1, Pallas kernels, heat_phase(): pl.pallas_call(heat_kernel, out_shape=(out, out, out), in_specs=[smem, sm...  8.34 us
    ppermute x2, starting transfers between devices, circular(): lax.ppermute(tail, axis, [(i, i + 1) for i in range(ends)])  6.66 us
    all_to_all x1, starting transfers between devices, head_chunk(): gathered = lax.all_to_all(copies, 'gy', 0, 0, tiled=False)  6.38 us
  transfers between devices with their start and end apart: 9, of which 7 were waited for; matrix products, arithmetic and copies ran while one was open for 4% of the time, Pallas kernels for 3%

profile of v9, /device:TPU:11, one launch (start us, length us, event | category | flops | bytes accessed | tf_op | source)
XLA Modules:
  0.0 149.5 jit_solution(802996329282952919)
XLA Ops:
  1.8 1.5 %pad_maximum_fusion.6 = (f32[6,16,2,256]{3,2,1,0:T(2,128)S(1)}, f32[6,16,2,256]{3,2,1,0:T(2,128)S(1)}) fusion(f32[1,16,16,256]{3,2,1,0:T(8,128)S(1)} %subtract_bitcast_fusion, f32[2,16,16,256]{3,2,1,0:T(8,128)} %param.13, f32[1,16,16,256]{3,2,1,0:T(8,128)} %bitcast.19, f32[2,16,16,256]{3,2,1,0:T(8,128)} %param.10), kind=kLoop, calls=%fused_computation.8 | loop fusion | flops 294912 | bytes 1966080 | tf_op jit(solution)/shard_map/slice | solution.py:178
  3.3 2.6 %collective-permute-start = (f32[6,16,2,256]{3,2,1,0:T(2,128)S(1)}, f32[6,16,2,256]{3,2,1,0:T(2,128)S(1)}, u32[]{:S(2)}, u32[]{:S(2)}) collective-permute-start(f32[6,16,2,256]{3,2,1,0:T(2,128)S(1)} %get-tuple-element.18), channel_id=1, source_target_pairs={{16,0},{32,16},{48,32},{64,48},{80,64},{96,80},{112,96},{128,112},... | collective-permute-start | bytes 589832 | tf_op jit(solution)/shard_map/ppermute | solution.py:185
  5.9 3.4 %collective-permute-start.1 = (f32[6,16,2,256]{3,2,1,0:T(2,128)S(1)}, f32[6,16,2,256]{3,2,1,0:T(2,128)S(1)}, u32[]{:S(2)}, u32[]{:S(2)}) collective-permute-start(f32[6,16,2,256]{3,2,1,0:T(2,128)S(1)} %get-tuple-element.19), channel_id=1, source_target_pairs={{0,16},{16,32},{32,48},{48,64},{64,80},{80,96},{96,112},{112,128},... | collective-permute-start | bytes 589832 | tf_op jit(solution)/shard_map/ppermute | solution.py:187
  9.3 1.4 collective-permute-done
  10.7 1.2 collective-permute-done.1
  14.4 2.1 %collective-permute-start.2 = (f32[6,16,24,2]{2,1,3,0:T(8,128)S(1)}, f32[6,16,24,2]{2,1,3,0:T(8,128)S(1)}, u32[]{:S(2)}, u32[]{:S(2)}) collective-permute-start(f32[6,16,24,2]{2,1,3,0:T(8,128)S(1)} %copy.13), channel_id=1, source_target_pairs={{1,0},{2,1},{3,2},{4,3},{5,4},{6,5},{7,6},{8,7},{9,8},{10,9},{11,1... | collective-permute-start | bytes 55304 | tf_op jit(solution)/shard_map/ppermute | solution.py:185
  17.1 3.2 %collective-permute-start.3 = (f32[6,16,24,2]{2,1,3,0:T(8,128)S(1)}, f32[6,16,24,2]{2,1,3,0:T(8,128)}, u32[]{:S(2)}, u32[]{:S(2)}) collective-permute-start(f32[6,16,24,2]{2,1,3,0:T(8,128)S(1)} %copy.14), channel_id=1, source_target_pairs={{0,1},{1,2},{2,3},{3,4},{4,5},{5,6},{6,7},{7,8},{8,9},{9,10},{10,1... | collective-permute-start | bytes 55304 | tf_op jit(solution)/shard_map/ppermute | solution.py:187
  22.4 1.4 collective-permute-done.3
  23.8 1.5 %copy.16 = f32[6,16,24,2]{3,2,1,0:T(8,128)S(1)} copy(f32[6,16,24,2]{2,1,3,0:T(8,128)} %collective-permute-done.3) | data formatting | bytes 36864 | tf_op jit(solution)/shard_map/ppermute | solution.py:187
  25.3 3.4 %pad_maximum_fusion.box_ref = f32[6,16,24,384]{3,2,1,0:T(8,128)} fusion(f32[6,16,24,2]{3,2,1,0:T(8,128)S(1)} %copy.16, f32[6,16,24,2]{3,2,1,0:T(8,128)S(1)} %copy.15, f32[6,16,2,256]{3,2,1,0:T(2,128)} %copy-done.7, f32[6,16,4,256]{3,2,1,0:T(4,128)} %copy-done.4, f32[6,16,2,256]{3,2,1,0:T(2,128)} %copy-done.6, f32[1,16,16,256]{3,2,1,0:T(8,128)} %copy-done.2, ...), kind=kLoop, calls=%fused_computation | loop fusion | flops 7962624 | bytes 5936640 | tf_op jit(solution)/shard_map/concatenate | solution.py:182
  28.7 8.3 %shard_map.113 = (f32[16,16,256]{2,1,0:T(8,128)}, f32[16,16,256]{2,1,0:T(8,128)}, f32[16,16,256]{2,1,0:T(8,128)}) custom-call(s32[2]{0:T(128)} %pad_add_fusion.offs_ref, s32[2,8,3]{2,1,0:T(8,128)} %copy.17.wells_ref, f32[2,2,8]{2,1,0:T(2,128)} %misfit_ref.1, f32[6,16,24,384]{3,2,1,0:T(8,128)} %pad_maximum_fusion.box_ref, bf16[2,2,16,16,256]{4,3,2,1,0:T(8,128)(2,1)} %temp_ref.1), custom_call_target="tpu_custom_call" | custom-call | tf_op jit(solution)/shard_map/pallas_call | solution.py:162
  38.2 15.0 %collective-permute-start.4 = (f32[8,16,256]{2,1,0:T(8,128)S(1)}, f32[8,16,256]{2,1,0:T(8,128)S(1)}, u32[]{:S(2)}, u32[]{:S(2)}) collective-permute-start(f32[8,16,256]{2,1,0:T(8,128)S(1)} %get-tuple-element.26), channel_id=1, source_target_pairs={{0,256},{256,0},{1,257},{257,1},{2,258},{258,2},{3,259},{259,3},{4... | collective-permute-start | bytes 393224 | tf_op jit(solution)/shard_map/ppermute | solution.py:233
  53.2 1.9 %collective-permute-start.5 = (f32[8,16,256]{2,1,0:T(8,128)S(1)}, f32[8,16,256]{2,1,0:T(8,128)S(1)}, u32[]{:S(2)}, u32[]{:S(2)}) collective-permute-start(f32[8,16,256]{2,1,0:T(8,128)S(1)} %get-tuple-element.27), channel_id=1, source_target_pairs={{0,256},{256,0},{1,257},{257,1},{2,258},{258,2},{3,259},{259,3},{4... | collective-permute-start | bytes 393224 | tf_op jit(solution)/shard_map/ppermute | solution.py:233
  55.1 10.9 %collective-permute-done.4 = f32[8,16,256]{2,1,0:T(8,128)S(1)} collective-permute-done((f32[8,16,256]{2,1,0:T(8,128)S(1)}, f32[8,16,256]{2,1,0:T(8,128)S(1)}, u32[]{:S(2)}, u32[]{:S(2)}) %collective-permute-start.4) | collective-permute-done | bytes 131104 | tf_op jit(solution)/shard_map/ppermute | solution.py:233
  65.9 15.3 %collective-permute-done.5 = f32[8,16,256]{2,1,0:T(8,128)S(1)} collective-permute-done((f32[8,16,256]{2,1,0:T(8,128)S(1)}, f32[8,16,256]{2,1,0:T(8,128)S(1)}, u32[]{:S(2)}, u32[]{:S(2)}) %collective-permute-start.5) | collective-permute-done | bytes 131104 | tf_op jit(solution)/shard_map/ppermute | solution.py:233
  81.4 20.9 %all_to_all.10 = bf16[16,8,16,256]{3,2,1,0:T(8,128)(2,1)} all-to-all(bf16[16,8,16,256]{3,2,1,0:T(8,128)(2,1)S(1)} %broadcast_in_dim.31), channel_id=1, replica_groups=mesh['sec'=2,'gx'=16,'gy'=16] {'gy'}, dimensions={0} | all-to-all | bytes 2097152 | tf_op jit(solution)/shard_map/all_to_all | solution.py:236
  103.4 6.4 %all-to-all-start.1 = ((bf16[16,8,16,256]{3,2,1,0:T(8,128)(2,1)}), bf16[16,8,16,256]{3,2,1,0:T(8,128)(2,1)S(1)}, u32[]{:S(2)}, u32[]{:S(2)}) async-start(bf16[16,8,16,256]{3,2,1,0:T(8,128)(2,1)} %broadcast_in_dim.32), calls=%async_computation.1 | async-start | bytes 2097152 | tf_op jit(solution)/shard_map/all_to_all | solution.py:236
  111.2 2.5 %shard_map.114 = (f32[128,256]{1,0:T(8,128)}, f32[128,256]{1,0:T(8,128)}) custom-call(s32[2,7]{1,0:T(2,128)} %cols_ref.3, bf16[16,128,256]{2,1,0:T(8,128)(2,1)} %bitcast.18, bf16[2,7,128,128]{3,2,1,0:T(8,128)(2,1)} %blocks_ref.3, f32[128,256]{1,0:T(8,128)} %bitcast.23, bf16[128,256]{1,0:T(8,128)(2,1)} %bitcast.25), custom_call_target="tpu_custom_call" | custom-call | flops 58720256 | bytes 1966080 | tf_op jit(solution)/shard_map/pallas_call | solution.py:214
  113.7 5.3 %collective-permute-start.6 = (f32[8,16,256]{2,1,0:T(8,128)}, f32[8,16,256]{2,1,0:T(8,128)S(1)}, u32[]{:S(2)}, u32[]{:S(2)}) collective-permute-start(f32[8,16,256]{2,1,0:T(8,128)} %bitcast.26), channel_id=1, source_target_pairs={{0,256},{256,0},{1,257},{257,1},{2,258},{258,2},{3,259},{259,3},{4... | collective-permute-start | bytes 393224 | tf_op jit(solution)/shard_map/ppermute | solution.py:247
  119.0 2.9 %all-to-all-done.1 = bf16[16,8,16,256]{3,2,1,0:T(8,128)(2,1)S(1)} async-done(((bf16[16,8,16,256]{3,2,1,0:T(8,128)(2,1)}), bf16[16,8,16,256]{3,2,1,0:T(8,128)(2,1)S(1)}, u32[]{:S(2)}, u32[]{:S(2)}) %all-to-all-start.1) | async-done | bytes 1048608 | tf_op jit(solution)/shard_map/all_to_all | solution.py:236
  122.9 2.5 %shard_map.115 = (f32[128,256]{1,0:T(8,128)}, f32[128,256]{1,0:T(8,128)}) custom-call(s32[2,7]{1,0:T(2,128)} %cols_ref.3, bf16[16,128,256]{2,1,0:T(8,128)(2,1)} %bitcast.17, bf16[2,7,128,128]{3,2,1,0:T(8,128)(2,1)} %blocks_ref.3, f32[128,256]{1,0:T(8,128)} %bitcast.22, bf16[128,256]{1,0:T(8,128)(2,1)} %bitcast.24), custom_call_target="tpu_custom_call" | custom-call | flops 58720256 | bytes 1966080 | tf_op jit(solution)/shard_map/pallas_call | solution.py:214
  125.4 5.8 %collective-permute-start.7 = (f32[8,16,256]{2,1,0:T(8,128)}, f32[8,16,256]{2,1,0:T(8,128)S(1)}, u32[]{:S(2)}, u32[]{:S(2)}) collective-permute-start(f32[8,16,256]{2,1,0:T(8,128)} %bitcast.28), channel_id=1, source_target_pairs={{0,256},{256,0},{1,257},{257,1},{2,258},{258,2},{3,259},{259,3},{4... | collective-permute-start | bytes 393224 | tf_op jit(solution)/shard_map/ppermute | solution.py:247
  131.2 1.7 %maximum_bitcast_fusion = f32[1,16,16,256]{3,2,1,0:T(8,128)} fusion(f32[8,16,256]{2,1,0:T(8,128)} %bitcast.31, f32[8,16,256]{2,1,0:T(8,128)} %bitcast.30), kind=kLoop, calls=%fused_computation.2 | loop fusion | flops 65536 | bytes 524288 | tf_op jit(solution)/shard_map/broadcast_in_dim | solution.py:285
  133.8 14.1 %collective-permute-done.7 = f32[8,16,256]{2,1,0:T(8,128)S(1)} collective-permute-done((f32[8,16,256]{2,1,0:T(8,128)}, f32[8,16,256]{2,1,0:T(8,128)S(1)}, u32[]{:S(2)}, u32[]{:S(2)}) %collective-permute-start.7) | collective-permute-done | bytes 131104 | tf_op jit(solution)/shard_map/ppermute | solution.py:247
  (45 shorter events, 13.4 us)
Async XLA Ops:
  0.6 12.0 %copy-start.5 = (f32[16,16,256]{2,1,0:T(8,128)S(1)}, f32[16,16,256]{2,1,0:T(8,128)}, u32[]{:S(2)}) copy-start(f32[16,16,256]{2,1,0:T(8,128)} %param.12) | copy-start | bytes 786436
  0.6 11.9 %copy-start.1 = (f32[2,16,16,256]{3,2,1,0:T(8,128)S(1)}, f32[2,16,16,256]{3,2,1,0:T(8,128)}, u32[]{:S(2)}) copy-start(f32[2,16,16,256]{3,2,1,0:T(8,128)} %param.10) | copy-start | bytes 1572868
  0.7 11.9 %copy-start = (f32[2,16,16,256]{3,2,1,0:T(8,128)S(1)}, f32[2,16,16,256]{3,2,1,0:T(8,128)}, u32[]{:S(2)}) copy-start(f32[2,16,16,256]{3,2,1,0:T(8,128)} %param.13) | copy-start | bytes 1572868
  1.7 10.2 %copy-start.2 = (f32[1,16,16,256]{3,2,1,0:T(8,128)}, f32[1,16,16,256]{3,2,1,0:T(8,128)S(1)}, u32[]{:S(2)}) copy-start(f32[1,16,16,256]{3,2,1,0:T(8,128)S(1)} %subtract_bitcast_fusion) | copy-start | bytes 786436
  3.3 7.5 %collective-permute-start = (f32[6,16,2,256]{3,2,1,0:T(2,128)S(1)}, f32[6,16,2,256]{3,2,1,0:T(2,128)S(1)}, u32[]{:S(2)}, u32[]{:S(2)}) collective-permute-start(f32[6,16,2,256]{3,2,1,0:T(2,128)S(1)} %get-tuple-element.18), channel_id=1, source_target_pairs={{16,0},{32,16},{48,32},{64,48},{80,64},{96,80},{112,96},{128,112},... | collective-permute-start | bytes 589832 | tf_op jit(solution)/shard_map/ppermute | solution.py:185
  5.9 6.0 %collective-permute-start.1 = (f32[6,16,2,256]{3,2,1,0:T(2,128)S(1)}, f32[6,16,2,256]{3,2,1,0:T(2,128)S(1)}, u32[]{:S(2)}, u32[]{:S(2)}) collective-permute-start(f32[6,16,2,256]{3,2,1,0:T(2,128)S(1)} %get-tuple-element.19), channel_id=1, source_target_pairs={{0,16},{16,32},{32,48},{48,64},{64,80},{80,96},{96,112},{112,128},... | collective-permute-start | bytes 589832 | tf_op jit(solution)/shard_map/ppermute | solution.py:187
  10.7 1.3 copy-start.6
  11.9 0.7 copy-start.7
  12.6 0.7 copy-start.4
  13.7 7.2 %copy-start.10 = (s32[2,8,3]{1,0,2:T(2,128)S(1)}, s32[2,8,3]{1,0,2:T(2,128)}, u32[]{:S(2)}) copy-start(s32[2,8,3]{1,0,2:T(2,128)} %param.15) | copy-start | bytes 580
  14.4 7.4 %collective-permute-start.2 = (f32[6,16,24,2]{2,1,3,0:T(8,128)S(1)}, f32[6,16,24,2]{2,1,3,0:T(8,128)S(1)}, u32[]{:S(2)}, u32[]{:S(2)}) collective-permute-start(f32[6,16,24,2]{2,1,3,0:T(8,128)S(1)} %copy.13), channel_id=1, source_target_pairs={{1,0},{2,1},{3,2},{4,3},{5,4},{6,5},{7,6},{8,7},{9,8},{10,9},{11,1... | collective-permute-start | bytes 55304 | tf_op jit(solution)/shard_map/ppermute | solution.py:185
  17.1 6.7 %collective-permute-start.3 = (f32[6,16,24,2]{2,1,3,0:T(8,128)S(1)}, f32[6,16,24,2]{2,1,3,0:T(8,128)}, u32[]{:S(2)}, u32[]{:S(2)}) collective-permute-start(f32[6,16,24,2]{2,1,3,0:T(8,128)S(1)} %copy.14), channel_id=1, source_target_pairs={{0,1},{1,2},{2,3},{3,4},{4,5},{5,6},{6,7},{7,8},{8,9},{9,10},{10,1... | collective-permute-start | bytes 55304 | tf_op jit(solution)/shard_map/ppermute | solution.py:187
  38.2 27.8 %collective-permute-start.4 = (f32[8,16,256]{2,1,0:T(8,128)S(1)}, f32[8,16,256]{2,1,0:T(8,128)S(1)}, u32[]{:S(2)}, u32[]{:S(2)}) collective-permute-start(f32[8,16,256]{2,1,0:T(8,128)S(1)} %get-tuple-element.26), channel_id=1, source_target_pairs={{0,256},{256,0},{1,257},{257,1},{2,258},{258,2},{3,259},{259,3},{4... | collective-permute-start | bytes 393224 | tf_op jit(solution)/shard_map/ppermute | solution.py:233
  53.2 28.1 %collective-permute-start.5 = (f32[8,16,256]{2,1,0:T(8,128)S(1)}, f32[8,16,256]{2,1,0:T(8,128)S(1)}, u32[]{:S(2)}, u32[]{:S(2)}) collective-permute-start(f32[8,16,256]{2,1,0:T(8,128)S(1)} %get-tuple-element.27), channel_id=1, source_target_pairs={{0,256},{256,0},{1,257},{257,1},{2,258},{258,2},{3,259},{259,3},{4... | collective-permute-start | bytes 393224 | tf_op jit(solution)/shard_map/ppermute | solution.py:233
  81.4 28.4 %copy-start.9 = (bf16[1,16,16,256]{3,2,1,0:T(8,128)(2,1)S(1)}, bf16[1,16,16,256]{3,2,1,0:T(8,128)(2,1)}, u32[]{:S(2)}) copy-start(bf16[1,16,16,256]{3,2,1,0:T(8,128)(2,1)} %param.17) | copy-start | bytes 393220
  81.4 29.1 %copy-start.8 = (f32[16,16,256]{2,1,0:T(8,128)S(1)}, f32[16,16,256]{2,1,0:T(8,128)}, u32[]{:S(2)}) copy-start(f32[16,16,256]{2,1,0:T(8,128)} %get-tuple-element.11) | copy-start | bytes 786436
  103.4 18.5 %all-to-all-start.1 = ((bf16[16,8,16,256]{3,2,1,0:T(8,128)(2,1)}), bf16[16,8,16,256]{3,2,1,0:T(8,128)(2,1)S(1)}, u32[]{:S(2)}, u32[]{:S(2)}) async-start(bf16[16,8,16,256]{3,2,1,0:T(8,128)(2,1)} %broadcast_in_dim.32), calls=%async_computation.1 | async-start | bytes 2097152 | tf_op jit(solution)/shard_map/all_to_all | solution.py:236
  113.7 19.2 %collective-permute-start.6 = (f32[8,16,256]{2,1,0:T(8,128)}, f32[8,16,256]{2,1,0:T(8,128)S(1)}, u32[]{:S(2)}, u32[]{:S(2)}) collective-permute-start(f32[8,16,256]{2,1,0:T(8,128)} %bitcast.26), channel_id=1, source_target_pairs={{0,256},{256,0},{1,257},{257,1},{2,258},{258,2},{3,259},{259,3},{4... | collective-permute-start | bytes 393224 | tf_op jit(solution)/shard_map/ppermute | solution.py:247
  121.9 1.0 copy-start.3
  125.4 22.5 %collective-permute-start.7 = (f32[8,16,256]{2,1,0:T(8,128)}, f32[8,16,256]{2,1,0:T(8,128)S(1)}, u32[]{:S(2)}, u32[]{:S(2)}) collective-permute-start(f32[8,16,256]{2,1,0:T(8,128)} %bitcast.28), channel_id=1, source_target_pairs={{0,256},{256,0},{1,257},{257,1},{2,258},{258,2},{3,259},{259,3},{4... | collective-permute-start | bytes 393224 | tf_op jit(solution)/shard_map/ppermute | solution.py:247

commit v10 on v8

--- a/solution.py
+++ b/solution.py
@@ -191,6 +191,44 @@
     return cells
 
 
+def halo_box(cells, width, sizes):
+    rows, cols = cells.shape[-2:]
+    count_x, count_y = lax.axis_size("gx"), lax.axis_size("gy")
+
+    def fetch(piece, step_x, step_y):
+        pairs = [
+            ((i + step_x) * count_y + j + step_y, i * count_y + j)
+            for i in range(count_x)
+            for j in range(count_y)
+            if 0 <= i + step_x < count_x and 0 <= j + step_y < count_y
+        ]
+        return lax.ppermute(piece, ("gx", "gy"), pairs)
+
+    top, bottom = slice(0, width), slice(rows - width, rows)
+    left, right = slice(0, width), slice(cols - width, cols)
+    lead = cells.shape[:-2]
+
+    def gap(height, length):
+        return jnp.zeros(lead + (height, length), cells.dtype)
+
+    def strip(middle, after, before):
+        height = middle.shape[-2]
+        return jnp.concatenate([middle, after, gap(height, sizes[1] - cols - 2 * width), before], axis=-1)
+
+    body = strip(cells, fetch(cells[..., :, left], 0, 1), fetch(cells[..., :, right], 0, -1))
+    below = strip(
+        fetch(cells[..., top, :], 1, 0),
+        fetch(cells[..., top, left], 1, 1),
+        fetch(cells[..., top, right], 1, -1),
+    )
+    above = strip(
+        fetch(cells[..., bottom, :], -1, 0),
+        fetch(cells[..., bottom, left], -1, 1),
+        fetch(cells[..., bottom, right], -1, -1),
+    )
+    return jnp.concatenate([body, below, gap(sizes[0] - rows - 2 * width, sizes[1]), above], axis=-2)
+
+
 def head_kernel(cols_ref, gathered_ref, blocks_ref, heat_ref, grad_ref, head_ref, part_ref):
     row_blocks, per_row, size, _ = blocks_ref.shape
     halves = gathered_ref.shape[2] // size
@@ -244,7 +282,7 @@
     packed = jnp.concatenate([terminal, conductivity[None], velocity, keep[None]], axis=0)
     width = 2
     sizes = (-(-(rows_x + 2 * width) // 8) * 8, -(-(cols_y + 2 * width) // 128) * 128)
-    box = circular(packed, (("gx", 2), ("gy", 3)), width, sizes)
+    box = halo_box(packed, width, sizes)
     offs = jnp.stack([lax.axis_index("gx") * rows_x, lax.axis_index("gy") * cols_y]).astype(jnp.int32)
     heat_sens, flow_x, flow_y = heat_phase(offs, wells, misfit, box, forward_temp)
     first = lax.axis_index("sec") == 0

time: 149 us -> 170 us (1.14)
  the two profiles are of different devices: /device:TPU:1 before, /device:TPU:32 now
where the time goes in v10:
time: 170 us; the launch traced here: 169 us
  starting transfers between devices  50.5 us (30%)
  blocking collectives  47.3 us (28%)
  waiting for transfers between devices  36.3 us (21%)
  other arithmetic  12.8 us (8%)
  Pallas kernels  11.3 us (7%)
  local copies, waits for them, and re-layouts  10.1 us (6%)
    all_to_all x1, blocking collectives, shards(): gathered = lax.all_to_all(copies, 'gy', 0, 0, tiled=False)  47.3 us
    ppermute x8, starting transfers between devices, fetch(): return lax.ppermute(piece, ('gx', 'gy'), pairs)  23.7 us
    ppermute x1, waiting for transfers between devices, shards(): sensitivity = partial_sens + lax.ppermute(partial_sens, 'sec', partner)  17.9 us
    ppermute x1, starting transfers between devices, shards(): rounded = (mine + lax.ppermute(other, 'sec', partner)).astype(jnp.bfloat16)  13.9 us
    ppermute x1, starting transfers between devices, shards(): sensitivity = partial_sens + lax.ppermute(partial_sens, 'sec', partner)  12.9 us
    ppermute x1, waiting for transfers between devices, shards(): rounded = (mine + lax.ppermute(other, 'sec', partner)).astype(jnp.bfloat16)  12.9 us
    pallas_call x1, Pallas kernels, heat_phase(): pl.pallas_call(heat_kernel, out_shape=(out, out, out), in_specs=[smem, sm...  8.34 us
    ppermute x8, waiting for transfers between devices, fetch(): return lax.ppermute(piece, ('gx', 'gy'), pairs)  5.63 us
  transfers between devices with their start and end apart: 10, of which 3 were waited for; matrix products, arithmetic and copies ran while one was open for 5% of the time, Pallas kernels for 0%

profile of v10, /device:TPU:32, one launch (start us, length us, event | category | flops | bytes accessed | tf_op | source)
XLA Modules:
  0.0 169.2 jit_solution(40023092715704061)
XLA Ops:
  1.6 1.5 pad_maximum_fusion
  3.2 1.4 fusion
  4.6 2.4 %copy.13 = f32[6,16,16,2]{2,1,3,0:T(8,128)} copy(f32[6,16,16,2]{3,2,1,0:T(8,128)} %get-tuple-element.12) | data formatting | bytes 24576 | tf_op jit(solution)/shard_map/slice | solution.py:218
  7.0 1.3 collective-permute-start
  8.3 2.4 %copy.14 = f32[6,16,16,2]{2,1,3,0:T(8,128)} copy(f32[6,16,16,2]{3,2,1,0:T(8,128)} %get-tuple-element.13) | data formatting | bytes 24576 | tf_op jit(solution)/shard_map/slice | solution.py:218
  10.7 4.5 %collective-permute-start.1 = (f32[6,16,16,2]{2,1,3,0:T(8,128)}, f32[6,16,16,2]{2,1,3,0:T(8,128)S(1)}, u32[]{:S(2)}, u32[]{:S(2)}) collective-permute-start(f32[6,16,16,2]{2,1,3,0:T(8,128)} %copy.14), channel_id=1, source_target_pairs={{0,1},{1,2},{2,3},{3,4},{4,5},{5,6},{6,7},{7,8},{8,9},{9,10},{10,1... | collective-permute-start | bytes 36872 | tf_op jit(solution)/shard_map/ppermute | solution.py:205
  15.3 1.9 %collective-permute-start.2 = (f32[6,16,2,256]{3,2,1,0:T(2,128)S(1)}, f32[6,16,2,256]{3,2,1,0:T(2,128)}, u32[]{:S(2)}, u32[]{:S(2)}) collective-permute-start(f32[6,16,2,256]{3,2,1,0:T(2,128)S(1)} %slice.34), channel_id=1, source_target_pairs={{16,0},{17,1},{18,2},{19,3},{20,4},{21,5},{22,6},{23,7},{24,8},{25... | collective-permute-start | bytes 589832 | tf_op jit(solution)/shard_map/ppermute | solution.py:205
  17.4 2.4 %collective-permute-start.5 = (f32[6,16,2,256]{3,2,1,0:T(2,128)S(1)}, f32[6,16,2,256]{3,2,1,0:T(2,128)}, u32[]{:S(2)}, u32[]{:S(2)}) collective-permute-start(f32[6,16,2,256]{3,2,1,0:T(2,128)S(1)} %pad_maximum_fusion.1), channel_id=1, source_target_pairs={{0,16},{1,17},{2,18},{3,19},{4,20},{5,21},{6,22},{7,23},{8,24},{9,... | collective-permute-start | bytes 589832 | tf_op jit(solution)/shard_map/ppermute | solution.py:205
  20.7 1.3 collective-permute-start.3
  22.0 5.6 %collective-permute-done.3 = f32[6,16,2,2]{3,2,1,0:T(2,128)S(1)} collective-permute-done((f32[6,16,2,2]{3,2,1,0:T(2,128)S(1)}, f32[6,16,2,2]{3,2,1,0:T(2,128)S(1)}, u32[]{:S(2)}, u32[]{:S(2)}) %collective-permute-start.3) | collective-permute-done | bytes 1568 | tf_op jit(solution)/shard_map/ppermute | solution.py:205
  27.6 7.5 %collective-permute-start.4 = (f32[6,16,2,2]{3,2,1,0:T(2,128)}, f32[6,16,2,2]{3,2,1,0:T(2,128)}, u32[]{:S(2)}, u32[]{:S(2)}) collective-permute-start(f32[6,16,2,2]{3,2,1,0:T(2,128)} %get-tuple-element.17), channel_id=1, source_target_pairs={{16,1},{17,2},{18,3},{19,4},{20,5},{21,6},{22,7},{23,8},{24,9},{25... | collective-permute-start | bytes 4616 | tf_op jit(solution)/shard_map/ppermute | solution.py:205
  35.1 1.3 collective-permute-start.6
  36.4 3.5 %collective-permute-start.7 = (f32[6,16,2,2]{3,2,1,0:T(2,128)}, f32[6,16,2,2]{3,2,1,0:T(2,128)}, u32[]{:S(2)}, u32[]{:S(2)}) collective-permute-start(f32[6,16,2,2]{3,2,1,0:T(2,128)} %get-tuple-element.15), channel_id=1, source_target_pairs={{0,17},{1,18},{2,19},{3,20},{4,21},{5,22},{6,23},{7,24},{8,25},{9,... | collective-permute-start | bytes 4616 | tf_op jit(solution)/shard_map/ppermute | solution.py:205
  42.6 1.5 copy.16
  44.2 5.0 %maximum_maximum_fusion.box_ref = f32[6,16,24,384]{3,2,1,0:T(8,128)} fusion(f32[6,16,2,2]{3,2,1,0:T(2,128)} %collective-permute-done.7, f32[6,16,2,124]{3,2,1,0:T(2,128)S(1)} %broadcast.4, f32[6,16,2,2]{3,2,1,0:T(2,128)} %collective-permute-done.6, f32[6,16,2,256]{3,2,1,0:T(2,128)} %collective-permute-done.5, f32[6,16,2,2]{3,2,1,0:T(2,128)} %collective-permute-done.4, ...), kind=kLoop, calls=%fused_computation | loop fusion | flops 13271040 | bytes 5667936 | tf_op jit(solution)/shard_map/concatenate | solution.py:229
  49.2 8.3 %shard_map.113 = (f32[16,16,256]{2,1,0:T(8,128)}, f32[16,16,256]{2,1,0:T(8,128)}, f32[16,16,256]{2,1,0:T(8,128)}) custom-call(s32[2]{0:T(128)} %pad_add_fusion.offs_ref, s32[2,8,3]{2,1,0:T(8,128)} %copy.17.wells_ref, f32[2,2,8]{2,1,0:T(2,128)} %misfit_ref.1, f32[6,16,24,384]{3,2,1,0:T(8,128)} %maximum_maximum_fusion.box_ref, ...), custom_call_target="tpu_custom_call" | custom-call | tf_op jit(solution)/shard_map/pallas_call | solution.py:162
  58.5 13.9 %collective-permute-start.8 = (f32[16,16,256]{2,1,0:T(8,128)S(1)}, f32[16,16,256]{2,1,0:T(8,128)S(1)}, u32[]{:S(2)}, u32[]{:S(2)}) collective-permute-start(f32[16,16,256]{2,1,0:T(8,128)S(1)} %broadcast_select_fusion), channel_id=1, source_target_pairs={{0,256},{256,0},{1,257},{257,1},{2,258},{258,2},{3,259},{259,3},{4... | collective-permute-start | bytes 786440 | tf_op jit(solution)/shard_map/ppermute | solution.py:292
  72.5 12.9 %collective-permute-done.8 = f32[16,16,256]{2,1,0:T(8,128)S(1)} collective-permute-done((f32[16,16,256]{2,1,0:T(8,128)S(1)}, f32[16,16,256]{2,1,0:T(8,128)S(1)}, u32[]{:S(2)}, u32[]{:S(2)}) %collective-permute-start.8) | collective-permute-done | bytes 262176 | tf_op jit(solution)/shard_map/ppermute | solution.py:292
  85.3 1.0 add_convert_fusion
  86.6 47.3 %all_to_all.5 = bf16[16,16,16,256]{3,2,1,0:T(8,128)(2,1)} all-to-all(bf16[16,16,16,256]{3,2,1,0:T(8,128)(2,1)S(1)} %broadcast_in_dim.22), channel_id=1, replica_groups=mesh['sec'=2,'gx'=16,'gy'=16] {'gy'}, dimensions={0} | all-to-all | bytes 4194304 | tf_op jit(solution)/shard_map/all_to_all | solution.py:296
  133.9 2.9 %shard_map.114 = (f32[256,256]{1,0:T(8,128)}, f32[256,256]{1,0:T(8,128)}) custom-call(s32[2,7]{1,0:T(2,128)} %cols_ref.1, bf16[16,256,256]{2,1,0:T(8,128)(2,1)} %bitcast.10, bf16[2,7,128,128]{3,2,1,0:T(8,128)(2,1)} %blocks_ref.1, f32[256,256]{1,0:T(8,128)} %bitcast.17, bf16[256,256]{1,0:T(8,128)(2,1)} %bitcast.18), custom_call_target="tpu_custom_call" | custom-call | flops 117440512 | bytes 3473408 | tf_op jit(solution)/shard_map/pallas_call | solution.py:252
  136.8 12.9 %collective-permute-start.9 = (f32[16,16,256]{2,1,0:T(8,128)}, f32[16,16,256]{2,1,0:T(8,128)S(1)}, u32[]{:S(2)}, u32[]{:S(2)}) collective-permute-start(f32[16,16,256]{2,1,0:T(8,128)} %bitcast.15), channel_id=1, source_target_pairs={{0,256},{256,0},{1,257},{257,1},{2,258},{258,2},{3,259},{259,3},{4... | collective-permute-start | bytes 786440 | tf_op jit(solution)/shard_map/ppermute | solution.py:307
  149.7 17.9 %collective-permute-done.9 = f32[16,16,256]{2,1,0:T(8,128)S(1)} collective-permute-done((f32[16,16,256]{2,1,0:T(8,128)}, f32[16,16,256]{2,1,0:T(8,128)S(1)}, u32[]{:S(2)}, u32[]{:S(2)}) %collective-permute-start.9) | collective-permute-done | bytes 262176 | tf_op jit(solution)/shard_map/ppermute | solution.py:307
  167.5 1.7 add.7
  (33 shorter events, 6.0 us)
Async XLA Ops:
  1.6 15.6 %copy-start = (f32[2,16,16,256]{3,2,1,0:T(8,128)S(1)}, f32[2,16,16,256]{3,2,1,0:T(8,128)}, u32[]{:S(2)}) copy-start(f32[2,16,16,256]{3,2,1,0:T(8,128)} %param.13) | copy-start | bytes 1572868
  1.6 15.6 %copy-start.1 = (f32[2,16,16,256]{3,2,1,0:T(8,128)S(1)}, f32[2,16,16,256]{3,2,1,0:T(8,128)}, u32[]{:S(2)}) copy-start(f32[2,16,16,256]{3,2,1,0:T(8,128)} %param.10) | copy-start | bytes 1572868
  1.6 15.6 %copy-start.2 = (f32[16,16,256]{2,1,0:T(8,128)S(1)}, f32[16,16,256]{2,1,0:T(8,128)}, u32[]{:S(2)}) copy-start(f32[16,16,256]{2,1,0:T(8,128)} %param.12) | copy-start | bytes 786436
  4.6 36.7 %copy-start.5 = (s32[2,8,3]{1,0,2:T(2,128)S(1)}, s32[2,8,3]{1,0,2:T(2,128)}, u32[]{:S(2)}) copy-start(s32[2,8,3]{1,0,2:T(2,128)} %param.15) | copy-start | bytes 580
  7.0 28.1 %collective-permute-start = (f32[6,16,16,2]{2,1,3,0:T(8,128)}, f32[6,16,16,2]{2,1,3,0:T(8,128)S(1)}, u32[]{:S(2)}, u32[]{:S(2)}) collective-permute-start(f32[6,16,16,2]{2,1,3,0:T(8,128)} %copy.13), channel_id=1, source_target_pairs={{1,0},{2,1},{3,2},{4,3},{5,4},{6,5},{7,6},{8,7},{9,8},{10,9},{11,1... | collective-permute-start | bytes 36872 | tf_op jit(solution)/shard_map/ppermute | solution.py:205
  10.7 25.7 %collective-permute-start.1 = (f32[6,16,16,2]{2,1,3,0:T(8,128)}, f32[6,16,16,2]{2,1,3,0:T(8,128)S(1)}, u32[]{:S(2)}, u32[]{:S(2)}) collective-permute-start(f32[6,16,16,2]{2,1,3,0:T(8,128)} %copy.14), channel_id=1, source_target_pairs={{0,1},{1,2},{2,3},{3,4},{4,5},{5,6},{6,7},{7,8},{8,9},{9,10},{10,1... | collective-permute-start | bytes 36872 | tf_op jit(solution)/shard_map/ppermute | solution.py:205
  15.3 28.8 %collective-permute-start.2 = (f32[6,16,2,256]{3,2,1,0:T(2,128)S(1)}, f32[6,16,2,256]{3,2,1,0:T(2,128)}, u32[]{:S(2)}, u32[]{:S(2)}) collective-permute-start(f32[6,16,2,256]{3,2,1,0:T(2,128)S(1)} %slice.34), channel_id=1, source_target_pairs={{16,0},{17,1},{18,2},{19,3},{20,4},{21,5},{22,6},{23,7},{24,8},{25... | collective-permute-start | bytes 589832 | tf_op jit(solution)/shard_map/ppermute | solution.py:205
  17.4 26.8 %collective-permute-start.5 = (f32[6,16,2,256]{3,2,1,0:T(2,128)S(1)}, f32[6,16,2,256]{3,2,1,0:T(2,128)}, u32[]{:S(2)}, u32[]{:S(2)}) collective-permute-start(f32[6,16,2,256]{3,2,1,0:T(2,128)S(1)} %pad_maximum_fusion.1), channel_id=1, source_target_pairs={{0,16},{1,17},{2,18},{3,19},{4,20},{5,21},{6,22},{7,23},{8,24},{9,... | collective-permute-start | bytes 589832 | tf_op jit(solution)/shard_map/ppermute | solution.py:205
  20.7 6.9 %collective-permute-start.3 = (f32[6,16,2,2]{3,2,1,0:T(2,128)S(1)}, f32[6,16,2,2]{3,2,1,0:T(2,128)S(1)}, u32[]{:S(2)}, u32[]{:S(2)}) collective-permute-start(f32[6,16,2,2]{3,2,1,0:T(2,128)S(1)} %get-tuple-element.14), channel_id=1, source_target_pairs={{17,0},{18,1},{19,2},{20,3},{21,4},{22,5},{23,6},{24,7},{25,8},{26... | collective-permute-start | bytes 4616 | tf_op jit(solution)/shard_map/ppermute | solution.py:205
  27.6 14.3 %copy-start.3 = (f32[6,16,2,2]{3,2,1,0:T(2,128)}, f32[6,16,2,2]{3,2,1,0:T(2,128)S(1)}, u32[]{:S(2)}) copy-start(f32[6,16,2,2]{3,2,1,0:T(2,128)S(1)} %collective-permute-done.3) | copy-start | bytes 4612
  27.6 16.5 %collective-permute-start.4 = (f32[6,16,2,2]{3,2,1,0:T(2,128)}, f32[6,16,2,2]{3,2,1,0:T(2,128)}, u32[]{:S(2)}, u32[]{:S(2)}) collective-permute-start(f32[6,16,2,2]{3,2,1,0:T(2,128)} %get-tuple-element.17), channel_id=1, source_target_pairs={{16,1},{17,2},{18,3},{19,4},{20,5},{21,6},{22,7},{23,8},{24,9},{25... | collective-permute-start | bytes 4616 | tf_op jit(solution)/shard_map/ppermute | solution.py:205
  35.1 9.0 %collective-permute-start.6 = (f32[6,16,2,2]{3,2,1,0:T(2,128)}, f32[6,16,2,2]{3,2,1,0:T(2,128)}, u32[]{:S(2)}, u32[]{:S(2)}) collective-permute-start(f32[6,16,2,2]{3,2,1,0:T(2,128)} %get-tuple-element.16), channel_id=1, source_target_pairs={{1,16},{2,17},{3,18},{4,19},{5,20},{6,21},{7,22},{8,23},{9,24},{10... | collective-permute-start | bytes 4616 | tf_op jit(solution)/shard_map/ppermute | solution.py:205
  36.4 5.5 %copy-start.4 = (f32[6,16,16,2]{2,1,3,0:T(8,128)}, f32[6,16,16,2]{2,1,3,0:T(8,128)S(1)}, u32[]{:S(2)}) copy-start(f32[6,16,16,2]{2,1,3,0:T(8,128)S(1)} %collective-permute-done.1) | copy-start | bytes 36868
  36.4 7.7 %collective-permute-start.7 = (f32[6,16,2,2]{3,2,1,0:T(2,128)}, f32[6,16,2,2]{3,2,1,0:T(2,128)}, u32[]{:S(2)}, u32[]{:S(2)}) collective-permute-start(f32[6,16,2,2]{3,2,1,0:T(2,128)} %get-tuple-element.15), channel_id=1, source_target_pairs={{0,17},{1,18},{2,19},{3,20},{4,21},{5,22},{6,23},{7,24},{8,25},{9,... | collective-permute-start | bytes 4616 | tf_op jit(solution)/shard_map/ppermute | solution.py:205
  58.5 26.8 %collective-permute-start.8 = (f32[16,16,256]{2,1,0:T(8,128)S(1)}, f32[16,16,256]{2,1,0:T(8,128)S(1)}, u32[]{:S(2)}, u32[]{:S(2)}) collective-permute-start(f32[16,16,256]{2,1,0:T(8,128)S(1)} %broadcast_select_fusion), channel_id=1, source_target_pairs={{0,256},{256,0},{1,257},{257,1},{2,258},{258,2},{3,259},{259,3},{4... | collective-permute-start | bytes 786440 | tf_op jit(solution)/shard_map/ppermute | solution.py:292
  136.8 30.7 %collective-permute-start.9 = (f32[16,16,256]{2,1,0:T(8,128)}, f32[16,16,256]{2,1,0:T(8,128)S(1)}, u32[]{:S(2)}, u32[]{:S(2)}) collective-permute-start(f32[16,16,256]{2,1,0:T(8,128)} %bitcast.15), channel_id=1, source_target_pairs={{0,256},{256,0},{1,257},{257,1},{2,258},{258,2},{3,259},{259,3},{4... | collective-permute-start | bytes 786440 | tf_op jit(solution)/shard_map/ppermute | solution.py:307

commit v11 on v8

--- a/solution.py
+++ b/solution.py
@@ -244,7 +244,25 @@
     packed = jnp.concatenate([terminal, conductivity[None], velocity, keep[None]], axis=0)
     width = 2
     sizes = (-(-(rows_x + 2 * width) // 8) * 8, -(-(cols_y + 2 * width) // 128) * 128)
-    box = circular(packed, (("gx", 2), ("gy", 3)), width, sizes)
+    def rows(lo, hi):
+        cut = (Ellipsis, slice(lo, hi), slice(None))
+        edge_keep = 1.0 - fixed_mask[cut].astype(jnp.float32)
+        return jnp.concatenate(
+            [terminal[cut], conductivity[None][cut], velocity[cut], edge_keep[None]], axis=0
+        )
+
+    ends = lax.axis_size("gx") - 1
+    gap = jnp.zeros(packed.shape[:2] + (sizes[0] - rows_x - 2 * width, cols_y), packed.dtype)
+    stacked = jnp.concatenate(
+        [
+            packed,
+            lax.ppermute(rows(0, width), "gx", [(i + 1, i) for i in range(ends)]),
+            gap,
+            lax.ppermute(rows(rows_x - width, rows_x), "gx", [(i, i + 1) for i in range(ends)]),
+        ],
+        axis=2,
+    )
+    box = circular(stacked, (("gy", 3),), width, sizes[1:])
     offs = jnp.stack([lax.axis_index("gx") * rows_x, lax.axis_index("gy") * cols_y]).astype(jnp.int32)
     heat_sens, flow_x, flow_y = heat_phase(offs, wells, misfit, box, forward_temp)
     first = lax.axis_index("sec") == 0

time: 149 us -> 150 us (level)
  local copies, waits for them, and re-layouts: 5.79 us -> 8.46 us
    ppermute x0 -> x2, starting transfers between devices: none -> 10.7 us  [the longest x1 8.79 us: shards(): lax.ppermute(rows(0, width), 'gx', [(i + 1, i) for i in range(ends)])]
    ppermute x2 -> x1, starting transfers between devices: 10.1 us -> 1.28 us  [circular(): lax.ppermute(head, axis, [(i + 1, i) for i in range(ends)])]
    ppermute x2 -> x1, waiting for transfers between devices: 2.57 us -> 0.01 us  [circular(): lax.ppermute(tail, axis, [(i, i + 1) for i in range(ends)])]
    slice x0 -> x2, local copies, waits for them, and re-layouts: none -> 2.38 us  [the longest x1 1.29 us: rows(): terminal[cut]]
    ppermute x2 -> x1, starting transfers between devices: 6.57 us -> 4.65 us  [circular(): lax.ppermute(tail, axis, [(i, i + 1) for i in range(ends)])]
    ppermute x0 -> x2, waiting for transfers between devices: none -> 1.59 us  [the longest x1 1.59 us: shards(): lax.ppermute(rows(rows_x - width, rows_x), 'gx', [(i, i + 1) for i in ran...]
    slice x1 -> x0, other arithmetic: 1.51 us -> none  [circular(): head = lax.slice_in_dim(cells, 0, width, axis=dim)]
    concatenate x2 -> x1, other arithmetic: 3.79 us -> 3.32 us  [circular(): jnp.concatenate([cells, lax.ppermute(head, axis, [(i + 1, i) for i in ran...]
where the time goes in v11:
time: 150 us
  starting transfers between devices  50.2 us (33%)
  blocking collectives  34.9 us (23%)
  waiting for transfers between devices  33.9 us (23%)
  Pallas kernels  11.3 us (8%)
  other arithmetic  10.2 us (7%)
  local copies, waits for them, and re-layouts  8.46 us (6%)
    all_to_all x1, blocking collectives, shards(): gathered = lax.all_to_all(copies, 'gy', 0, 0, tiled=False)  34.9 us
    ppermute x1, starting transfers between devices, shards(): sensitivity = partial_sens + lax.ppermute(partial_sens, 'sec', partner)  22.4 us
    ppermute x1, waiting for transfers between devices, shards(): sensitivity = partial_sens + lax.ppermute(partial_sens, 'sec', partner)  19.6 us
    ppermute x1, waiting for transfers between devices, shards(): rounded = (mine + lax.ppermute(other, 'sec', partner)).astype(jnp.bfloat16)  12.7 us
    ppermute x1, starting transfers between devices, shards(): rounded = (mine + lax.ppermute(other, 'sec', partner)).astype(jnp.bfloat16)  11.1 us
    ppermute x1, starting transfers between devices, shards(): lax.ppermute(rows(0, width), 'gx', [(i + 1, i) for i in range(ends)])  8.79 us
    pallas_call x1, Pallas kernels, heat_phase(): pl.pallas_call(heat_kernel, out_shape=(out, out, out), in_specs=[smem, sm...  8.33 us
    ppermute x1, starting transfers between devices, circular(): lax.ppermute(tail, axis, [(i, i + 1) for i in range(ends)])  4.65 us
  transfers between devices with their start and end apart: 6, of which 3 were waited for; matrix products, arithmetic and copies ran while one was open for 2% of the time, Pallas kernels for 0%

profile of v11, /device:TPU:1, one launch (start us, length us, event | category | flops | bytes accessed | tf_op | source)
XLA Modules:
  0.0 149.7 jit_solution(12443488274283534194)
XLA Ops:
  0.7 1.1 fusion.3
  1.8 1.0 subtract_bitcast_fusion.2
  2.8 1.3 fusion.1
  4.2 8.8 %collective-permute-start = (f32[6,16,2,256]{3,2,1,0:T(2,128)S(1)}, f32[6,16,2,256]{3,2,1,0:T(2,128)S(1)}, u32[]{:S(2)}, u32[]{:S(2)}) collective-permute-start(f32[6,16,2,256]{3,2,1,0:T(2,128)S(1)} %pad_maximum_fusion.2), channel_id=1, source_target_pairs={{16,0},{32,16},{48,32},{64,48},{80,64},{96,80},{112,96},{128,112},... | collective-permute-start | bytes 589832 | tf_op jit(solution)/shard_map/ppermute | solution.py:259
  13.1 1.9 %collective-permute-start.1 = (f32[6,16,2,256]{3,2,1,0:T(2,128)S(1)}, f32[6,16,2,256]{3,2,1,0:T(2,128)S(1)}, u32[]{:S(2)}, u32[]{:S(2)}) collective-permute-start(f32[6,16,2,256]{3,2,1,0:T(2,128)S(1)} %pad_maximum_fusion.3), channel_id=1, source_target_pairs={{0,16},{16,32},{32,48},{48,64},{64,80},{80,96},{96,112},{112,128},... | collective-permute-start | bytes 589832 | tf_op jit(solution)/shard_map/ppermute | solution.py:261
  15.0 1.0 subtract_bitcast_fusion
  16.0 1.6 %collective-permute-done.1 = f32[6,16,2,256]{3,2,1,0:T(2,128)S(1)} collective-permute-done((f32[6,16,2,256]{3,2,1,0:T(2,128)S(1)}, f32[6,16,2,256]{3,2,1,0:T(2,128)S(1)}, u32[]{:S(2)}, u32[]{:S(2)}) %collective-permute-start.1) | collective-permute-done | bytes 196640 | tf_op jit(solution)/shard_map/ppermute | solution.py:261
  19.0 1.3 copy.13
  20.3 1.3 collective-permute-start.2
  22.2 4.6 %collective-permute-start.3 = (f32[6,16,24,2]{2,1,3,0:T(8,128)S(1)}, f32[6,16,24,2]{2,1,3,0:T(8,128)}, u32[]{:S(2)}, u32[]{:S(2)}) collective-permute-start(f32[6,16,24,2]{2,1,3,0:T(8,128)S(1)} %copy.14), channel_id=1, source_target_pairs={{0,1},{1,2},{2,3},{3,4},{4,5},{5,6},{6,7},{7,8},{8,9},{9,10},{10,1... | collective-permute-start | bytes 55304 | tf_op jit(solution)/shard_map/ppermute | solution.py:187
  26.9 0.6 pad_add_fusion.offs_ref
  27.5 0.7 copy.17.wells_ref
  28.9 1.5 %copy.16 = f32[6,16,24,2]{3,2,1,0:T(8,128)S(1)} copy(f32[6,16,24,2]{2,1,3,0:T(8,128)} %collective-permute-done.3) | data formatting | bytes 36864 | tf_op jit(solution)/shard_map/ppermute | solution.py:187
  30.4 3.3 %pad_maximum_fusion.box_ref = f32[6,16,24,384]{3,2,1,0:T(8,128)} fusion(f32[6,16,24,2]{3,2,1,0:T(8,128)S(1)} %copy.16, f32[6,16,24,2]{3,2,1,0:T(8,128)S(1)} %copy.15, f32[6,16,2,256]{3,2,1,0:T(2,128)} %copy-done.4, f32[6,16,4,256]{3,2,1,0:T(4,128)S(1)} %broadcast_in_dim.29, f32[6,16,2,256]{3,2,1,0:T(2,128)} %copy-done.3, ...), kind=kLoop, calls=%fused_computation | loop fusion | flops 7962624 | bytes 5936640 | tf_op jit(solution)/shard_map/concatenate | solution.py:182
  33.8 8.3 %shard_map.113 = (f32[16,16,256]{2,1,0:T(8,128)}, f32[16,16,256]{2,1,0:T(8,128)}, f32[16,16,256]{2,1,0:T(8,128)}) custom-call(s32[2]{0:T(128)} %pad_add_fusion.offs_ref, s32[2,8,3]{2,1,0:T(8,128)} %copy.17.wells_ref, f32[2,2,8]{2,1,0:T(2,128)} %misfit_ref.1, f32[6,16,24,384]{3,2,1,0:T(8,128)} %pad_maximum_fusion.box_ref, bf16[2,2,16,16,256]{4,3,2,1,0:T(8,128)(2,1)} %temp_ref.1), custom_call_target="tpu_custom_call" | custom-call | tf_op jit(solution)/shard_map/pallas_call | solution.py:162
  42.1 1.0 broadcast_select_fusion
  43.1 11.1 %collective-permute-start.4 = (f32[16,16,256]{2,1,0:T(8,128)S(1)}, f32[16,16,256]{2,1,0:T(8,128)S(1)}, u32[]{:S(2)}, u32[]{:S(2)}) collective-permute-start(f32[16,16,256]{2,1,0:T(8,128)S(1)} %broadcast_select_fusion), channel_id=1, source_target_pairs={{0,256},{256,0},{1,257},{257,1},{2,258},{258,2},{3,259},{259,3},{4... | collective-permute-start | bytes 786440 | tf_op jit(solution)/shard_map/ppermute | solution.py:272
  54.2 12.7 %collective-permute-done.4 = f32[16,16,256]{2,1,0:T(8,128)S(1)} collective-permute-done((f32[16,16,256]{2,1,0:T(8,128)S(1)}, f32[16,16,256]{2,1,0:T(8,128)S(1)}, u32[]{:S(2)}, u32[]{:S(2)}) %collective-permute-start.4) | collective-permute-done | bytes 262176 | tf_op jit(solution)/shard_map/ppermute | solution.py:272
  66.9 1.0 add_convert_fusion
  68.1 34.9 %all_to_all.5 = bf16[16,16,16,256]{3,2,1,0:T(8,128)(2,1)} all-to-all(bf16[16,16,16,256]{3,2,1,0:T(8,128)(2,1)S(1)} %broadcast_in_dim.32), channel_id=1, replica_groups=mesh['sec'=2,'gx'=16,'gy'=16] {'gy'}, dimensions={0} | all-to-all | bytes 4194304 | tf_op jit(solution)/shard_map/all_to_all | solution.py:276
  103.1 3.0 %shard_map.114 = (f32[256,256]{1,0:T(8,128)}, f32[256,256]{1,0:T(8,128)}) custom-call(s32[2,7]{1,0:T(2,128)} %cols_ref.1, bf16[16,256,256]{2,1,0:T(8,128)(2,1)} %bitcast.14, bf16[2,7,128,128]{3,2,1,0:T(8,128)(2,1)} %blocks_ref.1, f32[256,256]{1,0:T(8,128)} %bitcast.20, bf16[256,256]{1,0:T(8,128)(2,1)} %bitcast.21), custom_call_target="tpu_custom_call" | custom-call | flops 117440512 | bytes 3473408 | tf_op jit(solution)/shard_map/pallas_call | solution.py:214
  106.0 22.4 %collective-permute-start.5 = (f32[16,16,256]{2,1,0:T(8,128)}, f32[16,16,256]{2,1,0:T(8,128)S(1)}, u32[]{:S(2)}, u32[]{:S(2)}) collective-permute-start(f32[16,16,256]{2,1,0:T(8,128)} %bitcast.18), channel_id=1, source_target_pairs={{0,256},{256,0},{1,257},{257,1},{2,258},{258,2},{3,259},{259,3},{4... | collective-permute-start | bytes 786440 | tf_op jit(solution)/shard_map/ppermute | solution.py:287
  128.4 19.6 %collective-permute-done.5 = f32[16,16,256]{2,1,0:T(8,128)S(1)} collective-permute-done((f32[16,16,256]{2,1,0:T(8,128)}, f32[16,16,256]{2,1,0:T(8,128)S(1)}, u32[]{:S(2)}, u32[]{:S(2)}) %collective-permute-start.5) | collective-permute-done | bytes 262176 | tf_op jit(solution)/shard_map/ppermute | solution.py:287
  148.0 1.7 %add.7 = f32[16,16,256]{2,1,0:T(8,128)} add(f32[16,16,256]{2,1,0:T(8,128)} %bitcast.19, f32[16,16,256]{2,1,0:T(8,128)S(1)} %collective-permute-done.5) | non-fusion elementwise | flops 65536 | bytes 786432 | tf_op jit(solution)/shard_map/add | solution.py:287
  (25 shorter events, 3.2 us)
Async XLA Ops:
  0.6 17.6 %copy-start.2 = (f32[16,16,256]{2,1,0:T(8,128)S(1)}, f32[16,16,256]{2,1,0:T(8,128)}, u32[]{:S(2)}) copy-start(f32[16,16,256]{2,1,0:T(8,128)} %param.12) | copy-start | bytes 786436
  0.6 17.6 %copy-start = (f32[2,16,16,256]{3,2,1,0:T(8,128)S(1)}, f32[2,16,16,256]{3,2,1,0:T(8,128)}, u32[]{:S(2)}) copy-start(f32[2,16,16,256]{3,2,1,0:T(8,128)} %param.10) | copy-start | bytes 1572868
  0.7 17.6 %copy-start.1 = (f32[2,16,16,256]{3,2,1,0:T(8,128)S(1)}, f32[2,16,16,256]{3,2,1,0:T(8,128)}, u32[]{:S(2)}) copy-start(f32[2,16,16,256]{3,2,1,0:T(8,128)} %param.13) | copy-start | bytes 1572868
  4.2 11.8 %collective-permute-start = (f32[6,16,2,256]{3,2,1,0:T(2,128)S(1)}, f32[6,16,2,256]{3,2,1,0:T(2,128)S(1)}, u32[]{:S(2)}, u32[]{:S(2)}) collective-permute-start(f32[6,16,2,256]{3,2,1,0:T(2,128)S(1)} %pad_maximum_fusion.2), channel_id=1, source_target_pairs={{16,0},{32,16},{48,32},{64,48},{80,64},{96,80},{112,96},{128,112},... | collective-permute-start | bytes 589832 | tf_op jit(solution)/shard_map/ppermute | solution.py:259
  13.1 4.5 %collective-permute-start.1 = (f32[6,16,2,256]{3,2,1,0:T(2,128)S(1)}, f32[6,16,2,256]{3,2,1,0:T(2,128)S(1)}, u32[]{:S(2)}, u32[]{:S(2)}) collective-permute-start(f32[6,16,2,256]{3,2,1,0:T(2,128)S(1)} %pad_maximum_fusion.3), channel_id=1, source_target_pairs={{0,16},{16,32},{32,48},{48,64},{64,80},{80,96},{96,112},{112,128},... | collective-permute-start | bytes 589832 | tf_op jit(solution)/shard_map/ppermute | solution.py:261
  16.0 1.7 %copy-start.3 = (f32[6,16,2,256]{3,2,1,0:T(2,128)}, f32[6,16,2,256]{3,2,1,0:T(2,128)S(1)}, u32[]{:S(2)}) copy-start(f32[6,16,2,256]{3,2,1,0:T(2,128)S(1)} %collective-permute-done) | copy-start | bytes 589828
  17.6 0.7 copy-start.4
  19.0 8.5 %copy-start.5 = (s32[2,8,3]{1,0,2:T(2,128)S(1)}, s32[2,8,3]{1,0,2:T(2,128)}, u32[]{:S(2)}) copy-start(s32[2,8,3]{1,0,2:T(2,128)} %param.15) | copy-start | bytes 580
  20.3 8.0 %collective-permute-start.2 = (f32[6,16,24,2]{2,1,3,0:T(8,128)}, f32[6,16,24,2]{2,1,3,0:T(8,128)S(1)}, u32[]{:S(2)}, u32[]{:S(2)}) collective-permute-start(f32[6,16,24,2]{2,1,3,0:T(8,128)} %copy.13), channel_id=1, source_target_pairs={{1,0},{2,1},{3,2},{4,3},{5,4},{6,5},{7,6},{8,7},{9,8},{10,9},{11,1... | collective-permute-start | bytes 55304 | tf_op jit(solution)/shard_map/ppermute | solution.py:185
  22.2 6.7 %collective-permute-start.3 = (f32[6,16,24,2]{2,1,3,0:T(8,128)S(1)}, f32[6,16,24,2]{2,1,3,0:T(8,128)}, u32[]{:S(2)}, u32[]{:S(2)}) collective-permute-start(f32[6,16,24,2]{2,1,3,0:T(8,128)S(1)} %copy.14), channel_id=1, source_target_pairs={{0,1},{1,2},{2,3},{3,4},{4,5},{5,6},{6,7},{7,8},{8,9},{9,10},{10,1... | collective-permute-start | bytes 55304 | tf_op jit(solution)/shard_map/ppermute | solution.py:187
  43.1 23.8 %collective-permute-start.4 = (f32[16,16,256]{2,1,0:T(8,128)S(1)}, f32[16,16,256]{2,1,0:T(8,128)S(1)}, u32[]{:S(2)}, u32[]{:S(2)}) collective-permute-start(f32[16,16,256]{2,1,0:T(8,128)S(1)} %broadcast_select_fusion), channel_id=1, source_target_pairs={{0,256},{256,0},{1,257},{257,1},{2,258},{258,2},{3,259},{259,3},{4... | collective-permute-start | bytes 786440 | tf_op jit(solution)/shard_map/ppermute | solution.py:272
  106.0 42.0 %collective-permute-start.5 = (f32[16,16,256]{2,1,0:T(8,128)}, f32[16,16,256]{2,1,0:T(8,128)S(1)}, u32[]{:S(2)}, u32[]{:S(2)}) collective-permute-start(f32[16,16,256]{2,1,0:T(8,128)} %bitcast.18), channel_id=1, source_target_pairs={{0,256},{256,0},{1,257},{257,1},{2,258},{258,2},{3,259},{259,3},{4... | collective-permute-start | bytes 786440 | tf_op jit(solution)/shard_map/ppermute | solution.py:287

commit v12 on v8

--- a/solution.py
+++ b/solution.py
@@ -74,7 +74,20 @@
     return 2.0 * centre * other / jnp.where(centre + other > 0.0, centre + other, 1.0)
 
 
-def heat_kernel(offs_ref, wells_ref, misfit_ref, box_ref, temp_ref, heat_ref, fx_ref, fy_ref, adj_ref, w_ref):
+def heat_kernel(
+    offs_ref, wells_ref, misfit_ref, tile_ref, after_ref, before_ref, side_ref, temp_ref,
+    heat_ref, fx_ref, fy_ref, adj_ref, w_ref, box_ref,
+):
+    channels, layers, tile_x, tile_y = tile_ref.shape
+    width = after_ref.shape[2]
+    rows = box_ref.shape[2]
+    box_ref[:, :, 0:tile_x, 0:tile_y] = tile_ref[...]
+    box_ref[:, :, tile_x:tile_x + width, 0:tile_y] = after_ref[...]
+    box_ref[:, :, tile_x + width:rows - width, 0:tile_y] = jnp.zeros(
+        (channels, layers, rows - tile_x - 2 * width, tile_y), jnp.float32
+    )
+    box_ref[:, :, rows - width:rows, 0:tile_y] = before_ref[...]
+    box_ref[:, :, :, tile_y:] = side_ref[...]
     tests, layers, rows, cols = adj_ref.shape
     tile_x, tile_y = heat_ref.shape[1], heat_ref.shape[2]
     zero = jnp.zeros((rows, cols), jnp.float32)
@@ -152,23 +165,25 @@
     advance(adj_ref, 0, False)
 
 
-def heat_phase(offs, wells, misfit, box, temp):
-    channels, layers, rows, cols = box.shape
+def heat_phase(offs, wells, misfit, tile, after, before, side, temp, rows):
+    channels, layers = tile.shape[:2]
+    cols = tile.shape[3] + side.shape[3]
     tests = temp.shape[1]
-    tile = temp.shape[3:]
+    plane_shape = temp.shape[3:]
     smem = pl.BlockSpec(memory_space=pltpu.SMEM)
     vmem = pl.BlockSpec(memory_space=pltpu.VMEM)
-    out = jax.ShapeDtypeStruct((layers,) + tile, jnp.float32)
+    out = jax.ShapeDtypeStruct((layers,) + plane_shape, jnp.float32)
     return pl.pallas_call(
         heat_kernel,
         out_shape=(out, out, out),
-        in_specs=[smem, smem, smem, vmem, vmem],
+        in_specs=[smem, smem, smem, vmem, vmem, vmem, vmem, vmem],
         out_specs=(vmem, vmem, vmem),
         scratch_shapes=[
             pltpu.VMEM((tests, layers, rows, cols), jnp.float32),
             pltpu.VMEM((6, layers, rows, cols), jnp.float32),
+            pltpu.VMEM((channels, layers, rows, cols), jnp.float32),
         ],
-    )(offs, wells, misfit, box, temp)
+    )(offs, wells, misfit, tile, after, before, side, temp)
 
 
 def circular(cells, sides, width, sizes):
@@ -244,9 +259,27 @@
     packed = jnp.concatenate([terminal, conductivity[None], velocity, keep[None]], axis=0)
     width = 2
     sizes = (-(-(rows_x + 2 * width) // 8) * 8, -(-(cols_y + 2 * width) // 128) * 128)
-    box = circular(packed, (("gx", 2), ("gy", 3)), width, sizes)
+    ends_x = lax.axis_size("gx") - 1
+    ends_y = lax.axis_size("gy") - 1
+    after = lax.ppermute(packed[:, :, :width], "gx", [(i + 1, i) for i in range(ends_x)])
+    before = lax.ppermute(packed[:, :, rows_x - width:], "gx", [(i, i + 1) for i in range(ends_x)])
+
+    def column(cut):
+        gap = jnp.zeros(packed.shape[:2] + (sizes[0] - rows_x - 2 * width, width), packed.dtype)
+        return jnp.concatenate([packed[..., cut], after[..., cut], gap, before[..., cut]], axis=2)
+
+    side = jnp.concatenate(
+        [
+            lax.ppermute(column(slice(0, width)), "gy", [(i + 1, i) for i in range(ends_y)]),
+            jnp.zeros(packed.shape[:2] + (sizes[0], sizes[1] - cols_y - 2 * width), packed.dtype),
+            lax.ppermute(column(slice(cols_y - width, cols_y)), "gy", [(i, i + 1) for i in range(ends_y)]),
+        ],
+        axis=3,
+    )
     offs = jnp.stack([lax.axis_index("gx") * rows_x, lax.axis_index("gy") * cols_y]).astype(jnp.int32)
-    heat_sens, flow_x, flow_y = heat_phase(offs, wells, misfit, box, forward_temp)
+    heat_sens, flow_x, flow_y = heat_phase(
+        offs, wells, misfit, packed, after, before, side, forward_temp, sizes[0]
+    )
     first = lax.axis_index("sec") == 0
     mine = jnp.where(first, flow_x, flow_y)
     other = jnp.where(first, flow_y, flow_x)

time: 149 us -> 140 us (0.940)
  the two profiles are of different devices: /device:TPU:1 before, /device:TPU:32 now
where the time goes in v12:
time: 140 us; the launch traced here: 139 us
  waiting for transfers between devices  48.8 us (35%)
  starting transfers between devices  34.4 us (25%)
  blocking collectives  27.4 us (20%)
  Pallas kernels  11.6 us (8%)
  other arithmetic  8.31 us (6%)
  local copies, waits for them, and re-layouts  7.97 us (6%)
    all_to_all x1, blocking collectives, shards(): gathered = lax.all_to_all(copies, 'gy', 0, 0, tiled=False)  27.4 us
    ppermute x1, waiting for transfers between devices, shards(): sensitivity = partial_sens + lax.ppermute(partial_sens, 'sec', partner)  21.5 us
    ppermute x1, waiting for transfers between devices, shards(): rounded = (mine + lax.ppermute(other, 'sec', partner)).astype(jnp.bfloat16)  21 us
    ppermute x1, starting transfers between devices, shards(): sensitivity = partial_sens + lax.ppermute(partial_sens, 'sec', partner)  12.9 us
    ppermute x1, starting transfers between devices, shards(): rounded = (mine + lax.ppermute(other, 'sec', partner)).astype(jnp.bfloat16)  11.4 us
    pallas_call x1, Pallas kernels, heat_phase(): pl.pallas_call(heat_kernel, out_shape=(out, out, out), in_specs=[smem, sm...  8.63 us
    ppermute x1, waiting for transfers between devices, shards(): lax.ppermute(packed[:, :, rows_x - width:], 'gx', [(i, i + 1) for i in ra...  6.13 us
    ppermute x1, starting transfers between devices, shards(): lax.ppermute(column(slice(cols_y - width, cols_y)), 'gy', [(i, i + 1) for...  4.55 us
  transfers between devices with their start and end apart: 6, of which 4 were waited for; matrix products, arithmetic and copies ran while one was open for 3% of the time, Pallas kernels for 0%

profile of v12, /device:TPU:32, one launch (start us, length us, event | category | flops | bytes accessed | tf_op | source)
XLA Modules:
  0.0 139.3 jit_solution(1584303444986556768)
XLA Ops:
  0.6 1.0 subtract_bitcast_fusion
  1.6 1.4 %pad_maximum_fusion.tile_ref = f32[6,16,16,256]{3,2,1,0:T(8,128)S(1)} fusion(f32[1,16,16,256]{3,2,1,0:T(8,128)S(1)} %subtract_bitcast_fusion, f32[2,16,16,256]{3,2,1,0:T(8,128)} %param.13, f32[1,16,16,256]{3,2,1,0:T(8,128)} %bitcast.11, f32[2,16,16,256]{3,2,1,0:T(8,128)} %param.10), kind=kLoop, calls=%fused_computation | loop fusion | flops 1179648 | bytes 3145728 | tf_op jit(solution)/shard_map/concatenate | solution.py:259
  3.0 1.0 fusion.1
  4.1 1.9 %collective-permute-start = (f32[6,16,2,256]{3,2,1,0:T(2,128)}, f32[6,16,2,256]{3,2,1,0:T(2,128)S(1)}, u32[]{:S(2)}, u32[]{:S(2)}) collective-permute-start(f32[6,16,2,256]{3,2,1,0:T(2,128)} %get-tuple-element.15), channel_id=1, source_target_pairs={{16,0},{32,16},{48,32},{64,48},{80,64},{96,80},{112,96},{128,112},... | collective-permute-start | bytes 589832 | tf_op jit(solution)/shard_map/ppermute | solution.py:264
  6.0 2.4 %collective-permute-start.1 = (f32[6,16,2,256]{3,2,1,0:T(2,128)}, f32[6,16,2,256]{3,2,1,0:T(2,128)S(1)}, u32[]{:S(2)}, u32[]{:S(2)}) collective-permute-start(f32[6,16,2,256]{3,2,1,0:T(2,128)} %get-tuple-element.14), channel_id=1, source_target_pairs={{0,16},{16,32},{32,48},{48,64},{64,80},{80,96},{96,112},{112,128},... | collective-permute-start | bytes 589832 | tf_op jit(solution)/shard_map/ppermute | solution.py:265
  10.2 0.7 copy.14
  10.9 6.1 %collective-permute-done.1.before_ref = f32[6,16,2,256]{3,2,1,0:T(2,128)S(1)} collective-permute-done((f32[6,16,2,256]{3,2,1,0:T(2,128)}, f32[6,16,2,256]{3,2,1,0:T(2,128)S(1)}, u32[]{:S(2)}, u32[]{:S(2)}) %collective-permute-start.1) | collective-permute-done | bytes 196640 | tf_op jit(solution)/shard_map/ppermute | solution.py:265
  17.2 0.7 copy.15
  17.9 0.7 copy.17
  18.6 0.7 copy.18
  19.4 1.3 collective-permute-start.2
  20.7 4.6 %collective-permute-start.3 = (f32[6,16,24,2]{2,1,3,0:T(8,128)S(1)}, f32[6,16,24,2]{2,1,3,0:T(8,128)S(1)}, u32[]{:S(2)}, u32[]{:S(2)}) collective-permute-start(f32[6,16,24,2]{2,1,3,0:T(8,128)S(1)} %get-tuple-element.21), channel_id=1, source_target_pairs={{0,1},{1,2},{2,3},{3,4},{4,5},{5,6},{6,7},{7,8},{8,9},{9,10},{10,1... | collective-permute-start | bytes 55304 | tf_op jit(solution)/shard_map/ppermute | solution.py:275
  26.0 0.7 copy.21.wells_ref
  28.1 1.4 %pad_maximum_fusion.1.side_ref = f32[6,16,24,128]{3,2,1,0:T(8,128)} fusion(f32[6,16,24,2]{3,2,1,0:T(8,128)S(1)} %copy.20, f32[6,16,24,2]{3,2,1,0:T(8,128)S(1)} %copy.19, f32[128]{0:T(128)S(1)} %pad.1.clone), kind=kLoop, calls=%fused_computation.1 | loop fusion | flops 589824 | bytes 1217024 | tf_op jit(solution)/shard_map/concatenate | solution.py:271
  29.5 8.6 %shard_map.113 = (f32[16,16,256]{2,1,0:T(8,128)}, f32[16,16,256]{2,1,0:T(8,128)}, f32[16,16,256]{2,1,0:T(8,128)}) custom-call(s32[2]{0:T(128)} %pad_add_fusion.offs_ref, s32[2,8,3]{2,1,0:T(8,128)} %copy.21.wells_ref, f32[2,2,8]{2,1,0:T(2,128)} %misfit_ref.1, f32[6,16,16,256]{3,2,1,0:T(8,128)} %copy-done, f32[6,16,2,256]{3,2,1,0:T(2,128)} %copy-done.1, ...), custom_call_target="tpu_custom_call" | custom-call | tf_op jit(solution)/shard_map/pallas_call | solution.py:176
  38.1 1.0 broadcast_select_fusion
  39.1 11.4 %collective-permute-start.4 = (f32[16,16,256]{2,1,0:T(8,128)S(1)}, f32[16,16,256]{2,1,0:T(8,128)S(1)}, u32[]{:S(2)}, u32[]{:S(2)}) collective-permute-start(f32[16,16,256]{2,1,0:T(8,128)S(1)} %broadcast_select_fusion), channel_id=1, source_target_pairs={{0,256},{256,0},{1,257},{257,1},{2,258},{258,2},{3,259},{259,3},{4... | collective-permute-start | bytes 786440 | tf_op jit(solution)/shard_map/ppermute | solution.py:287
  50.6 21.0 %collective-permute-done.4 = f32[16,16,256]{2,1,0:T(8,128)S(1)} collective-permute-done((f32[16,16,256]{2,1,0:T(8,128)S(1)}, f32[16,16,256]{2,1,0:T(8,128)S(1)}, u32[]{:S(2)}, u32[]{:S(2)}) %collective-permute-start.4) | collective-permute-done | bytes 262176 | tf_op jit(solution)/shard_map/ppermute | solution.py:287
  71.6 1.0 add_convert_fusion
  72.8 27.4 %all_to_all.5 = bf16[16,16,16,256]{3,2,1,0:T(8,128)(2,1)} all-to-all(bf16[16,16,16,256]{3,2,1,0:T(8,128)(2,1)S(1)} %broadcast_in_dim.18), channel_id=1, replica_groups=mesh['sec'=2,'gx'=16,'gy'=16] {'gy'}, dimensions={0} | all-to-all | bytes 4194304 | tf_op jit(solution)/shard_map/all_to_all | solution.py:291
  100.2 3.0 %shard_map.114 = (f32[256,256]{1,0:T(8,128)}, f32[256,256]{1,0:T(8,128)}) custom-call(s32[2,7]{1,0:T(2,128)} %cols_ref.1, bf16[16,256,256]{2,1,0:T(8,128)(2,1)} %bitcast.10, bf16[2,7,128,128]{3,2,1,0:T(8,128)(2,1)} %blocks_ref.1, f32[256,256]{1,0:T(8,128)} %bitcast.14, bf16[256,256]{1,0:T(8,128)(2,1)} %bitcast.15), custom_call_target="tpu_custom_call" | custom-call | flops 117440512 | bytes 3473408 | tf_op jit(solution)/shard_map/pallas_call | solution.py:229
  103.2 12.9 %collective-permute-start.5 = (f32[16,16,256]{2,1,0:T(8,128)}, f32[16,16,256]{2,1,0:T(8,128)S(1)}, u32[]{:S(2)}, u32[]{:S(2)}) collective-permute-start(f32[16,16,256]{2,1,0:T(8,128)} %bitcast.12), channel_id=1, source_target_pairs={{0,256},{256,0},{1,257},{257,1},{2,258},{258,2},{3,259},{259,3},{4... | collective-permute-start | bytes 786440 | tf_op jit(solution)/shard_map/ppermute | solution.py:302
  116.1 21.5 %collective-permute-done.5 = f32[16,16,256]{2,1,0:T(8,128)S(1)} collective-permute-done((f32[16,16,256]{2,1,0:T(8,128)}, f32[16,16,256]{2,1,0:T(8,128)S(1)}, u32[]{:S(2)}, u32[]{:S(2)}) %collective-permute-start.5) | collective-permute-done | bytes 262176 | tf_op jit(solution)/shard_map/ppermute | solution.py:302
  137.6 1.7 %add.7 = f32[16,16,256]{2,1,0:T(8,128)} add(f32[16,16,256]{2,1,0:T(8,128)} %bitcast.13, f32[16,16,256]{2,1,0:T(8,128)S(1)} %collective-permute-done.5) | non-fusion elementwise | flops 65536 | bytes 786432 | tf_op jit(solution)/shard_map/add | solution.py:302
  (25 shorter events, 4.5 us)
Async XLA Ops:
  3.0 5.7 %copy-start = (f32[6,16,16,256]{3,2,1,0:T(8,128)}, f32[6,16,16,256]{3,2,1,0:T(8,128)S(1)}, u32[]{:S(2)}) copy-start(f32[6,16,16,256]{3,2,1,0:T(8,128)S(1)} %pad_maximum_fusion.tile_ref) | copy-start | bytes 4718596
  4.1 6.0 %collective-permute-start = (f32[6,16,2,256]{3,2,1,0:T(2,128)}, f32[6,16,2,256]{3,2,1,0:T(2,128)S(1)}, u32[]{:S(2)}, u32[]{:S(2)}) collective-permute-start(f32[6,16,2,256]{3,2,1,0:T(2,128)} %get-tuple-element.15), channel_id=1, source_target_pairs={{16,0},{32,16},{48,32},{64,48},{80,64},{96,80},{112,96},{128,112},... | collective-permute-start | bytes 589832 | tf_op jit(solution)/shard_map/ppermute | solution.py:264
  6.0 11.1 %collective-permute-start.1 = (f32[6,16,2,256]{3,2,1,0:T(2,128)}, f32[6,16,2,256]{3,2,1,0:T(2,128)S(1)}, u32[]{:S(2)}, u32[]{:S(2)}) collective-permute-start(f32[6,16,2,256]{3,2,1,0:T(2,128)} %get-tuple-element.14), channel_id=1, source_target_pairs={{0,16},{16,32},{32,48},{48,64},{64,80},{80,96},{96,112},{112,128},... | collective-permute-start | bytes 589832 | tf_op jit(solution)/shard_map/ppermute | solution.py:265
  9.3 16.7 %copy-start.3 = (s32[2,8,3]{1,0,2:T(2,128)S(1)}, s32[2,8,3]{1,0,2:T(2,128)}, u32[]{:S(2)}) copy-start(s32[2,8,3]{1,0,2:T(2,128)} %param.15) | copy-start | bytes 580
  10.1 17.3 %copy-start.1 = (f32[6,16,2,256]{3,2,1,0:T(2,128)}, f32[6,16,2,256]{3,2,1,0:T(2,128)S(1)}, u32[]{:S(2)}) copy-start(f32[6,16,2,256]{3,2,1,0:T(2,128)S(1)} %collective-permute-done.after_ref) | copy-start | bytes 589828
  17.0 11.1 %copy-start.2 = (f32[6,16,2,256]{3,2,1,0:T(2,128)}, f32[6,16,2,256]{3,2,1,0:T(2,128)S(1)}, u32[]{:S(2)}) copy-start(f32[6,16,2,256]{3,2,1,0:T(2,128)S(1)} %collective-permute-done.1.before_ref) | copy-start | bytes 589828
  19.4 7.3 %collective-permute-start.2 = (f32[6,16,24,2]{2,1,3,0:T(8,128)S(1)}, f32[6,16,24,2]{2,1,3,0:T(8,128)S(1)}, u32[]{:S(2)}, u32[]{:S(2)}) collective-permute-start(f32[6,16,24,2]{2,1,3,0:T(8,128)S(1)} %get-tuple-element.20), channel_id=1, source_target_pairs={{1,0},{2,1},{3,2},{4,3},{5,4},{6,5},{7,6},{8,7},{9,8},{10,9},{11,1... | collective-permute-start | bytes 55304 | tf_op jit(solution)/shard_map/ppermute | solution.py:273
  20.7 6.8 %collective-permute-start.3 = (f32[6,16,24,2]{2,1,3,0:T(8,128)S(1)}, f32[6,16,24,2]{2,1,3,0:T(8,128)S(1)}, u32[]{:S(2)}, u32[]{:S(2)}) collective-permute-start(f32[6,16,24,2]{2,1,3,0:T(8,128)S(1)} %get-tuple-element.21), channel_id=1, source_target_pairs={{0,1},{1,2},{2,3},{3,4},{4,5},{5,6},{6,7},{7,8},{8,9},{9,10},{10,1... | collective-permute-start | bytes 55304 | tf_op jit(solution)/shard_map/ppermute | solution.py:275
  39.1 32.5 %collective-permute-start.4 = (f32[16,16,256]{2,1,0:T(8,128)S(1)}, f32[16,16,256]{2,1,0:T(8,128)S(1)}, u32[]{:S(2)}, u32[]{:S(2)}) collective-permute-start(f32[16,16,256]{2,1,0:T(8,128)S(1)} %broadcast_select_fusion), channel_id=1, source_target_pairs={{0,256},{256,0},{1,257},{257,1},{2,258},{258,2},{3,259},{259,3},{4... | collective-permute-start | bytes 786440 | tf_op jit(solution)/shard_map/ppermute | solution.py:287
  103.2 34.4 %collective-permute-start.5 = (f32[16,16,256]{2,1,0:T(8,128)}, f32[16,16,256]{2,1,0:T(8,128)S(1)}, u32[]{:S(2)}, u32[]{:S(2)}) collective-permute-start(f32[16,16,256]{2,1,0:T(8,128)} %bitcast.12), channel_id=1, source_target_pairs={{0,256},{256,0},{1,257},{257,1},{2,258},{258,2},{3,259},{259,3},{4... | collective-permute-start | bytes 786440 | tf_op jit(solution)/shard_map/ppermute | solution.py:302

commit v13 on v12

--- a/solution.py
+++ b/solution.py
@@ -75,18 +75,11 @@
 
 
 def heat_kernel(
-    offs_ref, wells_ref, misfit_ref, tile_ref, after_ref, before_ref, side_ref, temp_ref,
+    offs_ref, wells_ref, misfit_ref, ext_ref, side_ref, temp_ref,
     heat_ref, fx_ref, fy_ref, adj_ref, w_ref, box_ref,
 ):
-    channels, layers, tile_x, tile_y = tile_ref.shape
-    width = after_ref.shape[2]
-    rows = box_ref.shape[2]
-    box_ref[:, :, 0:tile_x, 0:tile_y] = tile_ref[...]
-    box_ref[:, :, tile_x:tile_x + width, 0:tile_y] = after_ref[...]
-    box_ref[:, :, tile_x + width:rows - width, 0:tile_y] = jnp.zeros(
-        (channels, layers, rows - tile_x - 2 * width, tile_y), jnp.float32
-    )
-    box_ref[:, :, rows - width:rows, 0:tile_y] = before_ref[...]
+    tile_y = ext_ref.shape[3]
+    box_ref[:, :, :, 0:tile_y] = ext_ref[...]
     box_ref[:, :, :, tile_y:] = side_ref[...]
     tests, layers, rows, cols = adj_ref.shape
     tile_x, tile_y = heat_ref.shape[1], heat_ref.shape[2]
@@ -165,9 +158,9 @@
     advance(adj_ref, 0, False)
 
 
-def heat_phase(offs, wells, misfit, tile, after, before, side, temp, rows):
-    channels, layers = tile.shape[:2]
-    cols = tile.shape[3] + side.shape[3]
+def heat_phase(offs, wells, misfit, ext, side, temp):
+    channels, layers, rows = ext.shape[:3]
+    cols = ext.shape[3] + side.shape[3]
     tests = temp.shape[1]
     plane_shape = temp.shape[3:]
     smem = pl.BlockSpec(memory_space=pltpu.SMEM)
@@ -176,14 +169,14 @@
     return pl.pallas_call(
         heat_kernel,
         out_shape=(out, out, out),
-        in_specs=[smem, smem, smem, vmem, vmem, vmem, vmem, vmem],
+        in_specs=[smem, smem, smem, vmem, vmem, vmem],
         out_specs=(vmem, vmem, vmem),
         scratch_shapes=[
             pltpu.VMEM((tests, layers, rows, cols), jnp.float32),
             pltpu.VMEM((6, layers, rows, cols), jnp.float32),
             pltpu.VMEM((channels, layers, rows, cols), jnp.float32),
         ],
-    )(offs, wells, misfit, tile, after, before, side, temp)
+    )(offs, wells, misfit, ext, side, temp)
 
 
 def circular(cells, sides, width, sizes):
@@ -264,22 +257,18 @@
     after = lax.ppermute(packed[:, :, :width], "gx", [(i + 1, i) for i in range(ends_x)])
     before = lax.ppermute(packed[:, :, rows_x - width:], "gx", [(i, i + 1) for i in range(ends_x)])
 
-    def column(cut):
-        gap = jnp.zeros(packed.shape[:2] + (sizes[0] - rows_x - 2 * width, width), packed.dtype)
-        return jnp.concatenate([packed[..., cut], after[..., cut], gap, before[..., cut]], axis=2)
-
+    gap = jnp.zeros(packed.shape[:2] + (sizes[0] - rows_x - 2 * width, cols_y), packed.dtype)
+    ext = jnp.concatenate([packed, after, gap, before], axis=2)
     side = jnp.concatenate(
         [
-            lax.ppermute(column(slice(0, width)), "gy", [(i + 1, i) for i in range(ends_y)]),
+            lax.ppermute(ext[..., :width], "gy", [(i + 1, i) for i in range(ends_y)]),
             jnp.zeros(packed.shape[:2] + (sizes[0], sizes[1] - cols_y - 2 * width), packed.dtype),
-            lax.ppermute(column(slice(cols_y - width, cols_y)), "gy", [(i, i + 1) for i in range(ends_y)]),
+            lax.ppermute(ext[..., cols_y - width:], "gy", [(i, i + 1) for i in range(ends_y)]),
         ],
         axis=3,
     )
     offs = jnp.stack([lax.axis_index("gx") * rows_x, lax.axis_index("gy") * cols_y]).astype(jnp.int32)
-    heat_sens, flow_x, flow_y = heat_phase(
-        offs, wells, misfit, packed, after, before, side, forward_temp, sizes[0]
-    )
+    heat_sens, flow_x, flow_y = heat_phase(offs, wells, misfit, ext, side, forward_temp)
     first = lax.axis_index("sec") == 0
     mine = jnp.where(first, flow_x, flow_y)
     other = jnp.where(first, flow_y, flow_x)

time: 140 us -> 146 us (1.043)
  the two profiles are of different devices: /device:TPU:32 before, /device:TPU:1 now
where the time goes in v13:
time: 146 us
  starting transfers between devices  49.3 us (34%)
  waiting for transfers between devices  35.4 us (24%)
  blocking collectives  35.1 us (24%)
  Pallas kernels  11.5 us (8%)
  other arithmetic  8.63 us (6%)
  local copies, waits for them, and re-layouts  4.99 us (3%)
    all_to_all x1, blocking collectives, shards(): gathered = lax.all_to_all(copies, 'gy', 0, 0, tiled=False)  35.1 us
    ppermute x1, starting transfers between devices, shards(): sensitivity = partial_sens + lax.ppermute(partial_sens, 'sec', partner)  22.4 us
    ppermute x1, waiting for transfers between devices, shards(): sensitivity = partial_sens + lax.ppermute(partial_sens, 'sec', partner)  19.6 us
    ppermute x1, waiting for transfers between devices, shards(): rounded = (mine + lax.ppermute(other, 'sec', partner)).astype(jnp.bfloat16)  13 us
    ppermute x1, starting transfers between devices, shards(): rounded = (mine + lax.ppermute(other, 'sec', partner)).astype(jnp.bfloat16)  10.9 us
    ppermute x1, starting transfers between devices, shards(): lax.ppermute(packed[:, :, :width], 'gx', [(i + 1, i) for i in range(ends_...  8.79 us
    pallas_call x1, Pallas kernels, heat_phase(): pl.pallas_call(heat_kernel, out_shape=(out, out, out), in_specs=[smem, sm...  8.56 us
    ppermute x1, starting transfers between devices, shards(): lax.ppermute(ext[..., cols_y - width:], 'gy', [(i, i + 1) for i in range(...  4 us
  transfers between devices with their start and end apart: 6, of which 4 were waited for; matrix products, arithmetic and copies ran while one was open for 2% of the time, Pallas kernels for 0%

profile of v13, /device:TPU:1, one launch (start us, length us, event | category | flops | bytes accessed | tf_op | source)
XLA Modules:
  0.0 145.7 jit_solution(17844312337481189853)
XLA Ops:
  0.7 1.1 subtract_bitcast_fusion
  1.7 1.4 pad_maximum_fusion.5
  3.2 8.8 %collective-permute-start = (f32[6,16,2,256]{3,2,1,0:T(2,128)S(1)}, f32[6,16,2,256]{3,2,1,0:T(2,128)S(1)}, u32[]{:S(2)}, u32[]{:S(2)}) collective-permute-start(f32[6,16,2,256]{3,2,1,0:T(2,128)S(1)} %get-tuple-element.14), channel_id=1, source_target_pairs={{16,0},{32,16},{48,32},{64,48},{80,64},{96,80},{112,96},{128,112},... | collective-permute-start | bytes 589832 | tf_op jit(solution)/shard_map/ppermute | solution.py:257
  12.0 1.9 %collective-permute-start.1 = (f32[6,16,2,256]{3,2,1,0:T(2,128)S(1)}, f32[6,16,2,256]{3,2,1,0:T(2,128)S(1)}, u32[]{:S(2)}, u32[]{:S(2)}) collective-permute-start(f32[6,16,2,256]{3,2,1,0:T(2,128)S(1)} %get-tuple-element.15), channel_id=1, source_target_pairs={{0,16},{16,32},{32,48},{48,64},{64,80},{80,96},{96,112},{112,128},... | collective-permute-start | bytes 589832 | tf_op jit(solution)/shard_map/ppermute | solution.py:258
  14.0 2.5 %collective-permute-done.1 = f32[6,16,2,256]{3,2,1,0:T(2,128)S(1)} collective-permute-done((f32[6,16,2,256]{3,2,1,0:T(2,128)S(1)}, f32[6,16,2,256]{3,2,1,0:T(2,128)S(1)}, u32[]{:S(2)}, u32[]{:S(2)}) %collective-permute-start.1) | collective-permute-done | bytes 196640 | tf_op jit(solution)/shard_map/ppermute | solution.py:258
  17.3 1.0 copy-done
  18.9 1.3 collective-permute-start.2
  20.2 0.6 copy.14
  20.9 4.0 %collective-permute-start.3 = (f32[6,16,24,2]{2,1,3,0:T(8,128)S(1)}, f32[6,16,24,2]{2,1,3,0:T(8,128)S(1)}, u32[]{:S(2)}, u32[]{:S(2)}) collective-permute-start(f32[6,16,24,2]{2,1,3,0:T(8,128)S(1)} %copy.14), channel_id=1, source_target_pairs={{0,1},{1,2},{2,3},{3,4},{4,5},{5,6},{6,7},{7,8},{8,9},{9,10},{10,1... | collective-permute-start | bytes 55304 | tf_op jit(solution)/shard_map/ppermute | solution.py:266
  24.9 0.7 pad_add_fusion.offs_ref
  25.6 0.7 copy.17.wells_ref
  26.3 0.6 copy.15
  27.2 0.6 copy.16
  27.8 1.4 pad_maximum_fusion.1.side_ref
  29.2 8.6 %shard_map.113 = (f32[16,16,256]{2,1,0:T(8,128)}, f32[16,16,256]{2,1,0:T(8,128)}, f32[16,16,256]{2,1,0:T(8,128)}) custom-call(s32[2]{0:T(128)} %pad_add_fusion.offs_ref, s32[2,8,3]{2,1,0:T(8,128)} %copy.17.wells_ref, f32[2,2,8]{2,1,0:T(2,128)} %misfit_ref.1, f32[6,16,24,256]{3,2,1,0:T(8,128)} %copy-done, f32[6,16,24,128]{3,2,1,0:T(8,128)} %pad_maximum_fusion.1.side_ref, ...), custom_call_target="tpu_custom_call" | custom-call | tf_op jit(solution)/shard_map/pallas_call | solution.py:169
  37.8 1.0 broadcast_select_fusion
  38.8 10.9 %collective-permute-start.4 = (f32[16,16,256]{2,1,0:T(8,128)S(1)}, f32[16,16,256]{2,1,0:T(8,128)S(1)}, u32[]{:S(2)}, u32[]{:S(2)}) collective-permute-start(f32[16,16,256]{2,1,0:T(8,128)S(1)} %broadcast_select_fusion), channel_id=1, source_target_pairs={{0,256},{256,0},{1,257},{257,1},{2,258},{258,2},{3,259},{259,3},{4... | collective-permute-start | bytes 786440 | tf_op jit(solution)/shard_map/ppermute | solution.py:276
  49.7 13.0 %collective-permute-done.4 = f32[16,16,256]{2,1,0:T(8,128)S(1)} collective-permute-done((f32[16,16,256]{2,1,0:T(8,128)S(1)}, f32[16,16,256]{2,1,0:T(8,128)S(1)}, u32[]{:S(2)}, u32[]{:S(2)}) %collective-permute-start.4) | collective-permute-done | bytes 262176 | tf_op jit(solution)/shard_map/ppermute | solution.py:276
  62.7 1.0 add_convert_fusion
  63.9 35.1 %all_to_all.5 = bf16[16,16,16,256]{3,2,1,0:T(8,128)(2,1)} all-to-all(bf16[16,16,16,256]{3,2,1,0:T(8,128)(2,1)S(1)} %broadcast_in_dim.22), channel_id=1, replica_groups=mesh['sec'=2,'gx'=16,'gy'=16] {'gy'}, dimensions={0} | all-to-all | bytes 4194304 | tf_op jit(solution)/shard_map/all_to_all | solution.py:280
  99.0 3.0 %shard_map.114 = (f32[256,256]{1,0:T(8,128)}, f32[256,256]{1,0:T(8,128)}) custom-call(s32[2,7]{1,0:T(2,128)} %cols_ref.1, bf16[16,256,256]{2,1,0:T(8,128)(2,1)} %bitcast.10, bf16[2,7,128,128]{3,2,1,0:T(8,128)(2,1)} %blocks_ref.1, f32[256,256]{1,0:T(8,128)} %bitcast.15, bf16[256,256]{1,0:T(8,128)(2,1)} %bitcast.16), custom_call_target="tpu_custom_call" | custom-call | flops 117440512 | bytes 3473408 | tf_op jit(solution)/shard_map/pallas_call | solution.py:222
  102.0 22.4 %collective-permute-start.5 = (f32[16,16,256]{2,1,0:T(8,128)}, f32[16,16,256]{2,1,0:T(8,128)S(1)}, u32[]{:S(2)}, u32[]{:S(2)}) collective-permute-start(f32[16,16,256]{2,1,0:T(8,128)} %bitcast.13), channel_id=1, source_target_pairs={{0,256},{256,0},{1,257},{257,1},{2,258},{258,2},{3,259},{259,3},{4... | collective-permute-start | bytes 786440 | tf_op jit(solution)/shard_map/ppermute | solution.py:291
  124.4 19.6 %collective-permute-done.5 = f32[16,16,256]{2,1,0:T(8,128)S(1)} collective-permute-done((f32[16,16,256]{2,1,0:T(8,128)}, f32[16,16,256]{2,1,0:T(8,128)S(1)}, u32[]{:S(2)}, u32[]{:S(2)}) %collective-permute-start.5) | collective-permute-done | bytes 262176 | tf_op jit(solution)/shard_map/ppermute | solution.py:291
  144.1 1.7 %add.7 = f32[16,16,256]{2,1,0:T(8,128)} add(f32[16,16,256]{2,1,0:T(8,128)} %bitcast.14, f32[16,16,256]{2,1,0:T(8,128)S(1)} %collective-permute-done.5) | non-fusion elementwise | flops 65536 | bytes 786432 | tf_op jit(solution)/shard_map/add | solution.py:291
  (20 shorter events, 2.0 us)
Async XLA Ops:
  0.6 15.9 %copy-start.3 = (f32[16,16,256]{2,1,0:T(8,128)S(1)}, f32[16,16,256]{2,1,0:T(8,128)}, u32[]{:S(2)}) copy-start(f32[16,16,256]{2,1,0:T(8,128)} %param.12) | copy-start | bytes 786436
  0.6 15.8 %copy-start.2 = (f32[2,16,16,256]{3,2,1,0:T(8,128)S(1)}, f32[2,16,16,256]{3,2,1,0:T(8,128)}, u32[]{:S(2)}) copy-start(f32[2,16,16,256]{3,2,1,0:T(8,128)} %param.10) | copy-start | bytes 1572868
  0.7 15.8 %copy-start.1 = (f32[2,16,16,256]{3,2,1,0:T(8,128)S(1)}, f32[2,16,16,256]{3,2,1,0:T(8,128)}, u32[]{:S(2)}) copy-start(f32[2,16,16,256]{3,2,1,0:T(8,128)} %param.13) | copy-start | bytes 1572868
  3.2 10.8 %collective-permute-start = (f32[6,16,2,256]{3,2,1,0:T(2,128)S(1)}, f32[6,16,2,256]{3,2,1,0:T(2,128)S(1)}, u32[]{:S(2)}, u32[]{:S(2)}) collective-permute-start(f32[6,16,2,256]{3,2,1,0:T(2,128)S(1)} %get-tuple-element.14), channel_id=1, source_target_pairs={{16,0},{32,16},{48,32},{64,48},{80,64},{96,80},{112,96},{128,112},... | collective-permute-start | bytes 589832 | tf_op jit(solution)/shard_map/ppermute | solution.py:257
  12.0 4.5 %collective-permute-start.1 = (f32[6,16,2,256]{3,2,1,0:T(2,128)S(1)}, f32[6,16,2,256]{3,2,1,0:T(2,128)S(1)}, u32[]{:S(2)}, u32[]{:S(2)}) collective-permute-start(f32[6,16,2,256]{3,2,1,0:T(2,128)S(1)} %get-tuple-element.15), channel_id=1, source_target_pairs={{0,16},{16,32},{32,48},{48,64},{64,80},{80,96},{96,112},{112,128},... | collective-permute-start | bytes 589832 | tf_op jit(solution)/shard_map/ppermute | solution.py:258
  16.9 1.4 copy-start
  18.3 7.3 %copy-start.4 = (s32[2,8,3]{1,0,2:T(2,128)S(1)}, s32[2,8,3]{1,0,2:T(2,128)}, u32[]{:S(2)}) copy-start(s32[2,8,3]{1,0,2:T(2,128)} %param.15) | copy-start | bytes 580
  18.9 7.4 %collective-permute-start.2 = (f32[6,16,24,2]{2,1,3,0:T(8,128)S(1)}, f32[6,16,24,2]{2,1,3,0:T(8,128)S(1)}, u32[]{:S(2)}, u32[]{:S(2)}) collective-permute-start(f32[6,16,24,2]{2,1,3,0:T(8,128)S(1)} %copy.13), channel_id=1, source_target_pairs={{1,0},{2,1},{3,2},{4,3},{5,4},{6,5},{7,6},{8,7},{9,8},{10,9},{11,1... | collective-permute-start | bytes 55304 | tf_op jit(solution)/shard_map/ppermute | solution.py:264
  20.9 6.3 %collective-permute-start.3 = (f32[6,16,24,2]{2,1,3,0:T(8,128)S(1)}, f32[6,16,24,2]{2,1,3,0:T(8,128)S(1)}, u32[]{:S(2)}, u32[]{:S(2)}) collective-permute-start(f32[6,16,24,2]{2,1,3,0:T(8,128)S(1)} %copy.14), channel_id=1, source_target_pairs={{0,1},{1,2},{2,3},{3,4},{4,5},{5,6},{6,7},{7,8},{8,9},{9,10},{10,1... | collective-permute-start | bytes 55304 | tf_op jit(solution)/shard_map/ppermute | solution.py:266
  38.8 23.9 %collective-permute-start.4 = (f32[16,16,256]{2,1,0:T(8,128)S(1)}, f32[16,16,256]{2,1,0:T(8,128)S(1)}, u32[]{:S(2)}, u32[]{:S(2)}) collective-permute-start(f32[16,16,256]{2,1,0:T(8,128)S(1)} %broadcast_select_fusion), channel_id=1, source_target_pairs={{0,256},{256,0},{1,257},{257,1},{2,258},{258,2},{3,259},{259,3},{4... | collective-permute-start | bytes 786440 | tf_op jit(solution)/shard_map/ppermute | solution.py:276
  102.0 42.0 %collective-permute-start.5 = (f32[16,16,256]{2,1,0:T(8,128)}, f32[16,16,256]{2,1,0:T(8,128)S(1)}, u32[]{:S(2)}, u32[]{:S(2)}) collective-permute-start(f32[16,16,256]{2,1,0:T(8,128)} %bitcast.13), channel_id=1, source_target_pairs={{0,256},{256,0},{1,257},{257,1},{2,258},{258,2},{3,259},{259,3},{4... | collective-permute-start | bytes 786440 | tf_op jit(solution)/shard_map/ppermute | solution.py:291

commit v14 on v12

--- a/solution.py
+++ b/solution.py
@@ -75,7 +75,7 @@
 
 
 def heat_kernel(
-    offs_ref, wells_ref, misfit_ref, tile_ref, after_ref, before_ref, side_ref, temp_ref,
+    wells_ref, misfit_ref, tile_ref, after_ref, before_ref, side_ref, temp_ref,
     heat_ref, fx_ref, fy_ref, adj_ref, w_ref, box_ref,
 ):
     channels, layers, tile_x, tile_y = tile_ref.shape
@@ -133,7 +133,10 @@
                 if store:
                     adj_ref[test, z] = updated
                 temper = temp_ref[level, test, z].astype(jnp.float32)
-                terms = [temper * v[:tile_x, :tile_y] for v in (diffusion, slope_x, slope_y)]
+                first = lax.axis_index("sec") == 0
+                mine = jnp.where(first, slope_x, slope_y)
+                other = jnp.where(first, slope_y, slope_x)
+                terms = [temper * v[:tile_x, :tile_y] for v in (diffusion, mine, other)]
                 if heat is None:
                     heat, fx, fy = terms
                 else:
@@ -154,8 +157,8 @@
     for test in range(tests):
         for well in range(wells_ref.shape[1]):
             depth = wells_ref[test, well, 0]
-            at_x = wells_ref[test, well, 1] - offs_ref[0]
-            at_y = wells_ref[test, well, 2] - offs_ref[1]
+            at_x = wells_ref[test, well, 1] - lax.axis_index("gx") * tile_x
+            at_y = wells_ref[test, well, 2] - lax.axis_index("gy") * tile_y
             inside = (at_x >= -2) & (at_x < tile_x + 2) & (at_y >= -2) & (at_y < tile_y + 2)
             amount = jnp.where(inside, misfit_ref[1, test, well], 0.0)
             hit = (row_ids == jnp.where(at_x < 0, at_x + rows, at_x)) & (
@@ -165,7 +168,7 @@
     advance(adj_ref, 0, False)
 
 
-def heat_phase(offs, wells, misfit, tile, after, before, side, temp, rows):
+def heat_phase(wells, misfit, tile, after, before, side, temp, rows):
     channels, layers = tile.shape[:2]
     cols = tile.shape[3] + side.shape[3]
     tests = temp.shape[1]
@@ -176,14 +179,14 @@
     return pl.pallas_call(
         heat_kernel,
         out_shape=(out, out, out),
-        in_specs=[smem, smem, smem, vmem, vmem, vmem, vmem, vmem],
+        in_specs=[smem, smem, vmem, vmem, vmem, vmem, vmem],
         out_specs=(vmem, vmem, vmem),
         scratch_shapes=[
             pltpu.VMEM((tests, layers, rows, cols), jnp.float32),
             pltpu.VMEM((6, layers, rows, cols), jnp.float32),
             pltpu.VMEM((channels, layers, rows, cols), jnp.float32),
         ],
-    )(offs, wells, misfit, tile, after, before, side, temp)
+    )(wells, misfit, tile, after, before, side, temp)
 
 
 def circular(cells, sides, width, sizes):
@@ -276,13 +279,9 @@
         ],
         axis=3,
     )
-    offs = jnp.stack([lax.axis_index("gx") * rows_x, lax.axis_index("gy") * cols_y]).astype(jnp.int32)
-    heat_sens, flow_x, flow_y = heat_phase(
-        offs, wells, misfit, packed, after, before, side, forward_temp, sizes[0]
-    )
-    first = lax.axis_index("sec") == 0
-    mine = jnp.where(first, flow_x, flow_y)
-    other = jnp.where(first, flow_y, flow_x)
+    heat_sens, mine, other = heat_phase(
+        wells, misfit, packed, after, before, side, forward_temp, sizes[0]
+    )
     partner = [(0, 1), (1, 0)]
     rounded = (mine + lax.ppermute(other, "sec", partner)).astype(jnp.bfloat16)
     row_blocks, per_row, block_size, _ = blocks.shape

time: 140 us -> 138 us (0.986)
  other arithmetic: 8.31 us -> 6.64 us
where the time goes in v14:
time: 138 us
  waiting for transfers between devices  48.3 us (35%)
  starting transfers between devices  34.5 us (25%)
  blocking collectives  28 us (20%)
  Pallas kernels  11.8 us (9%)
  local copies, waits for them, and re-layouts  7.97 us (6%)
  other arithmetic  6.64 us (5%)
    all_to_all x1, blocking collectives, shards(): gathered = lax.all_to_all(copies, 'gy', 0, 0, tiled=False)  28 us
    ppermute x1, waiting for transfers between devices, shards(): sensitivity = partial_sens + lax.ppermute(partial_sens, 'sec', partner)  20.8 us
    ppermute x1, waiting for transfers between devices, shards(): rounded = (mine + lax.ppermute(other, 'sec', partner)).astype(jnp.bfloat16)  20.5 us
    ppermute x1, starting transfers between devices, shards(): sensitivity = partial_sens + lax.ppermute(partial_sens, 'sec', partner)  13 us
    ppermute x1, starting transfers between devices, shards(): rounded = (mine + lax.ppermute(other, 'sec', partner)).astype(jnp.bfloat16)  11.4 us
    pallas_call x1, Pallas kernels, heat_phase(): pl.pallas_call(heat_kernel, out_shape=(out, out, out), in_specs=[smem, sm...  8.86 us
    ppermute x1, waiting for transfers between devices, shards(): lax.ppermute(packed[:, :, rows_x - width:], 'gx', [(i, i + 1) for i in ra...  6.13 us
    ppermute x1, starting transfers between devices, shards(): lax.ppermute(column(slice(cols_y - width, cols_y)), 'gy', [(i, i + 1) for...  4.55 us
  transfers between devices with their start and end apart: 6, of which 4 were waited for; matrix products, arithmetic and copies ran while one was open for 3% of the time, Pallas kernels for 0%

profile of v14, /device:TPU:32, one launch (start us, length us, event | category | flops | bytes accessed | tf_op | source)
XLA Modules:
  0.0 138.0 jit_solution(1786604543858212947)
XLA Ops:
  0.6 1.0 subtract_bitcast_fusion
  1.6 1.4 %pad_maximum_fusion.tile_ref = f32[6,16,16,256]{3,2,1,0:T(8,128)S(1)} fusion(f32[1,16,16,256]{3,2,1,0:T(8,128)S(1)} %subtract_bitcast_fusion, f32[2,16,16,256]{3,2,1,0:T(8,128)} %param.13, f32[1,16,16,256]{3,2,1,0:T(8,128)} %bitcast.9, f32[2,16,16,256]{3,2,1,0:T(8,128)} %param.10), kind=kLoop, calls=%fused_computation | loop fusion | flops 1179648 | bytes 3145728 | tf_op jit(solution)/shard_map/concatenate | solution.py:262
  3.0 1.0 fusion.1
  4.1 1.9 %collective-permute-start = (f32[6,16,2,256]{3,2,1,0:T(2,128)}, f32[6,16,2,256]{3,2,1,0:T(2,128)S(1)}, u32[]{:S(2)}, u32[]{:S(2)}) collective-permute-start(f32[6,16,2,256]{3,2,1,0:T(2,128)} %get-tuple-element.15), channel_id=1, source_target_pairs={{16,0},{32,16},{48,32},{64,48},{80,64},{96,80},{112,96},{128,112},... | collective-permute-start | bytes 589832 | tf_op jit(solution)/shard_map/ppermute | solution.py:267
  6.0 2.4 %collective-permute-start.1 = (f32[6,16,2,256]{3,2,1,0:T(2,128)}, f32[6,16,2,256]{3,2,1,0:T(2,128)S(1)}, u32[]{:S(2)}, u32[]{:S(2)}) collective-permute-start(f32[6,16,2,256]{3,2,1,0:T(2,128)} %get-tuple-element.14), channel_id=1, source_target_pairs={{0,16},{16,32},{32,48},{48,64},{64,80},{80,96},{96,112},{112,128},... | collective-permute-start | bytes 589832 | tf_op jit(solution)/shard_map/ppermute | solution.py:268
  10.2 0.7 copy.14
  10.9 6.1 %collective-permute-done.1.before_ref = f32[6,16,2,256]{3,2,1,0:T(2,128)S(1)} collective-permute-done((f32[6,16,2,256]{3,2,1,0:T(2,128)}, f32[6,16,2,256]{3,2,1,0:T(2,128)S(1)}, u32[]{:S(2)}, u32[]{:S(2)}) %collective-permute-start.1) | collective-permute-done | bytes 196640 | tf_op jit(solution)/shard_map/ppermute | solution.py:268
  17.2 0.7 copy.15
  17.9 0.7 copy.17
  18.6 0.7 copy.18
  19.4 1.3 collective-permute-start.2
  20.7 4.6 %collective-permute-start.3 = (f32[6,16,24,2]{2,1,3,0:T(8,128)S(1)}, f32[6,16,24,2]{2,1,3,0:T(8,128)S(1)}, u32[]{:S(2)}, u32[]{:S(2)}) collective-permute-start(f32[6,16,24,2]{2,1,3,0:T(8,128)S(1)} %get-tuple-element.21), channel_id=1, source_target_pairs={{0,1},{1,2},{2,3},{3,4},{4,5},{5,6},{6,7},{7,8},{8,9},{9,10},{10,1... | collective-permute-start | bytes 55304 | tf_op jit(solution)/shard_map/ppermute | solution.py:278
  25.4 0.7 copy.21.wells_ref
  26.7 0.8 collective-permute-done.3
  28.1 1.4 %pad_maximum_fusion.1.side_ref = f32[6,16,24,128]{3,2,1,0:T(8,128)} fusion(f32[6,16,24,2]{3,2,1,0:T(8,128)S(1)} %copy.20, f32[6,16,24,2]{3,2,1,0:T(8,128)S(1)} %copy.19, f32[128]{0:T(128)S(1)} %pad.1.clone), kind=kLoop, calls=%fused_computation.1 | loop fusion | flops 589824 | bytes 1217024 | tf_op jit(solution)/shard_map/concatenate | solution.py:274
  29.5 8.9 %shard_map.113 = (f32[16,16,256]{2,1,0:T(8,128)}, f32[16,16,256]{2,1,0:T(8,128)}, f32[16,16,256]{2,1,0:T(8,128)}) custom-call(s32[2,8,3]{2,1,0:T(8,128)} %copy.21.wells_ref, f32[2,2,8]{2,1,0:T(2,128)} %misfit_ref.1, f32[6,16,16,256]{3,2,1,0:T(8,128)} %copy-done, f32[6,16,2,256]{3,2,1,0:T(2,128)} %copy-done.1, f32[6,16,2,256]{3,2,1,0:T(2,128)} %copy-done.2, ...), custom_call_target="tpu_custom_call" | custom-call | tf_op jit(solution)/shard_map/pallas_call | solution.py:179
  38.4 11.4 %collective-permute-start.4 = (f32[16,16,256]{2,1,0:T(8,128)}, f32[16,16,256]{2,1,0:T(8,128)S(1)}, u32[]{:S(2)}, u32[]{:S(2)}) collective-permute-start(f32[16,16,256]{2,1,0:T(8,128)} %get-tuple-element.8), channel_id=1, source_target_pairs={{0,256},{256,0},{1,257},{257,1},{2,258},{258,2},{3,259},{259,3},{4... | collective-permute-start | bytes 786440 | tf_op jit(solution)/shard_map/ppermute | solution.py:286
  49.8 20.5 %collective-permute-done.4 = f32[16,16,256]{2,1,0:T(8,128)S(1)} collective-permute-done((f32[16,16,256]{2,1,0:T(8,128)}, f32[16,16,256]{2,1,0:T(8,128)S(1)}, u32[]{:S(2)}, u32[]{:S(2)}) %collective-permute-start.4) | collective-permute-done | bytes 262176 | tf_op jit(solution)/shard_map/ppermute | solution.py:286
  70.3 1.0 add_convert_fusion
  71.5 28.0 %all_to_all.5 = bf16[16,16,16,256]{3,2,1,0:T(8,128)(2,1)} all-to-all(bf16[16,16,16,256]{3,2,1,0:T(8,128)(2,1)S(1)} %broadcast_in_dim.18), channel_id=1, replica_groups=mesh['sec'=2,'gx'=16,'gy'=16] {'gy'}, dimensions={0} | all-to-all | bytes 4194304 | tf_op jit(solution)/shard_map/all_to_all | solution.py:290
  99.5 3.0 %shard_map.114 = (f32[256,256]{1,0:T(8,128)}, f32[256,256]{1,0:T(8,128)}) custom-call(s32[2,7]{1,0:T(2,128)} %cols_ref.1, bf16[16,256,256]{2,1,0:T(8,128)(2,1)} %bitcast.8, bf16[2,7,128,128]{3,2,1,0:T(8,128)(2,1)} %blocks_ref.1, f32[256,256]{1,0:T(8,128)} %bitcast.12, bf16[256,256]{1,0:T(8,128)(2,1)} %bitcast.13), custom_call_target="tpu_custom_call" | custom-call | flops 117440512 | bytes 3473408 | tf_op jit(solution)/shard_map/pallas_call | solution.py:232
  102.5 13.0 %collective-permute-start.5 = (f32[16,16,256]{2,1,0:T(8,128)}, f32[16,16,256]{2,1,0:T(8,128)S(1)}, u32[]{:S(2)}, u32[]{:S(2)}) collective-permute-start(f32[16,16,256]{2,1,0:T(8,128)} %bitcast.10), channel_id=1, source_target_pairs={{0,256},{256,0},{1,257},{257,1},{2,258},{258,2},{3,259},{259,3},{4... | collective-permute-start | bytes 786440 | tf_op jit(solution)/shard_map/ppermute | solution.py:301
  115.5 20.8 %collective-permute-done.5 = f32[16,16,256]{2,1,0:T(8,128)S(1)} collective-permute-done((f32[16,16,256]{2,1,0:T(8,128)}, f32[16,16,256]{2,1,0:T(8,128)S(1)}, u32[]{:S(2)}, u32[]{:S(2)}) %collective-permute-start.5) | collective-permute-done | bytes 262176 | tf_op jit(solution)/shard_map/ppermute | solution.py:301
  136.3 1.7 %add.7 = f32[16,16,256]{2,1,0:T(8,128)} add(f32[16,16,256]{2,1,0:T(8,128)} %bitcast.11, f32[16,16,256]{2,1,0:T(8,128)S(1)} %collective-permute-done.5) | non-fusion elementwise | flops 65536 | bytes 786432 | tf_op jit(solution)/shard_map/add | solution.py:301
  (23 shorter events, 3.7 us)
Async XLA Ops:
  3.0 5.7 %copy-start = (f32[6,16,16,256]{3,2,1,0:T(8,128)}, f32[6,16,16,256]{3,2,1,0:T(8,128)S(1)}, u32[]{:S(2)}) copy-start(f32[6,16,16,256]{3,2,1,0:T(8,128)S(1)} %pad_maximum_fusion.tile_ref) | copy-start | bytes 4718596
  4.1 6.0 %collective-permute-start = (f32[6,16,2,256]{3,2,1,0:T(2,128)}, f32[6,16,2,256]{3,2,1,0:T(2,128)S(1)}, u32[]{:S(2)}, u32[]{:S(2)}) collective-permute-start(f32[6,16,2,256]{3,2,1,0:T(2,128)} %get-tuple-element.15), channel_id=1, source_target_pairs={{16,0},{32,16},{48,32},{64,48},{80,64},{96,80},{112,96},{128,112},... | collective-permute-start | bytes 589832 | tf_op jit(solution)/shard_map/ppermute | solution.py:267
  6.0 11.1 %collective-permute-start.1 = (f32[6,16,2,256]{3,2,1,0:T(2,128)}, f32[6,16,2,256]{3,2,1,0:T(2,128)S(1)}, u32[]{:S(2)}, u32[]{:S(2)}) collective-permute-start(f32[6,16,2,256]{3,2,1,0:T(2,128)} %get-tuple-element.14), channel_id=1, source_target_pairs={{0,16},{16,32},{32,48},{48,64},{64,80},{80,96},{96,112},{112,128},... | collective-permute-start | bytes 589832 | tf_op jit(solution)/shard_map/ppermute | solution.py:268
  9.3 16.1 %copy-start.3 = (s32[2,8,3]{1,0,2:T(2,128)S(1)}, s32[2,8,3]{1,0,2:T(2,128)}, u32[]{:S(2)}) copy-start(s32[2,8,3]{1,0,2:T(2,128)} %param.15) | copy-start | bytes 580
  10.0 16.7 %copy-start.1 = (f32[6,16,2,256]{3,2,1,0:T(2,128)}, f32[6,16,2,256]{3,2,1,0:T(2,128)S(1)}, u32[]{:S(2)}) copy-start(f32[6,16,2,256]{3,2,1,0:T(2,128)S(1)} %collective-permute-done.after_ref) | copy-start | bytes 589828
  17.0 11.1 %copy-start.2 = (f32[6,16,2,256]{3,2,1,0:T(2,128)}, f32[6,16,2,256]{3,2,1,0:T(2,128)S(1)}, u32[]{:S(2)}) copy-start(f32[6,16,2,256]{3,2,1,0:T(2,128)S(1)} %collective-permute-done.1.before_ref) | copy-start | bytes 589828
  19.4 6.6 %collective-permute-start.2 = (f32[6,16,24,2]{2,1,3,0:T(8,128)S(1)}, f32[6,16,24,2]{2,1,3,0:T(8,128)S(1)}, u32[]{:S(2)}, u32[]{:S(2)}) collective-permute-start(f32[6,16,24,2]{2,1,3,0:T(8,128)S(1)} %get-tuple-element.20), channel_id=1, source_target_pairs={{1,0},{2,1},{3,2},{4,3},{5,4},{6,5},{7,6},{8,7},{9,8},{10,9},{11,1... | collective-permute-start | bytes 55304 | tf_op jit(solution)/shard_map/ppermute | solution.py:276
  20.7 6.8 %collective-permute-start.3 = (f32[6,16,24,2]{2,1,3,0:T(8,128)S(1)}, f32[6,16,24,2]{2,1,3,0:T(8,128)S(1)}, u32[]{:S(2)}, u32[]{:S(2)}) collective-permute-start(f32[6,16,24,2]{2,1,3,0:T(8,128)S(1)} %get-tuple-element.21), channel_id=1, source_target_pairs={{0,1},{1,2},{2,3},{3,4},{4,5},{5,6},{6,7},{7,8},{8,9},{9,10},{10,1... | collective-permute-start | bytes 55304 | tf_op jit(solution)/shard_map/ppermute | solution.py:278
  38.4 31.9 %collective-permute-start.4 = (f32[16,16,256]{2,1,0:T(8,128)}, f32[16,16,256]{2,1,0:T(8,128)S(1)}, u32[]{:S(2)}, u32[]{:S(2)}) collective-permute-start(f32[16,16,256]{2,1,0:T(8,128)} %get-tuple-element.8), channel_id=1, source_target_pairs={{0,256},{256,0},{1,257},{257,1},{2,258},{258,2},{3,259},{259,3},{4... | collective-permute-start | bytes 786440 | tf_op jit(solution)/shard_map/ppermute | solution.py:286
  102.5 33.8 %collective-permute-start.5 = (f32[16,16,256]{2,1,0:T(8,128)}, f32[16,16,256]{2,1,0:T(8,128)S(1)}, u32[]{:S(2)}, u32[]{:S(2)}) collective-permute-start(f32[16,16,256]{2,1,0:T(8,128)} %bitcast.10), channel_id=1, source_target_pairs={{0,256},{256,0},{1,257},{257,1},{2,258},{258,2},{3,259},{259,3},{4... | collective-permute-start | bytes 786440 | tf_op jit(solution)/shard_map/ppermute | solution.py:301

commit v15 on v14

--- a/solution.py
+++ b/solution.py
@@ -264,8 +264,15 @@
     sizes = (-(-(rows_x + 2 * width) // 8) * 8, -(-(cols_y + 2 * width) // 128) * 128)
     ends_x = lax.axis_size("gx") - 1
     ends_y = lax.axis_size("gy") - 1
-    after = lax.ppermute(packed[:, :, :width], "gx", [(i + 1, i) for i in range(ends_x)])
-    before = lax.ppermute(packed[:, :, rows_x - width:], "gx", [(i, i + 1) for i in range(ends_x)])
+    def edge(lo, hi):
+        cut = (Ellipsis, slice(lo, hi), slice(None))
+        edge_keep = 1.0 - fixed_mask[cut].astype(jnp.float32)
+        return jnp.concatenate(
+            [terminal[cut], conductivity[None][cut], velocity[cut], edge_keep[None]], axis=0
+        )
+
+    after = lax.ppermute(edge(0, width), "gx", [(i + 1, i) for i in range(ends_x)])
+    before = lax.ppermute(edge(rows_x - width, rows_x), "gx", [(i, i + 1) for i in range(ends_x)])
 
     def column(cut):
         gap = jnp.zeros(packed.shape[:2] + (sizes[0] - rows_x - 2 * width, width), packed.dtype)

time: 138 us -> 141 us (1.022)
  waiting for transfers between devices: 48.3 us -> 44.6 us
  local copies, waits for them, and re-layouts: 7.97 us -> 10.2 us
  blocking collectives: 28 us -> 30 us
  starting transfers between devices: 34.5 us -> 36 us
    ppermute x1, waiting for transfers between devices: 20.5 us -> 17.8 us  [shards(): rounded = (mine + lax.ppermute(other, 'sec', partner)).astype(jnp.bfloat16)]
    all_to_all x1, blocking collectives: 28 us -> 30 us  [shards(): gathered = lax.all_to_all(copies, 'gy', 0, 0, tiled=False)]
    concatenate x0 -> x2, other arithmetic: none -> 1.56 us  [edge(): jnp.concatenate([terminal[cut], conductivity[None][cut], velocity[cut], e...]
    ppermute x1, starting transfers between devices: 13 us -> 14.4 us  [shards(): sensitivity = partial_sens + lax.ppermute(partial_sens, 'sec', partner)]
where the time goes in v15:
time: 141 us; the launch traced here: 140 us
  waiting for transfers between devices  44.6 us (32%)
  starting transfers between devices  36 us (26%)
  blocking collectives  30 us (21%)
  Pallas kernels  11.8 us (8%)
  local copies, waits for them, and re-layouts  10.2 us (7%)
  other arithmetic  6.98 us (5%)
    all_to_all x1, blocking collectives, shards(): gathered = lax.all_to_all(copies, 'gy', 0, 0, tiled=False)  30 us
    ppermute x1, waiting for transfers between devices, shards(): sensitivity = partial_sens + lax.ppermute(partial_sens, 'sec', partner)  21 us
    ppermute x1, waiting for transfers between devices, shards(): rounded = (mine + lax.ppermute(other, 'sec', partner)).astype(jnp.bfloat16)  17.8 us
    ppermute x1, starting transfers between devices, shards(): sensitivity = partial_sens + lax.ppermute(partial_sens, 'sec', partner)  14.4 us
    ppermute x1, starting transfers between devices, shards(): rounded = (mine + lax.ppermute(other, 'sec', partner)).astype(jnp.bfloat16)  11.4 us
    pallas_call x1, Pallas kernels, heat_phase(): pl.pallas_call(heat_kernel, out_shape=(out, out, out), in_specs=[smem, sm...  8.86 us
    ppermute x1, waiting for transfers between devices, shards(): lax.ppermute(edge(rows_x - width, rows_x), 'gx', [(i, i + 1) for i in ran...  5.05 us
    ppermute x1, starting transfers between devices, shards(): lax.ppermute(column(slice(cols_y - width, cols_y)), 'gy', [(i, i + 1) for...  4.55 us
  transfers between devices with their start and end apart: 6, of which 4 were waited for; matrix products, arithmetic and copies ran while one was open for 3% of the time, Pallas kernels for 0%

profile of v15, /device:TPU:32, one launch (start us, length us, event | category | flops | bytes accessed | tf_op | source)
XLA Modules:
  0.0 140.4 jit_solution(1268819359476323542)
XLA Ops:
  0.7 1.1 fusion.3
  1.8 1.0 subtract_bitcast_fusion.1
  2.8 1.3 fusion.1
  4.1 0.8 pad_maximum_fusion.2
  4.9 1.9 %collective-permute-start = (f32[6,16,2,256]{3,2,1,0:T(2,128)}, f32[6,16,2,256]{3,2,1,0:T(2,128)S(1)}, u32[]{:S(2)}, u32[]{:S(2)}) collective-permute-start(f32[6,16,2,256]{3,2,1,0:T(2,128)} %pad_maximum_fusion.2), channel_id=1, source_target_pairs={{16,0},{32,16},{48,32},{64,48},{80,64},{96,80},{112,96},{128,112},... | collective-permute-start | bytes 589832 | tf_op jit(solution)/shard_map/ppermute | solution.py:274
  6.8 0.8 pad_maximum_fusion.3
  7.6 2.4 %collective-permute-start.1 = (f32[6,16,2,256]{3,2,1,0:T(2,128)}, f32[6,16,2,256]{3,2,1,0:T(2,128)S(1)}, u32[]{:S(2)}, u32[]{:S(2)}) collective-permute-start(f32[6,16,2,256]{3,2,1,0:T(2,128)} %pad_maximum_fusion.3), channel_id=1, source_target_pairs={{0,16},{16,32},{32,48},{48,64},{64,80},{80,96},{96,112},{112,128},... | collective-permute-start | bytes 589832 | tf_op jit(solution)/shard_map/ppermute | solution.py:275
  10.4 0.9 copy-done
  13.5 5.0 %collective-permute-done.1.before_ref = f32[6,16,2,256]{3,2,1,0:T(2,128)S(1)} collective-permute-done((f32[6,16,2,256]{3,2,1,0:T(2,128)}, f32[6,16,2,256]{3,2,1,0:T(2,128)S(1)}, u32[]{:S(2)}, u32[]{:S(2)}) %collective-permute-start.1) | collective-permute-done | bytes 196640 | tf_op jit(solution)/shard_map/ppermute | solution.py:275
  20.1 0.7 copy.18
  21.0 1.3 collective-permute-start.2
  22.3 4.6 %collective-permute-start.3 = (f32[6,16,24,2]{2,1,3,0:T(8,128)S(1)}, f32[6,16,24,2]{2,1,3,0:T(8,128)S(1)}, u32[]{:S(2)}, u32[]{:S(2)}) collective-permute-start(f32[6,16,24,2]{2,1,3,0:T(8,128)S(1)} %get-tuple-element.27), channel_id=1, source_target_pairs={{0,1},{1,2},{2,3},{3,4},{4,5},{5,6},{6,7},{7,8},{8,9},{9,10},{10,1... | collective-permute-start | bytes 55304 | tf_op jit(solution)/shard_map/ppermute | solution.py:285
  26.9 0.7 copy.21.wells_ref
  28.3 0.8 collective-permute-done.3
  29.7 1.4 pad_maximum_fusion.1.side_ref
  31.1 8.9 %shard_map.113 = (f32[16,16,256]{2,1,0:T(8,128)}, f32[16,16,256]{2,1,0:T(8,128)}, f32[16,16,256]{2,1,0:T(8,128)}) custom-call(s32[2,8,3]{2,1,0:T(8,128)} %copy.21.wells_ref, f32[2,2,8]{2,1,0:T(2,128)} %misfit_ref.1, f32[6,16,16,256]{3,2,1,0:T(8,128)} %copy-done, f32[6,16,2,256]{3,2,1,0:T(2,128)} %copy-done.3, f32[6,16,2,256]{3,2,1,0:T(2,128)} %copy-done.4, ...), custom_call_target="tpu_custom_call" | custom-call | tf_op jit(solution)/shard_map/pallas_call | solution.py:179
  39.9 11.4 %collective-permute-start.4 = (f32[16,16,256]{2,1,0:T(8,128)}, f32[16,16,256]{2,1,0:T(8,128)S(1)}, u32[]{:S(2)}, u32[]{:S(2)}) collective-permute-start(f32[16,16,256]{2,1,0:T(8,128)} %get-tuple-element.8), channel_id=1, source_target_pairs={{0,256},{256,0},{1,257},{257,1},{2,258},{258,2},{3,259},{259,3},{4... | collective-permute-start | bytes 786440 | tf_op jit(solution)/shard_map/ppermute | solution.py:293
  51.3 17.8 %collective-permute-done.4 = f32[16,16,256]{2,1,0:T(8,128)S(1)} collective-permute-done((f32[16,16,256]{2,1,0:T(8,128)}, f32[16,16,256]{2,1,0:T(8,128)S(1)}, u32[]{:S(2)}, u32[]{:S(2)}) %collective-permute-start.4) | collective-permute-done | bytes 262176 | tf_op jit(solution)/shard_map/ppermute | solution.py:293
  69.1 1.0 add_convert_fusion
  70.3 30.0 %all_to_all.5 = bf16[16,16,16,256]{3,2,1,0:T(8,128)(2,1)} all-to-all(bf16[16,16,16,256]{3,2,1,0:T(8,128)(2,1)S(1)} %broadcast_in_dim.28), channel_id=1, replica_groups=mesh['sec'=2,'gx'=16,'gy'=16] {'gy'}, dimensions={0} | all-to-all | bytes 4194304 | tf_op jit(solution)/shard_map/all_to_all | solution.py:297
  100.3 3.0 %shard_map.114 = (f32[256,256]{1,0:T(8,128)}, f32[256,256]{1,0:T(8,128)}) custom-call(s32[2,7]{1,0:T(2,128)} %cols_ref.1, bf16[16,256,256]{2,1,0:T(8,128)(2,1)} %bitcast.12, bf16[2,7,128,128]{3,2,1,0:T(8,128)(2,1)} %blocks_ref.1, f32[256,256]{1,0:T(8,128)} %bitcast.17, bf16[256,256]{1,0:T(8,128)(2,1)} %bitcast.18), custom_call_target="tpu_custom_call" | custom-call | flops 117440512 | bytes 3473408 | tf_op jit(solution)/shard_map/pallas_call | solution.py:232
  103.3 14.4 %collective-permute-start.5 = (f32[16,16,256]{2,1,0:T(8,128)}, f32[16,16,256]{2,1,0:T(8,128)S(1)}, u32[]{:S(2)}, u32[]{:S(2)}) collective-permute-start(f32[16,16,256]{2,1,0:T(8,128)} %bitcast.15), channel_id=1, source_target_pairs={{0,256},{256,0},{1,257},{257,1},{2,258},{258,2},{3,259},{259,3},{4... | collective-permute-start | bytes 786440 | tf_op jit(solution)/shard_map/ppermute | solution.py:308
  117.7 21.0 %collective-permute-done.5 = f32[16,16,256]{2,1,0:T(8,128)S(1)} collective-permute-done((f32[16,16,256]{2,1,0:T(8,128)}, f32[16,16,256]{2,1,0:T(8,128)S(1)}, u32[]{:S(2)}, u32[]{:S(2)}) %collective-permute-start.5) | collective-permute-done | bytes 262176 | tf_op jit(solution)/shard_map/ppermute | solution.py:308
  138.7 1.7 %add.7 = f32[16,16,256]{2,1,0:T(8,128)} add(f32[16,16,256]{2,1,0:T(8,128)} %bitcast.16, f32[16,16,256]{2,1,0:T(8,128)S(1)} %collective-permute-done.5) | non-fusion elementwise | flops 65536 | bytes 786432 | tf_op jit(solution)/shard_map/add | solution.py:308
  (35 shorter events, 5.9 us)
Async XLA Ops:
  0.6 9.4 %copy-start.5 = (f32[16,16,256]{2,1,0:T(8,128)S(1)}, f32[16,16,256]{2,1,0:T(8,128)}, u32[]{:S(2)}) copy-start(f32[16,16,256]{2,1,0:T(8,128)} %param.12) | copy-start | bytes 786436
  0.6 9.3 %copy-start.6 = (s32[16,16,256]{2,1,0:T(8,128)S(1)}, s32[16,16,256]{2,1,0:T(8,128)}, u32[]{:S(2)}) copy-start(s32[16,16,256]{2,1,0:T(8,128)} %param.14) | copy-start | bytes 786436
  0.7 9.4 %copy-start.2 = (f32[2,16,16,256]{3,2,1,0:T(8,128)S(1)}, f32[2,16,16,256]{3,2,1,0:T(8,128)}, u32[]{:S(2)}) copy-start(f32[2,16,16,256]{3,2,1,0:T(8,128)} %param.10) | copy-start | bytes 1572868
  0.7 9.4 %copy-start.1 = (f32[2,16,16,256]{3,2,1,0:T(8,128)S(1)}, f32[2,16,16,256]{3,2,1,0:T(8,128)}, u32[]{:S(2)}) copy-start(f32[2,16,16,256]{3,2,1,0:T(8,128)} %param.13) | copy-start | bytes 1572868
  4.9 7.8 %collective-permute-start = (f32[6,16,2,256]{3,2,1,0:T(2,128)}, f32[6,16,2,256]{3,2,1,0:T(2,128)S(1)}, u32[]{:S(2)}, u32[]{:S(2)}) collective-permute-start(f32[6,16,2,256]{3,2,1,0:T(2,128)} %pad_maximum_fusion.2), channel_id=1, source_target_pairs={{16,0},{32,16},{48,32},{64,48},{80,64},{96,80},{112,96},{128,112},... | collective-permute-start | bytes 589832 | tf_op jit(solution)/shard_map/ppermute | solution.py:274
  7.6 11.0 %collective-permute-start.1 = (f32[6,16,2,256]{3,2,1,0:T(2,128)}, f32[6,16,2,256]{3,2,1,0:T(2,128)S(1)}, u32[]{:S(2)}, u32[]{:S(2)}) collective-permute-start(f32[6,16,2,256]{3,2,1,0:T(2,128)} %pad_maximum_fusion.3), channel_id=1, source_target_pairs={{0,16},{16,32},{32,48},{48,64},{64,80},{80,96},{96,112},{112,128},... | collective-permute-start | bytes 589832 | tf_op jit(solution)/shard_map/ppermute | solution.py:275
  10.2 1.2 copy-start
  11.9 15.0 %copy-start.7 = (s32[2,8,3]{1,0,2:T(2,128)S(1)}, s32[2,8,3]{1,0,2:T(2,128)}, u32[]{:S(2)}) copy-start(s32[2,8,3]{1,0,2:T(2,128)} %param.15) | copy-start | bytes 580
  12.7 15.6 %copy-start.3 = (f32[6,16,2,256]{3,2,1,0:T(2,128)}, f32[6,16,2,256]{3,2,1,0:T(2,128)S(1)}, u32[]{:S(2)}) copy-start(f32[6,16,2,256]{3,2,1,0:T(2,128)S(1)} %collective-permute-done.after_ref) | copy-start | bytes 589828
  18.6 11.1 %copy-start.4 = (f32[6,16,2,256]{3,2,1,0:T(2,128)}, f32[6,16,2,256]{3,2,1,0:T(2,128)S(1)}, u32[]{:S(2)}) copy-start(f32[6,16,2,256]{3,2,1,0:T(2,128)S(1)} %collective-permute-done.1.before_ref) | copy-start | bytes 589828
  21.0 6.6 %collective-permute-start.2 = (f32[6,16,24,2]{2,1,3,0:T(8,128)S(1)}, f32[6,16,24,2]{2,1,3,0:T(8,128)S(1)}, u32[]{:S(2)}, u32[]{:S(2)}) collective-permute-start(f32[6,16,24,2]{2,1,3,0:T(8,128)S(1)} %get-tuple-element.26), channel_id=1, source_target_pairs={{1,0},{2,1},{3,2},{4,3},{5,4},{6,5},{7,6},{8,7},{9,8},{10,9},{11,1... | collective-permute-start | bytes 55304 | tf_op jit(solution)/shard_map/ppermute | solution.py:283
  22.3 6.8 %collective-permute-start.3 = (f32[6,16,24,2]{2,1,3,0:T(8,128)S(1)}, f32[6,16,24,2]{2,1,3,0:T(8,128)S(1)}, u32[]{:S(2)}, u32[]{:S(2)}) collective-permute-start(f32[6,16,24,2]{2,1,3,0:T(8,128)S(1)} %get-tuple-element.27), channel_id=1, source_target_pairs={{0,1},{1,2},{2,3},{3,4},{4,5},{5,6},{6,7},{7,8},{8,9},{9,10},{10,1... | collective-permute-start | bytes 55304 | tf_op jit(solution)/shard_map/ppermute | solution.py:285
  39.9 29.2 %collective-permute-start.4 = (f32[16,16,256]{2,1,0:T(8,128)}, f32[16,16,256]{2,1,0:T(8,128)S(1)}, u32[]{:S(2)}, u32[]{:S(2)}) collective-permute-start(f32[16,16,256]{2,1,0:T(8,128)} %get-tuple-element.8), channel_id=1, source_target_pairs={{0,256},{256,0},{1,257},{257,1},{2,258},{258,2},{3,259},{259,3},{4... | collective-permute-start | bytes 786440 | tf_op jit(solution)/shard_map/ppermute | solution.py:293
  103.3 35.4 %collective-permute-start.5 = (f32[16,16,256]{2,1,0:T(8,128)}, f32[16,16,256]{2,1,0:T(8,128)S(1)}, u32[]{:S(2)}, u32[]{:S(2)}) collective-permute-start(f32[16,16,256]{2,1,0:T(8,128)} %bitcast.15), channel_id=1, source_target_pairs={{0,256},{256,0},{1,257},{257,1},{2,258},{258,2},{3,259},{259,3},{4... | collective-permute-start | bytes 786440 | tf_op jit(solution)/shard_map/ppermute | solution.py:308

commit v16 on v14

--- a/solution.py
+++ b/solution.py
@@ -75,7 +75,7 @@
 
 
 def heat_kernel(
-    wells_ref, misfit_ref, tile_ref, after_ref, before_ref, side_ref, temp_ref,
+    wells_ref, misfit_ref, tile_ref, after_ref, before_ref, right_ref, left_ref, temp_ref,
     heat_ref, fx_ref, fy_ref, adj_ref, w_ref, box_ref,
 ):
     channels, layers, tile_x, tile_y = tile_ref.shape
@@ -87,7 +87,12 @@
         (channels, layers, rows - tile_x - 2 * width, tile_y), jnp.float32
     )
     box_ref[:, :, rows - width:rows, 0:tile_y] = before_ref[...]
-    box_ref[:, :, :, tile_y:] = side_ref[...]
+    cols = box_ref.shape[3]
+    box_ref[:, :, :, tile_y:tile_y + width] = right_ref[...]
+    box_ref[:, :, :, tile_y + width:cols - width] = jnp.zeros(
+        (channels, layers, rows, cols - tile_y - 2 * width), jnp.float32
+    )
+    box_ref[:, :, :, cols - width:] = left_ref[...]
     tests, layers, rows, cols = adj_ref.shape
     tile_x, tile_y = heat_ref.shape[1], heat_ref.shape[2]
     zero = jnp.zeros((rows, cols), jnp.float32)
@@ -168,9 +173,8 @@
     advance(adj_ref, 0, False)
 
 
-def heat_phase(wells, misfit, tile, after, before, side, temp, rows):
+def heat_phase(wells, misfit, tile, after, before, right, left, temp, rows, cols):
     channels, layers = tile.shape[:2]
-    cols = tile.shape[3] + side.shape[3]
     tests = temp.shape[1]
     plane_shape = temp.shape[3:]
     smem = pl.BlockSpec(memory_space=pltpu.SMEM)
@@ -179,14 +183,14 @@
     return pl.pallas_call(
         heat_kernel,
         out_shape=(out, out, out),
-        in_specs=[smem, smem, vmem, vmem, vmem, vmem, vmem],
+        in_specs=[smem, smem, vmem, vmem, vmem, vmem, vmem, vmem],
         out_specs=(vmem, vmem, vmem),
         scratch_shapes=[
             pltpu.VMEM((tests, layers, rows, cols), jnp.float32),
             pltpu.VMEM((6, layers, rows, cols), jnp.float32),
             pltpu.VMEM((channels, layers, rows, cols), jnp.float32),
         ],
-    )(wells, misfit, tile, after, before, side, temp)
+    )(wells, misfit, tile, after, before, right, left, temp)
 
 
 def circular(cells, sides, width, sizes):
@@ -271,16 +275,10 @@
         gap = jnp.zeros(packed.shape[:2] + (sizes[0] - rows_x - 2 * width, width), packed.dtype)
         return jnp.concatenate([packed[..., cut], after[..., cut], gap, before[..., cut]], axis=2)
 
-    side = jnp.concatenate(
-        [
-            lax.ppermute(column(slice(0, width)), "gy", [(i + 1, i) for i in range(ends_y)]),
-            jnp.zeros(packed.shape[:2] + (sizes[0], sizes[1] - cols_y - 2 * width), packed.dtype),
-            lax.ppermute(column(slice(cols_y - width, cols_y)), "gy", [(i, i + 1) for i in range(ends_y)]),
-        ],
-        axis=3,
-    )
+    right = lax.ppermute(column(slice(0, width)), "gy", [(i + 1, i) for i in range(ends_y)])
+    left = lax.ppermute(column(slice(cols_y - width, cols_y)), "gy", [(i, i + 1) for i in range(ends_y)])
     heat_sens, mine, other = heat_phase(
-        wells, misfit, packed, after, before, side, forward_temp, sizes[0]
+        wells, misfit, packed, after, before, right, left, forward_temp, sizes[0], sizes[1]
     )
     partner = [(0, 1), (1, 0)]
     rounded = (mine + lax.ppermute(other, "sec", partner)).astype(jnp.bfloat16)

time: 138 us -> 143 us (1.036)
  waiting for transfers between devices: 48.3 us -> 38.1 us
  blocking collectives: 28 us -> 37.6 us
  starting transfers between devices: 34.5 us -> 38 us
  local copies, waits for them, and re-layouts: 7.97 us -> 9.96 us
    all_to_all x1, blocking collectives: 28 us -> 37.6 us  [shards(): gathered = lax.all_to_all(copies, 'gy', 0, 0, tiled=False)]
    ppermute x1, waiting for transfers between devices: 20.8 us -> 13.9 us  [shards(): sensitivity = partial_sens + lax.ppermute(partial_sens, 'sec', partner)]
    ppermute x1, waiting for transfers between devices: 6.13 us -> 0.01 us  [shards(): lax.ppermute(packed[:, :, rows_x - width:], 'gx', [(i, i + 1) for i in ra...]
    ppermute x1, starting transfers between devices: 11.4 us -> 15.6 us  [shards(): rounded = (mine + lax.ppermute(other, 'sec', partner)).astype(jnp.bfloat16)]
    ppermute x1, waiting for transfers between devices: 20.5 us -> 23.9 us  [shards(): rounded = (mine + lax.ppermute(other, 'sec', partner)).astype(jnp.bfloat16)]
    ppermute x1, starting transfers between devices: 13 us -> 11 us  [shards(): sensitivity = partial_sens + lax.ppermute(partial_sens, 'sec', partner)]
    ppermute x1, starting transfers between devices: 1.91 us -> 3.64 us  [shards(): lax.ppermute(packed[:, :, :width], 'gx', [(i + 1, i) for i in range(ends_...]
  transfers between devices with their start and end apart: 6 -> 6, of which waited for: 4 -> 3; matrix products, arithmetic and copies ran while one was open for 3% -> 4% of each run, Pallas kernels for 0% -> 0%
where the time goes in v16:
time: 143 us; the launch traced here: 142 us
  waiting for transfers between devices  38.1 us (27%)
  starting transfers between devices  38 us (27%)
  blocking collectives  37.6 us (26%)
  Pallas kernels  12.3 us (9%)
  local copies, waits for them, and re-layouts  9.96 us (7%)
  other arithmetic  5.25 us (4%)
    all_to_all x1, blocking collectives, shards(): gathered = lax.all_to_all(copies, 'gy', 0, 0, tiled=False)  37.6 us
    ppermute x1, waiting for transfers between devices, shards(): rounded = (mine + lax.ppermute(other, 'sec', partner)).astype(jnp.bfloat16)  23.9 us
    ppermute x1, starting transfers between devices, shards(): rounded = (mine + lax.ppermute(other, 'sec', partner)).astype(jnp.bfloat16)  15.6 us
    ppermute x1, waiting for transfers between devices, shards(): sensitivity = partial_sens + lax.ppermute(partial_sens, 'sec', partner)  13.9 us
    ppermute x1, starting transfers between devices, shards(): sensitivity = partial_sens + lax.ppermute(partial_sens, 'sec', partner)  11 us
    pallas_call x1, Pallas kernels, heat_phase(): pl.pallas_call(heat_kernel, out_shape=(out, out, out), in_specs=[smem, sm...  9.37 us
    ppermute x1, starting transfers between devices, shards(): lax.ppermute(column(slice(cols_y - width, cols_y)), 'gy', [(i, i + 1) for...  4.55 us
    ppermute x1, starting transfers between devices, shards(): lax.ppermute(packed[:, :, :width], 'gx', [(i + 1, i) for i in range(ends_...  3.64 us
  transfers between devices with their start and end apart: 6, of which 3 were waited for; matrix products, arithmetic and copies ran while one was open for 4% of the time, Pallas kernels for 0%

profile of v16, /device:TPU:32, one launch (start us, length us, event | category | flops | bytes accessed | tf_op | source)
XLA Modules:
  0.0 142.0 jit_solution(16013531604761287247)
XLA Ops:
  0.6 1.0 subtract_bitcast_fusion
  1.6 1.4 pad_maximum_fusion.tile_ref
  3.0 1.1 fusion.1
  4.1 1.9 %collective-permute-start.1 = (f32[6,16,2,256]{3,2,1,0:T(2,128)}, f32[6,16,2,256]{3,2,1,0:T(2,128)S(1)}, u32[]{:S(2)}, u32[]{:S(2)}) collective-permute-start(f32[6,16,2,256]{3,2,1,0:T(2,128)} %get-tuple-element.14), channel_id=1, source_target_pairs={{0,16},{16,32},{32,48},{48,64},{64,80},{80,96},{96,112},{112,128},... | collective-permute-start | bytes 589832 | tf_op jit(solution)/shard_map/ppermute | solution.py:272
  6.0 3.6 %collective-permute-start = (f32[6,16,2,256]{3,2,1,0:T(2,128)}, f32[6,16,2,256]{3,2,1,0:T(2,128)S(1)}, u32[]{:S(2)}, u32[]{:S(2)}) collective-permute-start(f32[6,16,2,256]{3,2,1,0:T(2,128)} %get-tuple-element.15), channel_id=1, source_target_pairs={{16,0},{32,16},{48,32},{64,48},{80,64},{96,80},{112,96},{128,112},... | collective-permute-start | bytes 589832 | tf_op jit(solution)/shard_map/ppermute | solution.py:271
  10.6 0.6 copy.13
  11.5 0.7 copy.18
  12.2 0.7 copy.15
  13.3 0.7 copy.17
  14.0 0.7 copy.14
  14.9 1.3 collective-permute-start.2
  16.2 4.6 %collective-permute-start.3 = (f32[6,16,24,2]{2,1,3,0:T(8,128)S(1)}, f32[6,16,24,2]{2,1,3,0:T(8,128)S(1)}, u32[]{:S(2)}, u32[]{:S(2)}) collective-permute-start(f32[6,16,24,2]{2,1,3,0:T(8,128)S(1)} %get-tuple-element.20), channel_id=1, source_target_pairs={{0,1},{1,2},{2,3},{3,4},{4,5},{5,6},{6,7},{7,8},{8,9},{9,10},{10,1... | collective-permute-start | bytes 55304 | tf_op jit(solution)/shard_map/ppermute | solution.py:279
  20.7 0.7 copy.19.wells_ref
  21.4 1.7 %copy.20.right_ref = f32[6,16,24,2]{3,2,1,0:T(8,128)} copy(f32[6,16,24,2]{2,1,3,0:T(8,128)S(1)} %collective-permute-done.2) | data formatting | bytes 36864 | tf_op jit(solution)/shard_map/ppermute | solution.py:278
  23.1 1.7 %copy.21.left_ref = f32[6,16,24,2]{3,2,1,0:T(8,128)} copy(f32[6,16,24,2]{2,1,3,0:T(8,128)S(1)} %collective-permute-done.3) | data formatting | bytes 36864 | tf_op jit(solution)/shard_map/ppermute | solution.py:279
  24.7 9.4 %shard_map.113 = (f32[16,16,256]{2,1,0:T(8,128)}, f32[16,16,256]{2,1,0:T(8,128)}, f32[16,16,256]{2,1,0:T(8,128)}) custom-call(s32[2,8,3]{2,1,0:T(8,128)} %copy.19.wells_ref, f32[2,2,8]{2,1,0:T(2,128)} %misfit_ref.1, f32[6,16,16,256]{3,2,1,0:T(8,128)} %copy-done, f32[6,16,2,256]{3,2,1,0:T(2,128)} %copy-done.2, f32[6,16,2,256]{3,2,1,0:T(2,128)} %copy-done.1, ...), custom_call_target="tpu_custom_call" | custom-call | tf_op jit(solution)/shard_map/pallas_call | solution.py:183
  34.1 15.6 %collective-permute-start.4 = (f32[16,16,256]{2,1,0:T(8,128)}, f32[16,16,256]{2,1,0:T(8,128)S(1)}, u32[]{:S(2)}, u32[]{:S(2)}) collective-permute-start(f32[16,16,256]{2,1,0:T(8,128)} %get-tuple-element.8), channel_id=1, source_target_pairs={{0,256},{256,0},{1,257},{257,1},{2,258},{258,2},{3,259},{259,3},{4... | collective-permute-start | bytes 786440 | tf_op jit(solution)/shard_map/ppermute | solution.py:284
  49.7 23.9 %collective-permute-done.4 = f32[16,16,256]{2,1,0:T(8,128)S(1)} collective-permute-done((f32[16,16,256]{2,1,0:T(8,128)}, f32[16,16,256]{2,1,0:T(8,128)S(1)}, u32[]{:S(2)}, u32[]{:S(2)}) %collective-permute-start.4) | collective-permute-done | bytes 262176 | tf_op jit(solution)/shard_map/ppermute | solution.py:284
  73.6 1.0 add_convert_fusion
  74.8 37.6 %all_to_all.5 = bf16[16,16,16,256]{3,2,1,0:T(8,128)(2,1)} all-to-all(bf16[16,16,16,256]{3,2,1,0:T(8,128)(2,1)S(1)} %broadcast_in_dim.14), channel_id=1, replica_groups=mesh['sec'=2,'gx'=16,'gy'=16] {'gy'}, dimensions={0} | all-to-all | bytes 4194304 | tf_op jit(solution)/shard_map/all_to_all | solution.py:288
  112.4 3.0 %shard_map.114 = (f32[256,256]{1,0:T(8,128)}, f32[256,256]{1,0:T(8,128)}) custom-call(s32[2,7]{1,0:T(2,128)} %cols_ref.1, bf16[16,256,256]{2,1,0:T(8,128)(2,1)} %bitcast.8, bf16[2,7,128,128]{3,2,1,0:T(8,128)(2,1)} %blocks_ref.1, f32[256,256]{1,0:T(8,128)} %bitcast.12, bf16[256,256]{1,0:T(8,128)(2,1)} %bitcast.13), custom_call_target="tpu_custom_call" | custom-call | flops 117440512 | bytes 3473408 | tf_op jit(solution)/shard_map/pallas_call | solution.py:236
  115.3 11.0 %collective-permute-start.5 = (f32[16,16,256]{2,1,0:T(8,128)}, f32[16,16,256]{2,1,0:T(8,128)S(1)}, u32[]{:S(2)}, u32[]{:S(2)}) collective-permute-start(f32[16,16,256]{2,1,0:T(8,128)} %bitcast.10), channel_id=1, source_target_pairs={{0,256},{256,0},{1,257},{257,1},{2,258},{258,2},{3,259},{259,3},{4... | collective-permute-start | bytes 786440 | tf_op jit(solution)/shard_map/ppermute | solution.py:299
  126.4 13.9 %collective-permute-done.5 = f32[16,16,256]{2,1,0:T(8,128)S(1)} collective-permute-done((f32[16,16,256]{2,1,0:T(8,128)}, f32[16,16,256]{2,1,0:T(8,128)S(1)}, u32[]{:S(2)}, u32[]{:S(2)}) %collective-permute-start.5) | collective-permute-done | bytes 262176 | tf_op jit(solution)/shard_map/ppermute | solution.py:299
  140.3 1.7 %add.7 = f32[16,16,256]{2,1,0:T(8,128)} add(f32[16,16,256]{2,1,0:T(8,128)} %bitcast.11, f32[16,16,256]{2,1,0:T(8,128)S(1)} %collective-permute-done.5) | non-fusion elementwise | flops 65536 | bytes 786432 | tf_op jit(solution)/shard_map/add | solution.py:299
  (20 shorter events, 2.0 us)
Async XLA Ops:
  3.0 6.9 %copy-start = (f32[6,16,16,256]{3,2,1,0:T(8,128)}, f32[6,16,16,256]{3,2,1,0:T(8,128)S(1)}, u32[]{:S(2)}) copy-start(f32[6,16,16,256]{3,2,1,0:T(8,128)S(1)} %pad_maximum_fusion.tile_ref) | copy-start | bytes 4718596
  4.1 7.2 %collective-permute-start.1 = (f32[6,16,2,256]{3,2,1,0:T(2,128)}, f32[6,16,2,256]{3,2,1,0:T(2,128)S(1)}, u32[]{:S(2)}, u32[]{:S(2)}) collective-permute-start(f32[6,16,2,256]{3,2,1,0:T(2,128)} %get-tuple-element.14), channel_id=1, source_target_pairs={{0,16},{16,32},{32,48},{48,64},{64,80},{80,96},{96,112},{112,128},... | collective-permute-start | bytes 589832 | tf_op jit(solution)/shard_map/ppermute | solution.py:272
  6.0 7.1 %collective-permute-start = (f32[6,16,2,256]{3,2,1,0:T(2,128)}, f32[6,16,2,256]{3,2,1,0:T(2,128)S(1)}, u32[]{:S(2)}, u32[]{:S(2)}) collective-permute-start(f32[6,16,2,256]{3,2,1,0:T(2,128)} %get-tuple-element.15), channel_id=1, source_target_pairs={{16,0},{32,16},{48,32},{64,48},{80,64},{96,80},{112,96},{128,112},... | collective-permute-start | bytes 589832 | tf_op jit(solution)/shard_map/ppermute | solution.py:271
  10.6 10.1 %copy-start.3 = (s32[2,8,3]{1,0,2:T(2,128)S(1)}, s32[2,8,3]{1,0,2:T(2,128)}, u32[]{:S(2)}) copy-start(s32[2,8,3]{1,0,2:T(2,128)} %param.15) | copy-start | bytes 580
  11.3 11.8 %copy-start.1 = (f32[6,16,2,256]{3,2,1,0:T(2,128)}, f32[6,16,2,256]{3,2,1,0:T(2,128)S(1)}, u32[]{:S(2)}) copy-start(f32[6,16,2,256]{3,2,1,0:T(2,128)S(1)} %collective-permute-done.1.before_ref) | copy-start | bytes 589828
  13.2 11.6 %copy-start.2 = (f32[6,16,2,256]{3,2,1,0:T(2,128)}, f32[6,16,2,256]{3,2,1,0:T(2,128)S(1)}, u32[]{:S(2)}) copy-start(f32[6,16,2,256]{3,2,1,0:T(2,128)S(1)} %collective-permute-done.after_ref) | copy-start | bytes 589828
  14.9 6.6 %collective-permute-start.2 = (f32[6,16,24,2]{2,1,3,0:T(8,128)S(1)}, f32[6,16,24,2]{2,1,3,0:T(8,128)S(1)}, u32[]{:S(2)}, u32[]{:S(2)}) collective-permute-start(f32[6,16,24,2]{2,1,3,0:T(8,128)S(1)} %get-tuple-element.21), channel_id=1, source_target_pairs={{1,0},{2,1},{3,2},{4,3},{5,4},{6,5},{7,6},{8,7},{9,8},{10,9},{11,1... | collective-permute-start | bytes 55304 | tf_op jit(solution)/shard_map/ppermute | solution.py:278
  16.2 6.9 %collective-permute-start.3 = (f32[6,16,24,2]{2,1,3,0:T(8,128)S(1)}, f32[6,16,24,2]{2,1,3,0:T(8,128)S(1)}, u32[]{:S(2)}, u32[]{:S(2)}) collective-permute-start(f32[6,16,24,2]{2,1,3,0:T(8,128)S(1)} %get-tuple-element.20), channel_id=1, source_target_pairs={{0,1},{1,2},{2,3},{3,4},{4,5},{5,6},{6,7},{7,8},{8,9},{9,10},{10,1... | collective-permute-start | bytes 55304 | tf_op jit(solution)/shard_map/ppermute | solution.py:279
  34.1 39.5 %collective-permute-start.4 = (f32[16,16,256]{2,1,0:T(8,128)}, f32[16,16,256]{2,1,0:T(8,128)S(1)}, u32[]{:S(2)}, u32[]{:S(2)}) collective-permute-start(f32[16,16,256]{2,1,0:T(8,128)} %get-tuple-element.8), channel_id=1, source_target_pairs={{0,256},{256,0},{1,257},{257,1},{2,258},{258,2},{3,259},{259,3},{4... | collective-permute-start | bytes 786440 | tf_op jit(solution)/shard_map/ppermute | solution.py:284
  115.3 25.0 %collective-permute-start.5 = (f32[16,16,256]{2,1,0:T(8,128)}, f32[16,16,256]{2,1,0:T(8,128)S(1)}, u32[]{:S(2)}, u32[]{:S(2)}) collective-permute-start(f32[16,16,256]{2,1,0:T(8,128)} %bitcast.10), channel_id=1, source_target_pairs={{0,256},{256,0},{1,257},{257,1},{2,258},{258,2},{3,259},{259,3},{4... | collective-permute-start | bytes 786440 | tf_op jit(solution)/shard_map/ppermute | solution.py:299

commit v17 on v14

--- a/solution.py
+++ b/solution.py
@@ -209,17 +209,28 @@
     return cells
 
 
-def head_kernel(cols_ref, gathered_ref, blocks_ref, heat_ref, grad_ref, head_ref, part_ref):
+def head_kernel(cols_ref, gathered_ref, blocks_ref, heat_ref, grad_ref, head_ref, part_ref, slabs, sems):
     row_blocks, per_row, size, _ = blocks_ref.shape
     halves = gathered_ref.shape[2] // size
+    copies = []
+    for row in range(row_blocks):
+        for k in range(per_row):
+            col = cols_ref[row, k]
+            start = pl.multiple_of((col % halves) * size, size)
+            copy = pltpu.make_async_copy(
+                gathered_ref.at[col // halves, :, pl.ds(start, size)],
+                slabs.at[row * per_row + k],
+                sems.at[row * per_row + k],
+            )
+            copy.start()
+            copies.append(copy)
     for row in range(row_blocks):
         total = jnp.zeros((gathered_ref.shape[1], size), jnp.float32)
         for k in range(per_row):
-            col = cols_ref[row, k]
-            start = pl.multiple_of((col % halves) * size, size)
-            slab = gathered_ref[col // halves, :, pl.ds(start, size)]
+            copies[row * per_row + k].wait()
             total = total + lax.dot_general(
-                slab, blocks_ref[row, k], (((1,), (1,)), ((), ())), preferred_element_type=jnp.float32
+                slabs[row * per_row + k], blocks_ref[row, k], (((1,), (1,)), ((), ())),
+                preferred_element_type=jnp.float32,
             )
         out = slice(row * size, (row + 1) * size)
         head_ref[:, out] = total
@@ -235,8 +246,13 @@
             jax.ShapeDtypeStruct((cells, width), jnp.float32),
             jax.ShapeDtypeStruct((cells, width), jnp.float32),
         ),
-        in_specs=[pl.BlockSpec(memory_space=pltpu.SMEM)] + [pl.BlockSpec(memory_space=vmem)] * 4,
+        in_specs=[pl.BlockSpec(memory_space=pltpu.SMEM), pl.BlockSpec(memory_space=pl.ANY)]
+        + [pl.BlockSpec(memory_space=vmem)] * 3,
         out_specs=(pl.BlockSpec(memory_space=vmem), pl.BlockSpec(memory_space=vmem)),
+        scratch_shapes=[
+            pltpu.VMEM((blocks.shape[0] * blocks.shape[1], cells, blocks.shape[2]), gathered.dtype),
+            pltpu.SemaphoreType.DMA((blocks.shape[0] * blocks.shape[1],)),
+        ],
         cost_estimate=pl.CostEstimate(
             flops=2 * cells * width * blocks.shape[1] * blocks.shape[2],
             bytes_accessed=gathered.size * 2 + blocks.size * 2 + cells * width * 14,

time: 138 us -> 140 us (1.014)
  no operation moved by 1% of the time
where the time goes in v17:
time: 140 us; the launch traced here: 139 us
  waiting for transfers between devices  48.2 us (34%)
  starting transfers between devices  34.5 us (25%)
  blocking collectives  28 us (20%)
  Pallas kernels  12.9 us (9%)
  local copies, waits for them, and re-layouts  7.97 us (6%)
  other arithmetic  6.64 us (5%)
    all_to_all x1, blocking collectives, shards(): gathered = lax.all_to_all(copies, 'gy', 0, 0, tiled=False)  28 us
    ppermute x1, waiting for transfers between devices, shards(): sensitivity = partial_sens + lax.ppermute(partial_sens, 'sec', partner)  20.8 us
    ppermute x1, waiting for transfers between devices, shards(): rounded = (mine + lax.ppermute(other, 'sec', partner)).astype(jnp.bfloat16)  20.5 us
    ppermute x1, starting transfers between devices, shards(): sensitivity = partial_sens + lax.ppermute(partial_sens, 'sec', partner)  13 us
    ppermute x1, starting transfers between devices, shards(): rounded = (mine + lax.ppermute(other, 'sec', partner)).astype(jnp.bfloat16)  11.4 us
    pallas_call x1, Pallas kernels, heat_phase(): pl.pallas_call(heat_kernel, out_shape=(out, out, out), in_specs=[smem, sm...  8.86 us
    ppermute x1, waiting for transfers between devices, shards(): lax.ppermute(packed[:, :, rows_x - width:], 'gx', [(i, i + 1) for i in ra...  6.13 us
    ppermute x1, starting transfers between devices, shards(): lax.ppermute(column(slice(cols_y - width, cols_y)), 'gy', [(i, i + 1) for...  4.55 us
  transfers between devices with their start and end apart: 6, of which 4 were waited for; matrix products, arithmetic and copies ran while one was open for 3% of the time, Pallas kernels for 0%

profile of v17, /device:TPU:32, one launch (start us, length us, event | category | flops | bytes accessed | tf_op | source)
XLA Modules:
  0.0 139.1 jit_solution(16002681711092240502)
XLA Ops:
  0.6 1.0 subtract_bitcast_fusion
  1.6 1.4 %pad_maximum_fusion.tile_ref = f32[6,16,16,256]{3,2,1,0:T(8,128)S(1)} fusion(f32[1,16,16,256]{3,2,1,0:T(8,128)S(1)} %subtract_bitcast_fusion, f32[2,16,16,256]{3,2,1,0:T(8,128)} %param.13, f32[1,16,16,256]{3,2,1,0:T(8,128)} %bitcast.9, f32[2,16,16,256]{3,2,1,0:T(8,128)} %param.10), kind=kLoop, calls=%fused_computation | loop fusion | flops 1179648 | bytes 3145728 | tf_op jit(solution)/shard_map/concatenate | solution.py:278
  3.0 1.0 fusion.1
  4.1 1.9 %collective-permute-start = (f32[6,16,2,256]{3,2,1,0:T(2,128)}, f32[6,16,2,256]{3,2,1,0:T(2,128)S(1)}, u32[]{:S(2)}, u32[]{:S(2)}) collective-permute-start(f32[6,16,2,256]{3,2,1,0:T(2,128)} %get-tuple-element.15), channel_id=1, source_target_pairs={{16,0},{32,16},{48,32},{64,48},{80,64},{96,80},{112,96},{128,112},... | collective-permute-start | bytes 589832 | tf_op jit(solution)/shard_map/ppermute | solution.py:283
  6.0 2.4 %collective-permute-start.1 = (f32[6,16,2,256]{3,2,1,0:T(2,128)}, f32[6,16,2,256]{3,2,1,0:T(2,128)S(1)}, u32[]{:S(2)}, u32[]{:S(2)}) collective-permute-start(f32[6,16,2,256]{3,2,1,0:T(2,128)} %get-tuple-element.14), channel_id=1, source_target_pairs={{0,16},{16,32},{32,48},{48,64},{64,80},{80,96},{96,112},{112,128},... | collective-permute-start | bytes 589832 | tf_op jit(solution)/shard_map/ppermute | solution.py:284
  10.2 0.7 copy.14
  10.9 6.1 %collective-permute-done.1.before_ref = f32[6,16,2,256]{3,2,1,0:T(2,128)S(1)} collective-permute-done((f32[6,16,2,256]{3,2,1,0:T(2,128)}, f32[6,16,2,256]{3,2,1,0:T(2,128)S(1)}, u32[]{:S(2)}, u32[]{:S(2)}) %collective-permute-start.1) | collective-permute-done | bytes 196640 | tf_op jit(solution)/shard_map/ppermute | solution.py:284
  17.2 0.7 copy.15
  17.9 0.7 copy.17
  18.6 0.7 copy.18
  19.4 1.3 collective-permute-start.2
  20.7 4.6 %collective-permute-start.3 = (f32[6,16,24,2]{2,1,3,0:T(8,128)S(1)}, f32[6,16,24,2]{2,1,3,0:T(8,128)S(1)}, u32[]{:S(2)}, u32[]{:S(2)}) collective-permute-start(f32[6,16,24,2]{2,1,3,0:T(8,128)S(1)} %get-tuple-element.21), channel_id=1, source_target_pairs={{0,1},{1,2},{2,3},{3,4},{4,5},{5,6},{6,7},{7,8},{8,9},{9,10},{10,1... | collective-permute-start | bytes 55304 | tf_op jit(solution)/shard_map/ppermute | solution.py:294
  25.4 0.7 copy.21.wells_ref
  26.7 0.8 collective-permute-done.3
  28.1 1.4 %pad_maximum_fusion.1.side_ref = f32[6,16,24,128]{3,2,1,0:T(8,128)} fusion(f32[6,16,24,2]{3,2,1,0:T(8,128)S(1)} %copy.20, f32[6,16,24,2]{3,2,1,0:T(8,128)S(1)} %copy.19, f32[128]{0:T(128)S(1)} %pad.1.clone), kind=kLoop, calls=%fused_computation.1 | loop fusion | flops 589824 | bytes 1217024 | tf_op jit(solution)/shard_map/concatenate | solution.py:290
  29.5 8.9 %shard_map.113 = (f32[16,16,256]{2,1,0:T(8,128)}, f32[16,16,256]{2,1,0:T(8,128)}, f32[16,16,256]{2,1,0:T(8,128)}) custom-call(s32[2,8,3]{2,1,0:T(8,128)} %copy.21.wells_ref, f32[2,2,8]{2,1,0:T(2,128)} %misfit_ref.1, f32[6,16,16,256]{3,2,1,0:T(8,128)} %copy-done, f32[6,16,2,256]{3,2,1,0:T(2,128)} %copy-done.1, f32[6,16,2,256]{3,2,1,0:T(2,128)} %copy-done.2, ...), custom_call_target="tpu_custom_call" | custom-call | tf_op jit(solution)/shard_map/pallas_call | solution.py:179
  38.4 11.4 %collective-permute-start.4 = (f32[16,16,256]{2,1,0:T(8,128)}, f32[16,16,256]{2,1,0:T(8,128)S(1)}, u32[]{:S(2)}, u32[]{:S(2)}) collective-permute-start(f32[16,16,256]{2,1,0:T(8,128)} %get-tuple-element.8), channel_id=1, source_target_pairs={{0,256},{256,0},{1,257},{257,1},{2,258},{258,2},{3,259},{259,3},{4... | collective-permute-start | bytes 786440 | tf_op jit(solution)/shard_map/ppermute | solution.py:302
  49.8 20.5 %collective-permute-done.4 = f32[16,16,256]{2,1,0:T(8,128)S(1)} collective-permute-done((f32[16,16,256]{2,1,0:T(8,128)}, f32[16,16,256]{2,1,0:T(8,128)S(1)}, u32[]{:S(2)}, u32[]{:S(2)}) %collective-permute-start.4) | collective-permute-done | bytes 262176 | tf_op jit(solution)/shard_map/ppermute | solution.py:302
  70.3 1.0 add_convert_fusion
  71.5 28.0 %all_to_all.5 = bf16[16,16,16,256]{3,2,1,0:T(8,128)(2,1)} all-to-all(bf16[16,16,16,256]{3,2,1,0:T(8,128)(2,1)S(1)} %broadcast_in_dim.18), channel_id=1, replica_groups=mesh['sec'=2,'gx'=16,'gy'=16] {'gy'}, dimensions={0} | all-to-all | bytes 4194304 | tf_op jit(solution)/shard_map/all_to_all | solution.py:306
  99.5 4.1 %shard_map.114 = (f32[256,256]{1,0:T(8,128)}, f32[256,256]{1,0:T(8,128)}) custom-call(s32[2,7]{1,0:T(2,128)} %cols_ref.1, bf16[16,256,256]{2,1,0:T(8,128)(2,1)} %bitcast.8, bf16[2,7,128,128]{3,2,1,0:T(8,128)(2,1)} %blocks_ref.1, f32[256,256]{1,0:T(8,128)} %bitcast.12, bf16[256,256]{1,0:T(8,128)(2,1)} %bitcast.13), custom_call_target="tpu_custom_call" | custom-call | flops 117440512 | bytes 3473408 | tf_op jit(solution)/shard_map/pallas_call | solution.py:243
  103.6 13.0 %collective-permute-start.5 = (f32[16,16,256]{2,1,0:T(8,128)}, f32[16,16,256]{2,1,0:T(8,128)S(1)}, u32[]{:S(2)}, u32[]{:S(2)}) collective-permute-start(f32[16,16,256]{2,1,0:T(8,128)} %bitcast.10), channel_id=1, source_target_pairs={{0,256},{256,0},{1,257},{257,1},{2,258},{258,2},{3,259},{259,3},{4... | collective-permute-start | bytes 786440 | tf_op jit(solution)/shard_map/ppermute | solution.py:317
  116.6 20.8 %collective-permute-done.5 = f32[16,16,256]{2,1,0:T(8,128)S(1)} collective-permute-done((f32[16,16,256]{2,1,0:T(8,128)}, f32[16,16,256]{2,1,0:T(8,128)S(1)}, u32[]{:S(2)}, u32[]{:S(2)}) %collective-permute-start.5) | collective-permute-done | bytes 262176 | tf_op jit(solution)/shard_map/ppermute | solution.py:317
  137.4 1.7 %add.7 = f32[16,16,256]{2,1,0:T(8,128)} add(f32[16,16,256]{2,1,0:T(8,128)} %bitcast.11, f32[16,16,256]{2,1,0:T(8,128)S(1)} %collective-permute-done.5) | non-fusion elementwise | flops 65536 | bytes 786432 | tf_op jit(solution)/shard_map/add | solution.py:317
  (23 shorter events, 3.7 us)
Async XLA Ops:
  3.0 5.7 %copy-start = (f32[6,16,16,256]{3,2,1,0:T(8,128)}, f32[6,16,16,256]{3,2,1,0:T(8,128)S(1)}, u32[]{:S(2)}) copy-start(f32[6,16,16,256]{3,2,1,0:T(8,128)S(1)} %pad_maximum_fusion.tile_ref) | copy-start | bytes 4718596
  4.1 6.0 %collective-permute-start = (f32[6,16,2,256]{3,2,1,0:T(2,128)}, f32[6,16,2,256]{3,2,1,0:T(2,128)S(1)}, u32[]{:S(2)}, u32[]{:S(2)}) collective-permute-start(f32[6,16,2,256]{3,2,1,0:T(2,128)} %get-tuple-element.15), channel_id=1, source_target_pairs={{16,0},{32,16},{48,32},{64,48},{80,64},{96,80},{112,96},{128,112},... | collective-permute-start | bytes 589832 | tf_op jit(solution)/shard_map/ppermute | solution.py:283
  6.0 11.1 %collective-permute-start.1 = (f32[6,16,2,256]{3,2,1,0:T(2,128)}, f32[6,16,2,256]{3,2,1,0:T(2,128)S(1)}, u32[]{:S(2)}, u32[]{:S(2)}) collective-permute-start(f32[6,16,2,256]{3,2,1,0:T(2,128)} %get-tuple-element.14), channel_id=1, source_target_pairs={{0,16},{16,32},{32,48},{48,64},{64,80},{80,96},{96,112},{112,128},... | collective-permute-start | bytes 589832 | tf_op jit(solution)/shard_map/ppermute | solution.py:284
  9.3 16.1 %copy-start.3 = (s32[2,8,3]{1,0,2:T(2,128)S(1)}, s32[2,8,3]{1,0,2:T(2,128)}, u32[]{:S(2)}) copy-start(s32[2,8,3]{1,0,2:T(2,128)} %param.15) | copy-start | bytes 580
  10.0 16.7 %copy-start.1 = (f32[6,16,2,256]{3,2,1,0:T(2,128)}, f32[6,16,2,256]{3,2,1,0:T(2,128)S(1)}, u32[]{:S(2)}) copy-start(f32[6,16,2,256]{3,2,1,0:T(2,128)S(1)} %collective-permute-done.after_ref) | copy-start | bytes 589828
  17.0 11.1 %copy-start.2 = (f32[6,16,2,256]{3,2,1,0:T(2,128)}, f32[6,16,2,256]{3,2,1,0:T(2,128)S(1)}, u32[]{:S(2)}) copy-start(f32[6,16,2,256]{3,2,1,0:T(2,128)S(1)} %collective-permute-done.1.before_ref) | copy-start | bytes 589828
  19.4 6.6 %collective-permute-start.2 = (f32[6,16,24,2]{2,1,3,0:T(8,128)S(1)}, f32[6,16,24,2]{2,1,3,0:T(8,128)S(1)}, u32[]{:S(2)}, u32[]{:S(2)}) collective-permute-start(f32[6,16,24,2]{2,1,3,0:T(8,128)S(1)} %get-tuple-element.20), channel_id=1, source_target_pairs={{1,0},{2,1},{3,2},{4,3},{5,4},{6,5},{7,6},{8,7},{9,8},{10,9},{11,1... | collective-permute-start | bytes 55304 | tf_op jit(solution)/shard_map/ppermute | solution.py:292
  20.7 6.8 %collective-permute-start.3 = (f32[6,16,24,2]{2,1,3,0:T(8,128)S(1)}, f32[6,16,24,2]{2,1,3,0:T(8,128)S(1)}, u32[]{:S(2)}, u32[]{:S(2)}) collective-permute-start(f32[6,16,24,2]{2,1,3,0:T(8,128)S(1)} %get-tuple-element.21), channel_id=1, source_target_pairs={{0,1},{1,2},{2,3},{3,4},{4,5},{5,6},{6,7},{7,8},{8,9},{9,10},{10,1... | collective-permute-start | bytes 55304 | tf_op jit(solution)/shard_map/ppermute | solution.py:294
  38.4 31.9 %collective-permute-start.4 = (f32[16,16,256]{2,1,0:T(8,128)}, f32[16,16,256]{2,1,0:T(8,128)S(1)}, u32[]{:S(2)}, u32[]{:S(2)}) collective-permute-start(f32[16,16,256]{2,1,0:T(8,128)} %get-tuple-element.8), channel_id=1, source_target_pairs={{0,256},{256,0},{1,257},{257,1},{2,258},{258,2},{3,259},{259,3},{4... | collective-permute-start | bytes 786440 | tf_op jit(solution)/shard_map/ppermute | solution.py:302
  103.6 33.8 %collective-permute-start.5 = (f32[16,16,256]{2,1,0:T(8,128)}, f32[16,16,256]{2,1,0:T(8,128)S(1)}, u32[]{:S(2)}, u32[]{:S(2)}) collective-permute-start(f32[16,16,256]{2,1,0:T(8,128)} %bitcast.10), channel_id=1, source_target_pairs={{0,256},{256,0},{1,257},{257,1},{2,258},{258,2},{3,259},{259,3},{4... | collective-permute-start | bytes 786440 | tf_op jit(solution)/shard_map/ppermute | solution.py:317

commit v18 on v14

--- a/solution.py
+++ b/solution.py
@@ -267,15 +267,25 @@
     after = lax.ppermute(packed[:, :, :width], "gx", [(i + 1, i) for i in range(ends_x)])
     before = lax.ppermute(packed[:, :, rows_x - width:], "gx", [(i, i + 1) for i in range(ends_x)])
 
+    picks = jnp.concatenate(
+        [jnp.arange(width), jnp.arange(cols_y - width, cols_y)]
+    )[None, :] == jnp.arange(cols_y)[:, None]
+    picks = picks.astype(jnp.float32)
+
+    def edges(part):
+        return jnp.einsum("czxy,ye->czxe", part, picks, precision=lax.Precision.HIGHEST)
+
+    gap = jnp.zeros(packed.shape[:2] + (sizes[0] - rows_x - 2 * width, 2 * width), packed.dtype)
+    strips = jnp.concatenate([edges(packed), edges(after), gap, edges(before)], axis=2)
+
     def column(cut):
-        gap = jnp.zeros(packed.shape[:2] + (sizes[0] - rows_x - 2 * width, width), packed.dtype)
-        return jnp.concatenate([packed[..., cut], after[..., cut], gap, before[..., cut]], axis=2)
+        return strips[..., cut]
 
     side = jnp.concatenate(
         [
             lax.ppermute(column(slice(0, width)), "gy", [(i + 1, i) for i in range(ends_y)]),
             jnp.zeros(packed.shape[:2] + (sizes[0], sizes[1] - cols_y - 2 * width), packed.dtype),
-            lax.ppermute(column(slice(cols_y - width, cols_y)), "gy", [(i, i + 1) for i in range(ends_y)]),
+            lax.ppermute(column(slice(width, 2 * width)), "gy", [(i, i + 1) for i in range(ends_y)]),
         ],
         axis=3,
     )

time: 138 us -> 138 us (level)
  the two profiles are of different devices: /device:TPU:32 before, /device:TPU:96 now
where the time goes in v18:
time: 138 us; the launch traced here: 137 us
  waiting for transfers between devices  39.4 us (29%)
  blocking collectives  38.5 us (28%)
  starting transfers between devices  33.1 us (24%)
  Pallas kernels  11.8 us (9%)
  other arithmetic  6.71 us (5%)
  matrix products  3.83 us (3%)
  local copies, waits for them, and re-layouts  2.95 us (2%)
    all_to_all x1, blocking collectives, shards(): gathered = lax.all_to_all(copies, 'gy', 0, 0, tiled=False)  38.5 us
    ppermute x1, waiting for transfers between devices, shards(): rounded = (mine + lax.ppermute(other, 'sec', partner)).astype(jnp.bfloat16)  22.3 us
    ppermute x1, waiting for transfers between devices, shards(): sensitivity = partial_sens + lax.ppermute(partial_sens, 'sec', partner)  15.3 us
    ppermute x1, starting transfers between devices, shards(): rounded = (mine + lax.ppermute(other, 'sec', partner)).astype(jnp.bfloat16)  14 us
    ppermute x1, starting transfers between devices, shards(): sensitivity = partial_sens + lax.ppermute(partial_sens, 'sec', partner)  8.98 us
    pallas_call x1, Pallas kernels, heat_phase(): pl.pallas_call(heat_kernel, out_shape=(out, out, out), in_specs=[smem, sm...  8.85 us
    ppermute x1, starting transfers between devices, shards(): lax.ppermute(column(slice(width, 2 * width)), 'gy', [(i, i + 1) for i in...  4.55 us
    dot_general x3, matrix products, edges(): jnp.einsum('czxy,ye->czxe', part, picks, precision=lax.Precision.HIGHEST)  3.83 us
  transfers between devices with their start and end apart: 6, of which 4 were waited for; matrix products, arithmetic and copies ran while one was open for 4% of the time, Pallas kernels for 0%

profile of v18, /device:TPU:96, one launch (start us, length us, event | category | flops | bytes accessed | tf_op | source)
XLA Modules:
  0.0 137.1 jit_solution(7385571630207294121)
XLA Ops:
  0.6 1.0 subtract_bitcast_fusion
  1.6 1.4 %pad_maximum_fusion.tile_ref = f32[6,16,16,256]{3,2,1,0:T(8,128)S(1)} fusion(f32[1,16,16,256]{3,2,1,0:T(8,128)S(1)} %subtract_bitcast_fusion, f32[2,16,16,256]{3,2,1,0:T(8,128)} %param.13, f32[1,16,16,256]{3,2,1,0:T(8,128)} %bitcast.17, f32[2,16,16,256]{3,2,1,0:T(8,128)} %param.10), kind=kLoop, calls=%fused_computation | loop fusion | flops 1179648 | bytes 3145728 | tf_op jit(solution)/shard_map/concatenate | solution.py:262
  3.2 1.9 %collective-permute-start = (f32[6,16,2,256]{3,2,1,0:T(2,128)S(1)}, f32[6,16,2,256]{3,2,1,0:T(2,128)S(1)}, u32[]{:S(2)}, u32[]{:S(2)}) collective-permute-start(f32[6,16,2,256]{3,2,1,0:T(2,128)S(1)} %get-tuple-element.13), channel_id=1, source_target_pairs={{16,0},{32,16},{48,32},{64,48},{80,64},{96,80},{112,96},{128,112},... | collective-permute-start | bytes 589832 | tf_op jit(solution)/shard_map/ppermute | solution.py:267
  5.1 2.4 %collective-permute-start.1 = (f32[6,16,2,256]{3,2,1,0:T(2,128)S(1)}, f32[6,16,2,256]{3,2,1,0:T(2,128)S(1)}, u32[]{:S(2)}, u32[]{:S(2)}) collective-permute-start(f32[6,16,2,256]{3,2,1,0:T(2,128)S(1)} %get-tuple-element.12), channel_id=1, source_target_pairs={{0,16},{16,32},{32,48},{48,64},{64,80},{80,96},{96,112},{112,128},... | collective-permute-start | bytes 589832 | tf_op jit(solution)/shard_map/ppermute | solution.py:268
  7.6 2.9 %fusion.7 = f32[6,16,16,4]{2,3,1,0:T(4,128)S(1)} fusion(f32[6,16,16,256]{3,2,1,0:T(8,128)S(1)} %pad_maximum_fusion.tile_ref, s32[4]{0:T(128)S(1)} %pad_add_fusion), kind=kOutput, calls=%fused_computation.13 | convolution fusion | flops 18875392 | bytes 1597456 | tf_op jit(solution)/shard_map/czxy,ye->czxe/dot_general | solution.py:276
  10.6 0.5 fusion.2
  11.3 0.8 collective-permute-done.1.before_ref
  12.1 0.5 fusion
  13.0 1.3 collective-permute-start.2
  14.3 4.6 %collective-permute-start.3 = (f32[6,16,24,2]{2,1,3,0:T(8,128)S(1)}, f32[6,16,24,2]{2,1,3,0:T(8,128)S(1)}, u32[]{:S(2)}, u32[]{:S(2)}) collective-permute-start(f32[6,16,24,2]{2,1,3,0:T(8,128)S(1)} %get-tuple-element.15), channel_id=1, source_target_pairs={{0,1},{1,2},{2,3},{3,4},{4,5},{5,6},{6,7},{7,8},{8,9},{9,10},{10,1... | collective-permute-start | bytes 55304 | tf_op jit(solution)/shard_map/ppermute | solution.py:288
  19.0 0.7 copy.25.wells_ref
  19.6 0.6 copy.23
  20.3 1.1 collective-permute-done.3
  21.3 0.6 copy.24
  22.0 1.4 %pad_maximum_fusion.1.side_ref = f32[6,16,24,128]{3,2,1,0:T(8,128)} fusion(f32[6,16,24,2]{3,2,1,0:T(8,128)S(1)} %copy.24, f32[6,16,24,2]{3,2,1,0:T(8,128)S(1)} %copy.23, f32[128]{0:T(128)S(1)} %pad.1.clone), kind=kLoop, calls=%fused_computation.1 | loop fusion | flops 589824 | bytes 1217024 | tf_op jit(solution)/shard_map/concatenate | solution.py:284
  23.4 8.9 %shard_map.113 = (f32[16,16,256]{2,1,0:T(8,128)}, f32[16,16,256]{2,1,0:T(8,128)}, f32[16,16,256]{2,1,0:T(8,128)}) custom-call(s32[2,8,3]{2,1,0:T(8,128)} %copy.25.wells_ref, f32[2,2,8]{2,1,0:T(2,128)} %misfit_ref.1, f32[6,16,16,256]{3,2,1,0:T(8,128)} %copy-done, f32[6,16,2,256]{3,2,1,0:T(2,128)} %copy-done.1, f32[6,16,2,256]{3,2,1,0:T(2,128)} %copy-done.2, ...), custom_call_target="tpu_custom_call" | custom-call | tf_op jit(solution)/shard_map/pallas_call | solution.py:179
  32.2 14.0 %collective-permute-start.4 = (f32[16,16,256]{2,1,0:T(8,128)}, f32[16,16,256]{2,1,0:T(8,128)S(1)}, u32[]{:S(2)}, u32[]{:S(2)}) collective-permute-start(f32[16,16,256]{2,1,0:T(8,128)} %get-tuple-element.8), channel_id=1, source_target_pairs={{0,256},{256,0},{1,257},{257,1},{2,258},{258,2},{3,259},{259,3},{4... | collective-permute-start | bytes 786440 | tf_op jit(solution)/shard_map/ppermute | solution.py:296
  46.2 22.3 %collective-permute-done.4 = f32[16,16,256]{2,1,0:T(8,128)S(1)} collective-permute-done((f32[16,16,256]{2,1,0:T(8,128)}, f32[16,16,256]{2,1,0:T(8,128)S(1)}, u32[]{:S(2)}, u32[]{:S(2)}) %collective-permute-start.4) | collective-permute-done | bytes 262176 | tf_op jit(solution)/shard_map/ppermute | solution.py:296
  68.5 1.0 add_convert_fusion
  69.7 38.5 %all_to_all.5 = bf16[16,16,16,256]{3,2,1,0:T(8,128)(2,1)} all-to-all(bf16[16,16,16,256]{3,2,1,0:T(8,128)(2,1)S(1)} %broadcast_in_dim.24), channel_id=1, replica_groups=mesh['sec'=2,'gx'=16,'gy'=16] {'gy'}, dimensions={0} | all-to-all | bytes 4194304 | tf_op jit(solution)/shard_map/all_to_all | solution.py:300
  108.2 2.9 %shard_map.114 = (f32[256,256]{1,0:T(8,128)}, f32[256,256]{1,0:T(8,128)}) custom-call(s32[2,7]{1,0:T(2,128)} %cols_ref.1, bf16[16,256,256]{2,1,0:T(8,128)(2,1)} %bitcast.16, bf16[2,7,128,128]{3,2,1,0:T(8,128)(2,1)} %blocks_ref.1, f32[256,256]{1,0:T(8,128)} %bitcast.20, bf16[256,256]{1,0:T(8,128)(2,1)} %bitcast.21), custom_call_target="tpu_custom_call" | custom-call | flops 117440512 | bytes 3473408 | tf_op jit(solution)/shard_map/pallas_call | solution.py:232
  111.2 9.0 %collective-permute-start.5 = (f32[16,16,256]{2,1,0:T(8,128)}, f32[16,16,256]{2,1,0:T(8,128)S(1)}, u32[]{:S(2)}, u32[]{:S(2)}) collective-permute-start(f32[16,16,256]{2,1,0:T(8,128)} %bitcast.18), channel_id=1, source_target_pairs={{0,256},{256,0},{1,257},{257,1},{2,258},{258,2},{3,259},{259,3},{4... | collective-permute-start | bytes 786440 | tf_op jit(solution)/shard_map/ppermute | solution.py:311
  120.2 15.3 %collective-permute-done.5 = f32[16,16,256]{2,1,0:T(8,128)S(1)} collective-permute-done((f32[16,16,256]{2,1,0:T(8,128)}, f32[16,16,256]{2,1,0:T(8,128)S(1)}, u32[]{:S(2)}, u32[]{:S(2)}) %collective-permute-start.5) | collective-permute-done | bytes 262176 | tf_op jit(solution)/shard_map/ppermute | solution.py:311
  135.5 1.7 %add.11 = f32[16,16,256]{2,1,0:T(8,128)} add(f32[16,16,256]{2,1,0:T(8,128)} %bitcast.19, f32[16,16,256]{2,1,0:T(8,128)S(1)} %collective-permute-done.5) | non-fusion elementwise | flops 65536 | bytes 786432 | tf_op jit(solution)/shard_map/add | solution.py:311
  (24 shorter events, 1.3 us)
Async XLA Ops:
  3.0 8.1 %copy-start = (f32[6,16,16,256]{3,2,1,0:T(8,128)}, f32[6,16,16,256]{3,2,1,0:T(8,128)S(1)}, u32[]{:S(2)}) copy-start(f32[6,16,16,256]{3,2,1,0:T(8,128)S(1)} %pad_maximum_fusion.tile_ref) | copy-start | bytes 4718596
  3.2 7.4 %collective-permute-start = (f32[6,16,2,256]{3,2,1,0:T(2,128)S(1)}, f32[6,16,2,256]{3,2,1,0:T(2,128)S(1)}, u32[]{:S(2)}, u32[]{:S(2)}) collective-permute-start(f32[6,16,2,256]{3,2,1,0:T(2,128)S(1)} %get-tuple-element.13), channel_id=1, source_target_pairs={{16,0},{32,16},{48,32},{64,48},{80,64},{96,80},{112,96},{128,112},... | collective-permute-start | bytes 589832 | tf_op jit(solution)/shard_map/ppermute | solution.py:267
  5.1 7.0 %collective-permute-start.1 = (f32[6,16,2,256]{3,2,1,0:T(2,128)S(1)}, f32[6,16,2,256]{3,2,1,0:T(2,128)S(1)}, u32[]{:S(2)}, u32[]{:S(2)}) collective-permute-start(f32[6,16,2,256]{3,2,1,0:T(2,128)S(1)} %get-tuple-element.12), channel_id=1, source_target_pairs={{0,16},{16,32},{32,48},{48,64},{64,80},{80,96},{96,112},{112,128},... | collective-permute-start | bytes 589832 | tf_op jit(solution)/shard_map/ppermute | solution.py:268
  10.5 8.5 %copy-start.3 = (s32[2,8,3]{1,0,2:T(2,128)S(1)}, s32[2,8,3]{1,0,2:T(2,128)}, u32[]{:S(2)}) copy-start(s32[2,8,3]{1,0,2:T(2,128)} %param.15) | copy-start | bytes 580
  10.6 9.7 %copy-start.1 = (f32[6,16,2,256]{3,2,1,0:T(2,128)}, f32[6,16,2,256]{3,2,1,0:T(2,128)S(1)}, u32[]{:S(2)}) copy-start(f32[6,16,2,256]{3,2,1,0:T(2,128)S(1)} %collective-permute-done.after_ref) | copy-start | bytes 589828
  12.1 9.9 %copy-start.2 = (f32[6,16,2,256]{3,2,1,0:T(2,128)}, f32[6,16,2,256]{3,2,1,0:T(2,128)S(1)}, u32[]{:S(2)}) copy-start(f32[6,16,2,256]{3,2,1,0:T(2,128)S(1)} %collective-permute-done.1.before_ref) | copy-start | bytes 589828
  13.0 6.6 %collective-permute-start.2 = (f32[6,16,24,2]{2,1,3,0:T(8,128)S(1)}, f32[6,16,24,2]{2,1,3,0:T(8,128)S(1)}, u32[]{:S(2)}, u32[]{:S(2)}) collective-permute-start(f32[6,16,24,2]{2,1,3,0:T(8,128)S(1)} %get-tuple-element.14), channel_id=1, source_target_pairs={{1,0},{2,1},{3,2},{4,3},{5,4},{6,5},{7,6},{8,7},{9,8},{10,9},{11,1... | collective-permute-start | bytes 55304 | tf_op jit(solution)/shard_map/ppermute | solution.py:286
  14.3 7.0 %collective-permute-start.3 = (f32[6,16,24,2]{2,1,3,0:T(8,128)S(1)}, f32[6,16,24,2]{2,1,3,0:T(8,128)S(1)}, u32[]{:S(2)}, u32[]{:S(2)}) collective-permute-start(f32[6,16,24,2]{2,1,3,0:T(8,128)S(1)} %get-tuple-element.15), channel_id=1, source_target_pairs={{0,1},{1,2},{2,3},{3,4},{4,5},{5,6},{6,7},{7,8},{8,9},{9,10},{10,1... | collective-permute-start | bytes 55304 | tf_op jit(solution)/shard_map/ppermute | solution.py:288
  32.2 36.3 %collective-permute-start.4 = (f32[16,16,256]{2,1,0:T(8,128)}, f32[16,16,256]{2,1,0:T(8,128)S(1)}, u32[]{:S(2)}, u32[]{:S(2)}) collective-permute-start(f32[16,16,256]{2,1,0:T(8,128)} %get-tuple-element.8), channel_id=1, source_target_pairs={{0,256},{256,0},{1,257},{257,1},{2,258},{258,2},{3,259},{259,3},{4... | collective-permute-start | bytes 786440 | tf_op jit(solution)/shard_map/ppermute | solution.py:296
  111.2 24.3 %collective-permute-start.5 = (f32[16,16,256]{2,1,0:T(8,128)}, f32[16,16,256]{2,1,0:T(8,128)S(1)}, u32[]{:S(2)}, u32[]{:S(2)}) collective-permute-start(f32[16,16,256]{2,1,0:T(8,128)} %bitcast.18), channel_id=1, source_target_pairs={{0,256},{256,0},{1,257},{257,1},{2,258},{258,2},{3,259},{259,3},{4... | collective-permute-start | bytes 786440 | tf_op jit(solution)/shard_map/ppermute | solution.py:311

commit v19 on v18

--- a/solution.py
+++ b/solution.py
@@ -264,8 +264,13 @@
     sizes = (-(-(rows_x + 2 * width) // 8) * 8, -(-(cols_y + 2 * width) // 128) * 128)
     ends_x = lax.axis_size("gx") - 1
     ends_y = lax.axis_size("gy") - 1
-    after = lax.ppermute(packed[:, :, :width], "gx", [(i + 1, i) for i in range(ends_x)])
-    before = lax.ppermute(packed[:, :, rows_x - width:], "gx", [(i, i + 1) for i in range(ends_x)])
+    rows_pick = (
+        jnp.concatenate([jnp.arange(width), jnp.arange(rows_x - width, rows_x)])[None, :]
+        == jnp.arange(rows_x)[:, None]
+    ).astype(jnp.float32)
+    rims = jnp.einsum("czxy,xe->czey", packed, rows_pick, precision=lax.Precision.HIGHEST)
+    after = lax.ppermute(rims[:, :, :width], "gx", [(i + 1, i) for i in range(ends_x)])
+    before = lax.ppermute(rims[:, :, width:], "gx", [(i, i + 1) for i in range(ends_x)])
 
     picks = jnp.concatenate(
         [jnp.arange(width), jnp.arange(cols_y - width, cols_y)]

time: 138 us -> 138 us (level)
  no operation moved by 1% of the time
where the time goes in v19:
time: 138 us; the launch traced here: 137 us
  waiting for transfers between devices  39.3 us (28%)
  blocking collectives  38.2 us (28%)
  starting transfers between devices  33.2 us (24%)
  Pallas kernels  11.8 us (9%)
  other arithmetic  6.7 us (5%)
  matrix products  4.47 us (3%)
  local copies, waits for them, and re-layouts  2.98 us (2%)
    all_to_all x1, blocking collectives, shards(): gathered = lax.all_to_all(copies, 'gy', 0, 0, tiled=False)  38.2 us
    ppermute x1, waiting for transfers between devices, shards(): rounded = (mine + lax.ppermute(other, 'sec', partner)).astype(jnp.bfloat16)  22.2 us
    ppermute x1, waiting for transfers between devices, shards(): sensitivity = partial_sens + lax.ppermute(partial_sens, 'sec', partner)  15 us
    ppermute x1, starting transfers between devices, shards(): rounded = (mine + lax.ppermute(other, 'sec', partner)).astype(jnp.bfloat16)  13.8 us
    ppermute x1, starting transfers between devices, shards(): sensitivity = partial_sens + lax.ppermute(partial_sens, 'sec', partner)  9.26 us
    pallas_call x1, Pallas kernels, heat_phase(): pl.pallas_call(heat_kernel, out_shape=(out, out, out), in_specs=[smem, sm...  8.86 us
    ppermute x1, starting transfers between devices, shards(): lax.ppermute(column(slice(width, 2 * width)), 'gy', [(i, i + 1) for i in...  4.55 us
    dot_general x3, matrix products, edges(): jnp.einsum('czxy,ye->czxe', part, picks, precision=lax.Precision.HIGHEST)  3.83 us
  transfers between devices with their start and end apart: 6, of which 4 were waited for; matrix products, arithmetic and copies ran while one was open for 4% of the time, Pallas kernels for 0%

profile of v19, /device:TPU:96, one launch (start us, length us, event | category | flops | bytes accessed | tf_op | source)
XLA Modules:
  0.0 137.4 jit_solution(13771140267323804809)
XLA Ops:
  0.6 1.0 subtract_bitcast_fusion
  1.7 1.4 %pad_maximum_fusion.tile_ref = f32[6,16,16,256]{3,2,1,0:T(8,128)S(1)} fusion(f32[1,16,16,256]{3,2,1,0:T(8,128)S(1)} %subtract_bitcast_fusion, f32[2,16,16,256]{3,2,1,0:T(8,128)} %param.13, f32[1,16,16,256]{3,2,1,0:T(8,128)} %bitcast.25, f32[2,16,16,256]{3,2,1,0:T(8,128)} %param.10), kind=kLoop, calls=%fused_computation | loop fusion | flops 1179648 | bytes 3145728 | tf_op jit(solution)/shard_map/concatenate | solution.py:262
  3.1 0.6 convolution_bitcast_fusion
  4.0 1.9 %collective-permute-start = (f32[6,16,2,256]{3,2,1,0:T(2,128)S(1)}, f32[6,16,2,256]{3,2,1,0:T(2,128)S(1)}, u32[]{:S(2)}, u32[]{:S(2)}) collective-permute-start(f32[6,16,2,256]{3,2,1,0:T(2,128)S(1)} %get-tuple-element.13), channel_id=1, source_target_pairs={{16,0},{32,16},{48,32},{64,48},{80,64},{96,80},{112,96},{128,112},... | collective-permute-start | bytes 589832 | tf_op jit(solution)/shard_map/ppermute | solution.py:272
  5.9 2.4 %collective-permute-start.1 = (f32[6,16,2,256]{3,2,1,0:T(2,128)S(1)}, f32[6,16,2,256]{3,2,1,0:T(2,128)S(1)}, u32[]{:S(2)}, u32[]{:S(2)}) collective-permute-start(f32[6,16,2,256]{3,2,1,0:T(2,128)S(1)} %get-tuple-element.12), channel_id=1, source_target_pairs={{0,16},{16,32},{32,48},{48,64},{64,80},{80,96},{96,112},{112,128},... | collective-permute-start | bytes 589832 | tf_op jit(solution)/shard_map/ppermute | solution.py:273
  8.3 2.9 %fusion.10 = f32[6,16,16,4]{2,3,1,0:T(4,128)S(1)} fusion(f32[6,16,16,256]{3,2,1,0:T(8,128)S(1)} %pad_maximum_fusion.tile_ref, s32[4]{0:T(128)S(1)} %get-tuple-element.16), kind=kOutput, calls=%fused_computation.19 | convolution fusion | flops 18875392 | bytes 1597456 | tf_op jit(solution)/shard_map/czxy,ye->czxe/dot_general | solution.py:281
  11.3 0.5 fusion.2
  12.0 0.9 collective-permute-done.1.before_ref
  13.8 1.3 collective-permute-start.2
  15.1 4.6 %collective-permute-start.3 = (f32[6,16,24,2]{2,1,3,0:T(8,128)S(1)}, f32[6,16,24,2]{2,1,3,0:T(8,128)S(1)}, u32[]{:S(2)}, u32[]{:S(2)}) collective-permute-start(f32[6,16,24,2]{2,1,3,0:T(8,128)S(1)} %get-tuple-element.15), channel_id=1, source_target_pairs={{0,1},{1,2},{2,3},{3,4},{4,5},{5,6},{6,7},{7,8},{8,9},{9,10},{10,1... | collective-permute-start | bytes 55304 | tf_op jit(solution)/shard_map/ppermute | solution.py:293
  19.7 0.7 copy.25.wells_ref
  20.4 0.6 copy.23
  21.1 1.1 collective-permute-done.3
  22.2 0.6 copy.24
  22.9 1.4 %pad_maximum_fusion.1.side_ref = f32[6,16,24,128]{3,2,1,0:T(8,128)} fusion(f32[6,16,24,2]{3,2,1,0:T(8,128)S(1)} %copy.24, f32[6,16,24,2]{3,2,1,0:T(8,128)S(1)} %copy.23, f32[128]{0:T(128)S(1)} %pad.1.clone), kind=kLoop, calls=%fused_computation.2 | loop fusion | flops 589824 | bytes 1217024 | tf_op jit(solution)/shard_map/concatenate | solution.py:289
  24.2 8.9 %shard_map.113 = (f32[16,16,256]{2,1,0:T(8,128)}, f32[16,16,256]{2,1,0:T(8,128)}, f32[16,16,256]{2,1,0:T(8,128)}) custom-call(s32[2,8,3]{2,1,0:T(8,128)} %copy.25.wells_ref, f32[2,2,8]{2,1,0:T(2,128)} %misfit_ref.1, f32[6,16,16,256]{3,2,1,0:T(8,128)} %copy-done, f32[6,16,2,256]{3,2,1,0:T(2,128)} %copy-done.1, f32[6,16,2,256]{3,2,1,0:T(2,128)} %copy-done.2, ...), custom_call_target="tpu_custom_call" | custom-call | tf_op jit(solution)/shard_map/pallas_call | solution.py:179
  33.1 13.8 %collective-permute-start.4 = (f32[16,16,256]{2,1,0:T(8,128)}, f32[16,16,256]{2,1,0:T(8,128)S(1)}, u32[]{:S(2)}, u32[]{:S(2)}) collective-permute-start(f32[16,16,256]{2,1,0:T(8,128)} %get-tuple-element.8), channel_id=1, source_target_pairs={{0,256},{256,0},{1,257},{257,1},{2,258},{258,2},{3,259},{259,3},{4... | collective-permute-start | bytes 786440 | tf_op jit(solution)/shard_map/ppermute | solution.py:301
  46.9 22.2 %collective-permute-done.4 = f32[16,16,256]{2,1,0:T(8,128)S(1)} collective-permute-done((f32[16,16,256]{2,1,0:T(8,128)}, f32[16,16,256]{2,1,0:T(8,128)S(1)}, u32[]{:S(2)}, u32[]{:S(2)}) %collective-permute-start.4) | collective-permute-done | bytes 262176 | tf_op jit(solution)/shard_map/ppermute | solution.py:301
  69.1 1.0 add_convert_fusion
  70.3 38.2 %all_to_all.5 = bf16[16,16,16,256]{3,2,1,0:T(8,128)(2,1)} all-to-all(bf16[16,16,16,256]{3,2,1,0:T(8,128)(2,1)S(1)} %broadcast_in_dim.26), channel_id=1, replica_groups=mesh['sec'=2,'gx'=16,'gy'=16] {'gy'}, dimensions={0} | all-to-all | bytes 4194304 | tf_op jit(solution)/shard_map/all_to_all | solution.py:305
  108.5 3.0 %shard_map.114 = (f32[256,256]{1,0:T(8,128)}, f32[256,256]{1,0:T(8,128)}) custom-call(s32[2,7]{1,0:T(2,128)} %cols_ref.1, bf16[16,256,256]{2,1,0:T(8,128)(2,1)} %bitcast.24, bf16[2,7,128,128]{3,2,1,0:T(8,128)(2,1)} %blocks_ref.1, f32[256,256]{1,0:T(8,128)} %bitcast.28, bf16[256,256]{1,0:T(8,128)(2,1)} %bitcast.29), custom_call_target="tpu_custom_call" | custom-call | flops 117440512 | bytes 3473408 | tf_op jit(solution)/shard_map/pallas_call | solution.py:232
  111.5 9.3 %collective-permute-start.5 = (f32[16,16,256]{2,1,0:T(8,128)}, f32[16,16,256]{2,1,0:T(8,128)S(1)}, u32[]{:S(2)}, u32[]{:S(2)}) collective-permute-start(f32[16,16,256]{2,1,0:T(8,128)} %bitcast.26), channel_id=1, source_target_pairs={{0,256},{256,0},{1,257},{257,1},{2,258},{258,2},{3,259},{259,3},{4... | collective-permute-start | bytes 786440 | tf_op jit(solution)/shard_map/ppermute | solution.py:316
  120.7 15.0 %collective-permute-done.5 = f32[16,16,256]{2,1,0:T(8,128)S(1)} collective-permute-done((f32[16,16,256]{2,1,0:T(8,128)}, f32[16,16,256]{2,1,0:T(8,128)S(1)}, u32[]{:S(2)}, u32[]{:S(2)}) %collective-permute-start.5) | collective-permute-done | bytes 262176 | tf_op jit(solution)/shard_map/ppermute | solution.py:316
  135.7 1.7 %add.15 = f32[16,16,256]{2,1,0:T(8,128)} add(f32[16,16,256]{2,1,0:T(8,128)} %bitcast.27, f32[16,16,256]{2,1,0:T(8,128)S(1)} %collective-permute-done.5) | non-fusion elementwise | flops 65536 | bytes 786432 | tf_op jit(solution)/shard_map/add | solution.py:316
  (25 shorter events, 1.8 us)
Async XLA Ops:
  3.1 8.1 %copy-start = (f32[6,16,16,256]{3,2,1,0:T(8,128)}, f32[6,16,16,256]{3,2,1,0:T(8,128)S(1)}, u32[]{:S(2)}) copy-start(f32[6,16,16,256]{3,2,1,0:T(8,128)S(1)} %pad_maximum_fusion.tile_ref) | copy-start | bytes 4718596
  4.0 7.3 %collective-permute-start = (f32[6,16,2,256]{3,2,1,0:T(2,128)S(1)}, f32[6,16,2,256]{3,2,1,0:T(2,128)S(1)}, u32[]{:S(2)}, u32[]{:S(2)}) collective-permute-start(f32[6,16,2,256]{3,2,1,0:T(2,128)S(1)} %get-tuple-element.13), channel_id=1, source_target_pairs={{16,0},{32,16},{48,32},{64,48},{80,64},{96,80},{112,96},{128,112},... | collective-permute-start | bytes 589832 | tf_op jit(solution)/shard_map/ppermute | solution.py:272
  5.9 7.0 %collective-permute-start.1 = (f32[6,16,2,256]{3,2,1,0:T(2,128)S(1)}, f32[6,16,2,256]{3,2,1,0:T(2,128)S(1)}, u32[]{:S(2)}, u32[]{:S(2)}) collective-permute-start(f32[6,16,2,256]{3,2,1,0:T(2,128)S(1)} %get-tuple-element.12), channel_id=1, source_target_pairs={{0,16},{16,32},{32,48},{48,64},{64,80},{80,96},{96,112},{112,128},... | collective-permute-start | bytes 589832 | tf_op jit(solution)/shard_map/ppermute | solution.py:273
  11.2 8.6 %copy-start.3 = (s32[2,8,3]{1,0,2:T(2,128)S(1)}, s32[2,8,3]{1,0,2:T(2,128)}, u32[]{:S(2)}) copy-start(s32[2,8,3]{1,0,2:T(2,128)} %param.15) | copy-start | bytes 580
  11.3 9.8 %copy-start.1 = (f32[6,16,2,256]{3,2,1,0:T(2,128)}, f32[6,16,2,256]{3,2,1,0:T(2,128)S(1)}, u32[]{:S(2)}) copy-start(f32[6,16,2,256]{3,2,1,0:T(2,128)S(1)} %collective-permute-done.after_ref) | copy-start | bytes 589828
  12.9 10.0 %copy-start.2 = (f32[6,16,2,256]{3,2,1,0:T(2,128)}, f32[6,16,2,256]{3,2,1,0:T(2,128)S(1)}, u32[]{:S(2)}) copy-start(f32[6,16,2,256]{3,2,1,0:T(2,128)S(1)} %collective-permute-done.1.before_ref) | copy-start | bytes 589828
  13.8 6.7 %collective-permute-start.2 = (f32[6,16,24,2]{2,1,3,0:T(8,128)S(1)}, f32[6,16,24,2]{2,1,3,0:T(8,128)S(1)}, u32[]{:S(2)}, u32[]{:S(2)}) collective-permute-start(f32[6,16,24,2]{2,1,3,0:T(8,128)S(1)} %get-tuple-element.14), channel_id=1, source_target_pairs={{1,0},{2,1},{3,2},{4,3},{5,4},{6,5},{7,6},{8,7},{9,8},{10,9},{11,1... | collective-permute-start | bytes 55304 | tf_op jit(solution)/shard_map/ppermute | solution.py:291
  15.1 7.1 %collective-permute-start.3 = (f32[6,16,24,2]{2,1,3,0:T(8,128)S(1)}, f32[6,16,24,2]{2,1,3,0:T(8,128)S(1)}, u32[]{:S(2)}, u32[]{:S(2)}) collective-permute-start(f32[6,16,24,2]{2,1,3,0:T(8,128)S(1)} %get-tuple-element.15), channel_id=1, source_target_pairs={{0,1},{1,2},{2,3},{3,4},{4,5},{5,6},{6,7},{7,8},{8,9},{9,10},{10,1... | collective-permute-start | bytes 55304 | tf_op jit(solution)/shard_map/ppermute | solution.py:293
  33.1 36.0 %collective-permute-start.4 = (f32[16,16,256]{2,1,0:T(8,128)}, f32[16,16,256]{2,1,0:T(8,128)S(1)}, u32[]{:S(2)}, u32[]{:S(2)}) collective-permute-start(f32[16,16,256]{2,1,0:T(8,128)} %get-tuple-element.8), channel_id=1, source_target_pairs={{0,256},{256,0},{1,257},{257,1},{2,258},{258,2},{3,259},{259,3},{4... | collective-permute-start | bytes 786440 | tf_op jit(solution)/shard_map/ppermute | solution.py:301
  111.5 24.3 %collective-permute-start.5 = (f32[16,16,256]{2,1,0:T(8,128)}, f32[16,16,256]{2,1,0:T(8,128)S(1)}, u32[]{:S(2)}, u32[]{:S(2)}) collective-permute-start(f32[16,16,256]{2,1,0:T(8,128)} %bitcast.26), channel_id=1, source_target_pairs={{0,256},{256,0},{1,257},{257,1},{2,258},{258,2},{3,259},{259,3},{4... | collective-permute-start | bytes 786440 | tf_op jit(solution)/shard_map/ppermute | solution.py:316
